TPU v7x, 32 devices: a whole 2x2x4 slice. The times are simulated.
32 devices in a mesh: tm: 8 (over z, y), head: 4 (over x, core).
Axes of the slice: x: 2, y: 2, z: 4, core: 2. Of those that a mesh axis runs over, the one named last changes fastest.
Arguments:
- queries: bfloat16 [6144, 1536], P('tm', 'head'), may hold values from -6 to 6
- key_rows: bfloat16 [6144, 1536], P('tm', 'head'), may hold values from -6 to 6
- value_rows: bfloat16 [6144, 1536], P('tm', 'head'), may hold values from -6 to 6
- grad_out: bfloat16 [6144, 3072], P('tm', 'head'), may hold values from -192 to 192
- w_out: bfloat16 [1536, 3072], P('head', 'tm'), may hold values from -0.109375 to 0.109375
Outputs:
- grad_queries: bfloat16 [6144, 1536], P('tm', 'head')
- grad_keys: bfloat16 [6144, 1536], P('tm', 'head')
- grad_values: bfloat16 [6144, 1536], P('tm', 'head')
All inputs are finite; a program needn't handle non-finite values.
Results may differ from a plain program's by a relative error of at most 0.0081.
Values may be sent and summed in bfloat16 or wider, within the bound.
No kernel may reach another device: no remote copies, remote signals or barrier semaphores. Data moves between devices by JAX's collectives and lax.ppermute only.
A program may use at most 128 MiB of HBM per device.

v0:
```python
import math

import jax
import jax.numpy as jnp
from jax import lax
from jax.sharding import PartitionSpec as P

HD = 128
TILE_T = 6
TILE_H = 8
TILE_W = 8
VT = 8


def passed_along(block, axis, distance):
    devices = range(lax.axis_size(axis))
    route = [(i - distance, i) for i in devices if i - distance in devices]
    return lax.ppermute(block, axis, route)


def tile_range(index, count):
    return (max(index - 1, 0), min(index + 1, count - 1))


def local(queries, key_rows, value_rows, grad_out, w_out):
    token_count, local_width = queries.shape
    head_count = local_width // HD
    tile_size = TILE_T * TILE_H * TILE_W
    tile_count = token_count // tile_size
    inverse_root = 1.0 / math.sqrt(HD)
    video_place = lax.axis_index("tm") % VT
    flags = (video_place > 0, video_place >= 0, video_place < VT - 1)
    full_grad = lax.all_gather(grad_out, "head", axis=1, tiled=True)
    attn_sum = jnp.einsum(
        "td,hd->th",
        full_grad,
        lax.all_gather(w_out, "tm", axis=1, tiled=True),
        preferred_element_type=jnp.float32,
    )
    attn_grad = attn_sum.astype(jnp.bfloat16)
    before_keys, before_values = passed_along((key_rows, value_rows), "tm", 1)
    after_keys, after_values = passed_along((key_rows, value_rows), "tm", -1)
    slab_keys = (before_keys, key_rows, after_keys)
    slab_values = (before_values, value_rows, after_values)
    zero_tile = jnp.zeros((tile_size, local_width), jnp.float32)
    key_sums = [[zero_tile] * tile_count for other in range(3)]
    value_sums = [[zero_tile] * tile_count for other in range(3)]
    query_grads = []
    for tile_index in range(tile_count):
        lower, upper = tile_range(tile_index, tile_count)
        width_rows = (upper - lower + 1) * tile_size
        key_block = jnp.concatenate([part for part in slab_keys], 0)
        key_block = key_block.reshape(3 * width_rows, head_count, HD)
        value_block = jnp.concatenate([part for part in slab_values], 0)
        value_block = value_block.reshape(3 * width_rows, head_count, HD)
        key_mask = jnp.concatenate([jnp.broadcast_to(flag, (width_rows,)) for flag in flags], 0)
        query_tile = queries[tile_index * tile_size : (tile_index + 1) * tile_size].reshape(
            tile_size, head_count, HD
        )
        grad_tile = attn_grad[tile_index * tile_size : (tile_index + 1) * tile_size].reshape(
            tile_size, head_count, HD
        )
        scores = (
            jnp.einsum("qhd,khd->hqk", query_tile, key_block, preferred_element_type=jnp.float32)
            * inverse_root
        )
        scores = jnp.where(key_mask[None, None, :], scores, -jnp.inf)
        row_peak = jnp.max(scores, axis=2, keepdims=True)
        weights = jnp.exp(scores - row_peak)
        row_total = jnp.sum(weights, axis=2, keepdims=True)
        softmax_rows = weights / row_total
        softmax_grad = jnp.einsum(
            "qhd,khd->hqk", grad_tile, value_block, preferred_element_type=jnp.float32
        )
        row_inner = jnp.sum(softmax_rows * softmax_grad, axis=2, keepdims=True)
        score_grad = (softmax_rows * (softmax_grad - row_inner)).astype(jnp.bfloat16)
        softmax_low = softmax_rows.astype(jnp.bfloat16)
        grad_query = (
            jnp.einsum("hqk,khd->qhd", score_grad, key_block, preferred_element_type=jnp.float32)
            * inverse_root
        )
        query_grads.append(grad_query.reshape(tile_size, local_width).astype(jnp.bfloat16))
        kept = (0, 1, 2)
        key_part = (
            jnp.einsum("hqk,qhd->khd", score_grad, query_tile, preferred_element_type=jnp.float32)
            * inverse_root
        )
        key_part = key_part.reshape(len(kept) * width_rows, local_width)
        value_part = jnp.einsum(
            "hqk,qhd->khd", softmax_low, grad_tile, preferred_element_type=jnp.float32
        )
        value_part = value_part.reshape(len(kept) * width_rows, local_width)
        for position, slab_index in enumerate(kept):
            for neighbour in range(lower, upper + 1):
                offset = position * width_rows + (neighbour - lower) * tile_size
                key_sums[slab_index][neighbour] = (
                    key_sums[slab_index][neighbour] + key_part[offset : offset + tile_size]
                )
                value_sums[slab_index][neighbour] = (
                    value_sums[slab_index][neighbour] + value_part[offset : offset + tile_size]
                )
    own_keys = jnp.concatenate(key_sums[1], 0)
    own_values = jnp.concatenate(value_sums[1], 0)
    later_keys, later_values = (
        passed_along(jnp.concatenate(key_sums[0], 0).astype(jnp.bfloat16), "tm", -1).astype(
            jnp.float32
        ),
        passed_along(jnp.concatenate(value_sums[0], 0).astype(jnp.bfloat16), "tm", -1).astype(
            jnp.float32
        ),
    )
    earlier_keys, earlier_values = (
        passed_along(jnp.concatenate(key_sums[2], 0).astype(jnp.bfloat16), "tm", 1).astype(
            jnp.float32
        ),
        passed_along(jnp.concatenate(value_sums[2], 0).astype(jnp.bfloat16), "tm", 1).astype(
            jnp.float32
        ),
    )
    grad_keys = own_keys + later_keys + earlier_keys
    grad_values = own_values + later_values + earlier_values
    grad_queries = jnp.concatenate(query_grads, 0)
    return (grad_queries, grad_keys.astype(jnp.bfloat16), grad_values.astype(jnp.bfloat16))


def solution(mesh):
    placed = (P("tm", "head"), P("tm", "head"), P("tm", "head"), P("tm", "head"), P("head", "tm"))
    return jax.shard_map(
        local,
        mesh=mesh,
        in_specs=placed,
        out_specs=(P("tm", "head"), P("tm", "head"), P("tm", "head")),
        check_vma=False,
    )
```

profile of v0, /device:TPU:0, one launch (start us, length us, event | category | flops | bytes accessed | tf_op | source)
XLA Modules:
  0.0 249.1 jit_solution(441162464719006397)
XLA Ops:
  8.7 1.3 copy.44
  10.0 1.3 collective-permute-start.3
  11.3 6.4 %collective-permute-start.2 = (bf16[768,384]{0,1:T(8,128)(2,1)S(1)}, bf16[768,384]{0,1:T(8,128)(2,1)}, u32[]{:S(2)}, u32[]{:S(2)}) collective-permute-start(bf16[768,384]{0,1:T(8,128)(2,1)S(1)} %copy.44), channel_id=1, source_target_pairs={{0,4},{4,8},{8,12},{12,16},{16,20},{20,24},{24,28},{1,5},{5,9},{9,... | collective-permute-start | bytes 1769480 | tf_op jit(solution)/shard_map/ppermute | solution.py:18
  17.6 1.3 copy.38
  18.9 1.3 collective-permute-start.1
  20.2 5.4 %collective-permute-start = (bf16[768,384]{0,1:T(8,128)(2,1)S(1)}, bf16[768,384]{0,1:T(8,128)(2,1)}, u32[]{:S(2)}, u32[]{:S(2)}) collective-permute-start(bf16[768,384]{0,1:T(8,128)(2,1)S(1)} %copy.38), channel_id=1, source_target_pairs={{0,4},{4,8},{8,12},{12,16},{16,20},{20,24},{24,28},{1,5},{5,9},{9,... | collective-permute-start | bytes 1769480 | tf_op jit(solution)/shard_map/ppermute | solution.py:18
  26.3 5.9 %collective-permute-done.3 = bf16[768,384]{0,1:T(8,128)(2,1)S(1)} collective-permute-done((bf16[768,384]{0,1:T(8,128)(2,1)S(1)}, bf16[768,384]{0,1:T(8,128)(2,1)S(1)}, u32[]{:S(2)}, u32[]{:S(2)}) %collective-permute-start.3) | collective-permute-done | bytes 589856 | tf_op jit(solution)/shard_map/ppermute | solution.py:18
  32.2 24.7 %collective-permute-done.2 = bf16[768,384]{0,1:T(8,128)(2,1)} collective-permute-done((bf16[768,384]{0,1:T(8,128)(2,1)S(1)}, bf16[768,384]{0,1:T(8,128)(2,1)}, u32[]{:S(2)}, u32[]{:S(2)}) %collective-permute-start.2) | collective-permute-done | bytes 589856 | tf_op jit(solution)/shard_map/ppermute | solution.py:18
  56.9 2.5 pad_maximum_fusion.1
  60.2 11.8 %collective-permute-done = bf16[768,384]{0,1:T(8,128)(2,1)} collective-permute-done((bf16[768,384]{0,1:T(8,128)(2,1)S(1)}, bf16[768,384]{0,1:T(8,128)(2,1)}, u32[]{:S(2)}, u32[]{:S(2)}) %collective-permute-start) | collective-permute-done | bytes 589856 | tf_op jit(solution)/shard_map/ppermute | solution.py:18
  72.0 1.4 pad_maximum_fusion
  73.4 7.7 %fusion.52 = (f32[3,384]{1,0:T(4,128)S(1)}, f32[3,384,2304]{1,2,0:T(8,128)}) fusion(pred[2304]{0:T(1024)(128)(4,1)S(1)} %pad_add_fusion, bf16[2304,3,128]{0,2,1:T(8,128)(2,1)S(1)} %bitcast.78, bf16[384,3,128]{0,2,1:T(8,128)(2,1)S(1)} %bitcast.95), kind=kOutput, calls=%fused_computation.81 | convolution fusion | flops 690096384 | bytes 12688128 | tf_op jit(solution)/shard_map/sub | solution.py:69
  81.0 7.8 %fusion.53 = (f32[3,384]{1,0:T(4,128)S(1)}, f32[3,384,2304]{1,2,0:T(8,128)}) fusion(pred[2304]{0:T(1024)(128)(4,1)S(1)} %pad_add_fusion, bf16[2304,3,128]{0,2,1:T(8,128)(2,1)S(1)} %bitcast.79, bf16[384,3,128]{0,2,1:T(8,128)(2,1)S(1)} %bitcast.92), kind=kOutput, calls=%fused_computation.82 | convolution fusion | flops 690096384 | bytes 12688128 | tf_op jit(solution)/shard_map/sub | solution.py:69
  88.9 3.6 %all-gather.5.cloned.1.call-done = bf16[384,3072]{1,0:T(8,128)(2,1)} async-done(((bf16[384,384]{1,0:T(8,128)(2,1)}), bf16[384,3072]{1,0:T(8,128)(2,1)}) %all-gather.5.cloned.1.call-update) | async-done | bytes 2359312 | tf_op jit(solution)/shard_map/all_gather | solution.py:37
  92.5 39.1 %all-gather.3.cloned.1.call-done = bf16[768,3072]{1,0:T(8,128)(2,1)} async-done(((bf16[768,768]{1,0:T(8,128)(2,1)}), bf16[768,3072]{1,0:T(8,128)(2,1)}) %all-gather.3.cloned.1.call-update) | async-done | bytes 4718608 | tf_op jit(solution)/shard_map/all_gather | solution.py:33
  131.6 5.1 %convolution_convert_fusion = bf16[768,384]{0,1:T(8,128)(2,1)S(1)} fusion(bf16[768,3072]{1,0:T(8,128)(2,1)} %all-gather.3.cloned.1.call-done, bf16[384,3072]{1,0:T(8,128)(2,1)} %all-gather.5.cloned.1.call-done), kind=kOutput, calls=%fused_computation.36 | convolution fusion | flops 1812234240 | bytes 7667712 | tf_op jit(solution)/shard_map/td,hd->th/dot_general | solution.py:34
  136.8 5.8 %fusion.25 = f32[2304,3,128]{0,2,1:T(8,128)S(1)} fusion(bf16[384,3,128]{0,2,1:T(8,128)(2,1)S(1)} %bitcast.108, f32[3,384,2304]{1,2,0:T(8,128)} %get-tuple-element.20, f32[3,384]{1,0:T(4,128)S(1)} %get-tuple-element.19), kind=kOutput, calls=%fused_computation.33 | convolution fusion | flops 684785664 | bytes 14455296 | tf_op jit(solution)/shard_map/hqk,qhd->khd/dot_general | solution.py:89
  144.3 5.0 %multiply_reduce_fusion = (f32[3,384]{1,0:T(4,128)S(1)}, f32[3,384,2304]{1,2,0:T(8,128)}) fusion(f32[3,384,2304]{1,2,0:T(8,128)S(1)} %bitcast.85, f32[3,384]{1,0:T(4,128)S(1)} %get-tuple-element.19, bf16[384,3,128]{0,2,1:T(8,128)(2,1)S(1)} %bitcast.109, bf16[2304,3,128]{0,2,1:T(8,128)(2,1)S(1)} %bitcast.90), kind=kOutput, calls=%fused_computation.11 | convolution fusion | flops 687438720 | bytes 23307264 | tf_op jit(solution)/shard_map/qhd,khd->hqk/dot_general | solution.py:72
  149.4 8.3 %multiply_convert_fusion = bf16[3,384,2304]{1,2,0:T(8,128)(2,1)S(1)} fusion(f32[3,384,2304]{1,2,0:T(8,128)} %get-tuple-element.22, f32[3,384]{1,0:T(4,128)S(1)} %get-tuple-element.21, f32[3,384,2304]{1,2,0:T(8,128)} %get-tuple-element.20, f32[3,384]{1,0:T(4,128)S(1)} %get-tuple-element.19), kind=kLoop, calls=%fused_computation.10 | loop fusion | flops 10616832 | bytes 26551296 | tf_op jit(solution)/shard_map/convert_element_type | solution.py:76
  157.7 1.9 fusion.29
  159.5 3.4 %fusion.21 = f32[2304,3,128]{0,2,1:T(8,128)} fusion(bf16[3,384,2304]{1,2,0:T(8,128)(2,1)S(1)} %multiply_convert_fusion, bf16[384,3,128]{0,2,1:T(8,128)(2,1)S(1)} %bitcast.96), kind=kOutput, calls=%fused_computation.31 | convolution fusion | flops 680361984 | bytes 9142272 | tf_op jit(solution)/shard_map/hqk,qhd->khd/dot_general | solution.py:85
  162.9 1.6 fusion.22
  164.5 5.0 %multiply_reduce_fusion.1 = (f32[3,384]{1,0:T(4,128)S(1)}, f32[3,384,2304]{1,2,0:T(8,128)}) fusion(f32[3,384,2304]{1,2,0:T(8,128)S(1)} %bitcast.83, f32[3,384]{1,0:T(4,128)S(1)} %get-tuple-element.23, bf16[384,3,128]{0,2,1:T(8,128)(2,1)S(1)} %bitcast.107, bf16[2304,3,128]{0,2,1:T(8,128)(2,1)S(1)} %bitcast.91), kind=kOutput, calls=%fused_computation.14 | convolution fusion | flops 687438720 | bytes 23307264 | tf_op jit(solution)/shard_map/qhd,khd->hqk/dot_general | solution.py:72
  170.7 1.9 copy.74
  172.6 1.8 copy.77
  174.4 1.8 copy.76
  177.2 2.0 pad_maximum_fusion.5
  179.2 1.3 collective-permute-start.6
  180.5 1.9 pad_maximum_fusion.6
  182.4 5.4 %collective-permute-start.7 = (bf16[768,384]{1,0:T(8,128)(2,1)}, bf16[768,384]{1,0:T(8,128)(2,1)}, u32[]{:S(2)}, u32[]{:S(2)}) collective-permute-start(bf16[768,384]{1,0:T(8,128)(2,1)} %pad_maximum_fusion.6), channel_id=1, source_target_pairs={{0,4},{4,8},{8,12},{12,16},{16,20},{20,24},{24,28},{1,5},{5,9},{9,... | collective-permute-start | bytes 1769480 | tf_op jit(solution)/shard_map/ppermute | solution.py:18
  187.7 7.9 %multiply_convert_fusion.1 = bf16[3,384,2304]{1,2,0:T(8,128)(2,1)S(1)} fusion(f32[3,384,2304]{1,2,0:T(8,128)} %get-tuple-element.26, f32[3,384]{1,0:T(4,128)S(1)} %get-tuple-element.25, f32[3,384,2304]{1,2,0:T(8,128)} %get-tuple-element.24, f32[3,384]{1,0:T(4,128)S(1)} %get-tuple-element.23), kind=kLoop, calls=%fused_computation.13 | loop fusion | flops 10616832 | bytes 26551296 | tf_op jit(solution)/shard_map/convert_element_type | solution.py:76
  195.7 1.6 fusion.20
  198.4 1.2 copy-done.1
  199.6 1.4 fusion.45
  201.0 1.9 copy.66
  202.8 1.9 copy.69
  204.7 1.9 copy.68
  206.5 1.8 copy.67
  208.4 1.9 pad_maximum_fusion.3
  210.3 1.3 collective-permute-start.4
  211.6 1.9 pad_maximum_fusion.4
  213.5 5.4 %collective-permute-start.5 = (bf16[768,384]{1,0:T(8,128)(2,1)}, bf16[768,384]{1,0:T(8,128)(2,1)}, u32[]{:S(2)}, u32[]{:S(2)}) collective-permute-start(bf16[768,384]{1,0:T(8,128)(2,1)} %pad_maximum_fusion.4), channel_id=1, source_target_pairs={{0,4},{4,8},{8,12},{12,16},{16,20},{20,24},{24,28},{1,5},{5,9},{9,... | collective-permute-start | bytes 1769480 | tf_op jit(solution)/shard_map/ppermute | solution.py:18
  218.9 4.3 %fusion.28 = bf16[3,128,384]{2,1,0:T(8,128)(2,1)} fusion(bf16[2304,3,128]{0,2,1:T(8,128)(2,1)S(1)} %bitcast.81, bf16[3,384,2304]{1,2,0:T(8,128)(2,1)} %copy-done), kind=kOutput, calls=%fused_computation.39 | convolution fusion | flops 679772160 | bytes 7372800 | tf_op jit(solution)/shard_map/hqk,khd->qhd/dot_general | solution.py:79
  223.2 1.9 copy.61
  227.3 1.8 pad_maximum_fusion.2
  229.1 2.2 fusion.33
  231.4 8.7 %collective-permute-done.5 = bf16[768,384]{1,0:T(8,128)(2,1)} collective-permute-done((bf16[768,384]{1,0:T(8,128)(2,1)}, bf16[768,384]{1,0:T(8,128)(2,1)}, u32[]{:S(2)}, u32[]{:S(2)}) %collective-permute-start.5) | collective-permute-done | bytes 589856 | tf_op jit(solution)/shard_map/ppermute | solution.py:18
  240.0 2.2 fusion.31
  (48 shorter events, 9.9 us)
Async XLA Ops:
  7.2 18.5 %copy-start.5 = (bf16[768,384]{1,0:T(8,128)(2,1)S(1)}, bf16[768,384]{1,0:T(8,128)(2,1)}, u32[]{:S(2)}) copy-start(bf16[768,384]{1,0:T(8,128)(2,1)} %param.5) | copy-start | bytes 1769476
  7.2 85.3 %all-gather.5.cloned.1.call-start = ((), (), s32[]{:S(2)}) async-start(), calls=%async_computation.1 | async-start | bytes 2654208 | tf_op jit(solution)/shard_map/all_gather | solution.py:37
  7.9 123.7 %all-gather.3.cloned.1.call-start = ((), (), s32[]{:S(2)}) async-start(), calls=%async_computation | async-start | bytes 5898240 | tf_op jit(solution)/shard_map/all_gather | solution.py:33
  10.0 22.2 %collective-permute-start.3 = (bf16[768,384]{0,1:T(8,128)(2,1)S(1)}, bf16[768,384]{0,1:T(8,128)(2,1)S(1)}, u32[]{:S(2)}, u32[]{:S(2)}) collective-permute-start(bf16[768,384]{0,1:T(8,128)(2,1)S(1)} %copy.44), channel_id=1, source_target_pairs={{4,0},{8,4},{12,8},{16,12},{20,16},{24,20},{28,24},{5,1},{9,5},{13... | collective-permute-start | bytes 1769480 | tf_op jit(solution)/shard_map/ppermute | solution.py:18
  11.3 45.6 %collective-permute-start.2 = (bf16[768,384]{0,1:T(8,128)(2,1)S(1)}, bf16[768,384]{0,1:T(8,128)(2,1)}, u32[]{:S(2)}, u32[]{:S(2)}) collective-permute-start(bf16[768,384]{0,1:T(8,128)(2,1)S(1)} %copy.44), channel_id=1, source_target_pairs={{0,4},{4,8},{8,12},{12,16},{16,20},{20,24},{24,28},{1,5},{5,9},{9,... | collective-permute-start | bytes 1769480 | tf_op jit(solution)/shard_map/ppermute | solution.py:18
  18.9 40.4 %collective-permute-start.1 = (bf16[768,384]{0,1:T(8,128)(2,1)S(1)}, bf16[768,384]{0,1:T(8,128)(2,1)S(1)}, u32[]{:S(2)}, u32[]{:S(2)}) collective-permute-start(bf16[768,384]{0,1:T(8,128)(2,1)S(1)} %copy.38), channel_id=1, source_target_pairs={{4,0},{8,4},{12,8},{16,12},{20,16},{24,20},{28,24},{5,1},{9,5},{13... | collective-permute-start | bytes 1769480 | tf_op jit(solution)/shard_map/ppermute | solution.py:18
  20.2 51.8 %collective-permute-start = (bf16[768,384]{0,1:T(8,128)(2,1)S(1)}, bf16[768,384]{0,1:T(8,128)(2,1)}, u32[]{:S(2)}, u32[]{:S(2)}) collective-permute-start(bf16[768,384]{0,1:T(8,128)(2,1)S(1)} %copy.38), channel_id=1, source_target_pairs={{0,4},{4,8},{8,12},{12,16},{16,20},{20,24},{24,28},{1,5},{5,9},{9,... | collective-permute-start | bytes 1769480 | tf_op jit(solution)/shard_map/ppermute | solution.py:18
  59.4 0.8 copy-start.4
  136.7 5.9 %slice-start.3 = ((s8[10616832]{0:T(1024)(128)(4,1)}), s8[4194304]{0:T(1024)(128)(4,1)S(1)}, s32[]{:S(2)}) async-start(s8[10616832]{0:T(1024)(128)(4,1)} %bitcast.84), calls=%async_computation.5 | async-start | bytes 8388608
  136.8 6.4 %slice-start.4 = ((s8[10616832]{0:T(1024)(128)(4,1)}), s8[4194304]{0:T(1024)(128)(4,1)S(1)}, s32[]{:S(2)}) async-start(s8[10616832]{0:T(1024)(128)(4,1)} %bitcast.84), calls=%async_computation.6 | async-start | bytes 8388608
  136.8 7.1 %slice-start.5 = ((s8[10616832]{0:T(1024)(128)(4,1)}), s8[2228224]{0:T(1024)(128)(4,1)S(1)}, s32[]{:S(2)}) async-start(s8[10616832]{0:T(1024)(128)(4,1)} %bitcast.84), calls=%async_computation.7 | async-start | bytes 4456448
  136.8 7.5 %copy-start.3 = (bf16[2304,384]{0,1:T(8,128)(2,1)S(1)}, bf16[2304,384]{0,1:T(8,128)(2,1)}, u32[]{:S(2)}) copy-start(bf16[2304,384]{0,1:T(8,128)(2,1)} %pad_maximum_fusion.1) | copy-start | bytes 5308420
  149.4 13.5 %slice-start = ((s8[10616832]{0:T(1024)(128)(4,1)}), s8[4194304]{0:T(1024)(128)(4,1)S(1)}, s32[]{:S(2)}) async-start(s8[10616832]{0:T(1024)(128)(4,1)} %bitcast.82), calls=%async_computation.2 | async-start | bytes 8388608
  149.4 13.5 %slice-start.1 = ((s8[10616832]{0:T(1024)(128)(4,1)}), s8[4194304]{0:T(1024)(128)(4,1)S(1)}, s32[]{:S(2)}) async-start(s8[10616832]{0:T(1024)(128)(4,1)} %bitcast.82), calls=%async_computation.3 | async-start | bytes 8388608
  157.7 5.2 %slice-start.2 = ((s8[10616832]{0:T(1024)(128)(4,1)}), s8[2228224]{0:T(1024)(128)(4,1)S(1)}, s32[]{:S(2)}) async-start(s8[10616832]{0:T(1024)(128)(4,1)} %bitcast.82), calls=%async_computation.4 | async-start | bytes 4456448
  179.2 49.9 %collective-permute-start.6 = (bf16[768,384]{1,0:T(8,128)(2,1)}, bf16[768,384]{1,0:T(8,128)(2,1)}, u32[]{:S(2)}, u32[]{:S(2)}) collective-permute-start(bf16[768,384]{1,0:T(8,128)(2,1)} %pad_maximum_fusion.5), channel_id=1, source_target_pairs={{4,0},{8,4},{12,8},{16,12},{20,16},{24,20},{28,24},{5,1},{9,5},{13... | collective-permute-start | bytes 1769480 | tf_op jit(solution)/shard_map/ppermute | solution.py:18
  182.4 46.7 %collective-permute-start.7 = (bf16[768,384]{1,0:T(8,128)(2,1)}, bf16[768,384]{1,0:T(8,128)(2,1)}, u32[]{:S(2)}, u32[]{:S(2)}) collective-permute-start(bf16[768,384]{1,0:T(8,128)(2,1)} %pad_maximum_fusion.6), channel_id=1, source_target_pairs={{0,4},{4,8},{8,12},{12,16},{16,20},{20,24},{24,28},{1,5},{5,9},{9,... | collective-permute-start | bytes 1769480 | tf_op jit(solution)/shard_map/ppermute | solution.py:18
  195.7 2.7 %copy-start = (bf16[3,384,2304]{1,2,0:T(8,128)(2,1)}, bf16[3,384,2304]{1,2,0:T(8,128)(2,1)S(1)}, u32[]{:S(2)}) copy-start(bf16[3,384,2304]{1,2,0:T(8,128)(2,1)S(1)} %multiply_convert_fusion.1) | copy-start | bytes 15925252
  195.7 3.9 %copy-start.1 = (f32[2304,3,128]{0,2,1:T(8,128)S(1)}, f32[2304,3,128]{0,2,1:T(8,128)}, u32[]{:S(2)}) copy-start(f32[2304,3,128]{0,2,1:T(8,128)} %fusion.21) | copy-start | bytes 10616836
  210.3 21.0 %collective-permute-start.4 = (bf16[768,384]{1,0:T(8,128)(2,1)}, bf16[768,384]{1,0:T(8,128)(2,1)}, u32[]{:S(2)}, u32[]{:S(2)}) collective-permute-start(bf16[768,384]{1,0:T(8,128)(2,1)} %pad_maximum_fusion.3), channel_id=1, source_target_pairs={{4,0},{8,4},{12,8},{16,12},{20,16},{24,20},{28,24},{5,1},{9,5},{13... | collective-permute-start | bytes 1769480 | tf_op jit(solution)/shard_map/ppermute | solution.py:18
  213.5 26.5 %collective-permute-start.5 = (bf16[768,384]{1,0:T(8,128)(2,1)}, bf16[768,384]{1,0:T(8,128)(2,1)}, u32[]{:S(2)}, u32[]{:S(2)}) collective-permute-start(bf16[768,384]{1,0:T(8,128)(2,1)} %pad_maximum_fusion.4), channel_id=1, source_target_pairs={{0,4},{4,8},{8,12},{12,16},{16,20},{20,24},{24,28},{1,5},{5,9},{9,... | collective-permute-start | bytes 1769480 | tf_op jit(solution)/shard_map/ppermute | solution.py:18
  223.2 3.6 %copy-start.2 = (f32[384,3,128]{0,2,1:T(8,128)S(1)}, f32[384,3,128]{0,2,1:T(8,128)}, u32[]{:S(2)}) copy-start(f32[384,3,128]{0,2,1:T(8,128)} %get-tuple-element.13) | copy-start | bytes 1769476
Sparse Core Ops, SparseCore 0:
  10.0 82.4 all-gather.4
  94.1 37.4 all-gather.2
where the time goes:
time: 250 us; the launch traced here: 249 us
  waiting for transfers between devices  95.2 us (38%)
  matrix products  49.2 us (20%)
  other arithmetic  36.7 us (15%)
  starting transfers between devices  27.8 us (11%)
  local copies, waits for them, and re-layouts  25.9 us (10%)
  between operations  14.3 us (6%)
    ppermute x8, waiting for transfers between devices, passed_along(): return lax.ppermute(block, axis, route)  51.1 us
    all_gather x1, waiting for transfers between devices, local(): full_grad = lax.all_gather(grad_out, 'head', axis=1, tiled=True)  39.1 us
    ppermute x8, starting transfers between devices, passed_along(): return lax.ppermute(block, axis, route)  27.7 us
    convert_element_type x2, other arithmetic, local(): (softmax_rows * (softmax_grad - row_inner)).astype(jnp.bfloat16)  16.2 us
    sub x2, matrix products, local(): weights = jnp.exp(scores - row_peak)  15.5 us
    dot_general x2, matrix products, local(): jnp.einsum('qhd,khd->hqk', grad_tile, value_block, preferred_element_type...  9.98 us
    add x6, local copies, waits for them, and re-layouts, local(): key_sums[slab_index][neighbour] + key_part[offset:offset + tile_size]  7.88 us
    unnamed x28, local copies, waits for them, and re-layouts  7.88 us
  transfers between devices with their start and end apart: 10, of which 6 were waited for; matrix products, arithmetic and copies ran while one was open for 24% of the time, Pallas kernels for 0%

commit v1 on v0

v1 whole, which is shorter than its diff:
```python
import functools
import math

import jax
import jax.numpy as jnp
from jax import lax
from jax.experimental import pallas as pl
from jax.experimental.pallas import tpu as pltpu
from jax.sharding import PartitionSpec as P

HD = 128
VT = 8
AXES = ("tm", "head")
NT = (((1,), (1,)), ((), ()))
TN = (((0,), (0,)), ((), ()))


def dot(a, b, dims=(((1,), (0,)), ((), ()))):
    return lax.dot_general(a, b, dims, preferred_element_type=jnp.float32)


def exchange(block, route, n_tm, n_head):
    pairs = []
    for t in range(n_tm):
        for h in range(n_head):
            to_t, to_h = route(t, h)
            pairs.append((t * n_head + h, to_t * n_head + to_h))
    return lax.ppermute(block, AXES, pairs)


def forward_kernel(heads, scale, flag_ref, q_ref, ko, vo, ks, vs, kz, vz, p_ref, o_ref, vt):
    rows = q_ref.shape[0]
    tile = p_ref.shape[2]
    keys = (ko, ks, kz)
    values = (vo, vs, vz)

    @pl.when(pl.program_id(1) == 0)
    def _():
        for i in range(3):
            vt[:, i * rows : (i + 1) * rows] = values[i][...].T

    start = pl.multiple_of(pl.program_id(1) * tile, tile)
    query = q_ref[pl.ds(start, tile), :]
    factor = scale * math.log2(math.e)
    scores = [dot(k[...], query, NT) for k in keys]
    peaks = [jnp.max(s, axis=0, keepdims=True) for s in scores]
    linked = flag_ref[0] > 0
    peak = jnp.maximum(
        jnp.maximum(peaks[0], peaks[1]), jnp.where(linked, peaks[2], -jnp.inf)
    )
    shift = peak * factor
    shifts = (shift, shift, jnp.where(linked, shift, jnp.inf))
    weights = [jnp.exp2(s * factor - m) for s, m in zip(scores, shifts)]
    total = sum(jnp.sum(w, axis=0, keepdims=True) for w in weights)
    inverse = 1.0 / total
    out = None
    for i in range(3):
        low = (weights[i] * inverse).astype(jnp.bfloat16)
        p_ref[0, i * rows : (i + 1) * rows, :] = low
        part = dot(vt[:, i * rows : (i + 1) * rows], low)
        out = part if out is None else out + part
    o_ref[...] = out


def forward(flag, query, own, side, far, heads, rows):
    tile = rows // 3
    scale = 1.0 / math.sqrt(HD)

    def key_spec():
        return pl.BlockSpec((rows, HD), lambda h, i: (0, h))

    def value_spec():
        return pl.BlockSpec((rows, HD), lambda h, i: (0, heads + h))

    return pl.pallas_call(
        functools.partial(forward_kernel, heads, scale),
        grid=(heads, 3),
        in_specs=[
            pl.BlockSpec(memory_space=pltpu.SMEM),
            key_spec(),
            key_spec(),
            value_spec(),
            key_spec(),
            value_spec(),
            key_spec(),
            value_spec(),
        ],
        out_specs=[
            pl.BlockSpec((1, 3 * rows, tile), lambda h, i: (h, 0, i)),
            pl.BlockSpec((HD, tile), lambda h, i: (h, i)),
        ],
        out_shape=[
            jax.ShapeDtypeStruct((heads, 3 * rows, rows), jnp.bfloat16),
            jax.ShapeDtypeStruct((heads * HD, rows), jnp.float32),
        ],
        scratch_shapes=[pltpu.VMEM((HD, 3 * rows), jnp.bfloat16)],
        name="forward_part",
    )(flag, query, own, own, side, side, far, far)


def backward_kernel(scale, p_ref, o_ref, g_ref, q_ref, ko, vo, ks, vs, kz, vz, dq, dko, dvo, dks, dvs, dkz, dvz):
    rows = q_ref.shape[0]
    step = 256
    grad = g_ref[...]
    query = q_ref[...]
    inner = jnp.sum(o_ref[...] * grad.astype(jnp.float32).T, axis=0, keepdims=True)
    total = None
    for i, (k, v, dk, dv) in enumerate(((kz, vz, dkz, dvz), (ks, vs, dks, dvs), (ko, vo, dko, dvo))):
        slot = 2 - i
        for first in range(0, rows, step):
            prob = p_ref[0, slot * rows + first : slot * rows + first + step, :]
            slope = dot(v[first : first + step, :], grad, NT)
            delta = (prob.astype(jnp.float32) * (slope - inner)).astype(jnp.bfloat16)
            dv[first : first + step, :] = dot(prob, grad).astype(dv.dtype)
            dk[first : first + step, :] = (dot(delta, query) * scale).astype(dk.dtype)
            part = dot(k[first : first + step, :], delta, TN)
            total = part if total is None else total + part
    dq[...] = (total * scale).T.astype(dq.dtype)


def backward(prob, out, grad, query, own, side, far, heads, rows):
    scale = 1.0 / math.sqrt(HD)

    def col():
        return pl.BlockSpec((rows, HD), lambda h: (0, h))

    def value_spec():
        return pl.BlockSpec((rows, HD), lambda h: (0, heads + h))

    width = heads * HD
    f32 = jax.ShapeDtypeStruct((rows, width), jnp.float32)
    bf16 = jax.ShapeDtypeStruct((rows, width), jnp.bfloat16)
    return pl.pallas_call(
        functools.partial(backward_kernel, scale),
        grid=(heads,),
        in_specs=[
            pl.BlockSpec((1, 3 * rows, rows), lambda h: (h, 0, 0)),
            pl.BlockSpec((HD, rows), lambda h: (h, 0)),
            col(),
            col(),
            col(),
            value_spec(),
            col(),
            value_spec(),
            col(),
            value_spec(),
        ],
        out_specs=[col()] * 7,
        out_shape=[bf16, f32, f32, bf16, bf16, bf16, bf16],
        name="backward_part",
    )(prob, out, grad, query, own, own, side, side, far, far)


def project_kernel(place_ref, g0, g1, g2, g3, *refs):
    shards = refs[:8]
    out_ref, gbuf, wbuf, gsem, wsem = refs[8:]
    z, y, h = place_ref[0], place_ref[1], place_ref[2]
    width = out_ref.shape[1]
    copies = []
    for m in range(4):
        for n in range(2):
            copies.append(
                pltpu.make_async_copy(
                    shards[2 * m + n], wbuf.at[z ^ m, y ^ n], wsem.at[2 * m + n]
                )
            )
    grads = [
        pltpu.make_async_copy(g, gbuf.at[m], gsem.at[m]) for m, g in enumerate((g0, g1, g2, g3))
    ]
    for c in copies:
        c.start()
    for c in grads:
        c.start()
    for c in copies:
        c.wait()
    total = None
    for m in range(4):
        grads[m].wait()
        for n in range(2):
            part = dot(gbuf[m, :, n * width : (n + 1) * width], wbuf[h ^ m, n], NT)
            total = part if total is None else total + part
    out_ref[...] = total.astype(out_ref.dtype)


def project(place, grads, shards, rows, width):
    anywhere = pl.BlockSpec(memory_space=pl.ANY)
    return pl.pallas_call(
        project_kernel,
        in_specs=[pl.BlockSpec(memory_space=pltpu.SMEM)] + [anywhere] * 12,
        out_specs=pl.BlockSpec(memory_space=pltpu.VMEM),
        out_shape=jax.ShapeDtypeStruct((rows, width), jnp.bfloat16),
        scratch_shapes=[
            pltpu.VMEM((4,) + grads[0].shape, jnp.bfloat16),
            pltpu.VMEM((4, 2) + shards[0].shape, jnp.bfloat16),
            pltpu.SemaphoreType.DMA((4,)),
            pltpu.SemaphoreType.DMA((8,)),
        ],
        name="project",
    )(place, *grads, *shards)


def local(n_tm, n_head, queries, key_rows, value_rows, grad_out, w_out):
    rows, width = queries.shape
    heads = width // HD
    t, h = lax.axis_index("tm"), lax.axis_index("head")
    y, c = t % 2, h % 2
    slab = t - y + c
    stays = y == c
    send = functools.partial(exchange, n_tm=n_tm, n_head=n_head)

    def turn_route(t, h):
        return (t, h ^ 2) if (t & 1) == (h & 1) else (t ^ 1, h ^ 1)

    def far_route(t, h):
        here = (t & ~1) + (h & 1)
        there = here + 1 if h & 1 else here - 1
        inside = 0 <= there < n_tm and there // VT == here // VT
        return (t + 2 if h & 1 else t - 2, h ^ 1) if inside else (t, h ^ 2)

    def side_route(t, h):
        return (t, h ^ 1)

    def turned(block):
        return jnp.where(stays, block, send(block, turn_route))

    place = slab % VT
    linked = jnp.where(c == 1, place < VT - 1, place > 0).astype(jnp.int32)

    own = turned(jnp.concatenate([key_rows, value_rows], 1))
    query = turned(queries)
    if n_head == 4 and n_tm == 2 * n_head:
        grads = [grad_out, send(grad_out, lambda t, h: (t, h ^ 1)), send(grad_out, lambda t, h: (t, h ^ 2))]
        grads.append(send(grads[2], lambda t, h: (t, h ^ 1)))
        w1 = send(w_out, lambda t, h: (t ^ 2, h))
        w2 = send(w_out, lambda t, h: (t ^ 4, h))
        w3 = send(w1, lambda t, h: (t ^ 4, h))
        shards = []
        for w in (w_out, w1, w2, w3):
            shards += [w, send(w, lambda t, h: (t ^ 1, h))]
        attn_grad = project(
            jnp.stack([t // 2, y, h]).astype(jnp.int32), grads, shards, rows, width
        )
    else:
        attn_grad = dot(
            lax.all_gather(grad_out, "head", axis=1, tiled=True),
            lax.all_gather(w_out, "tm", axis=1, tiled=True),
            NT,
        ).astype(jnp.bfloat16)
    side = send(own, side_route)
    far = send(own, far_route)
    prob, out = forward(linked[None], query, own, side, far, heads, rows)
    grad = turned(attn_grad)
    dq, dko, dvo, dks, dvs, dkz, dvz = backward(
        prob, out, grad, query, own, side, far, heads, rows
    )
    far_back = [send(d, far_route).astype(jnp.float32) for d in (dkz, dvz)]
    side_back = [send(d, side_route).astype(jnp.float32) for d in (dks, dvs)]
    linked_f = linked > 0
    sums = [
        (o + s + jnp.where(linked_f, f, 0.0)).astype(jnp.bfloat16)
        for o, s, f in zip((dko, dvo), side_back, far_back)
    ]
    return (turned(dq), turned(sums[0]), turned(sums[1]))


def solution(mesh):
    spec = P("tm", "head")
    body = functools.partial(local, mesh.shape["tm"], mesh.shape["head"])
    return jax.shard_map(
        body,
        mesh=mesh,
        in_specs=(spec, spec, spec, spec, P("head", "tm")),
        out_specs=(spec, spec, spec),
        check_vma=False,
    )
```

time: 250 us -> 146 us (0.58)
  matrix products: 49.2 us -> 0 us
  Pallas kernels: 0 us -> 40.7 us
  waiting for transfers between devices: 95.2 us -> 65.1 us
  other arithmetic: 36.7 us -> 8.12 us
  local copies, waits for them, and re-layouts: 25.9 us -> 3.43 us
  between operations: 14.3 us -> 0.77 us
    all_gather x2 -> x0, waiting for transfers between devices: 42.7 us -> none  [the longest x1 39.1 us: local(): full_grad = lax.all_gather(grad_out, 'head', axis=1, tiled=True)]
    pallas_call x0 -> x3, Pallas kernels: none -> 40.7 us  [the longest x1 18.2 us: forward(): pl.pallas_call(functools.partial(forward_kernel, heads, scale), grid=(hea...]
    dot_general x9 -> x0, matrix products: 33.7 us -> none  [the longest x2 9.98 us: local(): jnp.einsum('qhd,khd->hqk', grad_tile, value_block, preferred_element_type...]
    convert_element_type x4 -> x2, other arithmetic: 20.7 us -> 1.84 us  [local(): (o + s + jnp.where(linked_f, f, 0.0)).astype(jnp.bfloat16)]
    sub x2 -> x0, matrix products: 15.5 us -> none  [local(): weights = jnp.exp(scores - row_peak)]
    add x12 -> x0, local copies, waits for them, and re-layouts: 14.8 us -> none  [the longest x6 7.88 us: local(): key_sums[slab_index][neighbour] + key_part[offset:offset + tile_size]]
    ppermute x8 -> x22, waiting for transfers between devices: 51.1 us -> 65.1 us  [exchange(): return lax.ppermute(block, AXES, pairs)]
    concatenate x8 -> x0, other arithmetic: 13.5 us -> none  [the longest x1 2.49 us: local(): value_block = jnp.concatenate([part for part in slab_values], 0)]
  transfers between devices with their start and end apart: 10 -> 22, of which waited for: 6 -> 11; matrix products, arithmetic and copies ran while one was open for 24% -> 5% of each run, Pallas kernels for 0% -> 18%
where the time goes in v1:
time: 146 us; the launch traced here: 145 us
  waiting for transfers between devices  65.1 us (45%)
  Pallas kernels  40.7 us (28%)
  starting transfers between devices  27.2 us (19%)
  other arithmetic  8.12 us (6%)
  local copies, waits for them, and re-layouts  3.43 us (2%)
    ppermute x22, waiting for transfers between devices, exchange(): return lax.ppermute(block, AXES, pairs)  65.1 us
    ppermute x22, starting transfers between devices, exchange(): return lax.ppermute(block, AXES, pairs)  27.2 us
    pallas_call x1, Pallas kernels, forward(): pl.pallas_call(functools.partial(forward_kernel, heads, scale), grid=(hea...  18.2 us
    pallas_call x1, Pallas kernels, backward(): pl.pallas_call(functools.partial(backward_kernel, scale), grid=(heads,),...  14.5 us
    pallas_call x1, Pallas kernels, project(): pl.pallas_call(project_kernel, in_specs=[pl.BlockSpec(memory_space=pltpu....  7.98 us
    select_n x6, other arithmetic, turned(): return jnp.where(stays, block, send(block, turn_route))  5.63 us
    unnamed x27, local copies, waits for them, and re-layouts  3.34 us
  transfers between devices with their start and end apart: 22, of which 11 were waited for; matrix products, arithmetic and copies ran while one was open for 5% of the time, Pallas kernels for 18%

profile of v1, /device:TPU:0, one launch (start us, length us, event | category | flops | bytes accessed | tf_op | source)
XLA Modules:
  0.0 145.4 jit_solution(176246744459238670)
XLA Ops:
  0.6 0.0 copy-start.7
  0.7 3.0 %collective-permute-start.5 = (bf16[768,768]{1,0:T(8,128)(2,1)}, bf16[768,768]{1,0:T(8,128)(2,1)}, u32[]{:S(2)}, u32[]{:S(2)}) collective-permute-start(bf16[768,768]{1,0:T(8,128)(2,1)} %g0.1), channel_id=1, source_target_pairs={{0,2},{1,3},{2,0},{3,1},{4,6},{5,7},{6,4},{7,5},{8,10},{9,11},{10,... | collective-permute-start | bytes 3538952 | tf_op jit(solution)/shard_map/ppermute | solution.py:28
  3.7 1.1 constant_dynamic-update-slice_fusion.1
  4.8 0.1 constant_dynamic-update-slice_fusion
  4.9 0.1 collective-permute-start.1
  5.1 2.0 %collective-permute-start.8 = (bf16[384,384]{1,0:T(8,128)(2,1)S(1)}, bf16[384,384]{1,0:T(8,128)(2,1)}, u32[]{:S(2)}, u32[]{:S(2)}) collective-permute-start(bf16[384,384]{1,0:T(8,128)(2,1)S(1)} %copy-done.7), channel_id=1, source_target_pairs={{0,8},{1,9},{2,10},{3,11},{4,12},{5,13},{6,14},{7,15},{8,0},{9,1},... | collective-permute-start | bytes 884744 | tf_op jit(solution)/shard_map/ppermute | solution.py:28
  7.1 1.1 collective-permute-start.7
  8.2 2.6 %collective-permute-start.10 = (bf16[384,384]{1,0:T(8,128)(2,1)S(1)}, bf16[384,384]{1,0:T(8,128)(2,1)}, u32[]{:S(2)}, u32[]{:S(2)}) collective-permute-start(bf16[384,384]{1,0:T(8,128)(2,1)S(1)} %copy-done.7), channel_id=1, source_target_pairs={{0,16},{1,17},{2,18},{3,19},{4,20},{5,21},{6,22},{7,23},{8,24},{9,... | collective-permute-start | bytes 884744 | tf_op jit(solution)/shard_map/ppermute | solution.py:28
  10.8 9.8 %collective-permute-done.8.refs_2_ = bf16[384,384]{1,0:T(8,128)(2,1)} collective-permute-done((bf16[384,384]{1,0:T(8,128)(2,1)S(1)}, bf16[384,384]{1,0:T(8,128)(2,1)}, u32[]{:S(2)}, u32[]{:S(2)}) %collective-permute-start.8) | collective-permute-done | bytes 294944 | tf_op jit(solution)/shard_map/ppermute | solution.py:28
  20.6 0.7 collective-permute-start.4
  21.3 8.7 %collective-permute-done.5.g2 = bf16[768,768]{1,0:T(8,128)(2,1)} collective-permute-done((bf16[768,768]{1,0:T(8,128)(2,1)}, bf16[768,768]{1,0:T(8,128)(2,1)}, u32[]{:S(2)}, u32[]{:S(2)}) %collective-permute-start.5) | collective-permute-done | bytes 1179680 | tf_op jit(solution)/shard_map/ppermute | solution.py:28
  30.0 0.0 collective-permute-start.6
  30.0 2.9 %collective-permute-start.12 = (bf16[384,384]{1,0:T(8,128)(2,1)}, bf16[384,384]{1,0:T(8,128)(2,1)S(1)}, u32[]{:S(2)}, u32[]{:S(2)}) collective-permute-start(bf16[384,384]{1,0:T(8,128)(2,1)} %collective-permute-done.8.refs_2_), channel_id=1, source_target_pairs={{0,16},{1,17},{2,18},{3,19},{4,20},{5,21},{6,22},{7,23},{8,24},{9,... | collective-permute-start | bytes 884744 | tf_op jit(solution)/shard_map/ppermute | solution.py:28
  32.9 2.6 %collective-permute-start.9 = (bf16[384,384]{1,0:T(8,128)(2,1)}, bf16[384,384]{1,0:T(8,128)(2,1)S(1)}, u32[]{:S(2)}, u32[]{:S(2)}) collective-permute-start(bf16[384,384]{1,0:T(8,128)(2,1)} %collective-permute-done.8.refs_2_), channel_id=1, source_target_pairs={{0,4},{1,5},{2,6},{3,7},{4,0},{5,1},{6,2},{7,3},{8,12},{9,13},{10,... | collective-permute-start | bytes 884744 | tf_op jit(solution)/shard_map/ppermute | solution.py:28
  35.5 7.0 %collective-permute-done.1 = bf16[768,768]{1,0:T(8,128)(2,1)S(1)} collective-permute-done((bf16[768,768]{1,0:T(8,128)(2,1)S(1)}, bf16[768,768]{1,0:T(8,128)(2,1)S(1)}, u32[]{:S(2)}, u32[]{:S(2)}) %collective-permute-start.1) | collective-permute-done | bytes 1179680 | tf_op jit(solution)/shard_map/ppermute | solution.py:28
  42.5 0.1 broadcast_select_fusion.ko.vo
  42.6 4.4 %collective-permute-done.12.refs_6_ = bf16[384,384]{1,0:T(8,128)(2,1)S(1)} collective-permute-done((bf16[384,384]{1,0:T(8,128)(2,1)}, bf16[384,384]{1,0:T(8,128)(2,1)S(1)}, u32[]{:S(2)}, u32[]{:S(2)}) %collective-permute-start.12) | collective-permute-done | bytes 294944 | tf_op jit(solution)/shard_map/ppermute | solution.py:28
  47.0 1.5 %collective-permute-start.3 = (bf16[768,768]{1,0:T(8,128)(2,1)S(1)}, bf16[768,768]{1,0:T(8,128)(2,1)S(1)}, u32[]{:S(2)}, u32[]{:S(2)}) collective-permute-start(bf16[768,768]{1,0:T(8,128)(2,1)S(1)} %broadcast_select_fusion.ko.vo), channel_id=1, source_target_pairs={{0,2},{1,8},{2,0},{3,10},{4,6},{5,12},{6,4},{7,14},{8,1},{9,16},{1... | collective-permute-start | bytes 3538952 | tf_op jit(solution)/shard_map/ppermute | solution.py:28
  48.6 3.2 %collective-permute-done.11.refs_5_ = bf16[384,384]{1,0:T(8,128)(2,1)S(1)} collective-permute-done((bf16[384,384]{1,0:T(8,128)(2,1)}, bf16[384,384]{1,0:T(8,128)(2,1)S(1)}, u32[]{:S(2)}, u32[]{:S(2)}) %collective-permute-start.11) | collective-permute-done | bytes 294944 | tf_op jit(solution)/shard_map/ppermute | solution.py:28
  51.8 8.2 %collective-permute-done.13.refs_7_ = bf16[384,384]{1,0:T(8,128)(2,1)S(1)} collective-permute-done((bf16[384,384]{1,0:T(8,128)(2,1)S(1)}, bf16[384,384]{1,0:T(8,128)(2,1)S(1)}, u32[]{:S(2)}, u32[]{:S(2)}) %collective-permute-start.13) | collective-permute-done | bytes 294944 | tf_op jit(solution)/shard_map/ppermute | solution.py:28
  60.0 0.7 copy-done.12
  60.7 1.4 collective-permute-start
  62.1 0.7 pad_add_fusion.place_ref
  62.7 8.0 %project.1 = bf16[768,384]{1,0:T(8,128)(2,1)} custom-call(s32[3]{0:T(128)} %pad_add_fusion.place_ref, bf16[768,768]{1,0:T(8,128)(2,1)} %g0.1, bf16[768,768]{1,0:T(8,128)(2,1)} %collective-permute-done.4.g1, bf16[768,768]{1,0:T(8,128)(2,1)} %collective-permute-done.5.g2, bf16[768,768]{1,0:T(8,128)(2,1)} %collective-permute-done.6.g3, ...), custom_call_target="tpu_custom_call" | custom-call | tf_op jit(solution)/shard_map/project/pallas_call | solution.py:187
  70.7 0.7 collective-permute-start.14
  71.5 2.0 %broadcast_select_fusion.5.q_ref = bf16[768,384]{1,0:T(8,128)(2,1)} fusion(bf16[768,384]{1,0:T(8,128)(2,1)} %param.5, bf16[768,384]{1,0:T(8,128)(2,1)} %collective-permute-done, pred[]{:T(512)S(6)} %eq.10), kind=kLoop, calls=%fused_computation.7 | loop fusion | flops 294912 | bytes 1769473 | tf_op jit(solution)/shard_map/jit(_where)/select_n | solution.py:224
  73.4 1.0 copy-done.1
  74.4 0.4 copy-done.2
  74.9 18.2 %forward_part.1 = (bf16[3,2304,768]{2,1,0:T(8,128)(2,1)}, f32[384,768]{1,0:T(8,128)}) custom-call(s32[1]{0:T(128)} %bitcast.flag_ref, bf16[768,384]{1,0:T(8,128)(2,1)} %broadcast_select_fusion.5.q_ref, bf16[768,768]{1,0:T(8,128)(2,1)} %copy-done, bf16[768,768]{1,0:T(8,128)(2,1)} %copy-done, bf16[768,768]{1,0:T(8,128)(2,1)} %copy-done.2, ...), custom_call_target="tpu_custom_call" | custom-call | tf_op jit(solution)/shard_map/forward_part/pallas_call | solution.py:75
  93.1 0.9 broadcast_select_fusion.4.g_ref
  94.0 14.5 %backward_part.1 = (bf16[768,384]{1,0:T(8,128)(2,1)}, f32[768,384]{1,0:T(8,128)}, f32[768,384]{1,0:T(8,128)}, bf16[768,384]{1,0:T(8,128)(2,1)}, bf16[768,384]{1,...) custom-call(bf16[3,2304,768]{2,1,0:T(8,128)(2,1)} %get-tuple-element.12.p_ref, ...), custom_call_target="tpu_custom_call" | custom-call | tf_op jit(solution)/shard_map/backward_part/pallas_call | solution.py:133
  108.6 0.6 collective-permute-start.16
  109.2 1.7 %collective-permute-start.17 = (bf16[768,384]{1,0:T(8,128)(2,1)}, bf16[768,384]{1,0:T(8,128)(2,1)S(1)}, u32[]{:S(2)}, u32[]{:S(2)}) collective-permute-start(bf16[768,384]{1,0:T(8,128)(2,1)} %get-tuple-element.17), channel_id=1, source_target_pairs={{0,2},{1,8},{2,0},{3,10},{4,6},{5,12},{6,4},{7,14},{8,1},{9,16},{1... | collective-permute-start | bytes 1769480 | tf_op jit(solution)/shard_map/ppermute | solution.py:28
  110.9 0.5 collective-permute-start.19
  111.4 1.5 %collective-permute-start.20 = (bf16[768,384]{1,0:T(8,128)(2,1)}, bf16[768,384]{1,0:T(8,128)(2,1)S(1)}, u32[]{:S(2)}, u32[]{:S(2)}) collective-permute-start(bf16[768,384]{1,0:T(8,128)(2,1)} %get-tuple-element.20), channel_id=1, source_target_pairs={{0,2},{1,8},{2,0},{3,10},{4,6},{5,12},{6,4},{7,14},{8,1},{9,16},{1... | collective-permute-start | bytes 1769480 | tf_op jit(solution)/shard_map/ppermute | solution.py:28
  112.9 0.5 collective-permute-start.15
  113.4 5.8 %collective-permute-done.17 = bf16[768,384]{1,0:T(8,128)(2,1)S(1)} collective-permute-done((bf16[768,384]{1,0:T(8,128)(2,1)}, bf16[768,384]{1,0:T(8,128)(2,1)S(1)}, u32[]{:S(2)}, u32[]{:S(2)}) %collective-permute-start.17) | collective-permute-done | bytes 589856 | tf_op jit(solution)/shard_map/ppermute | solution.py:28
  119.3 1.6 %add_convert_fusion.1 = bf16[768,384]{1,0:T(8,128)(2,1)S(1)} fusion(bf16[768,384]{1,0:T(8,128)(2,1)S(1)} %collective-permute-done.17, f32[768,384]{1,0:T(8,128)} %get-tuple-element.15, bf16[768,384]{1,0:T(8,128)(2,1)S(1)} %collective-permute-done.16, pred[]{:T(512)S(6)} %gt.7), kind=kLoop, calls=%fused_computation.1 | loop fusion | flops 1769472 | bytes 2949121 | tf_op jit(solution)/shard_map/convert_element_type | solution.py:260
  120.9 1.8 %collective-permute-start.18 = (bf16[768,384]{1,0:T(8,128)(2,1)S(1)}, bf16[768,384]{1,0:T(8,128)(2,1)S(1)}, u32[]{:S(2)}, u32[]{:S(2)}) collective-permute-start(bf16[768,384]{1,0:T(8,128)(2,1)S(1)} %add_convert_fusion.1), channel_id=1, source_target_pairs={{0,2},{1,4},{2,0},{3,6},{4,1},{5,7},{6,3},{7,5},{8,10},{9,12},{10,... | collective-permute-start | bytes 1769480 | tf_op jit(solution)/shard_map/ppermute | solution.py:28
  122.7 2.9 %collective-permute-done.20 = bf16[768,384]{1,0:T(8,128)(2,1)S(1)} collective-permute-done((bf16[768,384]{1,0:T(8,128)(2,1)}, bf16[768,384]{1,0:T(8,128)(2,1)S(1)}, u32[]{:S(2)}, u32[]{:S(2)}) %collective-permute-start.20) | collective-permute-done | bytes 589856 | tf_op jit(solution)/shard_map/ppermute | solution.py:28
  125.6 0.2 add_convert_fusion
  125.9 1.8 %collective-permute-start.21 = (bf16[768,384]{1,0:T(8,128)(2,1)S(1)}, bf16[768,384]{1,0:T(8,128)(2,1)S(1)}, u32[]{:S(2)}, u32[]{:S(2)}) collective-permute-start(bf16[768,384]{1,0:T(8,128)(2,1)S(1)} %add_convert_fusion), channel_id=1, source_target_pairs={{0,2},{1,4},{2,0},{3,6},{4,1},{5,7},{6,3},{7,5},{8,10},{9,12},{10,... | collective-permute-start | bytes 1769480 | tf_op jit(solution)/shard_map/ppermute | solution.py:28
  127.7 4.3 %collective-permute-done.15 = bf16[768,384]{1,0:T(8,128)(2,1)S(1)} collective-permute-done((bf16[768,384]{1,0:T(8,128)(2,1)}, bf16[768,384]{1,0:T(8,128)(2,1)S(1)}, u32[]{:S(2)}, u32[]{:S(2)}) %collective-permute-start.15) | collective-permute-done | bytes 589856 | tf_op jit(solution)/shard_map/ppermute | solution.py:28
  131.9 0.9 broadcast_select_fusion.3
  132.8 5.4 %collective-permute-done.18 = bf16[768,384]{1,0:T(8,128)(2,1)S(1)} collective-permute-done((bf16[768,384]{1,0:T(8,128)(2,1)S(1)}, bf16[768,384]{1,0:T(8,128)(2,1)S(1)}, u32[]{:S(2)}, u32[]{:S(2)}) %collective-permute-start.18) | collective-permute-done | bytes 589856 | tf_op jit(solution)/shard_map/ppermute | solution.py:28
  138.2 0.9 broadcast_select_fusion.2
  139.1 5.4 %collective-permute-done.21 = bf16[768,384]{1,0:T(8,128)(2,1)S(1)} collective-permute-done((bf16[768,384]{1,0:T(8,128)(2,1)S(1)}, bf16[768,384]{1,0:T(8,128)(2,1)S(1)}, u32[]{:S(2)}, u32[]{:S(2)}) %collective-permute-start.21) | collective-permute-done | bytes 589856 | tf_op jit(solution)/shard_map/ppermute | solution.py:28
  144.6 0.9 broadcast_select_fusion.1
  (36 shorter events, 0.1 us)
Async XLA Ops:
  0.6 4.2 %copy-start.5 = (bf16[768,384]{1,0:T(8,128)(2,1)S(1)}, bf16[768,384]{1,0:T(8,128)(2,1)}, u32[]{:S(2)}) copy-start(bf16[768,384]{1,0:T(8,128)(2,1)} %param.7) | copy-start | bytes 1769476
  0.6 4.4 %copy-start.7 = (bf16[384,384]{1,0:T(8,128)(2,1)S(1)}, bf16[384,384]{1,0:T(8,128)(2,1)}, u32[]{:S(2)}) copy-start(bf16[384,384]{1,0:T(8,128)(2,1)} %refs_0_.1) | copy-start | bytes 884740
  0.7 29.3 %collective-permute-start.5 = (bf16[768,768]{1,0:T(8,128)(2,1)}, bf16[768,768]{1,0:T(8,128)(2,1)}, u32[]{:S(2)}, u32[]{:S(2)}) collective-permute-start(bf16[768,768]{1,0:T(8,128)(2,1)} %g0.1), channel_id=1, source_target_pairs={{0,2},{1,3},{2,0},{3,1},{4,6},{5,7},{6,4},{7,5},{8,10},{9,11},{10,... | collective-permute-start | bytes 3538952 | tf_op jit(solution)/shard_map/ppermute | solution.py:28
  4.9 37.6 %collective-permute-start.1 = (bf16[768,768]{1,0:T(8,128)(2,1)S(1)}, bf16[768,768]{1,0:T(8,128)(2,1)S(1)}, u32[]{:S(2)}, u32[]{:S(2)}) collective-permute-start(bf16[768,768]{1,0:T(8,128)(2,1)S(1)} %constant_dynamic-update-slice_fusion), channel_id=1, source_target_pairs={{0,2},{1,4},{2,0},{3,6},{4,1},{5,7},{6,3},{7,5},{8,10},{9,12},{10,... | collective-permute-start | bytes 3538952 | tf_op jit(solution)/shard_map/ppermute | solution.py:28
  5.1 15.5 %collective-permute-start.8 = (bf16[384,384]{1,0:T(8,128)(2,1)S(1)}, bf16[384,384]{1,0:T(8,128)(2,1)}, u32[]{:S(2)}, u32[]{:S(2)}) collective-permute-start(bf16[384,384]{1,0:T(8,128)(2,1)S(1)} %copy-done.7), channel_id=1, source_target_pairs={{0,8},{1,9},{2,10},{3,11},{4,12},{5,13},{6,14},{7,15},{8,0},{9,1},... | collective-permute-start | bytes 884744 | tf_op jit(solution)/shard_map/ppermute | solution.py:28
  7.1 22.9 %collective-permute-start.7 = (bf16[384,384]{1,0:T(8,128)(2,1)S(1)}, bf16[384,384]{1,0:T(8,128)(2,1)S(1)}, u32[]{:S(2)}, u32[]{:S(2)}) collective-permute-start(bf16[384,384]{1,0:T(8,128)(2,1)S(1)} %copy-done.7), channel_id=1, source_target_pairs={{0,4},{1,5},{2,6},{3,7},{4,0},{5,1},{6,2},{7,3},{8,12},{9,13},{10,... | collective-permute-start | bytes 884744 | tf_op jit(solution)/shard_map/ppermute | solution.py:28
  8.2 24.7 %collective-permute-start.10 = (bf16[384,384]{1,0:T(8,128)(2,1)S(1)}, bf16[384,384]{1,0:T(8,128)(2,1)}, u32[]{:S(2)}, u32[]{:S(2)}) collective-permute-start(bf16[384,384]{1,0:T(8,128)(2,1)S(1)} %copy-done.7), channel_id=1, source_target_pairs={{0,16},{1,17},{2,18},{3,19},{4,20},{5,21},{6,22},{7,23},{8,24},{9,... | collective-permute-start | bytes 884744 | tf_op jit(solution)/shard_map/ppermute | solution.py:28
  20.6 42.2 %collective-permute-start.4 = (bf16[768,768]{1,0:T(8,128)(2,1)}, bf16[768,768]{1,0:T(8,128)(2,1)}, u32[]{:S(2)}, u32[]{:S(2)}) collective-permute-start(bf16[768,768]{1,0:T(8,128)(2,1)} %g0.1), channel_id=1, source_target_pairs={{0,1},{1,0},{2,3},{3,2},{4,5},{5,4},{6,7},{7,6},{8,9},{9,8},{10,11... | collective-permute-start | bytes 3538952 | tf_op jit(solution)/shard_map/ppermute | solution.py:28
  30.0 32.8 %collective-permute-start.6 = (bf16[768,768]{1,0:T(8,128)(2,1)}, bf16[768,768]{1,0:T(8,128)(2,1)}, u32[]{:S(2)}, u32[]{:S(2)}) collective-permute-start(bf16[768,768]{1,0:T(8,128)(2,1)} %collective-permute-done.5.g2), channel_id=1, source_target_pairs={{0,1},{1,0},{2,3},{3,2},{4,5},{5,4},{6,7},{7,6},{8,9},{9,8},{10,11... | collective-permute-start | bytes 3538952 | tf_op jit(solution)/shard_map/ppermute | solution.py:28
  30.0 12.5 %copy-start.8 = (bf16[384,384]{1,0:T(8,128)(2,1)}, bf16[384,384]{1,0:T(8,128)(2,1)S(1)}, u32[]{:S(2)}) copy-start(bf16[384,384]{1,0:T(8,128)(2,1)S(1)} %collective-permute-done.7.refs_1_) | copy-start | bytes 884740
  30.0 17.0 %collective-permute-start.12 = (bf16[384,384]{1,0:T(8,128)(2,1)}, bf16[384,384]{1,0:T(8,128)(2,1)S(1)}, u32[]{:S(2)}, u32[]{:S(2)}) collective-permute-start(bf16[384,384]{1,0:T(8,128)(2,1)} %collective-permute-done.8.refs_2_), channel_id=1, source_target_pairs={{0,16},{1,17},{2,18},{3,19},{4,20},{5,21},{6,22},{7,23},{8,24},{9,... | collective-permute-start | bytes 884744 | tf_op jit(solution)/shard_map/ppermute | solution.py:28
  32.9 15.7 %collective-permute-start.9 = (bf16[384,384]{1,0:T(8,128)(2,1)}, bf16[384,384]{1,0:T(8,128)(2,1)S(1)}, u32[]{:S(2)}, u32[]{:S(2)}) collective-permute-start(bf16[384,384]{1,0:T(8,128)(2,1)} %collective-permute-done.8.refs_2_), channel_id=1, source_target_pairs={{0,4},{1,5},{2,6},{3,7},{4,0},{5,1},{6,2},{7,3},{8,12},{9,13},{10,... | collective-permute-start | bytes 884744 | tf_op jit(solution)/shard_map/ppermute | solution.py:28
  42.5 9.3 %collective-permute-start.11 = (bf16[384,384]{1,0:T(8,128)(2,1)}, bf16[384,384]{1,0:T(8,128)(2,1)S(1)}, u32[]{:S(2)}, u32[]{:S(2)}) collective-permute-start(bf16[384,384]{1,0:T(8,128)(2,1)} %collective-permute-done.10.refs_4_), channel_id=1, source_target_pairs={{0,4},{1,5},{2,6},{3,7},{4,0},{5,1},{6,2},{7,3},{8,12},{9,13},{10,... | collective-permute-start | bytes 884744 | tf_op jit(solution)/shard_map/ppermute | solution.py:28
  42.6 28.1 %copy-start = (bf16[768,768]{1,0:T(8,128)(2,1)}, bf16[768,768]{1,0:T(8,128)(2,1)S(1)}, u32[]{:S(2)}) copy-start(bf16[768,768]{1,0:T(8,128)(2,1)S(1)} %broadcast_select_fusion.ko.vo) | copy-start | bytes 3538948
  47.0 4.7 %copy-start.9 = (bf16[384,384]{1,0:T(8,128)(2,1)}, bf16[384,384]{1,0:T(8,128)(2,1)S(1)}, u32[]{:S(2)}) copy-start(bf16[384,384]{1,0:T(8,128)(2,1)S(1)} %collective-permute-done.12.refs_6_) | copy-start | bytes 884740
  47.0 26.4 %collective-permute-start.3 = (bf16[768,768]{1,0:T(8,128)(2,1)S(1)}, bf16[768,768]{1,0:T(8,128)(2,1)S(1)}, u32[]{:S(2)}, u32[]{:S(2)}) collective-permute-start(bf16[768,768]{1,0:T(8,128)(2,1)S(1)} %broadcast_select_fusion.ko.vo), channel_id=1, source_target_pairs={{0,2},{1,8},{2,0},{3,10},{4,6},{5,12},{6,4},{7,14},{8,1},{9,16},{1... | collective-permute-start | bytes 3538952 | tf_op jit(solution)/shard_map/ppermute | solution.py:28
  48.6 11.4 %copy-start.10 = (bf16[384,384]{1,0:T(8,128)(2,1)}, bf16[384,384]{1,0:T(8,128)(2,1)S(1)}, u32[]{:S(2)}) copy-start(bf16[384,384]{1,0:T(8,128)(2,1)S(1)} %collective-permute-done.9.refs_3_) | copy-start | bytes 884740
  48.6 24.8 %collective-permute-start.2 = (bf16[768,768]{1,0:T(8,128)(2,1)S(1)}, bf16[768,768]{1,0:T(8,128)(2,1)S(1)}, u32[]{:S(2)}, u32[]{:S(2)}) collective-permute-start(bf16[768,768]{1,0:T(8,128)(2,1)S(1)} %broadcast_select_fusion.ko.vo), channel_id=1, source_target_pairs={{0,1},{1,0},{2,3},{3,2},{4,5},{5,4},{6,7},{7,6},{8,9},{9,8},{10,11... | collective-permute-start | bytes 3538952 | tf_op jit(solution)/shard_map/ppermute | solution.py:28
  51.8 8.2 %copy-start.11 = (bf16[384,384]{1,0:T(8,128)(2,1)}, bf16[384,384]{1,0:T(8,128)(2,1)S(1)}, u32[]{:S(2)}) copy-start(bf16[384,384]{1,0:T(8,128)(2,1)S(1)} %collective-permute-done.11.refs_5_) | copy-start | bytes 884740
  51.8 8.2 %collective-permute-start.13 = (bf16[384,384]{1,0:T(8,128)(2,1)S(1)}, bf16[384,384]{1,0:T(8,128)(2,1)S(1)}, u32[]{:S(2)}, u32[]{:S(2)}) collective-permute-start(bf16[384,384]{1,0:T(8,128)(2,1)S(1)} %collective-permute-done.12.refs_6_), channel_id=1, source_target_pairs={{0,4},{1,5},{2,6},{3,7},{4,0},{5,1},{6,2},{7,3},{8,12},{9,13},{10,... | collective-permute-start | bytes 884744 | tf_op jit(solution)/shard_map/ppermute | solution.py:28
  60.0 0.7 copy-start.12
  60.7 10.7 %collective-permute-start = (bf16[768,384]{1,0:T(8,128)(2,1)}, bf16[768,384]{1,0:T(8,128)(2,1)}, u32[]{:S(2)}, u32[]{:S(2)}) collective-permute-start(bf16[768,384]{1,0:T(8,128)(2,1)} %param.5), channel_id=1, source_target_pairs={{0,2},{1,4},{2,0},{3,6},{4,1},{5,7},{6,3},{7,5},{8,10},{9,12},{10,... | collective-permute-start | bytes 1769480 | tf_op jit(solution)/shard_map/ppermute | solution.py:28
  70.7 22.4 %collective-permute-start.14 = (bf16[768,384]{1,0:T(8,128)(2,1)}, bf16[768,384]{1,0:T(8,128)(2,1)}, u32[]{:S(2)}, u32[]{:S(2)}) collective-permute-start(bf16[768,384]{1,0:T(8,128)(2,1)} %project.1), channel_id=1, source_target_pairs={{0,2},{1,4},{2,0},{3,6},{4,1},{5,7},{6,3},{7,5},{8,10},{9,12},{10,... | collective-permute-start | bytes 1769480 | tf_op jit(solution)/shard_map/ppermute | solution.py:28
  73.4 1.0 copy-start.1
  73.4 1.5 %copy-start.2 = (bf16[768,768]{1,0:T(8,128)(2,1)}, bf16[768,768]{1,0:T(8,128)(2,1)S(1)}, u32[]{:S(2)}) copy-start(bf16[768,768]{1,0:T(8,128)(2,1)S(1)} %collective-permute-done.2.ks.vs) | copy-start | bytes 3538948
  74.9 18.3 %copy-start.3 = (bf16[768,384]{1,0:T(8,128)(2,1)S(1)}, bf16[768,384]{1,0:T(8,128)(2,1)}, u32[]{:S(2)}) copy-start(bf16[768,384]{1,0:T(8,128)(2,1)} %project.1) | copy-start | bytes 1769476
  108.6 4.9 %collective-permute-start.16 = (bf16[768,384]{1,0:T(8,128)(2,1)}, bf16[768,384]{1,0:T(8,128)(2,1)S(1)}, u32[]{:S(2)}, u32[]{:S(2)}) collective-permute-start(bf16[768,384]{1,0:T(8,128)(2,1)} %get-tuple-element.16), channel_id=1, source_target_pairs={{0,1},{1,0},{2,3},{3,2},{4,5},{5,4},{6,7},{7,6},{8,9},{9,8},{10,11... | collective-permute-start | bytes 1769480 | tf_op jit(solution)/shard_map/ppermute | solution.py:28
  109.2 10.1 %collective-permute-start.17 = (bf16[768,384]{1,0:T(8,128)(2,1)}, bf16[768,384]{1,0:T(8,128)(2,1)S(1)}, u32[]{:S(2)}, u32[]{:S(2)}) collective-permute-start(bf16[768,384]{1,0:T(8,128)(2,1)} %get-tuple-element.17), channel_id=1, source_target_pairs={{0,2},{1,8},{2,0},{3,10},{4,6},{5,12},{6,4},{7,14},{8,1},{9,16},{1... | collective-permute-start | bytes 1769480 | tf_op jit(solution)/shard_map/ppermute | solution.py:28
  110.9 11.8 %collective-permute-start.19 = (bf16[768,384]{1,0:T(8,128)(2,1)}, bf16[768,384]{1,0:T(8,128)(2,1)S(1)}, u32[]{:S(2)}, u32[]{:S(2)}) collective-permute-start(bf16[768,384]{1,0:T(8,128)(2,1)} %get-tuple-element.19), channel_id=1, source_target_pairs={{0,1},{1,0},{2,3},{3,2},{4,5},{5,4},{6,7},{7,6},{8,9},{9,8},{10,11... | collective-permute-start | bytes 1769480 | tf_op jit(solution)/shard_map/ppermute | solution.py:28
  111.4 14.2 %collective-permute-start.20 = (bf16[768,384]{1,0:T(8,128)(2,1)}, bf16[768,384]{1,0:T(8,128)(2,1)S(1)}, u32[]{:S(2)}, u32[]{:S(2)}) collective-permute-start(bf16[768,384]{1,0:T(8,128)(2,1)} %get-tuple-element.20), channel_id=1, source_target_pairs={{0,2},{1,8},{2,0},{3,10},{4,6},{5,12},{6,4},{7,14},{8,1},{9,16},{1... | collective-permute-start | bytes 1769480 | tf_op jit(solution)/shard_map/ppermute | solution.py:28
  112.9 19.0 %collective-permute-start.15 = (bf16[768,384]{1,0:T(8,128)(2,1)}, bf16[768,384]{1,0:T(8,128)(2,1)S(1)}, u32[]{:S(2)}, u32[]{:S(2)}) collective-permute-start(bf16[768,384]{1,0:T(8,128)(2,1)} %get-tuple-element.14), channel_id=1, source_target_pairs={{0,2},{1,4},{2,0},{3,6},{4,1},{5,7},{6,3},{7,5},{8,10},{9,12},{10,... | collective-permute-start | bytes 1769480 | tf_op jit(solution)/shard_map/ppermute | solution.py:28
  119.3 6.3 %copy-start.4 = (f32[768,384]{1,0:T(8,128)S(1)}, f32[768,384]{1,0:T(8,128)}, u32[]{:S(2)}) copy-start(f32[768,384]{1,0:T(8,128)} %get-tuple-element.18) | copy-start | bytes 3538948
  120.9 17.4 %collective-permute-start.18 = (bf16[768,384]{1,0:T(8,128)(2,1)S(1)}, bf16[768,384]{1,0:T(8,128)(2,1)S(1)}, u32[]{:S(2)}, u32[]{:S(2)}) collective-permute-start(bf16[768,384]{1,0:T(8,128)(2,1)S(1)} %add_convert_fusion.1), channel_id=1, source_target_pairs={{0,2},{1,4},{2,0},{3,6},{4,1},{5,7},{6,3},{7,5},{8,10},{9,12},{10,... | collective-permute-start | bytes 1769480 | tf_op jit(solution)/shard_map/ppermute | solution.py:28
  125.6 6.3 %copy-start.6 = (bf16[768,384]{1,0:T(8,128)(2,1)S(1)}, bf16[768,384]{1,0:T(8,128)(2,1)}, u32[]{:S(2)}) copy-start(bf16[768,384]{1,0:T(8,128)(2,1)} %get-tuple-element.14) | copy-start | bytes 1769476
  125.9 18.7 %collective-permute-start.21 = (bf16[768,384]{1,0:T(8,128)(2,1)S(1)}, bf16[768,384]{1,0:T(8,128)(2,1)S(1)}, u32[]{:S(2)}, u32[]{:S(2)}) collective-permute-start(bf16[768,384]{1,0:T(8,128)(2,1)S(1)} %add_convert_fusion), channel_id=1, source_target_pairs={{0,2},{1,4},{2,0},{3,6},{4,1},{5,7},{6,3},{7,5},{8,10},{9,12},{10,... | collective-permute-start | bytes 1769480 | tf_op jit(solution)/shard_map/ppermute | solution.py:28

commit v2 on v1

--- a/solution.py
+++ b/solution.py
@@ -8,6 +8,7 @@
 from jax.experimental.pallas import tpu as pltpu
 from jax.sharding import PartitionSpec as P
 
+
 HD = 128
 VT = 8
 AXES = ("tm", "head")
@@ -23,13 +24,17 @@
     pairs = []
     for t in range(n_tm):
         for h in range(n_head):
-            to_t, to_h = route(t, h)
+            target = route(t, h)
+            if target is None:
+                continue
+            to_t, to_h = target
             pairs.append((t * n_head + h, to_t * n_head + to_h))
     return lax.ppermute(block, AXES, pairs)
 
 
-def forward_kernel(heads, scale, flag_ref, q_ref, ko, vo, ks, vs, kz, vz, p_ref, o_ref, vt):
-    rows = q_ref.shape[0]
+def forward_kernel(scale, flag_ref, qa, qb, ko, vo, ks, vs, kz, vz, *refs):
+    p_ref, o_ref, vt = refs[-3:]
+    rows = qa.shape[0]
     tile = p_ref.shape[2]
     keys = (ko, ks, kz)
     values = (vo, vs, vz)
@@ -40,7 +45,7 @@
             vt[:, i * rows : (i + 1) * rows] = values[i][...].T
 
     start = pl.multiple_of(pl.program_id(1) * tile, tile)
-    query = q_ref[pl.ds(start, tile), :]
+    query = jnp.where(flag_ref[1] > 0, qa[pl.ds(start, tile), :], qb[pl.ds(start, tile), :])
     factor = scale * math.log2(math.e)
     scores = [dot(k[...], query, NT) for k in keys]
     peaks = [jnp.max(s, axis=0, keepdims=True) for s in scores]
@@ -62,47 +67,35 @@
     o_ref[...] = out
 
 
-def forward(flag, query, own, side, far, heads, rows):
+def forward(flags, queries, own, side, far, first, count, rows, earlier=()):
+    heads = own[0].shape[1] // HD
     tile = rows // 3
     scale = 1.0 / math.sqrt(HD)
-
-    def key_spec():
-        return pl.BlockSpec((rows, HD), lambda h, i: (0, h))
-
-    def value_spec():
-        return pl.BlockSpec((rows, HD), lambda h, i: (0, heads + h))
-
+    spec = pl.BlockSpec((rows, HD), lambda h, i: (0, first + h))
+    anywhere = pl.BlockSpec(memory_space=pl.ANY)
     return pl.pallas_call(
-        functools.partial(forward_kernel, heads, scale),
-        grid=(heads, 3),
-        in_specs=[
-            pl.BlockSpec(memory_space=pltpu.SMEM),
-            key_spec(),
-            key_spec(),
-            value_spec(),
-            key_spec(),
-            value_spec(),
-            key_spec(),
-            value_spec(),
-        ],
+        functools.partial(forward_kernel, scale),
+        grid=(count, 3),
+        in_specs=[pl.BlockSpec(memory_space=pltpu.SMEM)] + [spec] * 8 + [anywhere] * len(earlier),
         out_specs=[
-            pl.BlockSpec((1, 3 * rows, tile), lambda h, i: (h, 0, i)),
-            pl.BlockSpec((HD, tile), lambda h, i: (h, i)),
+            pl.BlockSpec((1, 3 * rows, tile), lambda h, i: (first + h, 0, i)),
+            pl.BlockSpec((HD, tile), lambda h, i: (first + h, i)),
         ],
         out_shape=[
             jax.ShapeDtypeStruct((heads, 3 * rows, rows), jnp.bfloat16),
             jax.ShapeDtypeStruct((heads * HD, rows), jnp.float32),
         ],
         scratch_shapes=[pltpu.VMEM((HD, 3 * rows), jnp.bfloat16)],
-        name="forward_part",
-    )(flag, query, own, own, side, side, far, far)
-
-
-def backward_kernel(scale, p_ref, o_ref, g_ref, q_ref, ko, vo, ks, vs, kz, vz, dq, dko, dvo, dks, dvs, dkz, dvz):
-    rows = q_ref.shape[0]
+        input_output_aliases={9: 0, 10: 1} if earlier else {},
+    )(flags, *queries, *own, *side, *far, *earlier)
+
+
+def backward_kernel(scale, flag_ref, p_ref, o_ref, ga, gb, qa, qb, ko, vo, ks, vs, kz, vz, dq, dko, dvo, dks, dvs, dkz, dvz):
+    rows = qa.shape[0]
     step = 256
-    grad = g_ref[...]
-    query = q_ref[...]
+    stays = flag_ref[1] > 0
+    grad = jnp.where(stays, ga[...], gb[...])
+    query = jnp.where(stays, qa[...], qb[...])
     inner = jnp.sum(o_ref[...] * grad.astype(jnp.float32).T, axis=0, keepdims=True)
     total = None
     for i, (k, v, dk, dv) in enumerate(((kz, vz, dkz, dvz), (ks, vs, dks, dvs), (ko, vo, dko, dvo))):
@@ -118,37 +111,24 @@
     dq[...] = (total * scale).T.astype(dq.dtype)
 
 
-def backward(prob, out, grad, query, own, side, far, heads, rows):
-    scale = 1.0 / math.sqrt(HD)
-
-    def col():
-        return pl.BlockSpec((rows, HD), lambda h: (0, h))
-
-    def value_spec():
-        return pl.BlockSpec((rows, HD), lambda h: (0, heads + h))
-
-    width = heads * HD
+def backward(flags, prob, out, grads, queries, own, side, far, rows):
+    width = own[0].shape[1]
+    spec = pl.BlockSpec((rows, HD), lambda h: (0, h))
     f32 = jax.ShapeDtypeStruct((rows, width), jnp.float32)
     bf16 = jax.ShapeDtypeStruct((rows, width), jnp.bfloat16)
     return pl.pallas_call(
-        functools.partial(backward_kernel, scale),
-        grid=(heads,),
+        functools.partial(backward_kernel, 1.0 / math.sqrt(HD)),
+        grid=(width // HD,),
         in_specs=[
+            pl.BlockSpec(memory_space=pltpu.SMEM),
             pl.BlockSpec((1, 3 * rows, rows), lambda h: (h, 0, 0)),
             pl.BlockSpec((HD, rows), lambda h: (h, 0)),
-            col(),
-            col(),
-            col(),
-            value_spec(),
-            col(),
-            value_spec(),
-            col(),
-            value_spec(),
-        ],
-        out_specs=[col()] * 7,
+        ]
+        + [spec] * 10,
+        out_specs=[spec] * 7,
         out_shape=[bf16, f32, f32, bf16, bf16, bf16, bf16],
         name="backward_part",
-    )(prob, out, grad, query, own, own, side, side, far, far)
+    )(flags, prob, out, *grads, *queries, *own, *side, *far)
 
 
 def project_kernel(place_ref, g0, g1, g2, g3, *refs):
@@ -201,14 +181,18 @@
 
 def local(n_tm, n_head, queries, key_rows, value_rows, grad_out, w_out):
     rows, width = queries.shape
-    heads = width // HD
     t, h = lax.axis_index("tm"), lax.axis_index("head")
     y, c = t % 2, h % 2
     slab = t - y + c
     stays = y == c
-    send = functools.partial(exchange, n_tm=n_tm, n_head=n_head)
+
+    def send(block, route):
+        return exchange(block, route, n_tm, n_head)
 
     def turn_route(t, h):
+        return None if (t & 1) == (h & 1) else (t ^ 1, h ^ 1)
+
+    def busy_route(t, h):
         return (t, h ^ 2) if (t & 1) == (h & 1) else (t ^ 1, h ^ 1)
 
     def far_route(t, h):
@@ -220,23 +204,32 @@
     def side_route(t, h):
         return (t, h ^ 1)
 
-    def turned(block):
-        return jnp.where(stays, block, send(block, turn_route))
-
     place = slab % VT
-    linked = jnp.where(c == 1, place < VT - 1, place > 0).astype(jnp.int32)
-
-    own = turned(jnp.concatenate([key_rows, value_rows], 1))
-    query = turned(queries)
-    if n_head == 4 and n_tm == 2 * n_head:
-        grads = [grad_out, send(grad_out, lambda t, h: (t, h ^ 1)), send(grad_out, lambda t, h: (t, h ^ 2))]
-        grads.append(send(grads[2], lambda t, h: (t, h ^ 1)))
+    linked = jnp.where(c == 1, place < VT - 1, place > 0)
+    flags = jnp.stack([linked, stays]).astype(jnp.int32)
+
+    square = n_head == 4 and n_tm == 2 * n_head
+    keys = jnp.where(stays, key_rows, send(key_rows, turn_route))
+    values = jnp.where(stays, value_rows, send(value_rows, turn_route))
+    query_pair = (queries, send(queries, turn_route))
+    if square:
+        grads = [grad_out, send(grad_out, side_route), send(grad_out, lambda t, h: (t, h ^ 2))]
         w1 = send(w_out, lambda t, h: (t ^ 2, h))
         w2 = send(w_out, lambda t, h: (t ^ 4, h))
+        w0y = send(w_out, lambda t, h: (t ^ 1, h))
         w3 = send(w1, lambda t, h: (t ^ 4, h))
-        shards = []
-        for w in (w_out, w1, w2, w3):
-            shards += [w, send(w, lambda t, h: (t ^ 1, h))]
+        w1y = send(w0y, lambda t, h: (t ^ 2, h))
+        grads.append(send(grads[2], side_route))
+        w2y = send(w2, lambda t, h: (t ^ 1, h))
+        w3y = send(w3, lambda t, h: (t ^ 1, h))
+        shards = [w_out, w0y, w1, w1y, w2, w2y, w3, w3y]
+    own = (keys, values)
+    far = tuple(send(b, far_route) for b in own)
+    side = tuple(send(b, side_route) for b in own)
+    heads = width // HD
+    early = heads - 1
+    soft = forward(flags, query_pair, own, side, far, 0, early, rows)
+    if square:
         attn_grad = project(
             jnp.stack([t // 2, y, h]).astype(jnp.int32), grads, shards, rows, width
         )
@@ -246,26 +239,26 @@
             lax.all_gather(w_out, "tm", axis=1, tiled=True),
             NT,
         ).astype(jnp.bfloat16)
-    side = send(own, side_route)
-    far = send(own, far_route)
-    prob, out = forward(linked[None], query, own, side, far, heads, rows)
-    grad = turned(attn_grad)
+    grad_pair = (attn_grad, send(attn_grad, turn_route))
+    soft = forward(flags, query_pair, own, side, far, early, heads - early, rows, tuple(soft))
     dq, dko, dvo, dks, dvs, dkz, dvz = backward(
-        prob, out, grad, query, own, side, far, heads, rows
+        flags, *soft, grad_pair, query_pair, own, side, far, rows
     )
     far_back = [send(d, far_route).astype(jnp.float32) for d in (dkz, dvz)]
     side_back = [send(d, side_route).astype(jnp.float32) for d in (dks, dvs)]
-    linked_f = linked > 0
     sums = [
-        (o + s + jnp.where(linked_f, f, 0.0)).astype(jnp.bfloat16)
-        for o, s, f in zip((dko, dvo), side_back, far_back)
+        (o + s + f).astype(jnp.bfloat16) for o, s, f in zip((dko, dvo), side_back, far_back)
     ]
-    return (turned(dq), turned(sums[0]), turned(sums[1]))
+    return tuple(jnp.where(stays, b, send(b, busy_route)) for b in (dq, *sums))
 
 
 def solution(mesh):
     spec = P("tm", "head")
-    body = functools.partial(local, mesh.shape["tm"], mesh.shape["head"])
+    n_tm, n_head = mesh.shape["tm"], mesh.shape["head"]
+
+    def body(*args):
+        return local(n_tm, n_head, *args)
+
     return jax.shard_map(
         body,
         mesh=mesh,

time: 146 us -> 168 us (1.15)
  waiting for transfers between devices: 65.1 us -> 82.6 us
  starting transfers between devices: 27.2 us -> 33.3 us
  local copies, waits for them, and re-layouts: 3.43 us -> 0.07 us
  Pallas kernels: 40.7 us -> 43.1 us
    ppermute x22 -> x25, waiting for transfers between devices: 65.1 us -> 82.6 us  [exchange(): return lax.ppermute(block, AXES, pairs)]
    ppermute x22 -> x25, starting transfers between devices: 27.2 us -> 33.3 us  [exchange(): return lax.ppermute(block, AXES, pairs)]
    unnamed x27 -> x30, local copies, waits for them, and re-layouts: 3.34 us -> 0.07 us
    pallas_call x2 -> x3, Pallas kernels: 32.8 us -> 35.1 us  [the longest x2 20.4 us: forward(): pl.pallas_call(functools.partial(forward_kernel, scale), grid=(count, 3),...]
    select_n x6 -> x5, other arithmetic: 5.63 us -> 3.87 us  [the longest x3 2.66 us: local(): jnp.where(stays, b, send(b, busy_route))]
  transfers between devices with their start and end apart: 22 -> 25, of which waited for: 11 -> 11; matrix products, arithmetic and copies ran while one was open for 5% -> 4% of each run, Pallas kernels for 18% -> 17%
where the time goes in v2:
time: 168 us; the launch traced here: 167 us
  waiting for transfers between devices  82.6 us (49%)
  Pallas kernels  43.1 us (26%)
  starting transfers between devices  33.3 us (20%)
  other arithmetic  6.97 us (4%)
    ppermute x25, waiting for transfers between devices, exchange(): return lax.ppermute(block, AXES, pairs)  82.6 us
    ppermute x25, starting transfers between devices, exchange(): return lax.ppermute(block, AXES, pairs)  33.3 us
    pallas_call x2, Pallas kernels, forward(): pl.pallas_call(functools.partial(forward_kernel, scale), grid=(count, 3),...  20.4 us
    pallas_call x1, Pallas kernels, backward(): pl.pallas_call(functools.partial(backward_kernel, 1.0 / math.sqrt(HD)), g...  14.7 us
    pallas_call x1, Pallas kernels, project(): pl.pallas_call(project_kernel, in_specs=[pl.BlockSpec(memory_space=pltpu....  8 us
  transfers between devices with their start and end apart: 25, of which 11 were waited for; matrix products, arithmetic and copies ran while one was open for 4% of the time, Pallas kernels for 17%

profile of v2, /device:TPU:0, one launch (start us, length us, event | category | flops | bytes accessed | tf_op | source)
XLA Modules:
  0.0 166.9 jit_solution(8883917822894957401)
XLA Ops:
  0.6 3.0 %collective-permute-start.8 = (bf16[768,768]{1,0:T(8,128)(2,1)}, bf16[768,768]{1,0:T(8,128)(2,1)}, u32[]{:S(2)}, u32[]{:S(2)}) collective-permute-start(bf16[768,768]{1,0:T(8,128)(2,1)} %g0.1), channel_id=1, source_target_pairs={{0,2},{1,3},{2,0},{3,1},{4,6},{5,7},{6,4},{7,5},{8,10},{9,11},{10,... | collective-permute-start | bytes 3538952 | tf_op jit(solution)/shard_map/ppermute | solution.py:32
  3.7 1.6 collective-permute-start.11
  5.2 1.5 collective-permute-start.10
  6.8 0.7 collective-permute-start.1
  7.5 1.9 %collective-permute-start.7 = (bf16[768,768]{1,0:T(8,128)(2,1)}, bf16[768,768]{1,0:T(8,128)(2,1)}, u32[]{:S(2)}, u32[]{:S(2)}) collective-permute-start(bf16[768,768]{1,0:T(8,128)(2,1)} %g0.1), channel_id=1, source_target_pairs={{0,1},{1,0},{2,3},{3,2},{4,5},{5,4},{6,7},{7,6},{8,9},{9,8},{10,11... | collective-permute-start | bytes 3538952 | tf_op jit(solution)/shard_map/ppermute | solution.py:32
  9.4 20.6 %collective-permute-done.8.g2 = bf16[768,768]{1,0:T(8,128)(2,1)} collective-permute-done((bf16[768,768]{1,0:T(8,128)(2,1)}, bf16[768,768]{1,0:T(8,128)(2,1)}, u32[]{:S(2)}, u32[]{:S(2)}) %collective-permute-start.8) | collective-permute-done | bytes 1179680 | tf_op jit(solution)/shard_map/ppermute | solution.py:32
  30.0 0.7 collective-permute-start.2
  30.7 0.0 copy-start.10
  30.7 2.9 %collective-permute-start.13 = (bf16[384,384]{1,0:T(8,128)(2,1)}, bf16[384,384]{1,0:T(8,128)(2,1)S(1)}, u32[]{:S(2)}, u32[]{:S(2)}) collective-permute-start(bf16[384,384]{1,0:T(8,128)(2,1)} %refs_0_.1), channel_id=1, source_target_pairs={{0,16},{1,17},{2,18},{3,19},{4,20},{5,21},{6,22},{7,23},{8,24},{9,... | collective-permute-start | bytes 884744 | tf_op jit(solution)/shard_map/ppermute | solution.py:32
  33.6 13.1 %collective-permute-done.13.refs_4_ = bf16[384,384]{1,0:T(8,128)(2,1)S(1)} collective-permute-done((bf16[384,384]{1,0:T(8,128)(2,1)}, bf16[384,384]{1,0:T(8,128)(2,1)S(1)}, u32[]{:S(2)}, u32[]{:S(2)}) %collective-permute-start.13) | collective-permute-done | bytes 294944 | tf_op jit(solution)/shard_map/ppermute | solution.py:32
  46.7 5.6 %collective-permute-start.12 = (bf16[384,384]{1,0:T(8,128)(2,1)S(1)}, bf16[384,384]{1,0:T(8,128)(2,1)}, u32[]{:S(2)}, u32[]{:S(2)}) collective-permute-start(bf16[384,384]{1,0:T(8,128)(2,1)S(1)} %collective-permute-done.10.refs_1_), channel_id=1, source_target_pairs={{0,8},{1,9},{2,10},{3,11},{4,12},{5,13},{6,14},{7,15},{8,0},{9,1},... | collective-permute-start | bytes 884744 | tf_op jit(solution)/shard_map/ppermute | solution.py:32
  52.3 0.7 collective-permute-start
  53.0 10.7 %collective-permute-done.15.refs_6_ = bf16[384,384]{1,0:T(8,128)(2,1)S(1)} collective-permute-done((bf16[384,384]{1,0:T(8,128)(2,1)S(1)}, bf16[384,384]{1,0:T(8,128)(2,1)S(1)}, u32[]{:S(2)}, u32[]{:S(2)}) %collective-permute-start.15) | collective-permute-done | bytes 294944 | tf_op jit(solution)/shard_map/ppermute | solution.py:32
  63.7 0.9 collective-permute-start.14
  64.6 1.2 collective-permute-start.16
  65.8 1.1 broadcast_select_fusion.4.ko
  67.0 0.0 copy-start
  67.0 0.1 broadcast_select_fusion.3.vo
  67.1 0.0 copy-start.1
  67.1 6.5 %collective-permute-done.14.refs_5_ = bf16[384,384]{1,0:T(8,128)(2,1)S(1)} collective-permute-done((bf16[384,384]{1,0:T(8,128)(2,1)S(1)}, bf16[384,384]{1,0:T(8,128)(2,1)S(1)}, u32[]{:S(2)}, u32[]{:S(2)}) %collective-permute-start.14) | collective-permute-done | bytes 294944 | tf_op jit(solution)/shard_map/ppermute | solution.py:32
  73.6 5.4 %collective-permute-done.16.refs_7_ = bf16[384,384]{1,0:T(8,128)(2,1)S(1)} collective-permute-done((bf16[384,384]{1,0:T(8,128)(2,1)S(1)}, bf16[384,384]{1,0:T(8,128)(2,1)S(1)}, u32[]{:S(2)}, u32[]{:S(2)}) %collective-permute-start.16) | collective-permute-done | bytes 294944 | tf_op jit(solution)/shard_map/ppermute | solution.py:32
  79.0 2.1 %collective-permute-start.5 = (bf16[768,384]{1,0:T(8,128)(2,1)S(1)}, bf16[768,384]{1,0:T(8,128)(2,1)S(1)}, u32[]{:S(2)}, u32[]{:S(2)}) collective-permute-start(bf16[768,384]{1,0:T(8,128)(2,1)S(1)} %broadcast_select_fusion.4.ko), channel_id=1, source_target_pairs={{0,2},{1,8},{2,0},{3,10},{4,6},{5,12},{6,4},{7,14},{8,1},{9,16},{1... | collective-permute-start | bytes 1769480 | tf_op jit(solution)/shard_map/ppermute | solution.py:32
  81.2 0.7 collective-permute-start.6
  81.9 0.7 pad_add_fusion.place_ref
  82.5 8.0 %project.1.ga = bf16[768,384]{1,0:T(8,128)(2,1)} custom-call(s32[3]{0:T(128)} %pad_add_fusion.place_ref, bf16[768,768]{1,0:T(8,128)(2,1)} %g0.1, bf16[768,768]{1,0:T(8,128)(2,1)} %collective-permute-done.7.g1, bf16[768,768]{1,0:T(8,128)(2,1)} %collective-permute-done.8.g2, bf16[768,768]{1,0:T(8,128)(2,1)} %collective-permute-done.9.g3, ...), custom_call_target="tpu_custom_call" | custom-call | tf_op jit(solution)/shard_map/project/pallas_call | solution.py:167
  90.5 0.0 copy-start.2
  90.6 1.5 collective-permute-start.17
  92.1 0.6 add_convert_fusion.2.flag_ref
  92.8 2.7 %collective-permute-done.6.vz = bf16[768,384]{1,0:T(8,128)(2,1)} collective-permute-done((bf16[768,384]{1,0:T(8,128)(2,1)S(1)}, bf16[768,384]{1,0:T(8,128)(2,1)}, u32[]{:S(2)}, u32[]{:S(2)}) %collective-permute-start.6) | collective-permute-done | bytes 589856 | tf_op jit(solution)/shard_map/ppermute | solution.py:32
  95.4 12.8 %shard_map.76 = (bf16[3,2304,768]{2,1,0:T(8,128)(2,1)}, f32[384,768]{1,0:T(8,128)}) custom-call(s32[2]{0:T(128)} %add_convert_fusion.2.flag_ref, bf16[768,384]{1,0:T(8,128)(2,1)} %qa.5, bf16[768,384]{1,0:T(8,128)(2,1)} %copy-done.2, bf16[768,384]{1,0:T(8,128)(2,1)} %copy-done, bf16[768,384]{1,0:T(8,128)(2,1)} %copy-done.1, bf16[768,384]{1,0:T(8,128)(2,1)} %copy-done.3, ...), custom_call_target="tpu_custom_call" | custom-call | tf_op jit(solution)/shard_map/pallas_call | solution.py:76
  108.2 7.6 %shard_map.77 = (bf16[3,2304,768]{2,1,0:T(8,128)(2,1)}, f32[384,768]{1,0:T(8,128)}) custom-call(s32[2]{0:T(128)} %add_convert_fusion.2.flag_ref, bf16[768,384]{1,0:T(8,128)(2,1)} %qa.5, bf16[768,384]{1,0:T(8,128)(2,1)} %copy-done.2, bf16[768,384]{1,0:T(8,128)(2,1)} %copy-done, ...), custom_call_target="tpu_custom_call", output_to_operand_aliasing={{0}: (9, {}), {1}: (10, {})} | custom-call | tf_op jit(solution)/shard_map/pallas_call | solution.py:76
  115.8 14.7 %backward_part.1 = (bf16[768,384]{1,0:T(8,128)(2,1)}, f32[768,384]{1,0:T(8,128)}, f32[768,384]{1,0:T(8,128)}, bf16[768,384]{1,0:T(8,128)(2,1)}, bf16[768,384]{1,...) custom-call(s32[2]{0:T(128)} %add_convert_fusion.2.flag_ref, ...), custom_call_target="tpu_custom_call" | custom-call | tf_op jit(solution)/shard_map/backward_part/pallas_call | solution.py:119
  130.5 0.1 collective-permute-start.22
  130.6 2.1 %collective-permute-start.23 = (bf16[768,384]{1,0:T(8,128)(2,1)}, bf16[768,384]{1,0:T(8,128)(2,1)S(1)}, u32[]{:S(2)}, u32[]{:S(2)}) collective-permute-start(bf16[768,384]{1,0:T(8,128)(2,1)} %get-tuple-element.24), channel_id=1, source_target_pairs={{0,2},{1,8},{2,0},{3,10},{4,6},{5,12},{6,4},{7,14},{8,1},{9,16},{1... | collective-permute-start | bytes 1769480 | tf_op jit(solution)/shard_map/ppermute | solution.py:32
  132.7 0.4 collective-permute-start.20
  133.1 1.6 collective-permute-start.18
  134.7 6.0 %collective-permute-done.23 = bf16[768,384]{1,0:T(8,128)(2,1)S(1)} collective-permute-done((bf16[768,384]{1,0:T(8,128)(2,1)}, bf16[768,384]{1,0:T(8,128)(2,1)S(1)}, u32[]{:S(2)}, u32[]{:S(2)}) %collective-permute-start.23) | collective-permute-done | bytes 589856 | tf_op jit(solution)/shard_map/ppermute | solution.py:32
  140.8 1.6 add_convert_fusion
  142.4 2.1 %collective-permute-start.24 = (bf16[768,384]{1,0:T(8,128)(2,1)S(1)}, bf16[768,384]{1,0:T(8,128)(2,1)S(1)}, u32[]{:S(2)}, u32[]{:S(2)}) collective-permute-start(bf16[768,384]{1,0:T(8,128)(2,1)S(1)} %add_convert_fusion), channel_id=1, source_target_pairs={{0,2},{1,4},{2,0},{3,6},{4,1},{5,7},{6,3},{7,5},{8,10},{9,12},{10,... | collective-permute-start | bytes 1769480 | tf_op jit(solution)/shard_map/ppermute | solution.py:32
  144.5 2.6 %collective-permute-done.20 = bf16[768,384]{1,0:T(8,128)(2,1)S(1)} collective-permute-done((bf16[768,384]{1,0:T(8,128)(2,1)}, bf16[768,384]{1,0:T(8,128)(2,1)S(1)}, u32[]{:S(2)}, u32[]{:S(2)}) %collective-permute-start.20) | collective-permute-done | bytes 589856 | tf_op jit(solution)/shard_map/ppermute | solution.py:32
  147.1 0.2 add_convert_fusion.1
  147.3 2.1 %collective-permute-start.21 = (bf16[768,384]{1,0:T(8,128)(2,1)S(1)}, bf16[768,384]{1,0:T(8,128)(2,1)S(1)}, u32[]{:S(2)}, u32[]{:S(2)}) collective-permute-start(bf16[768,384]{1,0:T(8,128)(2,1)S(1)} %add_convert_fusion.1), channel_id=1, source_target_pairs={{0,2},{1,4},{2,0},{3,6},{4,1},{5,7},{6,3},{7,5},{8,10},{9,12},{10,... | collective-permute-start | bytes 1769480 | tf_op jit(solution)/shard_map/ppermute | solution.py:32
  149.4 4.0 %collective-permute-done.18 = bf16[768,384]{1,0:T(8,128)(2,1)S(1)} collective-permute-done((bf16[768,384]{1,0:T(8,128)(2,1)}, bf16[768,384]{1,0:T(8,128)(2,1)S(1)}, u32[]{:S(2)}, u32[]{:S(2)}) %collective-permute-start.18) | collective-permute-done | bytes 589856 | tf_op jit(solution)/shard_map/ppermute | solution.py:32
  153.4 0.9 broadcast_select_fusion.2
  154.3 5.4 %collective-permute-done.24 = bf16[768,384]{1,0:T(8,128)(2,1)S(1)} collective-permute-done((bf16[768,384]{1,0:T(8,128)(2,1)S(1)}, bf16[768,384]{1,0:T(8,128)(2,1)S(1)}, u32[]{:S(2)}, u32[]{:S(2)}) %collective-permute-start.24) | collective-permute-done | bytes 589856 | tf_op jit(solution)/shard_map/ppermute | solution.py:32
  159.7 0.9 broadcast_select_fusion
  160.6 5.4 %collective-permute-done.21 = bf16[768,384]{1,0:T(8,128)(2,1)S(1)} collective-permute-done((bf16[768,384]{1,0:T(8,128)(2,1)S(1)}, bf16[768,384]{1,0:T(8,128)(2,1)S(1)}, u32[]{:S(2)}, u32[]{:S(2)}) %collective-permute-start.21) | collective-permute-done | bytes 589856 | tf_op jit(solution)/shard_map/ppermute | solution.py:32
  166.0 0.9 broadcast_select_fusion.1
  (45 shorter events, 0.1 us)
Async XLA Ops:
  0.6 66.3 %copy-start.7 = (bf16[768,384]{1,0:T(8,128)(2,1)S(1)}, bf16[768,384]{1,0:T(8,128)(2,1)}, u32[]{:S(2)}) copy-start(bf16[768,384]{1,0:T(8,128)(2,1)} %param.7) | copy-start | bytes 1769476
  0.6 29.3 %collective-permute-start.8 = (bf16[768,768]{1,0:T(8,128)(2,1)}, bf16[768,768]{1,0:T(8,128)(2,1)}, u32[]{:S(2)}, u32[]{:S(2)}) collective-permute-start(bf16[768,768]{1,0:T(8,128)(2,1)} %g0.1), channel_id=1, source_target_pairs={{0,2},{1,3},{2,0},{3,1},{4,6},{5,7},{6,4},{7,5},{8,10},{9,11},{10,... | collective-permute-start | bytes 3538952 | tf_op jit(solution)/shard_map/ppermute | solution.py:32
  3.7 26.3 %collective-permute-start.11 = (bf16[384,384]{1,0:T(8,128)(2,1)}, bf16[384,384]{1,0:T(8,128)(2,1)S(1)}, u32[]{:S(2)}, u32[]{:S(2)}) collective-permute-start(bf16[384,384]{1,0:T(8,128)(2,1)} %refs_0_.1), channel_id=1, source_target_pairs={{0,8},{1,9},{2,10},{3,11},{4,12},{5,13},{6,14},{7,15},{8,0},{9,1},... | collective-permute-start | bytes 884744 | tf_op jit(solution)/shard_map/ppermute | solution.py:32
  5.2 25.4 %collective-permute-start.10 = (bf16[384,384]{1,0:T(8,128)(2,1)}, bf16[384,384]{1,0:T(8,128)(2,1)S(1)}, u32[]{:S(2)}, u32[]{:S(2)}) collective-permute-start(bf16[384,384]{1,0:T(8,128)(2,1)} %refs_0_.1), channel_id=1, source_target_pairs={{0,4},{1,5},{2,6},{3,7},{4,0},{5,1},{6,2},{7,3},{8,12},{9,13},{10,... | collective-permute-start | bytes 884744 | tf_op jit(solution)/shard_map/ppermute | solution.py:32
  6.8 40.0 %collective-permute-start.1 = (bf16[768,384]{1,0:T(8,128)(2,1)}, bf16[768,384]{1,0:T(8,128)(2,1)S(1)}, u32[]{:S(2)}, u32[]{:S(2)}) collective-permute-start(bf16[768,384]{1,0:T(8,128)(2,1)} %param.6), channel_id=1, source_target_pairs={{1,4},{3,6},{4,1},{6,3},{9,12},{11,14},{12,9},{14,11},{17,20},{19,... | collective-permute-start | bytes 1769480 | tf_op jit(solution)/shard_map/ppermute | solution.py:32
  7.5 73.7 %collective-permute-start.7 = (bf16[768,768]{1,0:T(8,128)(2,1)}, bf16[768,768]{1,0:T(8,128)(2,1)}, u32[]{:S(2)}, u32[]{:S(2)}) collective-permute-start(bf16[768,768]{1,0:T(8,128)(2,1)} %g0.1), channel_id=1, source_target_pairs={{0,1},{1,0},{2,3},{3,2},{4,5},{5,4},{6,7},{7,6},{8,9},{9,8},{10,11... | collective-permute-start | bytes 3538952 | tf_op jit(solution)/shard_map/ppermute | solution.py:32
  30.0 51.2 %collective-permute-start.9 = (bf16[768,768]{1,0:T(8,128)(2,1)}, bf16[768,768]{1,0:T(8,128)(2,1)}, u32[]{:S(2)}, u32[]{:S(2)}) collective-permute-start(bf16[768,768]{1,0:T(8,128)(2,1)} %collective-permute-done.8.g2), channel_id=1, source_target_pairs={{0,1},{1,0},{2,3},{3,2},{4,5},{5,4},{6,7},{7,6},{8,9},{9,8},{10,11... | collective-permute-start | bytes 3538952 | tf_op jit(solution)/shard_map/ppermute | solution.py:32
  30.0 34.6 %copy-start.9 = (bf16[384,384]{1,0:T(8,128)(2,1)}, bf16[384,384]{1,0:T(8,128)(2,1)S(1)}, u32[]{:S(2)}) copy-start(bf16[384,384]{1,0:T(8,128)(2,1)S(1)} %collective-permute-done.11.refs_2_) | copy-start | bytes 884740
  30.0 22.3 %collective-permute-start.2 = (bf16[768,384]{1,0:T(8,128)(2,1)}, bf16[768,384]{1,0:T(8,128)(2,1)S(1)}, u32[]{:S(2)}, u32[]{:S(2)}) collective-permute-start(bf16[768,384]{1,0:T(8,128)(2,1)} %param.7), channel_id=1, source_target_pairs={{1,4},{3,6},{4,1},{6,3},{9,12},{11,14},{12,9},{14,11},{17,20},{19,... | collective-permute-start | bytes 1769480 | tf_op jit(solution)/shard_map/ppermute | solution.py:32
  30.7 33.9 %copy-start.10 = (bf16[384,384]{1,0:T(8,128)(2,1)}, bf16[384,384]{1,0:T(8,128)(2,1)S(1)}, u32[]{:S(2)}) copy-start(bf16[384,384]{1,0:T(8,128)(2,1)S(1)} %collective-permute-done.10.refs_1_) | copy-start | bytes 884740
  30.7 16.0 %collective-permute-start.13 = (bf16[384,384]{1,0:T(8,128)(2,1)}, bf16[384,384]{1,0:T(8,128)(2,1)S(1)}, u32[]{:S(2)}, u32[]{:S(2)}) collective-permute-start(bf16[384,384]{1,0:T(8,128)(2,1)} %refs_0_.1), channel_id=1, source_target_pairs={{0,16},{1,17},{2,18},{3,19},{4,20},{5,21},{6,22},{7,23},{8,24},{9,... | collective-permute-start | bytes 884744 | tf_op jit(solution)/shard_map/ppermute | solution.py:32
  46.7 20.3 %copy-start.11 = (bf16[384,384]{1,0:T(8,128)(2,1)}, bf16[384,384]{1,0:T(8,128)(2,1)S(1)}, u32[]{:S(2)}) copy-start(bf16[384,384]{1,0:T(8,128)(2,1)S(1)} %collective-permute-done.13.refs_4_) | copy-start | bytes 884740
  46.7 17.0 %collective-permute-start.15 = (bf16[384,384]{1,0:T(8,128)(2,1)S(1)}, bf16[384,384]{1,0:T(8,128)(2,1)S(1)}, u32[]{:S(2)}, u32[]{:S(2)}) collective-permute-start(bf16[384,384]{1,0:T(8,128)(2,1)S(1)} %collective-permute-done.11.refs_2_), channel_id=1, source_target_pairs={{0,16},{1,17},{2,18},{3,19},{4,20},{5,21},{6,22},{7,23},{8,24},{9,... | collective-permute-start | bytes 884744 | tf_op jit(solution)/shard_map/ppermute | solution.py:32
  46.7 17.9 %collective-permute-start.12 = (bf16[384,384]{1,0:T(8,128)(2,1)S(1)}, bf16[384,384]{1,0:T(8,128)(2,1)}, u32[]{:S(2)}, u32[]{:S(2)}) collective-permute-start(bf16[384,384]{1,0:T(8,128)(2,1)S(1)} %collective-permute-done.10.refs_1_), channel_id=1, source_target_pairs={{0,8},{1,9},{2,10},{3,11},{4,12},{5,13},{6,14},{7,15},{8,0},{9,1},... | collective-permute-start | bytes 884744 | tf_op jit(solution)/shard_map/ppermute | solution.py:32
  52.3 38.3 %collective-permute-start = (bf16[768,384]{1,0:T(8,128)(2,1)}, bf16[768,384]{1,0:T(8,128)(2,1)S(1)}, u32[]{:S(2)}, u32[]{:S(2)}) collective-permute-start(bf16[768,384]{1,0:T(8,128)(2,1)} %qa.5), channel_id=1, source_target_pairs={{1,4},{3,6},{4,1},{6,3},{9,12},{11,14},{12,9},{14,11},{17,20},{19,... | collective-permute-start | bytes 1769480 | tf_op jit(solution)/shard_map/ppermute | solution.py:32
  63.7 3.4 %copy-start.12 = (bf16[384,384]{1,0:T(8,128)(2,1)}, bf16[384,384]{1,0:T(8,128)(2,1)S(1)}, u32[]{:S(2)}) copy-start(bf16[384,384]{1,0:T(8,128)(2,1)S(1)} %collective-permute-done.15.refs_6_) | copy-start | bytes 884740
  63.7 9.9 %collective-permute-start.14 = (bf16[384,384]{1,0:T(8,128)(2,1)S(1)}, bf16[384,384]{1,0:T(8,128)(2,1)S(1)}, u32[]{:S(2)}, u32[]{:S(2)}) collective-permute-start(bf16[384,384]{1,0:T(8,128)(2,1)S(1)} %collective-permute-done.13.refs_4_), channel_id=1, source_target_pairs={{0,4},{1,5},{2,6},{3,7},{4,0},{5,1},{6,2},{7,3},{8,12},{9,13},{10,... | collective-permute-start | bytes 884744 | tf_op jit(solution)/shard_map/ppermute | solution.py:32
  64.6 14.4 %collective-permute-start.16 = (bf16[384,384]{1,0:T(8,128)(2,1)S(1)}, bf16[384,384]{1,0:T(8,128)(2,1)S(1)}, u32[]{:S(2)}, u32[]{:S(2)}) collective-permute-start(bf16[384,384]{1,0:T(8,128)(2,1)S(1)} %collective-permute-done.15.refs_6_), channel_id=1, source_target_pairs={{0,4},{1,5},{2,6},{3,7},{4,0},{5,1},{6,2},{7,3},{8,12},{9,13},{10,... | collective-permute-start | bytes 884744 | tf_op jit(solution)/shard_map/ppermute | solution.py:32
  67.0 23.6 %copy-start = (bf16[768,384]{1,0:T(8,128)(2,1)}, bf16[768,384]{1,0:T(8,128)(2,1)S(1)}, u32[]{:S(2)}) copy-start(bf16[768,384]{1,0:T(8,128)(2,1)S(1)} %broadcast_select_fusion.4.ko) | copy-start | bytes 1769476
  67.1 23.5 %copy-start.1 = (bf16[768,384]{1,0:T(8,128)(2,1)}, bf16[768,384]{1,0:T(8,128)(2,1)S(1)}, u32[]{:S(2)}) copy-start(bf16[768,384]{1,0:T(8,128)(2,1)S(1)} %broadcast_select_fusion.3.vo) | copy-start | bytes 1769476
  73.6 7.5 %copy-start.13 = (bf16[384,384]{1,0:T(8,128)(2,1)}, bf16[384,384]{1,0:T(8,128)(2,1)S(1)}, u32[]{:S(2)}) copy-start(bf16[384,384]{1,0:T(8,128)(2,1)S(1)} %collective-permute-done.14.refs_5_) | copy-start | bytes 884740
  73.6 19.1 %collective-permute-start.3 = (bf16[768,384]{1,0:T(8,128)(2,1)S(1)}, bf16[768,384]{1,0:T(8,128)(2,1)S(1)}, u32[]{:S(2)}, u32[]{:S(2)}) collective-permute-start(bf16[768,384]{1,0:T(8,128)(2,1)S(1)} %broadcast_select_fusion.4.ko), channel_id=1, source_target_pairs={{0,1},{1,0},{2,3},{3,2},{4,5},{5,4},{6,7},{7,6},{8,9},{9,8},{10,11... | collective-permute-start | bytes 1769480 | tf_op jit(solution)/shard_map/ppermute | solution.py:32
  79.0 2.1 %copy-start.14 = (bf16[384,384]{1,0:T(8,128)(2,1)}, bf16[384,384]{1,0:T(8,128)(2,1)S(1)}, u32[]{:S(2)}) copy-start(bf16[384,384]{1,0:T(8,128)(2,1)S(1)} %collective-permute-done.16.refs_7_) | copy-start | bytes 884740
  79.0 13.7 %collective-permute-start.5 = (bf16[768,384]{1,0:T(8,128)(2,1)S(1)}, bf16[768,384]{1,0:T(8,128)(2,1)S(1)}, u32[]{:S(2)}, u32[]{:S(2)}) collective-permute-start(bf16[768,384]{1,0:T(8,128)(2,1)S(1)} %broadcast_select_fusion.4.ko), channel_id=1, source_target_pairs={{0,2},{1,8},{2,0},{3,10},{4,6},{5,12},{6,4},{7,14},{8,1},{9,16},{1... | collective-permute-start | bytes 1769480 | tf_op jit(solution)/shard_map/ppermute | solution.py:32
  81.1 11.6 %collective-permute-start.4 = (bf16[768,384]{1,0:T(8,128)(2,1)S(1)}, bf16[768,384]{1,0:T(8,128)(2,1)S(1)}, u32[]{:S(2)}, u32[]{:S(2)}) collective-permute-start(bf16[768,384]{1,0:T(8,128)(2,1)S(1)} %broadcast_select_fusion.3.vo), channel_id=1, source_target_pairs={{0,1},{1,0},{2,3},{3,2},{4,5},{5,4},{6,7},{7,6},{8,9},{9,8},{10,11... | collective-permute-start | bytes 1769480 | tf_op jit(solution)/shard_map/ppermute | solution.py:32
  81.2 14.3 %collective-permute-start.6 = (bf16[768,384]{1,0:T(8,128)(2,1)S(1)}, bf16[768,384]{1,0:T(8,128)(2,1)}, u32[]{:S(2)}, u32[]{:S(2)}) collective-permute-start(bf16[768,384]{1,0:T(8,128)(2,1)S(1)} %broadcast_select_fusion.3.vo), channel_id=1, source_target_pairs={{0,2},{1,8},{2,0},{3,10},{4,6},{5,12},{6,4},{7,14},{8,1},{9,16},{1... | collective-permute-start | bytes 1769480 | tf_op jit(solution)/shard_map/ppermute | solution.py:32
  90.5 4.9 %copy-start.2 = (bf16[768,384]{1,0:T(8,128)(2,1)}, bf16[768,384]{1,0:T(8,128)(2,1)S(1)}, u32[]{:S(2)}) copy-start(bf16[768,384]{1,0:T(8,128)(2,1)S(1)} %collective-permute-done.qb) | copy-start | bytes 1769476
  90.6 25.3 %collective-permute-start.17 = (bf16[768,384]{1,0:T(8,128)(2,1)}, bf16[768,384]{1,0:T(8,128)(2,1)}, u32[]{:S(2)}, u32[]{:S(2)}) collective-permute-start(bf16[768,384]{1,0:T(8,128)(2,1)} %project.1.ga), channel_id=1, source_target_pairs={{1,4},{3,6},{4,1},{6,3},{9,12},{11,14},{12,9},{14,11},{17,20},{19,... | collective-permute-start | bytes 1769480 | tf_op jit(solution)/shard_map/ppermute | solution.py:32
  92.7 2.7 %copy-start.3 = (bf16[768,384]{1,0:T(8,128)(2,1)}, bf16[768,384]{1,0:T(8,128)(2,1)S(1)}, u32[]{:S(2)}) copy-start(bf16[768,384]{1,0:T(8,128)(2,1)S(1)} %collective-permute-done.3.ks) | copy-start | bytes 1769476
  92.7 2.7 %copy-start.5 = (bf16[768,384]{1,0:T(8,128)(2,1)}, bf16[768,384]{1,0:T(8,128)(2,1)S(1)}, u32[]{:S(2)}) copy-start(bf16[768,384]{1,0:T(8,128)(2,1)S(1)} %collective-permute-done.4.vs) | copy-start | bytes 1769476
  92.7 2.7 %copy-start.4 = (bf16[768,384]{1,0:T(8,128)(2,1)}, bf16[768,384]{1,0:T(8,128)(2,1)S(1)}, u32[]{:S(2)}) copy-start(bf16[768,384]{1,0:T(8,128)(2,1)S(1)} %collective-permute-done.5.kz) | copy-start | bytes 1769476
  130.5 4.2 %collective-permute-start.22 = (bf16[768,384]{1,0:T(8,128)(2,1)}, bf16[768,384]{1,0:T(8,128)(2,1)S(1)}, u32[]{:S(2)}, u32[]{:S(2)}) collective-permute-start(bf16[768,384]{1,0:T(8,128)(2,1)} %get-tuple-element.23), channel_id=1, source_target_pairs={{0,1},{1,0},{2,3},{3,2},{4,5},{5,4},{6,7},{7,6},{8,9},{9,8},{10,11... | collective-permute-start | bytes 1769480 | tf_op jit(solution)/shard_map/ppermute | solution.py:32
  130.6 10.2 %collective-permute-start.23 = (bf16[768,384]{1,0:T(8,128)(2,1)}, bf16[768,384]{1,0:T(8,128)(2,1)S(1)}, u32[]{:S(2)}, u32[]{:S(2)}) collective-permute-start(bf16[768,384]{1,0:T(8,128)(2,1)} %get-tuple-element.24), channel_id=1, source_target_pairs={{0,2},{1,8},{2,0},{3,10},{4,6},{5,12},{6,4},{7,14},{8,1},{9,16},{1... | collective-permute-start | bytes 1769480 | tf_op jit(solution)/shard_map/ppermute | solution.py:32
  132.7 11.8 %collective-permute-start.19 = (bf16[768,384]{1,0:T(8,128)(2,1)}, bf16[768,384]{1,0:T(8,128)(2,1)S(1)}, u32[]{:S(2)}, u32[]{:S(2)}) collective-permute-start(bf16[768,384]{1,0:T(8,128)(2,1)} %get-tuple-element.20), channel_id=1, source_target_pairs={{0,1},{1,0},{2,3},{3,2},{4,5},{5,4},{6,7},{7,6},{8,9},{9,8},{10,11... | collective-permute-start | bytes 1769480 | tf_op jit(solution)/shard_map/ppermute | solution.py:32
  132.7 14.4 %collective-permute-start.20 = (bf16[768,384]{1,0:T(8,128)(2,1)}, bf16[768,384]{1,0:T(8,128)(2,1)S(1)}, u32[]{:S(2)}, u32[]{:S(2)}) collective-permute-start(bf16[768,384]{1,0:T(8,128)(2,1)} %get-tuple-element.21), channel_id=1, source_target_pairs={{0,2},{1,8},{2,0},{3,10},{4,6},{5,12},{6,4},{7,14},{8,1},{9,16},{1... | collective-permute-start | bytes 1769480 | tf_op jit(solution)/shard_map/ppermute | solution.py:32
  133.1 20.3 %collective-permute-start.18 = (bf16[768,384]{1,0:T(8,128)(2,1)}, bf16[768,384]{1,0:T(8,128)(2,1)S(1)}, u32[]{:S(2)}, u32[]{:S(2)}) collective-permute-start(bf16[768,384]{1,0:T(8,128)(2,1)} %get-tuple-element.18), channel_id=1, source_target_pairs={{0,2},{1,4},{2,0},{3,6},{4,1},{5,7},{6,3},{7,5},{8,10},{9,12},{10,... | collective-permute-start | bytes 1769480 | tf_op jit(solution)/shard_map/ppermute | solution.py:32
  140.8 6.3 %copy-start.6 = (f32[768,384]{1,0:T(8,128)S(1)}, f32[768,384]{1,0:T(8,128)}, u32[]{:S(2)}) copy-start(f32[768,384]{1,0:T(8,128)} %get-tuple-element.19) | copy-start | bytes 3538948
  142.4 17.4 %collective-permute-start.24 = (bf16[768,384]{1,0:T(8,128)(2,1)S(1)}, bf16[768,384]{1,0:T(8,128)(2,1)S(1)}, u32[]{:S(2)}, u32[]{:S(2)}) collective-permute-start(bf16[768,384]{1,0:T(8,128)(2,1)S(1)} %add_convert_fusion), channel_id=1, source_target_pairs={{0,2},{1,4},{2,0},{3,6},{4,1},{5,7},{6,3},{7,5},{8,10},{9,12},{10,... | collective-permute-start | bytes 1769480 | tf_op jit(solution)/shard_map/ppermute | solution.py:32
  147.1 6.3 %copy-start.8 = (bf16[768,384]{1,0:T(8,128)(2,1)S(1)}, bf16[768,384]{1,0:T(8,128)(2,1)}, u32[]{:S(2)}) copy-start(bf16[768,384]{1,0:T(8,128)(2,1)} %get-tuple-element.18) | copy-start | bytes 1769476
  147.3 18.8 %collective-permute-start.21 = (bf16[768,384]{1,0:T(8,128)(2,1)S(1)}, bf16[768,384]{1,0:T(8,128)(2,1)S(1)}, u32[]{:S(2)}, u32[]{:S(2)}) collective-permute-start(bf16[768,384]{1,0:T(8,128)(2,1)S(1)} %add_convert_fusion.1), channel_id=1, source_target_pairs={{0,2},{1,4},{2,0},{3,6},{4,1},{5,7},{6,3},{7,5},{8,10},{9,12},{10,... | collective-permute-start | bytes 1769480 | tf_op jit(solution)/shard_map/ppermute | solution.py:32

commit v3 on v2

v3 whole, which is shorter than its diff:
```python
import functools
import math

import jax
import jax.numpy as jnp
from jax import lax
from jax.experimental import pallas as pl
from jax.experimental.pallas import tpu as pltpu
from jax.sharding import PartitionSpec as P


HD = 128
VT = 8
AXES = ("tm", "head")
NT = (((1,), (1,)), ((), ()))
TN = (((0,), (0,)), ((), ()))


def dot(a, b, dims=(((1,), (0,)), ((), ()))):
    return lax.dot_general(a, b, dims, preferred_element_type=jnp.float32)


def exchange(block, route, n_tm, n_head):
    pairs = []
    for t in range(n_tm):
        for h in range(n_head):
            target = route(t, h)
            if target is None:
                continue
            to_t, to_h = target
            pairs.append((t * n_head + h, to_t * n_head + to_h))
    return lax.ppermute(block, AXES, pairs)


def fold(block, join):
    return join(block.reshape(block.shape[0] // 8, 8, block.shape[1]), axis=0)


def soften_kernel(parts, tile, flag_ref, qa, qb, *refs):
    keys, values = refs[:parts], refs[parts : 2 * parts]
    e_ref, o_ref, stat_ref, vt = refs[2 * parts : 2 * parts + 4]
    held = refs[2 * parts + 4 :]
    rows = qa.shape[0]
    step = 256
    factor = math.log2(math.e) / math.sqrt(HD)
    query = jnp.where(flag_ref[1] > 0, qa[...], qb[...])
    spots = [(i, first) for i in range(parts) for first in range(0, rows, step)]

    def score(n):
        peak = None
        for i, first in spots:
            s = dot(keys[i][first : first + step, :], query[n * tile : (n + 1) * tile], NT)
            held[n][i * rows + first : i * rows + first + step, :] = s
            top = fold(s, jnp.max)
            peak = top if peak is None else jnp.maximum(peak, top)
        return jnp.max(peak, axis=0, keepdims=True) * factor

    def soften(n, shift):
        total, out = None, None
        for i, first in spots:
            span = slice(i * rows + first, i * rows + first + step)
            w = jnp.exp2(held[n][span, :] * factor - shift)
            mass = fold(w, jnp.sum)
            total = mass if total is None else total + mass
            low = w.astype(jnp.bfloat16)
            e_ref[0, span, n * tile : (n + 1) * tile] = low
            part = dot(vt[:, span], low)
            out = part if out is None else out + part
        o_ref[:, n * tile : (n + 1) * tile] = out
        stat_ref[0:1, n * tile : (n + 1) * tile] = shift
        stat_ref[1:2, n * tile : (n + 1) * tile] = jnp.sum(total, axis=0, keepdims=True)

    shift = score(0)
    for i in range(parts):
        vt[:, i * rows : (i + 1) * rows] = values[i][...].T
    for n in range(rows // tile):
        later = score(n + 1) if (n + 1) * tile < rows else None
        soften(n, shift)
        shift = later


def soften(flags, queries, keys, values):
    rows, width = queries[0].shape
    parts, heads, tile = len(keys), width // HD, 256
    spec = pl.BlockSpec((rows, HD), lambda h: (0, h))
    return pl.pallas_call(
        functools.partial(soften_kernel, parts, tile),
        grid=(heads,),
        in_specs=[pl.BlockSpec(memory_space=pltpu.SMEM)] + [spec] * (2 + 2 * parts),
        out_specs=[
            pl.BlockSpec((1, parts * rows, rows), lambda h: (h, 0, 0)),
            pl.BlockSpec((HD, rows), lambda h: (h, 0)),
            pl.BlockSpec((8, rows), lambda h: (h, 0)),
        ],
        out_shape=[
            jax.ShapeDtypeStruct((heads, parts * rows, rows), jnp.bfloat16),
            jax.ShapeDtypeStruct((heads * HD, rows), jnp.float32),
            jax.ShapeDtypeStruct((heads * 8, rows), jnp.float32),
        ],
        scratch_shapes=[pltpu.VMEM((HD, parts * rows), jnp.bfloat16)]
        + [pltpu.VMEM((parts * rows, tile), jnp.float32)] * (rows // tile),
    )(flags, *queries, *keys, *values)


def backward_kernel(far, flag_ref, e_ref, on, sn, of, sf, ga, gb, qa, qb, *refs):
    rows = qa.shape[0]
    step = 256
    scale = 1.0 / math.sqrt(HD)
    stays = flag_ref[1] > 0
    query = jnp.where(stays, qa[...], qb[...])
    flipped = jnp.where(stays, ga[...], gb[...]).astype(jnp.float32).T
    near_top = sn[0:1, :]
    far_top = jnp.where(flag_ref[0] > 0, sf[0:1, :], -jnp.inf)
    top = jnp.maximum(near_top, far_top)
    near_share, far_share = jnp.exp2(near_top - top), jnp.exp2(far_top - top)
    inverse = 1.0 / (near_share * sn[1:2, :] + far_share * sf[1:2, :])
    near_share, far_share = near_share * inverse, far_share * inverse
    near_grad = (flipped * near_share).astype(jnp.bfloat16)
    far_grad = (flipped * far_share).astype(jnp.bfloat16)
    inner = jnp.sum(
        on[...] * near_grad.astype(jnp.float32) + of[...] * far_grad.astype(jnp.float32),
        axis=0,
        keepdims=True,
    )
    if far:
        kz, vz, dkz, dvz, dq = refs
        slabs = ((kz, vz, dkz, dvz),)
        total, grad_t, inner = None, far_grad, inner * far_share
    else:
        ks, vs, ko, vo, dq_far, dks, dvs, dko, dvo, dq = refs
        slabs = ((ks, vs, dks, dvs), (ko, vo, dko, dvo))
        total, grad_t, inner = dq_far[...], near_grad, inner * near_share
    grad = grad_t.T
    for i, (k, v, dk, dv) in enumerate(slabs):
        base = 0 if far else (1 - i) * rows
        for first in range(0, rows, step):
            weight = e_ref[0, base + first : base + first + step, :]
            slope = dot(v[first : first + step, :], grad_t)
            delta = (weight.astype(jnp.float32) * (slope - inner)).astype(jnp.bfloat16)
            dv[first : first + step, :] = dot(weight, grad).astype(dv.dtype)
            dk[first : first + step, :] = (dot(delta, query) * scale).astype(dk.dtype)
            part = dot(k[first : first + step, :], delta, TN)
            total = part if total is None else total + part
    dq[...] = total if far else (total * scale).T.astype(dq.dtype)


def backward(far, flags, weights, near, away, grads, queries, keys, values, dq_far=()):
    rows, width = queries[0].shape
    heads = width // HD
    spec = pl.BlockSpec((rows, HD), lambda h: (0, h))
    flip = pl.BlockSpec((HD, rows), lambda h: (h, 0))
    stat = pl.BlockSpec((8, rows), lambda h: (h, 0))
    f32 = jax.ShapeDtypeStruct((rows, width), jnp.float32)
    bf16 = jax.ShapeDtypeStruct((rows, width), jnp.bfloat16)
    slabs = [r for pair in zip(keys, values) for r in pair]
    if far:
        out_specs = [spec, spec, flip]
        out_shape = [bf16, bf16, jax.ShapeDtypeStruct((width, rows), jnp.float32)]
    else:
        out_specs = [spec] * 5
        out_shape = [bf16, bf16, f32, f32, bf16]
    return pl.pallas_call(
        functools.partial(backward_kernel, far),
        grid=(heads,),
        in_specs=[
            pl.BlockSpec(memory_space=pltpu.SMEM),
            pl.BlockSpec((1, weights.shape[1], rows), lambda h: (h, 0, 0)),
            flip,
            stat,
            flip,
            stat,
        ]
        + [spec] * (4 + len(slabs))
        + [flip] * len(dq_far),
        out_specs=out_specs,
        out_shape=out_shape,
        name="backward_far" if far else "backward_near",
    )(flags, weights, *near, *away, *grads, *queries, *slabs, *dq_far)


def project_kernel(place_ref, g0, g1, g2, g3, *refs):
    shards = refs[:8]
    out_ref, gbuf, wbuf, gsem, wsem = refs[8:]
    z, y, h = place_ref[0], place_ref[1], place_ref[2]
    width = out_ref.shape[1]
    copies = []
    for m in range(4):
        for n in range(2):
            copies.append(
                pltpu.make_async_copy(
                    shards[2 * m + n], wbuf.at[z ^ m, y ^ n], wsem.at[2 * m + n]
                )
            )
    grads = [
        pltpu.make_async_copy(g, gbuf.at[m], gsem.at[m]) for m, g in enumerate((g0, g1, g2, g3))
    ]
    for c in copies:
        c.start()
    for c in grads:
        c.start()
    for c in copies:
        c.wait()
    total = None
    for m in range(4):
        grads[m].wait()
        for n in range(2):
            part = dot(gbuf[m, :, n * width : (n + 1) * width], wbuf[h ^ m, n], NT)
            total = part if total is None else total + part
    out_ref[...] = total.astype(out_ref.dtype)


def project(place, grads, shards, rows, width):
    anywhere = pl.BlockSpec(memory_space=pl.ANY)
    return pl.pallas_call(
        project_kernel,
        in_specs=[pl.BlockSpec(memory_space=pltpu.SMEM)] + [anywhere] * 12,
        out_specs=pl.BlockSpec(memory_space=pltpu.VMEM),
        out_shape=jax.ShapeDtypeStruct((rows, width), jnp.bfloat16),
        scratch_shapes=[
            pltpu.VMEM((4,) + grads[0].shape, jnp.bfloat16),
            pltpu.VMEM((4, 2) + shards[0].shape, jnp.bfloat16),
            pltpu.SemaphoreType.DMA((4,)),
            pltpu.SemaphoreType.DMA((8,)),
        ],
        name="project",
    )(place, *grads, *shards)


def local(n_tm, n_head, queries, key_rows, value_rows, grad_out, w_out):
    rows, width = queries.shape
    t, h = lax.axis_index("tm"), lax.axis_index("head")
    y, c = t % 2, h % 2
    slab = t - y + c
    stays = y == c

    def send(block, route):
        return exchange(block, route, n_tm, n_head)

    def turn_route(t, h):
        return None if (t & 1) == (h & 1) else (t ^ 1, h ^ 1)

    def busy_route(t, h):
        return (t, h ^ 2) if (t & 1) == (h & 1) else (t ^ 1, h ^ 1)

    def far_route(t, h):
        here = (t & ~1) + (h & 1)
        there = here + 1 if h & 1 else here - 1
        inside = 0 <= there < n_tm and there // VT == here // VT
        return (t + 2 if h & 1 else t - 2, h ^ 1) if inside else (t, h ^ 2)

    def side_route(t, h):
        return (t, h ^ 1)

    place = slab % VT
    linked = jnp.where(c == 1, place < VT - 1, place > 0)
    flags = jnp.stack([linked, stays]).astype(jnp.int32)

    square = n_head == 4 and n_tm == 2 * n_head
    keys = jnp.where(stays, key_rows, send(key_rows, turn_route))
    values = jnp.where(stays, value_rows, send(value_rows, turn_route))
    query_pair = (queries, send(queries, turn_route))
    if square:
        grads = [
            grad_out,
            send(grad_out, side_route),
            send(grad_out, lambda t, h: (t, h ^ 2)),
        ]
        w1 = send(w_out, lambda t, h: (t ^ 2, h))
        w2 = send(w_out, lambda t, h: (t ^ 4, h))
        w0y = send(w_out, lambda t, h: (t ^ 1, h))
        w3 = send(w1, lambda t, h: (t ^ 4, h))
        w1y = send(w0y, lambda t, h: (t ^ 2, h))
        grads.append(send(grads[2], side_route))
        w2y = send(w2, lambda t, h: (t ^ 1, h))
        w3y = send(w3, lambda t, h: (t ^ 1, h))
        shards = [w_out, w0y, w1, w1y, w2, w2y, w3, w3y]
    far_k, far_v = send(keys, far_route), send(values, far_route)
    side_k, side_v = send(keys, side_route), send(values, side_route)
    near_weights, *near = soften(flags, query_pair, (keys, side_k), (values, side_v))
    if square:
        attn_grad = project(
            jnp.stack([t // 2, y, h]).astype(jnp.int32), grads, shards, rows, width
        )
    else:
        attn_grad = dot(
            lax.all_gather(grad_out, "head", axis=1, tiled=True),
            lax.all_gather(w_out, "tm", axis=1, tiled=True),
            NT,
        ).astype(jnp.bfloat16)
    grad_pair = (attn_grad, send(attn_grad, turn_route))
    far_weights, *away = soften(flags, query_pair, (far_k,), (far_v,))
    dkz, dvz, dq_far = backward(
        True, flags, far_weights, near, away, grad_pair, query_pair, (far_k,), (far_v,)
    )
    far_back = [send(d, far_route).astype(jnp.float32) for d in (dvz, dkz)]
    dks, dvs, dko, dvo, dq = backward(
        False,
        flags,
        near_weights,
        near,
        away,
        grad_pair,
        query_pair,
        (side_k, keys),
        (side_v, values),
        (dq_far,),
    )
    side_back = [send(d, side_route).astype(jnp.float32) for d in (dvs, dks)]
    dv, dk = [
        (o + s + f).astype(jnp.bfloat16) for o, s, f in zip((dvo, dko), side_back, far_back)
    ]
    return tuple(jnp.where(stays, b, send(b, busy_route)) for b in (dq, dk, dv))


def solution(mesh):
    spec = P("tm", "head")
    n_tm, n_head = mesh.shape["tm"], mesh.shape["head"]

    def body(*args):
        return local(n_tm, n_head, *args)

    return jax.shard_map(
        body,
        mesh=mesh,
        in_specs=(spec, spec, spec, spec, P("head", "tm")),
        out_specs=(spec, spec, spec),
        check_vma=False,
    )
```

time: 168 us -> 155 us (0.923)
  starting transfers between devices: 33.3 us -> 24.7 us
  waiting for transfers between devices: 82.6 us -> 77.6 us
    ppermute x25, starting transfers between devices: 33.3 us -> 24.7 us  [exchange(): return lax.ppermute(block, AXES, pairs)]
    ppermute x25, waiting for transfers between devices: 82.6 us -> 77.6 us  [exchange(): return lax.ppermute(block, AXES, pairs)]
    pallas_call x3 -> x4, Pallas kernels: 35.1 us -> 34.2 us  [the longest x2 19 us: backward(): pl.pallas_call(functools.partial(backward_kernel, far), grid=(heads,), in...]
  transfers between devices with their start and end apart: 25 -> 25, of which waited for: 11 -> 12; matrix products, arithmetic and copies ran while one was open for 4% -> 4% of each run, Pallas kernels for 17% -> 15%
where the time goes in v3:
time: 155 us; the launch traced here: 154 us
  waiting for transfers between devices  77.6 us (50%)
  Pallas kernels  42.2 us (27%)
  starting transfers between devices  24.7 us (16%)
  other arithmetic  6.93 us (4%)
  local copies, waits for them, and re-layouts  1.7 us (1%)
    ppermute x25, waiting for transfers between devices, exchange(): return lax.ppermute(block, AXES, pairs)  77.6 us
    ppermute x25, starting transfers between devices, exchange(): return lax.ppermute(block, AXES, pairs)  24.7 us
    pallas_call x2, Pallas kernels, backward(): pl.pallas_call(functools.partial(backward_kernel, far), grid=(heads,), in...  19 us
    pallas_call x2, Pallas kernels, soften(): pl.pallas_call(functools.partial(soften_kernel, parts, tile), grid=(heads...  15.2 us
    pallas_call x1, Pallas kernels, project(): pl.pallas_call(project_kernel, in_specs=[pl.BlockSpec(memory_space=pltpu....  8 us
  transfers between devices with their start and end apart: 25, of which 12 were waited for; matrix products, arithmetic and copies ran while one was open for 4% of the time, Pallas kernels for 15%

profile of v3, /device:TPU:0, one launch (start us, length us, event | category | flops | bytes accessed | tf_op | source)
XLA Modules:
  0.0 154.0 jit_solution(5778768190075893430)
XLA Ops:
  0.6 3.0 %collective-permute-start.8 = (bf16[768,768]{1,0:T(8,128)(2,1)}, bf16[768,768]{1,0:T(8,128)(2,1)}, u32[]{:S(2)}, u32[]{:S(2)}) collective-permute-start(bf16[768,768]{1,0:T(8,128)(2,1)} %g0.1), channel_id=1, source_target_pairs={{0,2},{1,3},{2,0},{3,1},{4,6},{5,7},{6,4},{7,5},{8,10},{9,11},{10,... | collective-permute-start | bytes 3538952 | tf_op jit(solution)/shard_map/ppermute | solution.py:32
  3.7 1.6 %collective-permute-start.11 = (bf16[384,384]{1,0:T(8,128)(2,1)}, bf16[384,384]{1,0:T(8,128)(2,1)S(1)}, u32[]{:S(2)}, u32[]{:S(2)}) collective-permute-start(bf16[384,384]{1,0:T(8,128)(2,1)} %refs_0_.1), channel_id=1, source_target_pairs={{0,8},{1,9},{2,10},{3,11},{4,12},{5,13},{6,14},{7,15},{8,0},{9,1},... | collective-permute-start | bytes 884744 | tf_op jit(solution)/shard_map/ppermute | solution.py:32
  5.2 1.5 collective-permute-start.10
  6.8 2.6 %collective-permute-start.13 = (bf16[384,384]{1,0:T(8,128)(2,1)}, bf16[384,384]{1,0:T(8,128)(2,1)S(1)}, u32[]{:S(2)}, u32[]{:S(2)}) collective-permute-start(bf16[384,384]{1,0:T(8,128)(2,1)} %refs_0_.1), channel_id=1, source_target_pairs={{0,16},{1,17},{2,18},{3,19},{4,20},{5,21},{6,22},{7,23},{8,24},{9,... | collective-permute-start | bytes 884744 | tf_op jit(solution)/shard_map/ppermute | solution.py:32
  9.4 7.9 %collective-permute-done.11.refs_2_ = bf16[384,384]{1,0:T(8,128)(2,1)S(1)} collective-permute-done((bf16[384,384]{1,0:T(8,128)(2,1)}, bf16[384,384]{1,0:T(8,128)(2,1)S(1)}, u32[]{:S(2)}, u32[]{:S(2)}) %collective-permute-start.11) | collective-permute-done | bytes 294944 | tf_op jit(solution)/shard_map/ppermute | solution.py:32
  17.3 0.7 collective-permute-start.15
  18.0 12.0 %collective-permute-done.8.g2 = bf16[768,768]{1,0:T(8,128)(2,1)} collective-permute-done((bf16[768,768]{1,0:T(8,128)(2,1)}, bf16[768,768]{1,0:T(8,128)(2,1)}, u32[]{:S(2)}, u32[]{:S(2)}) %collective-permute-start.8) | collective-permute-done | bytes 1179680 | tf_op jit(solution)/shard_map/ppermute | solution.py:32
  30.0 0.7 collective-permute-start.1
  30.7 0.7 collective-permute-start.3
  31.4 3.4 %collective-permute-done.15.refs_6_ = bf16[384,384]{1,0:T(8,128)(2,1)S(1)} collective-permute-done((bf16[384,384]{1,0:T(8,128)(2,1)S(1)}, bf16[384,384]{1,0:T(8,128)(2,1)S(1)}, u32[]{:S(2)}, u32[]{:S(2)}) %collective-permute-start.15) | collective-permute-done | bytes 294944 | tf_op jit(solution)/shard_map/ppermute | solution.py:32
  34.8 9.5 %collective-permute-done.12.refs_3_ = bf16[384,384]{1,0:T(8,128)(2,1)} collective-permute-done((bf16[384,384]{1,0:T(8,128)(2,1)S(1)}, bf16[384,384]{1,0:T(8,128)(2,1)}, u32[]{:S(2)}, u32[]{:S(2)}) %collective-permute-start.12) | collective-permute-done | bytes 294944 | tf_op jit(solution)/shard_map/ppermute | solution.py:32
  44.3 0.7 collective-permute-start
  45.0 0.6 pad_add_fusion.place_ref
  45.7 3.1 %collective-permute-start.14 = (bf16[384,384]{1,0:T(8,128)(2,1)S(1)}, bf16[384,384]{1,0:T(8,128)(2,1)S(1)}, u32[]{:S(2)}, u32[]{:S(2)}) collective-permute-start(bf16[384,384]{1,0:T(8,128)(2,1)S(1)} %collective-permute-done.13.refs_4_), channel_id=1, source_target_pairs={{0,4},{1,5},{2,6},{3,7},{4,0},{5,1},{6,2},{7,3},{8,12},{9,13},{10,... | collective-permute-start | bytes 884744 | tf_op jit(solution)/shard_map/ppermute | solution.py:32
  48.8 0.7 collective-permute-start.16
  49.5 1.1 broadcast_select_fusion.4.refs_0_.refs_2_
  50.6 0.1 broadcast_select_fusion.3.refs_2_.refs_3_
  50.7 14.8 %collective-permute-done.14.refs_5_ = bf16[384,384]{1,0:T(8,128)(2,1)S(1)} collective-permute-done((bf16[384,384]{1,0:T(8,128)(2,1)S(1)}, bf16[384,384]{1,0:T(8,128)(2,1)S(1)}, u32[]{:S(2)}, u32[]{:S(2)}) %collective-permute-start.14) | collective-permute-done | bytes 294944 | tf_op jit(solution)/shard_map/ppermute | solution.py:32
  65.6 0.6 collective-permute-start.5
  66.2 2.5 %collective-permute-done.16.refs_7_ = bf16[384,384]{1,0:T(8,128)(2,1)S(1)} collective-permute-done((bf16[384,384]{1,0:T(8,128)(2,1)S(1)}, bf16[384,384]{1,0:T(8,128)(2,1)S(1)}, u32[]{:S(2)}, u32[]{:S(2)}) %collective-permute-start.16) | collective-permute-done | bytes 294944 | tf_op jit(solution)/shard_map/ppermute | solution.py:32
  68.8 0.7 collective-permute-start.6
  69.5 8.0 %project.1.ga = bf16[768,384]{1,0:T(8,128)(2,1)} custom-call(s32[3]{0:T(128)} %pad_add_fusion.place_ref, bf16[768,768]{1,0:T(8,128)(2,1)} %g0.1, bf16[768,768]{1,0:T(8,128)(2,1)} %collective-permute-done.7.g1, bf16[768,768]{1,0:T(8,128)(2,1)} %collective-permute-done.8.g2, bf16[768,768]{1,0:T(8,128)(2,1)} %collective-permute-done.9.g3, ...), custom_call_target="tpu_custom_call" | custom-call | tf_op jit(solution)/shard_map/project/pallas_call | solution.py:214
  77.6 0.9 collective-permute-start.17
  78.5 0.6 add_convert_fusion.2.flag_ref
  79.1 2.7 %collective-permute-done.6.refs_1_ = bf16[768,384]{1,0:T(8,128)(2,1)S(1)} collective-permute-done((bf16[768,384]{1,0:T(8,128)(2,1)S(1)}, bf16[768,384]{1,0:T(8,128)(2,1)S(1)}, u32[]{:S(2)}, u32[]{:S(2)}) %collective-permute-start.6) | collective-permute-done | bytes 589856 | tf_op jit(solution)/shard_map/ppermute | solution.py:32
  81.8 0.8 copy-done.5
  82.6 6.3 %shard_map.77 = (bf16[3,768,768]{2,1,0:T(8,128)(2,1)}, f32[384,768]{1,0:T(8,128)}, f32[24,768]{1,0:T(8,128)}) custom-call(s32[2]{0:T(128)} %add_convert_fusion.2.flag_ref, bf16[768,384]{1,0:T(8,128)(2,1)} %qa.7, bf16[768,384]{1,0:T(8,128)(2,1)} %copy-done, bf16[768,384]{1,0:T(8,128)(2,1)} %copy-done.4, bf16[768,384]{1,0:T(8,128)(2,1)} %copy-done.5), custom_call_target="tpu_custom_call" | custom-call | tf_op jit(solution)/shard_map/pallas_call | solution.py:86
  88.9 8.9 %shard_map.76 = (bf16[3,1536,768]{2,1,0:T(8,128)(2,1)}, f32[384,768]{1,0:T(8,128)}, f32[24,768]{1,0:T(8,128)}) custom-call(s32[2]{0:T(128)} %add_convert_fusion.2.flag_ref, bf16[768,384]{1,0:T(8,128)(2,1)} %qa.7, bf16[768,384]{1,0:T(8,128)(2,1)} %copy-done, bf16[768,384]{1,0:T(8,128)(2,1)} %copy-done.1, ...), custom_call_target="tpu_custom_call" | custom-call | tf_op jit(solution)/shard_map/pallas_call | solution.py:86
  97.8 0.8 copy-done.3
  98.6 7.6 %backward_far.1 = (bf16[768,384]{1,0:T(8,128)(2,1)}, bf16[768,384]{1,0:T(8,128)(2,1)}, f32[384,768]{1,0:T(8,128)}) custom-call(s32[2]{0:T(128)} %add_convert_fusion.2.flag_ref, bf16[3,768,768]{2,1,0:T(8,128)(2,1)} %get-tuple-element.22.e_ref, f32[384,768]{1,0:T(8,128)} %get-tuple-element.18.on, f32[24,768]{1,0:T(8,128)} %get-tuple-element.19.sn, ...), custom_call_target="tpu_custom_call" | custom-call | tf_op jit(solution)/shard_map/backward_far/pallas_call | solution.py:162
  106.2 11.4 %backward_near.1 = (bf16[768,384]{1,0:T(8,128)(2,1)}, bf16[768,384]{1,0:T(8,128)(2,1)}, f32[768,384]{1,0:T(8,128)}, f32[768,384]{1,0:T(8,128)}, bf16[768,384]{1,0:T(8,128)(2,1)}) custom-call(s32[2]{0:T(128)} %add_convert_fusion.2.flag_ref, bf16[3,1536,768]{2,1,0:T(8,128)(2,1)} %get-tuple-element.17.e_ref, f32[384,768]{1,0:T(8,128)} %get-tuple-element.18.on, ...), custom_call_target="tpu_custom_call" | custom-call | tf_op jit(solution)/shard_map/backward_near/pallas_call | solution.py:162
  117.6 0.3 collective-permute-start.19
  118.0 1.5 collective-permute-start.20
  119.5 0.2 collective-permute-start.22
  119.7 1.5 collective-permute-start.23
  121.2 0.5 collective-permute-start.18
  121.7 6.2 %collective-permute-done.20 = bf16[768,384]{1,0:T(8,128)(2,1)S(1)} collective-permute-done((bf16[768,384]{1,0:T(8,128)(2,1)S(1)}, bf16[768,384]{1,0:T(8,128)(2,1)S(1)}, u32[]{:S(2)}, u32[]{:S(2)}) %collective-permute-start.20) | collective-permute-done | bytes 589856 | tf_op jit(solution)/shard_map/ppermute | solution.py:32
  127.8 1.6 %add_convert_fusion.1 = bf16[768,384]{1,0:T(8,128)(2,1)S(1)} fusion(bf16[768,384]{1,0:T(8,128)(2,1)S(1)} %collective-permute-done.20, f32[768,384]{1,0:T(8,128)} %get-tuple-element.25, bf16[768,384]{1,0:T(8,128)(2,1)S(1)} %collective-permute-done.19), kind=kLoop, calls=%fused_computation.1 | loop fusion | flops 1474560 | bytes 2949120 | tf_op jit(solution)/shard_map/convert_element_type | solution.py:310
  129.4 1.6 %collective-permute-start.21 = (bf16[768,384]{1,0:T(8,128)(2,1)S(1)}, bf16[768,384]{1,0:T(8,128)(2,1)S(1)}, u32[]{:S(2)}, u32[]{:S(2)}) collective-permute-start(bf16[768,384]{1,0:T(8,128)(2,1)S(1)} %add_convert_fusion.1), channel_id=1, source_target_pairs={{0,2},{1,4},{2,0},{3,6},{4,1},{5,7},{6,3},{7,5},{8,10},{9,12},{10,... | collective-permute-start | bytes 1769480 | tf_op jit(solution)/shard_map/ppermute | solution.py:32
  131.0 3.1 %collective-permute-done.23 = bf16[768,384]{1,0:T(8,128)(2,1)S(1)} collective-permute-done((bf16[768,384]{1,0:T(8,128)(2,1)S(1)}, bf16[768,384]{1,0:T(8,128)(2,1)S(1)}, u32[]{:S(2)}, u32[]{:S(2)}) %collective-permute-start.23) | collective-permute-done | bytes 589856 | tf_op jit(solution)/shard_map/ppermute | solution.py:32
  134.2 0.2 add_convert_fusion
  134.4 1.6 %collective-permute-start.24 = (bf16[768,384]{1,0:T(8,128)(2,1)S(1)}, bf16[768,384]{1,0:T(8,128)(2,1)S(1)}, u32[]{:S(2)}, u32[]{:S(2)}) collective-permute-start(bf16[768,384]{1,0:T(8,128)(2,1)S(1)} %add_convert_fusion), channel_id=1, source_target_pairs={{0,2},{1,4},{2,0},{3,6},{4,1},{5,7},{6,3},{7,5},{8,10},{9,12},{10,... | collective-permute-start | bytes 1769480 | tf_op jit(solution)/shard_map/ppermute | solution.py:32
  135.9 4.5 %collective-permute-done.18 = bf16[768,384]{1,0:T(8,128)(2,1)S(1)} collective-permute-done((bf16[768,384]{1,0:T(8,128)(2,1)}, bf16[768,384]{1,0:T(8,128)(2,1)S(1)}, u32[]{:S(2)}, u32[]{:S(2)}) %collective-permute-start.18) | collective-permute-done | bytes 589856 | tf_op jit(solution)/shard_map/ppermute | solution.py:32
  140.5 0.9 broadcast_select_fusion.2
  141.4 5.4 %collective-permute-done.21 = bf16[768,384]{1,0:T(8,128)(2,1)S(1)} collective-permute-done((bf16[768,384]{1,0:T(8,128)(2,1)S(1)}, bf16[768,384]{1,0:T(8,128)(2,1)S(1)}, u32[]{:S(2)}, u32[]{:S(2)}) %collective-permute-start.21) | collective-permute-done | bytes 589856 | tf_op jit(solution)/shard_map/ppermute | solution.py:32
  146.8 0.9 broadcast_select_fusion.1
  147.7 5.4 %collective-permute-done.24 = bf16[768,384]{1,0:T(8,128)(2,1)S(1)} collective-permute-done((bf16[768,384]{1,0:T(8,128)(2,1)S(1)}, bf16[768,384]{1,0:T(8,128)(2,1)S(1)}, u32[]{:S(2)}, u32[]{:S(2)}) %collective-permute-start.24) | collective-permute-done | bytes 589856 | tf_op jit(solution)/shard_map/ppermute | solution.py:32
  153.1 0.9 broadcast_select_fusion
  (50 shorter events, 0.2 us)
Async XLA Ops:
  0.6 50.0 %copy-start.7 = (bf16[768,384]{1,0:T(8,128)(2,1)S(1)}, bf16[768,384]{1,0:T(8,128)(2,1)}, u32[]{:S(2)}) copy-start(bf16[768,384]{1,0:T(8,128)(2,1)} %param.7) | copy-start | bytes 1769476
  0.6 29.3 %collective-permute-start.8 = (bf16[768,768]{1,0:T(8,128)(2,1)}, bf16[768,768]{1,0:T(8,128)(2,1)}, u32[]{:S(2)}, u32[]{:S(2)}) collective-permute-start(bf16[768,768]{1,0:T(8,128)(2,1)} %g0.1), channel_id=1, source_target_pairs={{0,2},{1,3},{2,0},{3,1},{4,6},{5,7},{6,4},{7,5},{8,10},{9,11},{10,... | collective-permute-start | bytes 3538952 | tf_op jit(solution)/shard_map/ppermute | solution.py:32
  3.7 13.6 %collective-permute-start.11 = (bf16[384,384]{1,0:T(8,128)(2,1)}, bf16[384,384]{1,0:T(8,128)(2,1)S(1)}, u32[]{:S(2)}, u32[]{:S(2)}) collective-permute-start(bf16[384,384]{1,0:T(8,128)(2,1)} %refs_0_.1), channel_id=1, source_target_pairs={{0,8},{1,9},{2,10},{3,11},{4,12},{5,13},{6,14},{7,15},{8,0},{9,1},... | collective-permute-start | bytes 884744 | tf_op jit(solution)/shard_map/ppermute | solution.py:32
  5.2 24.7 %collective-permute-start.10 = (bf16[384,384]{1,0:T(8,128)(2,1)}, bf16[384,384]{1,0:T(8,128)(2,1)S(1)}, u32[]{:S(2)}, u32[]{:S(2)}) collective-permute-start(bf16[384,384]{1,0:T(8,128)(2,1)} %refs_0_.1), channel_id=1, source_target_pairs={{0,4},{1,5},{2,6},{3,7},{4,0},{5,1},{6,2},{7,3},{8,12},{9,13},{10,... | collective-permute-start | bytes 884744 | tf_op jit(solution)/shard_map/ppermute | solution.py:32
  6.8 23.9 %collective-permute-start.13 = (bf16[384,384]{1,0:T(8,128)(2,1)}, bf16[384,384]{1,0:T(8,128)(2,1)S(1)}, u32[]{:S(2)}, u32[]{:S(2)}) collective-permute-start(bf16[384,384]{1,0:T(8,128)(2,1)} %refs_0_.1), channel_id=1, source_target_pairs={{0,16},{1,17},{2,18},{3,19},{4,20},{5,21},{6,22},{7,23},{8,24},{9,... | collective-permute-start | bytes 884744 | tf_op jit(solution)/shard_map/ppermute | solution.py:32
  17.3 13.4 %copy-start.9 = (bf16[384,384]{1,0:T(8,128)(2,1)}, bf16[384,384]{1,0:T(8,128)(2,1)S(1)}, u32[]{:S(2)}) copy-start(bf16[384,384]{1,0:T(8,128)(2,1)S(1)} %collective-permute-done.11.refs_2_) | copy-start | bytes 884740
  17.3 17.5 %collective-permute-start.15 = (bf16[384,384]{1,0:T(8,128)(2,1)S(1)}, bf16[384,384]{1,0:T(8,128)(2,1)S(1)}, u32[]{:S(2)}, u32[]{:S(2)}) collective-permute-start(bf16[384,384]{1,0:T(8,128)(2,1)S(1)} %collective-permute-done.11.refs_2_), channel_id=1, source_target_pairs={{0,16},{1,17},{2,18},{3,19},{4,20},{5,21},{6,22},{7,23},{8,24},{9,... | collective-permute-start | bytes 884744 | tf_op jit(solution)/shard_map/ppermute | solution.py:32
  18.0 50.8 %collective-permute-start.7 = (bf16[768,768]{1,0:T(8,128)(2,1)}, bf16[768,768]{1,0:T(8,128)(2,1)}, u32[]{:S(2)}, u32[]{:S(2)}) collective-permute-start(bf16[768,768]{1,0:T(8,128)(2,1)} %g0.1), channel_id=1, source_target_pairs={{0,1},{1,0},{2,3},{3,2},{4,5},{5,4},{6,7},{7,6},{8,9},{9,8},{10,11... | collective-permute-start | bytes 3538952 | tf_op jit(solution)/shard_map/ppermute | solution.py:32
  30.0 39.5 %collective-permute-start.9 = (bf16[768,768]{1,0:T(8,128)(2,1)}, bf16[768,768]{1,0:T(8,128)(2,1)}, u32[]{:S(2)}, u32[]{:S(2)}) collective-permute-start(bf16[768,768]{1,0:T(8,128)(2,1)} %collective-permute-done.8.g2), channel_id=1, source_target_pairs={{0,1},{1,0},{2,3},{3,2},{4,5},{5,4},{6,7},{7,6},{8,9},{9,8},{10,11... | collective-permute-start | bytes 3538952 | tf_op jit(solution)/shard_map/ppermute | solution.py:32
  30.0 4.9 %copy-start.10 = (bf16[384,384]{1,0:T(8,128)(2,1)}, bf16[384,384]{1,0:T(8,128)(2,1)S(1)}, u32[]{:S(2)}) copy-start(bf16[384,384]{1,0:T(8,128)(2,1)S(1)} %collective-permute-done.10.refs_1_) | copy-start | bytes 884740
  30.0 15.7 %collective-permute-start.1 = (bf16[768,384]{1,0:T(8,128)(2,1)}, bf16[768,384]{1,0:T(8,128)(2,1)S(1)}, u32[]{:S(2)}, u32[]{:S(2)}) collective-permute-start(bf16[768,384]{1,0:T(8,128)(2,1)} %param.6), channel_id=1, source_target_pairs={{1,4},{3,6},{4,1},{6,3},{9,12},{11,14},{12,9},{14,11},{17,20},{19,... | collective-permute-start | bytes 1769480 | tf_op jit(solution)/shard_map/ppermute | solution.py:32
  30.7 20.0 %copy-start.11 = (bf16[384,384]{1,0:T(8,128)(2,1)}, bf16[384,384]{1,0:T(8,128)(2,1)S(1)}, u32[]{:S(2)}) copy-start(bf16[384,384]{1,0:T(8,128)(2,1)S(1)} %collective-permute-done.13.refs_4_) | copy-start | bytes 884740
  30.7 18.1 %collective-permute-start.3 = (bf16[768,384]{1,0:T(8,128)(2,1)}, bf16[768,384]{1,0:T(8,128)(2,1)S(1)}, u32[]{:S(2)}, u32[]{:S(2)}) collective-permute-start(bf16[768,384]{1,0:T(8,128)(2,1)} %param.7), channel_id=1, source_target_pairs={{1,4},{3,6},{4,1},{6,3},{9,12},{11,14},{12,9},{14,11},{17,20},{19,... | collective-permute-start | bytes 1769480 | tf_op jit(solution)/shard_map/ppermute | solution.py:32
  34.8 15.9 %copy-start.12 = (bf16[384,384]{1,0:T(8,128)(2,1)}, bf16[384,384]{1,0:T(8,128)(2,1)S(1)}, u32[]{:S(2)}) copy-start(bf16[384,384]{1,0:T(8,128)(2,1)S(1)} %collective-permute-done.15.refs_6_) | copy-start | bytes 884740
  34.8 9.5 %collective-permute-start.12 = (bf16[384,384]{1,0:T(8,128)(2,1)S(1)}, bf16[384,384]{1,0:T(8,128)(2,1)}, u32[]{:S(2)}, u32[]{:S(2)}) collective-permute-start(bf16[384,384]{1,0:T(8,128)(2,1)S(1)} %collective-permute-done.10.refs_1_), channel_id=1, source_target_pairs={{0,8},{1,9},{2,10},{3,11},{4,12},{5,13},{6,14},{7,15},{8,0},{9,1},... | collective-permute-start | bytes 884744 | tf_op jit(solution)/shard_map/ppermute | solution.py:32
  44.3 33.2 %collective-permute-start = (bf16[768,384]{1,0:T(8,128)(2,1)}, bf16[768,384]{1,0:T(8,128)(2,1)S(1)}, u32[]{:S(2)}, u32[]{:S(2)}) collective-permute-start(bf16[768,384]{1,0:T(8,128)(2,1)} %qa.7), channel_id=1, source_target_pairs={{1,4},{3,6},{4,1},{6,3},{9,12},{11,14},{12,9},{14,11},{17,20},{19,... | collective-permute-start | bytes 1769480 | tf_op jit(solution)/shard_map/ppermute | solution.py:32
  45.7 19.9 %collective-permute-start.14 = (bf16[384,384]{1,0:T(8,128)(2,1)S(1)}, bf16[384,384]{1,0:T(8,128)(2,1)S(1)}, u32[]{:S(2)}, u32[]{:S(2)}) collective-permute-start(bf16[384,384]{1,0:T(8,128)(2,1)S(1)} %collective-permute-done.13.refs_4_), channel_id=1, source_target_pairs={{0,4},{1,5},{2,6},{3,7},{4,0},{5,1},{6,2},{7,3},{8,12},{9,13},{10,... | collective-permute-start | bytes 884744 | tf_op jit(solution)/shard_map/ppermute | solution.py:32
  48.8 19.9 %collective-permute-start.16 = (bf16[384,384]{1,0:T(8,128)(2,1)S(1)}, bf16[384,384]{1,0:T(8,128)(2,1)S(1)}, u32[]{:S(2)}, u32[]{:S(2)}) collective-permute-start(bf16[384,384]{1,0:T(8,128)(2,1)S(1)} %collective-permute-done.15.refs_6_), channel_id=1, source_target_pairs={{0,4},{1,5},{2,6},{3,7},{4,0},{5,1},{6,2},{7,3},{8,12},{9,13},{10,... | collective-permute-start | bytes 884744 | tf_op jit(solution)/shard_map/ppermute | solution.py:32
  50.6 26.9 %copy-start.1 = (bf16[768,384]{1,0:T(8,128)(2,1)}, bf16[768,384]{1,0:T(8,128)(2,1)S(1)}, u32[]{:S(2)}) copy-start(bf16[768,384]{1,0:T(8,128)(2,1)S(1)} %broadcast_select_fusion.4.refs_0_.refs_2_) | copy-start | bytes 1769476
  50.7 26.8 %copy-start.2 = (bf16[768,384]{1,0:T(8,128)(2,1)}, bf16[768,384]{1,0:T(8,128)(2,1)S(1)}, u32[]{:S(2)}) copy-start(bf16[768,384]{1,0:T(8,128)(2,1)S(1)} %broadcast_select_fusion.3.refs_2_.refs_3_) | copy-start | bytes 1769476
  65.6 3.9 %copy-start.13 = (bf16[384,384]{1,0:T(8,128)(2,1)}, bf16[384,384]{1,0:T(8,128)(2,1)S(1)}, u32[]{:S(2)}) copy-start(bf16[384,384]{1,0:T(8,128)(2,1)S(1)} %collective-permute-done.14.refs_5_) | copy-start | bytes 884740
  65.6 13.5 %collective-permute-start.5 = (bf16[768,384]{1,0:T(8,128)(2,1)S(1)}, bf16[768,384]{1,0:T(8,128)(2,1)S(1)}, u32[]{:S(2)}, u32[]{:S(2)}) collective-permute-start(bf16[768,384]{1,0:T(8,128)(2,1)S(1)} %broadcast_select_fusion.4.refs_0_.refs_2_), channel_id=1, source_target_pairs={{0,2},{1,8},{2,0},{3,10},{4,6},{5,12},{6,4},{7,14},{8,1},{9,16},{1... | collective-permute-start | bytes 1769480 | tf_op jit(solution)/shard_map/ppermute | solution.py:32
  68.7 0.7 copy-start.14
  68.7 20.2 %collective-permute-start.2 = (bf16[768,384]{1,0:T(8,128)(2,1)S(1)}, bf16[768,384]{1,0:T(8,128)(2,1)}, u32[]{:S(2)}, u32[]{:S(2)}) collective-permute-start(bf16[768,384]{1,0:T(8,128)(2,1)S(1)} %broadcast_select_fusion.4.refs_0_.refs_2_), channel_id=1, source_target_pairs={{0,1},{1,0},{2,3},{3,2},{4,5},{5,4},{6,7},{7,6},{8,9},{9,8},{10,11... | collective-permute-start | bytes 1769480 | tf_op jit(solution)/shard_map/ppermute | solution.py:32
  68.8 13.0 %collective-permute-start.6 = (bf16[768,384]{1,0:T(8,128)(2,1)S(1)}, bf16[768,384]{1,0:T(8,128)(2,1)S(1)}, u32[]{:S(2)}, u32[]{:S(2)}) collective-permute-start(bf16[768,384]{1,0:T(8,128)(2,1)S(1)} %broadcast_select_fusion.3.refs_2_.refs_3_), channel_id=1, source_target_pairs={{0,2},{1,8},{2,0},{3,10},{4,6},{5,12},{6,4},{7,14},{8,1},{9,16},{1... | collective-permute-start | bytes 1769480 | tf_op jit(solution)/shard_map/ppermute | solution.py:32
  69.5 19.4 %collective-permute-start.4 = (bf16[768,384]{1,0:T(8,128)(2,1)S(1)}, bf16[768,384]{1,0:T(8,128)(2,1)}, u32[]{:S(2)}, u32[]{:S(2)}) collective-permute-start(bf16[768,384]{1,0:T(8,128)(2,1)S(1)} %broadcast_select_fusion.3.refs_2_.refs_3_), channel_id=1, source_target_pairs={{0,1},{1,0},{2,3},{3,2},{4,5},{5,4},{6,7},{7,6},{8,9},{9,8},{10,11... | collective-permute-start | bytes 1769480 | tf_op jit(solution)/shard_map/ppermute | solution.py:32
  77.6 4.2 %copy-start = (bf16[768,384]{1,0:T(8,128)(2,1)}, bf16[768,384]{1,0:T(8,128)(2,1)S(1)}, u32[]{:S(2)}) copy-start(bf16[768,384]{1,0:T(8,128)(2,1)S(1)} %collective-permute-done.qb) | copy-start | bytes 1769476
  77.6 20.2 %collective-permute-start.17 = (bf16[768,384]{1,0:T(8,128)(2,1)}, bf16[768,384]{1,0:T(8,128)(2,1)S(1)}, u32[]{:S(2)}, u32[]{:S(2)}) collective-permute-start(bf16[768,384]{1,0:T(8,128)(2,1)} %project.1.ga), channel_id=1, source_target_pairs={{1,4},{3,6},{4,1},{6,3},{9,12},{11,14},{12,9},{14,11},{17,20},{19,... | collective-permute-start | bytes 1769480 | tf_op jit(solution)/shard_map/ppermute | solution.py:32
  79.1 2.7 %copy-start.4 = (bf16[768,384]{1,0:T(8,128)(2,1)}, bf16[768,384]{1,0:T(8,128)(2,1)S(1)}, u32[]{:S(2)}) copy-start(bf16[768,384]{1,0:T(8,128)(2,1)S(1)} %collective-permute-done.5.refs_0_) | copy-start | bytes 1769476
  81.8 0.8 copy-start.5
  97.8 0.8 copy-start.3
  106.2 11.8 %copy-start.16 = (bf16[768,384]{1,0:T(8,128)(2,1)S(1)}, bf16[768,384]{1,0:T(8,128)(2,1)}, u32[]{:S(2)}) copy-start(bf16[768,384]{1,0:T(8,128)(2,1)} %get-tuple-element.27) | copy-start | bytes 1769476
  106.2 13.5 %copy-start.15 = (bf16[768,384]{1,0:T(8,128)(2,1)S(1)}, bf16[768,384]{1,0:T(8,128)(2,1)}, u32[]{:S(2)}) copy-start(bf16[768,384]{1,0:T(8,128)(2,1)} %get-tuple-element.30) | copy-start | bytes 1769476
  117.6 4.0 %collective-permute-start.19 = (bf16[768,384]{1,0:T(8,128)(2,1)}, bf16[768,384]{1,0:T(8,128)(2,1)S(1)}, u32[]{:S(2)}, u32[]{:S(2)}) collective-permute-start(bf16[768,384]{1,0:T(8,128)(2,1)} %get-tuple-element.26), channel_id=1, source_target_pairs={{0,1},{1,0},{2,3},{3,2},{4,5},{5,4},{6,7},{7,6},{8,9},{9,8},{10,11... | collective-permute-start | bytes 1769480 | tf_op jit(solution)/shard_map/ppermute | solution.py:32
  118.0 9.9 %collective-permute-start.20 = (bf16[768,384]{1,0:T(8,128)(2,1)S(1)}, bf16[768,384]{1,0:T(8,128)(2,1)S(1)}, u32[]{:S(2)}, u32[]{:S(2)}) collective-permute-start(bf16[768,384]{1,0:T(8,128)(2,1)S(1)} %copy-done.16), channel_id=1, source_target_pairs={{0,2},{1,8},{2,0},{3,10},{4,6},{5,12},{6,4},{7,14},{8,1},{9,16},{1... | collective-permute-start | bytes 1769480 | tf_op jit(solution)/shard_map/ppermute | solution.py:32
  119.5 11.6 %collective-permute-start.22 = (bf16[768,384]{1,0:T(8,128)(2,1)}, bf16[768,384]{1,0:T(8,128)(2,1)S(1)}, u32[]{:S(2)}, u32[]{:S(2)}) collective-permute-start(bf16[768,384]{1,0:T(8,128)(2,1)} %get-tuple-element.29), channel_id=1, source_target_pairs={{0,1},{1,0},{2,3},{3,2},{4,5},{5,4},{6,7},{7,6},{8,9},{9,8},{10,11... | collective-permute-start | bytes 1769480 | tf_op jit(solution)/shard_map/ppermute | solution.py:32
  119.7 14.5 %collective-permute-start.23 = (bf16[768,384]{1,0:T(8,128)(2,1)S(1)}, bf16[768,384]{1,0:T(8,128)(2,1)S(1)}, u32[]{:S(2)}, u32[]{:S(2)}) collective-permute-start(bf16[768,384]{1,0:T(8,128)(2,1)S(1)} %copy-done.15), channel_id=1, source_target_pairs={{0,2},{1,8},{2,0},{3,10},{4,6},{5,12},{6,4},{7,14},{8,1},{9,16},{1... | collective-permute-start | bytes 1769480 | tf_op jit(solution)/shard_map/ppermute | solution.py:32
  121.2 19.3 %collective-permute-start.18 = (bf16[768,384]{1,0:T(8,128)(2,1)}, bf16[768,384]{1,0:T(8,128)(2,1)S(1)}, u32[]{:S(2)}, u32[]{:S(2)}) collective-permute-start(bf16[768,384]{1,0:T(8,128)(2,1)} %get-tuple-element.24), channel_id=1, source_target_pairs={{0,2},{1,4},{2,0},{3,6},{4,1},{5,7},{6,3},{7,5},{8,10},{9,12},{10,... | collective-permute-start | bytes 1769480 | tf_op jit(solution)/shard_map/ppermute | solution.py:32
  127.8 6.3 %copy-start.6 = (f32[768,384]{1,0:T(8,128)S(1)}, f32[768,384]{1,0:T(8,128)}, u32[]{:S(2)}) copy-start(f32[768,384]{1,0:T(8,128)} %get-tuple-element.28) | copy-start | bytes 3538948
  129.4 17.4 %collective-permute-start.21 = (bf16[768,384]{1,0:T(8,128)(2,1)S(1)}, bf16[768,384]{1,0:T(8,128)(2,1)S(1)}, u32[]{:S(2)}, u32[]{:S(2)}) collective-permute-start(bf16[768,384]{1,0:T(8,128)(2,1)S(1)} %add_convert_fusion.1), channel_id=1, source_target_pairs={{0,2},{1,4},{2,0},{3,6},{4,1},{5,7},{6,3},{7,5},{8,10},{9,12},{10,... | collective-permute-start | bytes 1769480 | tf_op jit(solution)/shard_map/ppermute | solution.py:32
  134.2 6.3 %copy-start.8 = (bf16[768,384]{1,0:T(8,128)(2,1)S(1)}, bf16[768,384]{1,0:T(8,128)(2,1)}, u32[]{:S(2)}) copy-start(bf16[768,384]{1,0:T(8,128)(2,1)} %get-tuple-element.24) | copy-start | bytes 1769476
  134.4 18.8 %collective-permute-start.24 = (bf16[768,384]{1,0:T(8,128)(2,1)S(1)}, bf16[768,384]{1,0:T(8,128)(2,1)S(1)}, u32[]{:S(2)}, u32[]{:S(2)}) collective-permute-start(bf16[768,384]{1,0:T(8,128)(2,1)S(1)} %add_convert_fusion), channel_id=1, source_target_pairs={{0,2},{1,4},{2,0},{3,6},{4,1},{5,7},{6,3},{7,5},{8,10},{9,12},{10,... | collective-permute-start | bytes 1769480 | tf_op jit(solution)/shard_map/ppermute | solution.py:32

commit v4 on v3

--- a/solution.py
+++ b/solution.py
@@ -12,6 +12,10 @@
 HD = 128
 VT = 8
 AXES = ("tm", "head")
+LIMIT = 24 << 20
+BIG = 768
+STEP = 768
+SMALL = 64
 NT = (((1,), (1,)), ((), ()))
 TN = (((0,), (0,)), ((), ()))
 
@@ -41,42 +45,48 @@
     e_ref, o_ref, stat_ref, vt = refs[2 * parts : 2 * parts + 4]
     held = refs[2 * parts + 4 :]
     rows = qa.shape[0]
-    step = 256
     factor = math.log2(math.e) / math.sqrt(HD)
     query = jnp.where(flag_ref[1] > 0, qa[...], qb[...])
-    spots = [(i, first) for i in range(parts) for first in range(0, rows, step)]
 
     def score(n):
+        for i in range(parts):
+            for first in range(0, rows, BIG):
+                held[n][i * rows + first : i * rows + first + BIG, :] = dot(
+                    keys[i][first : first + BIG, :], query[n * tile : (n + 1) * tile], NT
+                )
+
+    def highest(n):
         peak = None
-        for i, first in spots:
-            s = dot(keys[i][first : first + step, :], query[n * tile : (n + 1) * tile], NT)
-            held[n][i * rows + first : i * rows + first + step, :] = s
-            top = fold(s, jnp.max)
+        for first in range(0, parts * rows, SMALL):
+            top = fold(held[n][first : first + SMALL, :], jnp.max)
             peak = top if peak is None else jnp.maximum(peak, top)
         return jnp.max(peak, axis=0, keepdims=True) * factor
 
-    def soften(n, shift):
-        total, out = None, None
-        for i, first in spots:
-            span = slice(i * rows + first, i * rows + first + step)
-            w = jnp.exp2(held[n][span, :] * factor - shift)
+    def weigh(n, shift):
+        total = None
+        for first in range(0, parts * rows, SMALL):
+            w = jnp.exp2(held[n][first : first + SMALL, :] * factor - shift)
             mass = fold(w, jnp.sum)
             total = mass if total is None else total + mass
-            low = w.astype(jnp.bfloat16)
-            e_ref[0, span, n * tile : (n + 1) * tile] = low
-            part = dot(vt[:, span], low)
-            out = part if out is None else out + part
-        o_ref[:, n * tile : (n + 1) * tile] = out
+            e_ref[0, first : first + SMALL, n * tile : (n + 1) * tile] = w.astype(jnp.bfloat16)
         stat_ref[0:1, n * tile : (n + 1) * tile] = shift
         stat_ref[1:2, n * tile : (n + 1) * tile] = jnp.sum(total, axis=0, keepdims=True)
 
-    shift = score(0)
+    def gather(n):
+        o_ref[:, n * tile : (n + 1) * tile] = dot(vt[...], e_ref[0, :, n * tile : (n + 1) * tile])
+
+    count = rows // tile
+    score(0)
     for i in range(parts):
         vt[:, i * rows : (i + 1) * rows] = values[i][...].T
-    for n in range(rows // tile):
-        later = score(n + 1) if (n + 1) * tile < rows else None
-        soften(n, shift)
-        shift = later
+    for n in range(count):
+        shift = highest(n)
+        if n + 1 < count:
+            score(n + 1)
+        weigh(n, shift)
+        if n > 0:
+            gather(n - 1)
+    gather(count - 1)
 
 
 def soften(flags, queries, keys, values):
@@ -99,16 +109,17 @@
         ],
         scratch_shapes=[pltpu.VMEM((HD, parts * rows), jnp.bfloat16)]
         + [pltpu.VMEM((parts * rows, tile), jnp.float32)] * (rows // tile),
+        compiler_params=pltpu.CompilerParams(vmem_limit_bytes=LIMIT),
     )(flags, *queries, *keys, *values)
 
 
 def backward_kernel(far, flag_ref, e_ref, on, sn, of, sf, ga, gb, qa, qb, *refs):
     rows = qa.shape[0]
-    step = 256
+    step = STEP
     scale = 1.0 / math.sqrt(HD)
     stays = flag_ref[1] > 0
     query = jnp.where(stays, qa[...], qb[...])
-    flipped = jnp.where(stays, ga[...], gb[...]).astype(jnp.float32).T
+    flipped = jnp.where(stays, ga[...], gb[...]).astype(jnp.float32)
     near_top = sn[0:1, :]
     far_top = jnp.where(flag_ref[0] > 0, sf[0:1, :], -jnp.inf)
     top = jnp.maximum(near_top, far_top)
@@ -130,14 +141,13 @@
         ks, vs, ko, vo, dq_far, dks, dvs, dko, dvo, dq = refs
         slabs = ((ks, vs, dks, dvs), (ko, vo, dko, dvo))
         total, grad_t, inner = dq_far[...], near_grad, inner * near_share
-    grad = grad_t.T
     for i, (k, v, dk, dv) in enumerate(slabs):
         base = 0 if far else (1 - i) * rows
         for first in range(0, rows, step):
             weight = e_ref[0, base + first : base + first + step, :]
             slope = dot(v[first : first + step, :], grad_t)
             delta = (weight.astype(jnp.float32) * (slope - inner)).astype(jnp.bfloat16)
-            dv[first : first + step, :] = dot(weight, grad).astype(dv.dtype)
+            dv[first : first + step, :] = dot(weight, grad_t, NT).astype(dv.dtype)
             dk[first : first + step, :] = (dot(delta, query) * scale).astype(dk.dtype)
             part = dot(k[first : first + step, :], delta, TN)
             total = part if total is None else total + part
@@ -170,10 +180,12 @@
             flip,
             stat,
         ]
-        + [spec] * (4 + len(slabs))
+        + [flip] * 2
+        + [spec] * (2 + len(slabs))
         + [flip] * len(dq_far),
         out_specs=out_specs,
         out_shape=out_shape,
+        compiler_params=pltpu.CompilerParams(vmem_limit_bytes=LIMIT),
         name="backward_far" if far else "backward_near",
     )(flags, weights, *near, *away, *grads, *queries, *slabs, *dq_far)
 
@@ -182,30 +194,28 @@
     shards = refs[:8]
     out_ref, gbuf, wbuf, gsem, wsem = refs[8:]
     z, y, h = place_ref[0], place_ref[1], place_ref[2]
-    width = out_ref.shape[1]
+    width = out_ref.shape[0]
     copies = []
     for m in range(4):
         for n in range(2):
+            column = pl.multiple_of((y ^ n) * width, width)
             copies.append(
                 pltpu.make_async_copy(
-                    shards[2 * m + n], wbuf.at[z ^ m, y ^ n], wsem.at[2 * m + n]
+                    shards[2 * m + n], wbuf.at[z ^ m, :, pl.ds(column, width)], wsem.at[2 * m + n]
                 )
             )
     grads = [
         pltpu.make_async_copy(g, gbuf.at[m], gsem.at[m]) for m, g in enumerate((g0, g1, g2, g3))
     ]
-    for c in copies:
-        c.start()
-    for c in grads:
+    for c in copies + grads:
         c.start()
     for c in copies:
         c.wait()
     total = None
     for m in range(4):
         grads[m].wait()
-        for n in range(2):
-            part = dot(gbuf[m, :, n * width : (n + 1) * width], wbuf[h ^ m, n], NT)
-            total = part if total is None else total + part
+        part = dot(wbuf[h ^ m], gbuf[m], NT)
+        total = part if total is None else total + part
     out_ref[...] = total.astype(out_ref.dtype)
 
 
@@ -215,13 +225,14 @@
         project_kernel,
         in_specs=[pl.BlockSpec(memory_space=pltpu.SMEM)] + [anywhere] * 12,
         out_specs=pl.BlockSpec(memory_space=pltpu.VMEM),
-        out_shape=jax.ShapeDtypeStruct((rows, width), jnp.bfloat16),
+        out_shape=jax.ShapeDtypeStruct((width, rows), jnp.bfloat16),
         scratch_shapes=[
             pltpu.VMEM((4,) + grads[0].shape, jnp.bfloat16),
-            pltpu.VMEM((4, 2) + shards[0].shape, jnp.bfloat16),
+            pltpu.VMEM((4, width, grads[0].shape[1]), jnp.bfloat16),
             pltpu.SemaphoreType.DMA((4,)),
             pltpu.SemaphoreType.DMA((8,)),
         ],
+        compiler_params=pltpu.CompilerParams(vmem_limit_bytes=LIMIT),
         name="project",
     )(place, *grads, *shards)
 
@@ -260,11 +271,7 @@
     values = jnp.where(stays, value_rows, send(value_rows, turn_route))
     query_pair = (queries, send(queries, turn_route))
     if square:
-        grads = [
-            grad_out,
-            send(grad_out, side_route),
-            send(grad_out, lambda t, h: (t, h ^ 2)),
-        ]
+        grads = [grad_out, send(grad_out, side_route), send(grad_out, lambda t, h: (t, h ^ 2))]
         w1 = send(w_out, lambda t, h: (t ^ 2, h))
         w2 = send(w_out, lambda t, h: (t ^ 4, h))
         w0y = send(w_out, lambda t, h: (t ^ 1, h))
@@ -283,11 +290,11 @@
         )
     else:
         attn_grad = dot(
+            lax.all_gather(w_out, "tm", axis=1, tiled=True),
             lax.all_gather(grad_out, "head", axis=1, tiled=True),
-            lax.all_gather(w_out, "tm", axis=1, tiled=True),
             NT,
         ).astype(jnp.bfloat16)
-    grad_pair = (attn_grad, send(attn_grad, turn_route))
+    grad_pair = (attn_grad, send(attn_grad, busy_route))
     far_weights, *away = soften(flags, query_pair, (far_k,), (far_v,))
     dkz, dvz, dq_far = backward(
         True, flags, far_weights, near, away, grad_pair, query_pair, (far_k,), (far_v,)

time: 155 us -> 145 us (0.935)
  Pallas kernels: 42.2 us -> 32.1 us
  other arithmetic: 6.93 us -> 4.53 us
  local copies, waits for them, and re-layouts: 1.7 us -> 3.75 us
    pallas_call x2, Pallas kernels: 19 us -> 14.7 us  [backward(): pl.pallas_call(functools.partial(backward_kernel, far), grid=(heads,), in...]
    pallas_call x2, Pallas kernels: 15.2 us -> 12.2 us  [soften(): pl.pallas_call(functools.partial(soften_kernel, parts, tile), grid=(heads...]
    pallas_call x1, Pallas kernels: 8 us -> 5.19 us  [project(): pl.pallas_call(project_kernel, in_specs=[pl.BlockSpec(memory_space=pltpu....]
    unnamed x34 -> x24, local copies, waits for them, and re-layouts: 1.7 us -> 3.75 us
  transfers between devices with their start and end apart: 25 -> 25, of which waited for: 12 -> 12; matrix products, arithmetic and copies ran while one was open for 4% -> 3% of each run, Pallas kernels for 15% -> 12%
where the time goes in v4:
time: 145 us; the launch traced here: 144 us
  waiting for transfers between devices  77.7 us (54%)
  Pallas kernels  32.1 us (22%)
  starting transfers between devices  25.5 us (18%)
  other arithmetic  4.53 us (3%)
  local copies, waits for them, and re-layouts  3.75 us (3%)
    ppermute x25, waiting for transfers between devices, exchange(): return lax.ppermute(block, AXES, pairs)  77.7 us
    ppermute x25, starting transfers between devices, exchange(): return lax.ppermute(block, AXES, pairs)  25.5 us
    pallas_call x2, Pallas kernels, backward(): pl.pallas_call(functools.partial(backward_kernel, far), grid=(heads,), in...  14.7 us
    pallas_call x2, Pallas kernels, soften(): pl.pallas_call(functools.partial(soften_kernel, parts, tile), grid=(heads...  12.2 us
    pallas_call x1, Pallas kernels, project(): pl.pallas_call(project_kernel, in_specs=[pl.BlockSpec(memory_space=pltpu....  5.19 us
    unnamed x24, local copies, waits for them, and re-layouts  3.75 us
  transfers between devices with their start and end apart: 25, of which 12 were waited for; matrix products, arithmetic and copies ran while one was open for 3% of the time, Pallas kernels for 12%

profile of v4, /device:TPU:0, one launch (start us, length us, event | category | flops | bytes accessed | tf_op | source)
XLA Modules:
  0.0 144.5 jit_solution(5166454039388937523)
XLA Ops:
  0.6 3.0 %collective-permute-start.8 = (bf16[768,768]{1,0:T(8,128)(2,1)}, bf16[768,768]{1,0:T(8,128)(2,1)}, u32[]{:S(2)}, u32[]{:S(2)}) collective-permute-start(bf16[768,768]{1,0:T(8,128)(2,1)} %g0.1), channel_id=1, source_target_pairs={{0,2},{1,3},{2,0},{3,1},{4,6},{5,7},{6,4},{7,5},{8,10},{9,11},{10,... | collective-permute-start | bytes 3538952 | tf_op jit(solution)/shard_map/ppermute | solution.py:36
  3.7 1.6 %collective-permute-start.11 = (bf16[384,384]{1,0:T(8,128)(2,1)}, bf16[384,384]{1,0:T(8,128)(2,1)S(1)}, u32[]{:S(2)}, u32[]{:S(2)}) collective-permute-start(bf16[384,384]{1,0:T(8,128)(2,1)} %refs_0_.1), channel_id=1, source_target_pairs={{0,8},{1,9},{2,10},{3,11},{4,12},{5,13},{6,14},{7,15},{8,0},{9,1},... | collective-permute-start | bytes 884744 | tf_op jit(solution)/shard_map/ppermute | solution.py:36
  5.2 1.5 %collective-permute-start.10 = (bf16[384,384]{1,0:T(8,128)(2,1)}, bf16[384,384]{1,0:T(8,128)(2,1)S(1)}, u32[]{:S(2)}, u32[]{:S(2)}) collective-permute-start(bf16[384,384]{1,0:T(8,128)(2,1)} %refs_0_.1), channel_id=1, source_target_pairs={{0,4},{1,5},{2,6},{3,7},{4,0},{5,1},{6,2},{7,3},{8,12},{9,13},{10,... | collective-permute-start | bytes 884744 | tf_op jit(solution)/shard_map/ppermute | solution.py:36
  6.8 2.6 %collective-permute-start.13 = (bf16[384,384]{1,0:T(8,128)(2,1)}, bf16[384,384]{1,0:T(8,128)(2,1)S(1)}, u32[]{:S(2)}, u32[]{:S(2)}) collective-permute-start(bf16[384,384]{1,0:T(8,128)(2,1)} %refs_0_.1), channel_id=1, source_target_pairs={{0,16},{1,17},{2,18},{3,19},{4,20},{5,21},{6,22},{7,23},{8,24},{9,... | collective-permute-start | bytes 884744 | tf_op jit(solution)/shard_map/ppermute | solution.py:36
  9.3 7.9 %collective-permute-done.11.refs_2_ = bf16[384,384]{1,0:T(8,128)(2,1)S(1)} collective-permute-done((bf16[384,384]{1,0:T(8,128)(2,1)}, bf16[384,384]{1,0:T(8,128)(2,1)S(1)}, u32[]{:S(2)}, u32[]{:S(2)}) %collective-permute-start.11) | collective-permute-done | bytes 294944 | tf_op jit(solution)/shard_map/ppermute | solution.py:36
  17.3 0.7 collective-permute-start.15
  18.0 12.0 %collective-permute-done.8.g2 = bf16[768,768]{1,0:T(8,128)(2,1)} collective-permute-done((bf16[768,768]{1,0:T(8,128)(2,1)}, bf16[768,768]{1,0:T(8,128)(2,1)}, u32[]{:S(2)}, u32[]{:S(2)}) %collective-permute-start.8) | collective-permute-done | bytes 1179680 | tf_op jit(solution)/shard_map/ppermute | solution.py:36
  30.0 0.7 collective-permute-start.1
  30.7 0.7 collective-permute-start.3
  31.4 3.4 %collective-permute-done.15.refs_6_ = bf16[384,384]{1,0:T(8,128)(2,1)S(1)} collective-permute-done((bf16[384,384]{1,0:T(8,128)(2,1)S(1)}, bf16[384,384]{1,0:T(8,128)(2,1)S(1)}, u32[]{:S(2)}, u32[]{:S(2)}) %collective-permute-start.15) | collective-permute-done | bytes 294944 | tf_op jit(solution)/shard_map/ppermute | solution.py:36
  34.8 9.4 %collective-permute-done.12.refs_3_ = bf16[384,384]{1,0:T(8,128)(2,1)S(1)} collective-permute-done((bf16[384,384]{1,0:T(8,128)(2,1)S(1)}, bf16[384,384]{1,0:T(8,128)(2,1)S(1)}, u32[]{:S(2)}, u32[]{:S(2)}) %collective-permute-start.12) | collective-permute-done | bytes 294944 | tf_op jit(solution)/shard_map/ppermute | solution.py:36
  44.2 0.7 collective-permute-start
  44.9 0.1 pad_add_fusion.place_ref
  45.0 3.2 %collective-permute-start.14 = (bf16[384,384]{1,0:T(8,128)(2,1)S(1)}, bf16[384,384]{1,0:T(8,128)(2,1)S(1)}, u32[]{:S(2)}, u32[]{:S(2)}) collective-permute-start(bf16[384,384]{1,0:T(8,128)(2,1)S(1)} %collective-permute-done.13.refs_4_), channel_id=1, source_target_pairs={{0,4},{1,5},{2,6},{3,7},{4,0},{5,1},{6,2},{7,3},{8,12},{9,13},{10,... | collective-permute-start | bytes 884744 | tf_op jit(solution)/shard_map/ppermute | solution.py:36
  48.2 0.8 copy-done.10
  49.0 1.3 collective-permute-start.16
  50.3 1.2 broadcast_select_fusion.4.refs_0_.refs_2_
  51.5 0.1 broadcast_select_fusion.3.refs_2_.refs_3_
  51.6 13.3 %collective-permute-done.14.refs_5_ = bf16[384,384]{1,0:T(8,128)(2,1)S(1)} collective-permute-done((bf16[384,384]{1,0:T(8,128)(2,1)S(1)}, bf16[384,384]{1,0:T(8,128)(2,1)S(1)}, u32[]{:S(2)}, u32[]{:S(2)}) %collective-permute-start.14) | collective-permute-done | bytes 294944 | tf_op jit(solution)/shard_map/ppermute | solution.py:36
  64.9 1.2 collective-permute-start.5
  66.1 2.0 %collective-permute-done.16.refs_7_ = bf16[384,384]{1,0:T(8,128)(2,1)S(1)} collective-permute-done((bf16[384,384]{1,0:T(8,128)(2,1)S(1)}, bf16[384,384]{1,0:T(8,128)(2,1)S(1)}, u32[]{:S(2)}, u32[]{:S(2)}) %collective-permute-start.16) | collective-permute-done | bytes 294944 | tf_op jit(solution)/shard_map/ppermute | solution.py:36
  68.1 1.2 collective-permute-start.6
  69.3 1.0 copy-done.4
  70.3 1.0 copy-done.6
  71.2 1.0 copy-done.8
  72.2 5.2 %project.1.ga = bf16[384,768]{1,0:T(8,128)(2,1)S(1)} custom-call(s32[3]{0:T(128)S(1)} %pad_add_fusion.place_ref, bf16[768,768]{1,0:T(8,128)(2,1)S(1)} %copy-done.1, bf16[768,768]{1,0:T(8,128)(2,1)} %collective-permute-done.7.g1, bf16[768,768]{1,0:T(8,128)(2,1)} %collective-permute-done.8.g2, bf16[768,768]{1,0:T(8,128)(2,1)} %collective-permute-done.9.g3, ...), custom_call_target="tpu_custom_call" | custom-call | tf_op jit(solution)/shard_map/project/pallas_call | solution.py:224
  77.4 1.5 %collective-permute-start.17 = (bf16[384,768]{1,0:T(8,128)(2,1)S(1)}, bf16[384,768]{1,0:T(8,128)(2,1)S(1)}, u32[]{:S(2)}, u32[]{:S(2)}) collective-permute-start(bf16[384,768]{1,0:T(8,128)(2,1)S(1)} %project.1.ga), channel_id=1, source_target_pairs={{0,2},{1,4},{2,0},{3,6},{4,1},{5,7},{6,3},{7,5},{8,10},{9,12},{10,... | collective-permute-start | bytes 1769480 | tf_op jit(solution)/shard_map/ppermute | solution.py:36
  78.9 0.1 add_convert_fusion.2.flag_ref
  79.0 2.2 %collective-permute-done.6.refs_1_ = bf16[768,384]{1,0:T(8,128)(2,1)} collective-permute-done((bf16[768,384]{1,0:T(8,128)(2,1)S(1)}, bf16[768,384]{1,0:T(8,128)(2,1)}, u32[]{:S(2)}, u32[]{:S(2)}) %collective-permute-start.6) | collective-permute-done | bytes 589856 | tf_op jit(solution)/shard_map/ppermute | solution.py:36
  81.3 4.6 %shard_map.77 = (bf16[3,768,768]{2,1,0:T(8,128)(2,1)S(1)}, f32[384,768]{1,0:T(8,128)S(1)}, f32[24,768]{1,0:T(8,128)S(1)}) custom-call(s32[2]{0:T(128)S(1)} %add_convert_fusion.2.flag_ref, bf16[768,384]{1,0:T(8,128)(2,1)S(1)} %copy-done, bf16[768,384]{1,0:T(8,128)(2,1)S(1)} %collective-permute-done.qb, bf16[768,384]{1,0:T(8,128)(2,1)} %collective-permute-done.5.refs_0_, ...), custom_call_target="tpu_custom_call" | custom-call | tf_op jit(solution)/shard_map/pallas_call | solution.py:96
  85.9 7.6 %shard_map.76 = (bf16[3,1536,768]{2,1,0:T(8,128)(2,1)S(1)}, f32[384,768]{1,0:T(8,128)S(1)}, f32[24,768]{1,0:T(8,128)S(1)}) custom-call(s32[2]{0:T(128)S(1)} %add_convert_fusion.2.flag_ref, bf16[768,384]{1,0:T(8,128)(2,1)S(1)} %copy-done, bf16[768,384]{1,0:T(8,128)(2,1)S(1)} %collective-permute-done.qb, ...), custom_call_target="tpu_custom_call" | custom-call | tf_op jit(solution)/shard_map/pallas_call | solution.py:96
  93.5 5.4 %backward_far.1 = (bf16[768,384]{1,0:T(8,128)(2,1)S(1)}, bf16[768,384]{1,0:T(8,128)(2,1)S(1)}, f32[384,768]{1,0:T(8,128)S(1)}) custom-call(s32[2]{0:T(128)S(1)} %add_convert_fusion.2.flag_ref, bf16[3,768,768]{2,1,0:T(8,128)(2,1)S(1)} %get-tuple-element.22.e_ref, f32[384,768]{1,0:T(8,128)S(1)} %get-tuple-element.18.on, f32[24,768]{1,0:T(8,128)S(1)} %get-tuple-element.19.sn, ...), custom_call_target="tpu_custom_call" | custom-call | tf_op jit(solution)/shard_map/backward_far/pallas_call | solution.py:172
  98.9 9.4 %backward_near.1 = (bf16[768,384]{1,0:T(8,128)(2,1)S(1)}, bf16[768,384]{1,0:T(8,128)(2,1)S(1)}, f32[768,384]{1,0:T(8,128)S(1)}, f32[768,384]{1,0:T(8,128)S(1)}, bf16[768,384]{1,0:T(8,128)(2,1)S(1)}) custom-call(s32[2]{0:T(128)S(1)} %add_convert_fusion.2.flag_ref, bf16[3,1536,768]{2,1,0:T(8,128)(2,1)S(1)} %get-tuple-element.17.e_ref, ...), custom_call_target="tpu_custom_call" | custom-call | tf_op jit(solution)/shard_map/backward_near/pallas_call | solution.py:172
  108.3 1.2 collective-permute-start.20
  109.6 1.0 collective-permute-start.23
  110.5 1.1 collective-permute-start.18
  111.6 6.7 %collective-permute-done.20 = bf16[768,384]{1,0:T(8,128)(2,1)S(1)} collective-permute-done((bf16[768,384]{1,0:T(8,128)(2,1)S(1)}, bf16[768,384]{1,0:T(8,128)(2,1)S(1)}, u32[]{:S(2)}, u32[]{:S(2)}) %collective-permute-start.20) | collective-permute-done | bytes 589856 | tf_op jit(solution)/shard_map/ppermute | solution.py:36
  118.3 0.2 add_convert_fusion.1
  118.5 1.2 collective-permute-start.21
  119.7 4.9 %collective-permute-done.23 = bf16[768,384]{1,0:T(8,128)(2,1)S(1)} collective-permute-done((bf16[768,384]{1,0:T(8,128)(2,1)S(1)}, bf16[768,384]{1,0:T(8,128)(2,1)S(1)}, u32[]{:S(2)}, u32[]{:S(2)}) %collective-permute-start.23) | collective-permute-done | bytes 589856 | tf_op jit(solution)/shard_map/ppermute | solution.py:36
  124.6 0.2 add_convert_fusion
  124.9 1.2 collective-permute-start.24
  126.1 4.9 %collective-permute-done.18 = bf16[768,384]{1,0:T(8,128)(2,1)S(1)} collective-permute-done((bf16[768,384]{1,0:T(8,128)(2,1)S(1)}, bf16[768,384]{1,0:T(8,128)(2,1)S(1)}, u32[]{:S(2)}, u32[]{:S(2)}) %collective-permute-start.18) | collective-permute-done | bytes 589856 | tf_op jit(solution)/shard_map/ppermute | solution.py:36
  130.9 0.9 broadcast_select_fusion.2
  131.8 5.4 %collective-permute-done.21 = bf16[768,384]{1,0:T(8,128)(2,1)S(1)} collective-permute-done((bf16[768,384]{1,0:T(8,128)(2,1)S(1)}, bf16[768,384]{1,0:T(8,128)(2,1)S(1)}, u32[]{:S(2)}, u32[]{:S(2)}) %collective-permute-start.21) | collective-permute-done | bytes 589856 | tf_op jit(solution)/shard_map/ppermute | solution.py:36
  137.3 0.9 broadcast_select_fusion.1
  138.1 5.4 %collective-permute-done.24 = bf16[768,384]{1,0:T(8,128)(2,1)S(1)} collective-permute-done((bf16[768,384]{1,0:T(8,128)(2,1)S(1)}, bf16[768,384]{1,0:T(8,128)(2,1)S(1)}, u32[]{:S(2)}, u32[]{:S(2)}) %collective-permute-start.24) | collective-permute-done | bytes 589856 | tf_op jit(solution)/shard_map/ppermute | solution.py:36
  143.6 0.9 broadcast_select_fusion
  (40 shorter events, 0.2 us)
Async XLA Ops:
  0.6 29.3 %collective-permute-start.8 = (bf16[768,768]{1,0:T(8,128)(2,1)}, bf16[768,768]{1,0:T(8,128)(2,1)}, u32[]{:S(2)}, u32[]{:S(2)}) collective-permute-start(bf16[768,768]{1,0:T(8,128)(2,1)} %g0.1), channel_id=1, source_target_pairs={{0,2},{1,3},{2,0},{3,1},{4,6},{5,7},{6,4},{7,5},{8,10},{9,11},{10,... | collective-permute-start | bytes 3538952 | tf_op jit(solution)/shard_map/ppermute | solution.py:36
  3.7 13.6 %collective-permute-start.11 = (bf16[384,384]{1,0:T(8,128)(2,1)}, bf16[384,384]{1,0:T(8,128)(2,1)S(1)}, u32[]{:S(2)}, u32[]{:S(2)}) collective-permute-start(bf16[384,384]{1,0:T(8,128)(2,1)} %refs_0_.1), channel_id=1, source_target_pairs={{0,8},{1,9},{2,10},{3,11},{4,12},{5,13},{6,14},{7,15},{8,0},{9,1},... | collective-permute-start | bytes 884744 | tf_op jit(solution)/shard_map/ppermute | solution.py:36
  5.2 24.7 %collective-permute-start.10 = (bf16[384,384]{1,0:T(8,128)(2,1)}, bf16[384,384]{1,0:T(8,128)(2,1)S(1)}, u32[]{:S(2)}, u32[]{:S(2)}) collective-permute-start(bf16[384,384]{1,0:T(8,128)(2,1)} %refs_0_.1), channel_id=1, source_target_pairs={{0,4},{1,5},{2,6},{3,7},{4,0},{5,1},{6,2},{7,3},{8,12},{9,13},{10,... | collective-permute-start | bytes 884744 | tf_op jit(solution)/shard_map/ppermute | solution.py:36
  6.8 23.9 %collective-permute-start.13 = (bf16[384,384]{1,0:T(8,128)(2,1)}, bf16[384,384]{1,0:T(8,128)(2,1)S(1)}, u32[]{:S(2)}, u32[]{:S(2)}) collective-permute-start(bf16[384,384]{1,0:T(8,128)(2,1)} %refs_0_.1), channel_id=1, source_target_pairs={{0,16},{1,17},{2,18},{3,19},{4,20},{5,21},{6,22},{7,23},{8,24},{9,... | collective-permute-start | bytes 884744 | tf_op jit(solution)/shard_map/ppermute | solution.py:36
  17.3 17.5 %collective-permute-start.15 = (bf16[384,384]{1,0:T(8,128)(2,1)S(1)}, bf16[384,384]{1,0:T(8,128)(2,1)S(1)}, u32[]{:S(2)}, u32[]{:S(2)}) collective-permute-start(bf16[384,384]{1,0:T(8,128)(2,1)S(1)} %collective-permute-done.11.refs_2_), channel_id=1, source_target_pairs={{0,16},{1,17},{2,18},{3,19},{4,20},{5,21},{6,22},{7,23},{8,24},{9,... | collective-permute-start | bytes 884744 | tf_op jit(solution)/shard_map/ppermute | solution.py:36
  18.0 50.1 %collective-permute-start.7 = (bf16[768,768]{1,0:T(8,128)(2,1)}, bf16[768,768]{1,0:T(8,128)(2,1)}, u32[]{:S(2)}, u32[]{:S(2)}) collective-permute-start(bf16[768,768]{1,0:T(8,128)(2,1)} %g0.1), channel_id=1, source_target_pairs={{0,1},{1,0},{2,3},{3,2},{4,5},{5,4},{6,7},{7,6},{8,9},{9,8},{10,11... | collective-permute-start | bytes 3538952 | tf_op jit(solution)/shard_map/ppermute | solution.py:36
  29.9 39.3 %collective-permute-start.9 = (bf16[768,768]{1,0:T(8,128)(2,1)}, bf16[768,768]{1,0:T(8,128)(2,1)}, u32[]{:S(2)}, u32[]{:S(2)}) collective-permute-start(bf16[768,768]{1,0:T(8,128)(2,1)} %collective-permute-done.8.g2), channel_id=1, source_target_pairs={{0,1},{1,0},{2,3},{3,2},{4,5},{5,4},{6,7},{7,6},{8,9},{9,8},{10,11... | collective-permute-start | bytes 3538952 | tf_op jit(solution)/shard_map/ppermute | solution.py:36
  30.0 15.1 %collective-permute-start.1 = (bf16[768,384]{1,0:T(8,128)(2,1)}, bf16[768,384]{1,0:T(8,128)(2,1)S(1)}, u32[]{:S(2)}, u32[]{:S(2)}) collective-permute-start(bf16[768,384]{1,0:T(8,128)(2,1)} %param.6), channel_id=1, source_target_pairs={{1,4},{3,6},{4,1},{6,3},{9,12},{11,14},{12,9},{14,11},{17,20},{19,... | collective-permute-start | bytes 1769480 | tf_op jit(solution)/shard_map/ppermute | solution.py:36
  30.7 20.9 %copy-start.3 = (bf16[384,384]{1,0:T(8,128)(2,1)}, bf16[384,384]{1,0:T(8,128)(2,1)S(1)}, u32[]{:S(2)}) copy-start(bf16[384,384]{1,0:T(8,128)(2,1)S(1)} %collective-permute-done.13.refs_4_) | copy-start | bytes 884740
  30.7 17.5 %collective-permute-start.3 = (bf16[768,384]{1,0:T(8,128)(2,1)}, bf16[768,384]{1,0:T(8,128)(2,1)S(1)}, u32[]{:S(2)}, u32[]{:S(2)}) collective-permute-start(bf16[768,384]{1,0:T(8,128)(2,1)} %param.7), channel_id=1, source_target_pairs={{1,4},{3,6},{4,1},{6,3},{9,12},{11,14},{12,9},{14,11},{17,20},{19,... | collective-permute-start | bytes 1769480 | tf_op jit(solution)/shard_map/ppermute | solution.py:36
  34.8 16.8 %copy-start.5 = (bf16[384,384]{1,0:T(8,128)(2,1)}, bf16[384,384]{1,0:T(8,128)(2,1)S(1)}, u32[]{:S(2)}) copy-start(bf16[384,384]{1,0:T(8,128)(2,1)S(1)} %collective-permute-done.15.refs_6_) | copy-start | bytes 884740
  34.8 9.4 %collective-permute-start.12 = (bf16[384,384]{1,0:T(8,128)(2,1)S(1)}, bf16[384,384]{1,0:T(8,128)(2,1)S(1)}, u32[]{:S(2)}, u32[]{:S(2)}) collective-permute-start(bf16[384,384]{1,0:T(8,128)(2,1)S(1)} %collective-permute-done.10.refs_1_), channel_id=1, source_target_pairs={{0,8},{1,9},{2,10},{3,11},{4,12},{5,13},{6,14},{7,15},{8,0},{9,1},... | collective-permute-start | bytes 884744 | tf_op jit(solution)/shard_map/ppermute | solution.py:36
  44.2 7.2 %copy-start.7 = (bf16[384,384]{1,0:T(8,128)(2,1)}, bf16[384,384]{1,0:T(8,128)(2,1)S(1)}, u32[]{:S(2)}) copy-start(bf16[384,384]{1,0:T(8,128)(2,1)S(1)} %collective-permute-done.12.refs_3_) | copy-start | bytes 884740
  44.2 33.2 %collective-permute-start = (bf16[768,384]{1,0:T(8,128)(2,1)}, bf16[768,384]{1,0:T(8,128)(2,1)S(1)}, u32[]{:S(2)}, u32[]{:S(2)}) collective-permute-start(bf16[768,384]{1,0:T(8,128)(2,1)} %qa.7), channel_id=1, source_target_pairs={{1,4},{3,6},{4,1},{6,3},{9,12},{11,14},{12,9},{14,11},{17,20},{19,... | collective-permute-start | bytes 1769480 | tf_op jit(solution)/shard_map/ppermute | solution.py:36
  45.0 6.5 %copy-start.9 = (bf16[768,384]{1,0:T(8,128)(2,1)S(1)}, bf16[768,384]{1,0:T(8,128)(2,1)}, u32[]{:S(2)}) copy-start(bf16[768,384]{1,0:T(8,128)(2,1)} %param.7) | copy-start | bytes 1769476
  45.0 19.9 %collective-permute-start.14 = (bf16[384,384]{1,0:T(8,128)(2,1)S(1)}, bf16[384,384]{1,0:T(8,128)(2,1)S(1)}, u32[]{:S(2)}, u32[]{:S(2)}) collective-permute-start(bf16[384,384]{1,0:T(8,128)(2,1)S(1)} %collective-permute-done.13.refs_4_), channel_id=1, source_target_pairs={{0,4},{1,5},{2,6},{3,7},{4,0},{5,1},{6,2},{7,3},{8,12},{9,13},{10,... | collective-permute-start | bytes 884744 | tf_op jit(solution)/shard_map/ppermute | solution.py:36
  48.2 0.8 copy-start.10
  49.0 19.1 %collective-permute-start.16 = (bf16[384,384]{1,0:T(8,128)(2,1)S(1)}, bf16[384,384]{1,0:T(8,128)(2,1)S(1)}, u32[]{:S(2)}, u32[]{:S(2)}) collective-permute-start(bf16[384,384]{1,0:T(8,128)(2,1)S(1)} %collective-permute-done.15.refs_6_), channel_id=1, source_target_pairs={{0,4},{1,5},{2,6},{3,7},{4,0},{5,1},{6,2},{7,3},{8,12},{9,13},{10,... | collective-permute-start | bytes 884744 | tf_op jit(solution)/shard_map/ppermute | solution.py:36
  50.3 1.2 copy-start.11
  51.5 17.8 %copy-start.1 = (bf16[768,768]{1,0:T(8,128)(2,1)S(1)}, bf16[768,768]{1,0:T(8,128)(2,1)}, u32[]{:S(2)}) copy-start(bf16[768,768]{1,0:T(8,128)(2,1)} %g0.1) | copy-start | bytes 3538948
  51.5 17.8 %copy-start.2 = (bf16[384,384]{1,0:T(8,128)(2,1)S(1)}, bf16[384,384]{1,0:T(8,128)(2,1)}, u32[]{:S(2)}) copy-start(bf16[384,384]{1,0:T(8,128)(2,1)} %refs_0_.1) | copy-start | bytes 884740
  51.6 29.6 %copy-start = (bf16[768,384]{1,0:T(8,128)(2,1)S(1)}, bf16[768,384]{1,0:T(8,128)(2,1)}, u32[]{:S(2)}) copy-start(bf16[768,384]{1,0:T(8,128)(2,1)} %qa.7) | copy-start | bytes 1769476
  64.9 14.1 %collective-permute-start.5 = (bf16[768,384]{1,0:T(8,128)(2,1)S(1)}, bf16[768,384]{1,0:T(8,128)(2,1)}, u32[]{:S(2)}, u32[]{:S(2)}) collective-permute-start(bf16[768,384]{1,0:T(8,128)(2,1)S(1)} %broadcast_select_fusion.4.refs_0_.refs_2_), channel_id=1, source_target_pairs={{0,2},{1,8},{2,0},{3,10},{4,6},{5,12},{6,4},{7,14},{8,1},{9,16},{1... | collective-permute-start | bytes 1769480 | tf_op jit(solution)/shard_map/ppermute | solution.py:36
  68.1 17.8 %collective-permute-start.2 = (bf16[768,384]{1,0:T(8,128)(2,1)S(1)}, bf16[768,384]{1,0:T(8,128)(2,1)}, u32[]{:S(2)}, u32[]{:S(2)}) collective-permute-start(bf16[768,384]{1,0:T(8,128)(2,1)S(1)} %broadcast_select_fusion.4.refs_0_.refs_2_), channel_id=1, source_target_pairs={{0,1},{1,0},{2,3},{3,2},{4,5},{5,4},{6,7},{7,6},{8,9},{9,8},{10,11... | collective-permute-start | bytes 1769480 | tf_op jit(solution)/shard_map/ppermute | solution.py:36
  68.1 13.1 %collective-permute-start.6 = (bf16[768,384]{1,0:T(8,128)(2,1)S(1)}, bf16[768,384]{1,0:T(8,128)(2,1)}, u32[]{:S(2)}, u32[]{:S(2)}) collective-permute-start(bf16[768,384]{1,0:T(8,128)(2,1)S(1)} %broadcast_select_fusion.3.refs_2_.refs_3_), channel_id=1, source_target_pairs={{0,2},{1,8},{2,0},{3,10},{4,6},{5,12},{6,4},{7,14},{8,1},{9,16},{1... | collective-permute-start | bytes 1769480 | tf_op jit(solution)/shard_map/ppermute | solution.py:36
  69.3 16.7 %collective-permute-start.4 = (bf16[768,384]{1,0:T(8,128)(2,1)S(1)}, bf16[768,384]{1,0:T(8,128)(2,1)}, u32[]{:S(2)}, u32[]{:S(2)}) collective-permute-start(bf16[768,384]{1,0:T(8,128)(2,1)S(1)} %broadcast_select_fusion.3.refs_2_.refs_3_), channel_id=1, source_target_pairs={{0,1},{1,0},{2,3},{3,2},{4,5},{5,4},{6,7},{7,6},{8,9},{9,8},{10,11... | collective-permute-start | bytes 1769480 | tf_op jit(solution)/shard_map/ppermute | solution.py:36
  69.3 1.0 copy-start.4
  70.3 1.0 copy-start.6
  71.2 1.0 copy-start.8
  77.4 16.1 %collective-permute-start.17 = (bf16[384,768]{1,0:T(8,128)(2,1)S(1)}, bf16[384,768]{1,0:T(8,128)(2,1)S(1)}, u32[]{:S(2)}, u32[]{:S(2)}) collective-permute-start(bf16[384,768]{1,0:T(8,128)(2,1)S(1)} %project.1.ga), channel_id=1, source_target_pairs={{0,2},{1,4},{2,0},{3,6},{4,1},{5,7},{6,3},{7,5},{8,10},{9,12},{10,... | collective-permute-start | bytes 1769480 | tf_op jit(solution)/shard_map/ppermute | solution.py:36
  108.3 3.3 %collective-permute-start.19 = (bf16[768,384]{1,0:T(8,128)(2,1)S(1)}, bf16[768,384]{1,0:T(8,128)(2,1)S(1)}, u32[]{:S(2)}, u32[]{:S(2)}) collective-permute-start(bf16[768,384]{1,0:T(8,128)(2,1)S(1)} %get-tuple-element.26), channel_id=1, source_target_pairs={{0,1},{1,0},{2,3},{3,2},{4,5},{5,4},{6,7},{7,6},{8,9},{9,8},{10,11... | collective-permute-start | bytes 1769480 | tf_op jit(solution)/shard_map/ppermute | solution.py:36
  108.3 9.9 %collective-permute-start.20 = (bf16[768,384]{1,0:T(8,128)(2,1)S(1)}, bf16[768,384]{1,0:T(8,128)(2,1)S(1)}, u32[]{:S(2)}, u32[]{:S(2)}) collective-permute-start(bf16[768,384]{1,0:T(8,128)(2,1)S(1)} %get-tuple-element.27), channel_id=1, source_target_pairs={{0,2},{1,8},{2,0},{3,10},{4,6},{5,12},{6,4},{7,14},{8,1},{9,16},{1... | collective-permute-start | bytes 1769480 | tf_op jit(solution)/shard_map/ppermute | solution.py:36
  109.6 10.2 %collective-permute-start.22 = (bf16[768,384]{1,0:T(8,128)(2,1)S(1)}, bf16[768,384]{1,0:T(8,128)(2,1)S(1)}, u32[]{:S(2)}, u32[]{:S(2)}) collective-permute-start(bf16[768,384]{1,0:T(8,128)(2,1)S(1)} %get-tuple-element.29), channel_id=1, source_target_pairs={{0,1},{1,0},{2,3},{3,2},{4,5},{5,4},{6,7},{7,6},{8,9},{9,8},{10,11... | collective-permute-start | bytes 1769480 | tf_op jit(solution)/shard_map/ppermute | solution.py:36
  109.6 15.0 %collective-permute-start.23 = (bf16[768,384]{1,0:T(8,128)(2,1)S(1)}, bf16[768,384]{1,0:T(8,128)(2,1)S(1)}, u32[]{:S(2)}, u32[]{:S(2)}) collective-permute-start(bf16[768,384]{1,0:T(8,128)(2,1)S(1)} %get-tuple-element.30), channel_id=1, source_target_pairs={{0,2},{1,8},{2,0},{3,10},{4,6},{5,12},{6,4},{7,14},{8,1},{9,16},{1... | collective-permute-start | bytes 1769480 | tf_op jit(solution)/shard_map/ppermute | solution.py:36
  110.5 20.4 %collective-permute-start.18 = (bf16[768,384]{1,0:T(8,128)(2,1)S(1)}, bf16[768,384]{1,0:T(8,128)(2,1)S(1)}, u32[]{:S(2)}, u32[]{:S(2)}) collective-permute-start(bf16[768,384]{1,0:T(8,128)(2,1)S(1)} %get-tuple-element.24), channel_id=1, source_target_pairs={{0,2},{1,4},{2,0},{3,6},{4,1},{5,7},{6,3},{7,5},{8,10},{9,12},{10,... | collective-permute-start | bytes 1769480 | tf_op jit(solution)/shard_map/ppermute | solution.py:36
  118.5 18.8 %collective-permute-start.21 = (bf16[768,384]{1,0:T(8,128)(2,1)S(1)}, bf16[768,384]{1,0:T(8,128)(2,1)S(1)}, u32[]{:S(2)}, u32[]{:S(2)}) collective-permute-start(bf16[768,384]{1,0:T(8,128)(2,1)S(1)} %add_convert_fusion.1), channel_id=1, source_target_pairs={{0,2},{1,4},{2,0},{3,6},{4,1},{5,7},{6,3},{7,5},{8,10},{9,12},{10,... | collective-permute-start | bytes 1769480 | tf_op jit(solution)/shard_map/ppermute | solution.py:36
  124.9 18.7 %collective-permute-start.24 = (bf16[768,384]{1,0:T(8,128)(2,1)S(1)}, bf16[768,384]{1,0:T(8,128)(2,1)S(1)}, u32[]{:S(2)}, u32[]{:S(2)}) collective-permute-start(bf16[768,384]{1,0:T(8,128)(2,1)S(1)} %add_convert_fusion), channel_id=1, source_target_pairs={{0,2},{1,4},{2,0},{3,6},{4,1},{5,7},{6,3},{7,5},{8,10},{9,12},{10,... | collective-permute-start | bytes 1769480 | tf_op jit(solution)/shard_map/ppermute | solution.py:36

commit v5 on v4

--- a/solution.py
+++ b/solution.py
@@ -14,7 +14,6 @@
 AXES = ("tm", "head")
 LIMIT = 24 << 20
 BIG = 768
-STEP = 768
 SMALL = 64
 NT = (((1,), (1,)), ((), ()))
 TN = (((0,), (0,)), ((), ()))
@@ -113,128 +112,108 @@
     )(flags, *queries, *keys, *values)
 
 
-def backward_kernel(far, flag_ref, e_ref, on, sn, of, sf, ga, gb, qa, qb, *refs):
+def backward_kernel(flag_ref, en, on, sn, ef, of, sf, ga, gb, qa, qb, ks, vs, ko, vo, kz, vz, *refs):
+    dq, own, side, away = refs
     rows = qa.shape[0]
-    step = STEP
     scale = 1.0 / math.sqrt(HD)
     stays = flag_ref[1] > 0
     query = jnp.where(stays, qa[...], qb[...])
-    flipped = jnp.where(stays, ga[...], gb[...]).astype(jnp.float32)
+    grad = jnp.where(stays, ga[...], gb[...]).astype(jnp.float32)
     near_top = sn[0:1, :]
     far_top = jnp.where(flag_ref[0] > 0, sf[0:1, :], -jnp.inf)
     top = jnp.maximum(near_top, far_top)
     near_share, far_share = jnp.exp2(near_top - top), jnp.exp2(far_top - top)
     inverse = 1.0 / (near_share * sn[1:2, :] + far_share * sf[1:2, :])
     near_share, far_share = near_share * inverse, far_share * inverse
-    near_grad = (flipped * near_share).astype(jnp.bfloat16)
-    far_grad = (flipped * far_share).astype(jnp.bfloat16)
+    near_grad = (grad * near_share).astype(jnp.bfloat16)
+    far_grad = (grad * far_share).astype(jnp.bfloat16)
     inner = jnp.sum(
         on[...] * near_grad.astype(jnp.float32) + of[...] * far_grad.astype(jnp.float32),
         axis=0,
         keepdims=True,
     )
-    if far:
-        kz, vz, dkz, dvz, dq = refs
-        slabs = ((kz, vz, dkz, dvz),)
-        total, grad_t, inner = None, far_grad, inner * far_share
-    else:
-        ks, vs, ko, vo, dq_far, dks, dvs, dko, dvo, dq = refs
-        slabs = ((ks, vs, dks, dvs), (ko, vo, dko, dvo))
-        total, grad_t, inner = dq_far[...], near_grad, inner * near_share
-    for i, (k, v, dk, dv) in enumerate(slabs):
-        base = 0 if far else (1 - i) * rows
-        for first in range(0, rows, step):
-            weight = e_ref[0, base + first : base + first + step, :]
-            slope = dot(v[first : first + step, :], grad_t)
-            delta = (weight.astype(jnp.float32) * (slope - inner)).astype(jnp.bfloat16)
-            dv[first : first + step, :] = dot(weight, grad_t, NT).astype(dv.dtype)
-            dk[first : first + step, :] = (dot(delta, query) * scale).astype(dk.dtype)
-            part = dot(k[first : first + step, :], delta, TN)
-            total = part if total is None else total + part
-    dq[...] = total if far else (total * scale).T.astype(dq.dtype)
-
-
-def backward(far, flags, weights, near, away, grads, queries, keys, values, dq_far=()):
-    rows, width = queries[0].shape
-    heads = width // HD
-    spec = pl.BlockSpec((rows, HD), lambda h: (0, h))
-    flip = pl.BlockSpec((HD, rows), lambda h: (h, 0))
-    stat = pl.BlockSpec((8, rows), lambda h: (h, 0))
-    f32 = jax.ShapeDtypeStruct((rows, width), jnp.float32)
-    bf16 = jax.ShapeDtypeStruct((rows, width), jnp.bfloat16)
-    slabs = [r for pair in zip(keys, values) for r in pair]
-    if far:
-        out_specs = [spec, spec, flip]
-        out_shape = [bf16, bf16, jax.ShapeDtypeStruct((width, rows), jnp.float32)]
-    else:
-        out_specs = [spec] * 5
-        out_shape = [bf16, bf16, f32, f32, bf16]
+    near_inner, far_inner = inner * near_share, inner * far_share
+    total = None
+    for weights, base, k, v, out, part_grad, part_inner in (
+        (ef, 0, kz, vz, away, far_grad, far_inner),
+        (en, rows, ks, vs, side, near_grad, near_inner),
+        (en, 0, ko, vo, own, near_grad, near_inner),
+    ):
+        weight = weights[0, base : base + rows, :]
+        slope = dot(v[...], part_grad)
+        delta = (weight.astype(jnp.float32) * (slope - part_inner)).astype(jnp.bfloat16)
+        out[:, HD:] = dot(weight, part_grad, NT).astype(out.dtype)
+        out[:, :HD] = (dot(delta, query) * scale).astype(out.dtype)
+        part = dot(k[...], delta, TN)
+        total = part if total is None else total + part
+    dq[...] = (total * scale).T.astype(dq.dtype)
+
+
+def backward(head, flags, near, away, grads, queries, side, own, far):
+    rows, _ = queries[0].shape
+    spec = pl.BlockSpec((rows, HD), lambda i: (0, head))
+    flip = pl.BlockSpec((HD, rows), lambda i: (head, 0))
+    stat = pl.BlockSpec((8, rows), lambda i: (head, 0))
+
+    def weight_spec(e):
+        return pl.BlockSpec((1,) + e.shape[1:], lambda i: (head, 0, 0))
+
+    def whole(columns):
+        return pl.BlockSpec((rows, columns), lambda i: (0, 0))
+
     return pl.pallas_call(
-        functools.partial(backward_kernel, far),
-        grid=(heads,),
+        backward_kernel,
+        grid=(1,),
         in_specs=[
             pl.BlockSpec(memory_space=pltpu.SMEM),
-            pl.BlockSpec((1, weights.shape[1], rows), lambda h: (h, 0, 0)),
+            weight_spec(near[0]),
             flip,
             stat,
+            weight_spec(away[0]),
             flip,
             stat,
         ]
         + [flip] * 2
-        + [spec] * (2 + len(slabs))
-        + [flip] * len(dq_far),
-        out_specs=out_specs,
-        out_shape=out_shape,
+        + [spec] * 8,
+        out_specs=[whole(HD)] + [whole(2 * HD)] * 3,
+        out_shape=[
+            jax.ShapeDtypeStruct((rows, HD), jnp.bfloat16),
+            jax.ShapeDtypeStruct((rows, 2 * HD), jnp.float32),
+            jax.ShapeDtypeStruct((rows, 2 * HD), jnp.bfloat16),
+            jax.ShapeDtypeStruct((rows, 2 * HD), jnp.bfloat16),
+        ],
         compiler_params=pltpu.CompilerParams(vmem_limit_bytes=LIMIT),
-        name="backward_far" if far else "backward_near",
-    )(flags, weights, *near, *away, *grads, *queries, *slabs, *dq_far)
+    )(flags, *near, *away, *grads, *queries, *side, *own, *far)
 
 
 def project_kernel(place_ref, g0, g1, g2, g3, *refs):
     shards = refs[:8]
-    out_ref, gbuf, wbuf, gsem, wsem = refs[8:]
+    out_ref, wbuf = refs[8:]
     z, y, h = place_ref[0], place_ref[1], place_ref[2]
     width = out_ref.shape[0]
-    copies = []
     for m in range(4):
         for n in range(2):
             column = pl.multiple_of((y ^ n) * width, width)
-            copies.append(
-                pltpu.make_async_copy(
-                    shards[2 * m + n], wbuf.at[z ^ m, :, pl.ds(column, width)], wsem.at[2 * m + n]
-                )
-            )
-    grads = [
-        pltpu.make_async_copy(g, gbuf.at[m], gsem.at[m]) for m, g in enumerate((g0, g1, g2, g3))
-    ]
-    for c in copies + grads:
-        c.start()
-    for c in copies:
-        c.wait()
+            wbuf[z ^ m, :, pl.ds(column, width)] = shards[2 * m + n][...]
     total = None
-    for m in range(4):
-        grads[m].wait()
-        part = dot(wbuf[h ^ m], gbuf[m], NT)
+    for m, g in enumerate((g0, g1, g2, g3)):
+        part = dot(wbuf[h ^ m], g[...], NT)
         total = part if total is None else total + part
     out_ref[...] = total.astype(out_ref.dtype)
 
 
 def project(place, grads, shards, rows, width):
-    anywhere = pl.BlockSpec(memory_space=pl.ANY)
+    vmem = pl.BlockSpec(memory_space=pltpu.VMEM)
+    held = [pltpu.with_memory_space_constraint(x, pltpu.VMEM) for x in (*grads, *shards)]
     return pl.pallas_call(
         project_kernel,
-        in_specs=[pl.BlockSpec(memory_space=pltpu.SMEM)] + [anywhere] * 12,
-        out_specs=pl.BlockSpec(memory_space=pltpu.VMEM),
+        in_specs=[pl.BlockSpec(memory_space=pltpu.SMEM)] + [vmem] * 12,
+        out_specs=vmem,
         out_shape=jax.ShapeDtypeStruct((width, rows), jnp.bfloat16),
-        scratch_shapes=[
-            pltpu.VMEM((4,) + grads[0].shape, jnp.bfloat16),
-            pltpu.VMEM((4, width, grads[0].shape[1]), jnp.bfloat16),
-            pltpu.SemaphoreType.DMA((4,)),
-            pltpu.SemaphoreType.DMA((8,)),
-        ],
+        scratch_shapes=[pltpu.VMEM((4, width, grads[0].shape[1]), jnp.bfloat16)],
         compiler_params=pltpu.CompilerParams(vmem_limit_bytes=LIMIT),
         name="project",
-    )(place, *grads, *shards)
+    )(place, *held)
 
 
 def local(n_tm, n_head, queries, key_rows, value_rows, grad_out, w_out):
@@ -252,6 +231,9 @@
 
     def busy_route(t, h):
         return (t, h ^ 2) if (t & 1) == (h & 1) else (t ^ 1, h ^ 1)
+
+    def spare_route(t, h):
+        return (t ^ 2, h) if (t & 1) == (h & 1) else (t ^ 1, h ^ 1)
 
     def far_route(t, h):
         here = (t & ~1) + (h & 1)
@@ -283,7 +265,7 @@
         shards = [w_out, w0y, w1, w1y, w2, w2y, w3, w3y]
     far_k, far_v = send(keys, far_route), send(values, far_route)
     side_k, side_v = send(keys, side_route), send(values, side_route)
-    near_weights, *near = soften(flags, query_pair, (keys, side_k), (values, side_v))
+    near = soften(flags, query_pair, (keys, side_k), (values, side_v))
     if square:
         attn_grad = project(
             jnp.stack([t // 2, y, h]).astype(jnp.int32), grads, shards, rows, width
@@ -295,28 +277,38 @@
             NT,
         ).astype(jnp.bfloat16)
     grad_pair = (attn_grad, send(attn_grad, busy_route))
-    far_weights, *away = soften(flags, query_pair, (far_k,), (far_v,))
-    dkz, dvz, dq_far = backward(
-        True, flags, far_weights, near, away, grad_pair, query_pair, (far_k,), (far_v,)
+    away = soften(flags, query_pair, (far_k,), (far_v,))
+
+    done = []
+    for head in range(width // HD):
+        dq, own, side, far = backward(
+            head,
+            flags,
+            near,
+            away,
+            grad_pair,
+            query_pair,
+            (side_k, side_v),
+            (keys, values),
+            (far_k, far_v),
+        )
+        far = send(far, far_route)
+        side = send(side, side_route)
+        own = (own + side.astype(jnp.float32) + far.astype(jnp.float32)).astype(jnp.bfloat16)
+        done.append(((dq, send(dq, spare_route)), (own, send(own, busy_route))))
+
+    def collect(i, columns):
+        kept, received = [
+            jnp.concatenate([pair[i][j][:, columns] for pair in done], 1) for j in range(2)
+        ]
+        return jnp.where(stays, kept, received)
+
+    first = collect(0, slice(0, HD))
+    return (
+        first,
+        collect(1, slice(0, HD)),
+        collect(1, slice(HD, 2 * HD)),
     )
-    far_back = [send(d, far_route).astype(jnp.float32) for d in (dvz, dkz)]
-    dks, dvs, dko, dvo, dq = backward(
-        False,
-        flags,
-        near_weights,
-        near,
-        away,
-        grad_pair,
-        query_pair,
-        (side_k, keys),
-        (side_v, values),
-        (dq_far,),
-    )
-    side_back = [send(d, side_route).astype(jnp.float32) for d in (dvs, dks)]
-    dv, dk = [
-        (o + s + f).astype(jnp.bfloat16) for o, s, f in zip((dvo, dko), side_back, far_back)
-    ]
-    return tuple(jnp.where(stays, b, send(b, busy_route)) for b in (dq, dk, dv))
 
 
 def solution(mesh):

time: 145 us -> 149 us (1.028)
  starting transfers between devices: 25.5 us -> 30.6 us
    ppermute x25 -> x30, starting transfers between devices: 25.5 us -> 30.6 us  [exchange(): return lax.ppermute(block, AXES, pairs)]
    ppermute x25 -> x30, waiting for transfers between devices: 77.7 us -> 76.3 us  [exchange(): return lax.ppermute(block, AXES, pairs)]
    unnamed x24 -> x28, local copies, waits for them, and re-layouts: 3.75 us -> 4.6 us
    pallas_call x2 -> x3, Pallas kernels: 14.7 us -> 14.3 us  [backward(): pl.pallas_call(backward_kernel, grid=(1,), in_specs=[pl.BlockSpec(memory_...]
  transfers between devices with their start and end apart: 25 -> 30, of which waited for: 12 -> 11; matrix products, arithmetic and copies ran while one was open for 3% -> 2% of each run, Pallas kernels for 12% -> 18%
where the time goes in v5:
time: 149 us; the launch traced here: 148 us
  waiting for transfers between devices  76.3 us (51%)
  Pallas kernels  31.4 us (21%)
  starting transfers between devices  30.6 us (21%)
  local copies, waits for them, and re-layouts  4.76 us (3%)
  other arithmetic  4.15 us (3%)
    ppermute x30, waiting for transfers between devices, exchange(): return lax.ppermute(block, AXES, pairs)  76.3 us
    ppermute x30, starting transfers between devices, exchange(): return lax.ppermute(block, AXES, pairs)  30.6 us
    pallas_call x3, Pallas kernels, backward(): pl.pallas_call(backward_kernel, grid=(1,), in_specs=[pl.BlockSpec(memory_...  14.3 us
    pallas_call x2, Pallas kernels, soften(): pl.pallas_call(functools.partial(soften_kernel, parts, tile), grid=(heads...  12.1 us
    pallas_call x1, Pallas kernels, project(): pl.pallas_call(project_kernel, in_specs=[pl.BlockSpec(memory_space=pltpu....  4.99 us
    unnamed x28, local copies, waits for them, and re-layouts  4.6 us
  transfers between devices with their start and end apart: 30, of which 11 were waited for; matrix products, arithmetic and copies ran while one was open for 2% of the time, Pallas kernels for 18%

profile of v5, /device:TPU:0, one launch (start us, length us, event | category | flops | bytes accessed | tf_op | source)
XLA Modules:
  0.0 148.1 jit_solution(17934276794368981120)
XLA Ops:
  0.6 3.0 %collective-permute-start.8 = (bf16[768,768]{1,0:T(8,128)(2,1)}, bf16[768,768]{1,0:T(8,128)(2,1)}, u32[]{:S(2)}, u32[]{:S(2)}) collective-permute-start(bf16[768,768]{1,0:T(8,128)(2,1)} %g0.1), channel_id=1, source_target_pairs={{0,2},{1,3},{2,0},{3,1},{4,6},{5,7},{6,4},{7,5},{8,10},{9,11},{10,... | collective-permute-start | bytes 3538952 | tf_op jit(solution)/shard_map/ppermute | solution.py:35
  3.7 1.6 %collective-permute-start.11 = (bf16[384,384]{1,0:T(8,128)(2,1)}, bf16[384,384]{1,0:T(8,128)(2,1)S(1)}, u32[]{:S(2)}, u32[]{:S(2)}) collective-permute-start(bf16[384,384]{1,0:T(8,128)(2,1)} %refs_0_.1), channel_id=1, source_target_pairs={{0,8},{1,9},{2,10},{3,11},{4,12},{5,13},{6,14},{7,15},{8,0},{9,1},... | collective-permute-start | bytes 884744 | tf_op jit(solution)/shard_map/ppermute | solution.py:35
  5.2 1.5 %collective-permute-start.10 = (bf16[384,384]{1,0:T(8,128)(2,1)}, bf16[384,384]{1,0:T(8,128)(2,1)S(1)}, u32[]{:S(2)}, u32[]{:S(2)}) collective-permute-start(bf16[384,384]{1,0:T(8,128)(2,1)} %refs_0_.1), channel_id=1, source_target_pairs={{0,4},{1,5},{2,6},{3,7},{4,0},{5,1},{6,2},{7,3},{8,12},{9,13},{10,... | collective-permute-start | bytes 884744 | tf_op jit(solution)/shard_map/ppermute | solution.py:35
  6.8 0.7 collective-permute-start.1
  7.5 1.5 %collective-permute-start.3 = (bf16[768,384]{1,0:T(8,128)(2,1)}, bf16[768,384]{1,0:T(8,128)(2,1)}, u32[]{:S(2)}, u32[]{:S(2)}) collective-permute-start(bf16[768,384]{1,0:T(8,128)(2,1)} %param.7), channel_id=1, source_target_pairs={{1,4},{3,6},{4,1},{6,3},{9,12},{11,14},{12,9},{14,11},{17,20},{19,... | collective-permute-start | bytes 1769480 | tf_op jit(solution)/shard_map/ppermute | solution.py:35
  8.9 3.4 %collective-permute-done.11.refs_2_ = bf16[384,384]{1,0:T(8,128)(2,1)S(1)} collective-permute-done((bf16[384,384]{1,0:T(8,128)(2,1)}, bf16[384,384]{1,0:T(8,128)(2,1)S(1)}, u32[]{:S(2)}, u32[]{:S(2)}) %collective-permute-start.11) | collective-permute-done | bytes 294944 | tf_op jit(solution)/shard_map/ppermute | solution.py:35
  12.4 17.6 %collective-permute-done.8.g2 = bf16[768,768]{1,0:T(8,128)(2,1)} collective-permute-done((bf16[768,768]{1,0:T(8,128)(2,1)}, bf16[768,768]{1,0:T(8,128)(2,1)}, u32[]{:S(2)}, u32[]{:S(2)}) %collective-permute-start.8) | collective-permute-done | bytes 1179680 | tf_op jit(solution)/shard_map/ppermute | solution.py:35
  30.0 2.9 %collective-permute-start.13 = (bf16[384,384]{1,0:T(8,128)(2,1)}, bf16[384,384]{1,0:T(8,128)(2,1)S(1)}, u32[]{:S(2)}, u32[]{:S(2)}) collective-permute-start(bf16[384,384]{1,0:T(8,128)(2,1)} %refs_0_.1), channel_id=1, source_target_pairs={{0,16},{1,17},{2,18},{3,19},{4,20},{5,21},{6,22},{7,23},{8,24},{9,... | collective-permute-start | bytes 884744 | tf_op jit(solution)/shard_map/ppermute | solution.py:35
  32.9 14.1 %collective-permute-done.13.refs_4_ = bf16[384,384]{1,0:T(8,128)(2,1)S(1)} collective-permute-done((bf16[384,384]{1,0:T(8,128)(2,1)}, bf16[384,384]{1,0:T(8,128)(2,1)S(1)}, u32[]{:S(2)}, u32[]{:S(2)}) %collective-permute-start.13) | collective-permute-done | bytes 294944 | tf_op jit(solution)/shard_map/ppermute | solution.py:35
  47.0 4.1 %collective-permute-start.12 = (bf16[384,384]{1,0:T(8,128)(2,1)S(1)}, bf16[384,384]{1,0:T(8,128)(2,1)S(1)}, u32[]{:S(2)}, u32[]{:S(2)}) collective-permute-start(bf16[384,384]{1,0:T(8,128)(2,1)S(1)} %collective-permute-done.10.refs_1_), channel_id=1, source_target_pairs={{0,8},{1,9},{2,10},{3,11},{4,12},{5,13},{6,14},{7,15},{8,0},{9,1},... | collective-permute-start | bytes 884744 | tf_op jit(solution)/shard_map/ppermute | solution.py:35
  51.1 0.7 collective-permute-start
  51.9 11.1 %collective-permute-done.15.refs_6_ = bf16[384,384]{1,0:T(8,128)(2,1)S(1)} collective-permute-done((bf16[384,384]{1,0:T(8,128)(2,1)S(1)}, bf16[384,384]{1,0:T(8,128)(2,1)S(1)}, u32[]{:S(2)}, u32[]{:S(2)}) %collective-permute-start.15) | collective-permute-done | bytes 294944 | tf_op jit(solution)/shard_map/ppermute | solution.py:35
  63.0 1.4 collective-permute-start.14
  64.4 0.7 copy-done.11
  65.1 0.6 collective-permute-start.16
  65.8 1.1 broadcast_select_fusion.1.refs_0_.ko
  67.1 5.8 %collective-permute-done.14.refs_5_ = bf16[384,384]{1,0:T(8,128)(2,1)S(1)} collective-permute-done((bf16[384,384]{1,0:T(8,128)(2,1)S(1)}, bf16[384,384]{1,0:T(8,128)(2,1)S(1)}, u32[]{:S(2)}, u32[]{:S(2)}) %collective-permute-start.14) | collective-permute-done | bytes 294944 | tf_op jit(solution)/shard_map/ppermute | solution.py:35
  72.9 4.2 %collective-permute-done.16.refs_7_ = bf16[384,384]{1,0:T(8,128)(2,1)S(1)} collective-permute-done((bf16[384,384]{1,0:T(8,128)(2,1)S(1)}, bf16[384,384]{1,0:T(8,128)(2,1)S(1)}, u32[]{:S(2)}, u32[]{:S(2)}) %collective-permute-start.16) | collective-permute-done | bytes 294944 | tf_op jit(solution)/shard_map/ppermute | solution.py:35
  77.1 1.2 collective-permute-start.5
  78.3 0.9 collective-permute-start.6
  79.2 1.0 copy-done.4
  80.2 1.0 copy-done.6
  81.2 1.0 copy-done.8
  82.1 1.0 copy-done.10
  83.1 5.0 %project.1.ga = bf16[384,768]{1,0:T(8,128)(2,1)} custom-call(s32[3]{0:T(128)S(1)} %pad_add_fusion.place_ref, bf16[768,768]{1,0:T(8,128)(2,1)S(1)} %copy-done.1, bf16[768,768]{1,0:T(8,128)(2,1)} %collective-permute-done.7.g1, bf16[768,768]{1,0:T(8,128)(2,1)} %collective-permute-done.8.g2, bf16[768,768]{1,0:T(8,128)(2,1)} %collective-permute-done.9.g3, ...), custom_call_target="tpu_custom_call" | custom-call | tf_op jit(solution)/shard_map/project/pallas_call | solution.py:208
  88.1 1.2 collective-permute-start.17
  89.3 7.6 %shard_map.76 = (bf16[3,1536,768]{2,1,0:T(8,128)(2,1)S(1)}, f32[384,768]{1,0:T(8,128)S(1)}, f32[24,768]{1,0:T(8,128)S(1)}) custom-call(s32[2]{0:T(128)S(1)} %add_convert_fusion.3.flag_ref, bf16[768,384]{1,0:T(8,128)(2,1)S(1)} %copy-done, bf16[768,384]{1,0:T(8,128)(2,1)S(1)} %collective-permute-done.qb, ...), custom_call_target="tpu_custom_call" | custom-call | tf_op jit(solution)/shard_map/pallas_call | solution.py:95
  96.9 4.5 %shard_map.77 = (bf16[3,768,768]{2,1,0:T(8,128)(2,1)S(1)}, f32[384,768]{1,0:T(8,128)S(1)}, f32[24,768]{1,0:T(8,128)S(1)}) custom-call(s32[2]{0:T(128)S(1)} %add_convert_fusion.3.flag_ref, bf16[768,384]{1,0:T(8,128)(2,1)S(1)} %copy-done, bf16[768,384]{1,0:T(8,128)(2,1)S(1)} %collective-permute-done.qb, ...), custom_call_target="tpu_custom_call" | custom-call | tf_op jit(solution)/shard_map/pallas_call | solution.py:95
  101.4 4.8 %shard_map.78 = (bf16[768,128]{1,0:T(8,128)(2,1)S(1)}, f32[768,256]{1,0:T(8,128)S(1)}, bf16[768,256]{1,0:T(8,128)(2,1)S(1)}, bf16[768,256]{1,0:T(8,128)(2,1)S(1)}) custom-call(s32[2]{0:T(128)S(1)} %add_convert_fusion.3.flag_ref, bf16[3,1536,768]{2,1,0:T(8,128)(2,1)S(1)} %get-tuple-element.21.en, f32[384,768]{1,0:T(8,128)S(1)} %get-tuple-element.22.on, ...), custom_call_target="tpu_custom_call" | custom-call | tf_op jit(solution)/shard_map/pallas_call | solution.py:164
  106.4 1.5 %collective-permute-start.22 = (bf16[768,256]{1,0:T(8,128)(2,1)S(1)}, bf16[768,256]{1,0:T(8,128)(2,1)S(1)}, u32[]{:S(2)}, u32[]{:S(2)}) collective-permute-start(bf16[768,256]{1,0:T(8,128)(2,1)S(1)} %get-tuple-element.32), channel_id=1, source_target_pairs={{0,2},{1,8},{2,0},{3,10},{4,6},{5,12},{6,4},{7,14},{8,1},{9,16},{1... | collective-permute-start | bytes 1179656 | tf_op jit(solution)/shard_map/ppermute | solution.py:35
  107.9 0.5 collective-permute-start.18
  108.4 4.8 %shard_map.79 = (bf16[768,128]{1,0:T(8,128)(2,1)S(1)}, f32[768,256]{1,0:T(8,128)S(1)}, bf16[768,256]{1,0:T(8,128)(2,1)S(1)}, bf16[768,256]{1,0:T(8,128)(2,1)S(1)}) custom-call(s32[2]{0:T(128)S(1)} %add_convert_fusion.3.flag_ref, bf16[3,1536,768]{2,1,0:T(8,128)(2,1)S(1)} %get-tuple-element.21.en, f32[384,768]{1,0:T(8,128)S(1)} %get-tuple-element.22.on, ...), custom_call_target="tpu_custom_call" | custom-call | tf_op jit(solution)/shard_map/pallas_call | solution.py:164
  113.2 1.6 %collective-permute-start.19 = (bf16[768,128]{1,0:T(8,128)(2,1)S(1)}, bf16[768,128]{1,0:T(8,128)(2,1)S(1)}, u32[]{:S(2)}, u32[]{:S(2)}) collective-permute-start(bf16[768,128]{1,0:T(8,128)(2,1)S(1)} %get-tuple-element.28), channel_id=1, source_target_pairs={{0,8},{1,4},{2,10},{3,6},{4,1},{5,13},{6,3},{7,15},{8,0},{9,12},{1... | collective-permute-start | bytes 589832 | tf_op jit(solution)/shard_map/ppermute | solution.py:35
  114.8 4.8 %shard_map.80 = (bf16[768,128]{1,0:T(8,128)(2,1)S(1)}, f32[768,256]{1,0:T(8,128)S(1)}, bf16[768,256]{1,0:T(8,128)(2,1)S(1)}, bf16[768,256]{1,0:T(8,128)(2,1)S(1)}) custom-call(s32[2]{0:T(128)S(1)} %add_convert_fusion.3.flag_ref, bf16[3,1536,768]{2,1,0:T(8,128)(2,1)S(1)} %get-tuple-element.21.en, f32[384,768]{1,0:T(8,128)S(1)} %get-tuple-element.22.on, ...), custom_call_target="tpu_custom_call" | custom-call | tf_op jit(solution)/shard_map/pallas_call | solution.py:164
  119.6 0.6 collective-permute-start.20
  120.1 0.3 collective-permute-start.23
  120.5 1.0 collective-permute-start.24
  121.4 3.9 %collective-permute-done.20 = bf16[768,128]{1,0:T(8,128)(2,1)S(1)} collective-permute-done((bf16[768,128]{1,0:T(8,128)(2,1)S(1)}, bf16[768,128]{1,0:T(8,128)(2,1)S(1)}, u32[]{:S(2)}, u32[]{:S(2)}) %collective-permute-start.20) | collective-permute-done | bytes 196640 | tf_op jit(solution)/shard_map/ppermute | solution.py:35
  125.3 1.0 maximum_select_fusion
  126.3 0.7 collective-permute-start.26
  127.2 1.3 collective-permute-start.27
  128.7 0.8 collective-permute-start.28
  129.5 4.6 %collective-permute-done.26 = bf16[768,256]{1,0:T(8,128)(2,1)S(1)} collective-permute-done((bf16[768,256]{1,0:T(8,128)(2,1)S(1)}, bf16[768,256]{1,0:T(8,128)(2,1)S(1)}, u32[]{:S(2)}, u32[]{:S(2)}) %collective-permute-start.26) | collective-permute-done | bytes 393248 | tf_op jit(solution)/shard_map/ppermute | solution.py:35
  134.3 0.8 collective-permute-start.29
  135.1 3.2 %collective-permute-done.27 = bf16[768,256]{1,0:T(8,128)(2,1)S(1)} collective-permute-done((bf16[768,256]{1,0:T(8,128)(2,1)S(1)}, bf16[768,256]{1,0:T(8,128)(2,1)S(1)}, u32[]{:S(2)}, u32[]{:S(2)}) %collective-permute-start.27) | collective-permute-done | bytes 393248 | tf_op jit(solution)/shard_map/ppermute | solution.py:35
  138.3 4.2 %collective-permute-done.28 = bf16[768,256]{1,0:T(8,128)(2,1)S(1)} collective-permute-done((bf16[768,256]{1,0:T(8,128)(2,1)S(1)}, bf16[768,256]{1,0:T(8,128)(2,1)S(1)}, u32[]{:S(2)}, u32[]{:S(2)}) %collective-permute-start.28) | collective-permute-done | bytes 393248 | tf_op jit(solution)/shard_map/ppermute | solution.py:35
  142.5 4.2 %collective-permute-done.29 = bf16[768,256]{1,0:T(8,128)(2,1)S(1)} collective-permute-done((bf16[768,256]{1,0:T(8,128)(2,1)S(1)}, bf16[768,256]{1,0:T(8,128)(2,1)S(1)}, u32[]{:S(2)}, u32[]{:S(2)}) %collective-permute-start.29) | collective-permute-done | bytes 393248 | tf_op jit(solution)/shard_map/ppermute | solution.py:35
  146.8 1.4 maximum_select_fusion.1
  (61 shorter events, 1.1 us)
Async XLA Ops:
  0.6 66.3 %copy-start.13 = (bf16[768,384]{1,0:T(8,128)(2,1)S(1)}, bf16[768,384]{1,0:T(8,128)(2,1)}, u32[]{:S(2)}) copy-start(bf16[768,384]{1,0:T(8,128)(2,1)} %param.7) | copy-start | bytes 1769476
  0.6 29.3 %collective-permute-start.8 = (bf16[768,768]{1,0:T(8,128)(2,1)}, bf16[768,768]{1,0:T(8,128)(2,1)}, u32[]{:S(2)}, u32[]{:S(2)}) collective-permute-start(bf16[768,768]{1,0:T(8,128)(2,1)} %g0.1), channel_id=1, source_target_pairs={{0,2},{1,3},{2,0},{3,1},{4,6},{5,7},{6,4},{7,5},{8,10},{9,11},{10,... | collective-permute-start | bytes 3538952 | tf_op jit(solution)/shard_map/ppermute | solution.py:35
  3.7 8.7 %collective-permute-start.11 = (bf16[384,384]{1,0:T(8,128)(2,1)}, bf16[384,384]{1,0:T(8,128)(2,1)S(1)}, u32[]{:S(2)}, u32[]{:S(2)}) collective-permute-start(bf16[384,384]{1,0:T(8,128)(2,1)} %refs_0_.1), channel_id=1, source_target_pairs={{0,8},{1,9},{2,10},{3,11},{4,12},{5,13},{6,14},{7,15},{8,0},{9,1},... | collective-permute-start | bytes 884744 | tf_op jit(solution)/shard_map/ppermute | solution.py:35
  5.2 24.7 %collective-permute-start.10 = (bf16[384,384]{1,0:T(8,128)(2,1)}, bf16[384,384]{1,0:T(8,128)(2,1)S(1)}, u32[]{:S(2)}, u32[]{:S(2)}) collective-permute-start(bf16[384,384]{1,0:T(8,128)(2,1)} %refs_0_.1), channel_id=1, source_target_pairs={{0,4},{1,5},{2,6},{3,7},{4,0},{5,1},{6,2},{7,3},{8,12},{9,13},{10,... | collective-permute-start | bytes 884744 | tf_op jit(solution)/shard_map/ppermute | solution.py:35
  6.8 40.3 %collective-permute-start.1 = (bf16[768,384]{1,0:T(8,128)(2,1)}, bf16[768,384]{1,0:T(8,128)(2,1)S(1)}, u32[]{:S(2)}, u32[]{:S(2)}) collective-permute-start(bf16[768,384]{1,0:T(8,128)(2,1)} %param.6), channel_id=1, source_target_pairs={{1,4},{3,6},{4,1},{6,3},{9,12},{11,14},{12,9},{14,11},{17,20},{19,... | collective-permute-start | bytes 1769480 | tf_op jit(solution)/shard_map/ppermute | solution.py:35
  7.5 43.7 %collective-permute-start.3 = (bf16[768,384]{1,0:T(8,128)(2,1)}, bf16[768,384]{1,0:T(8,128)(2,1)}, u32[]{:S(2)}, u32[]{:S(2)}) collective-permute-start(bf16[768,384]{1,0:T(8,128)(2,1)} %param.7), channel_id=1, source_target_pairs={{1,4},{3,6},{4,1},{6,3},{9,12},{11,14},{12,9},{14,11},{17,20},{19,... | collective-permute-start | bytes 1769480 | tf_op jit(solution)/shard_map/ppermute | solution.py:35
  12.4 54.6 %copy-start.3 = (bf16[384,384]{1,0:T(8,128)(2,1)}, bf16[384,384]{1,0:T(8,128)(2,1)S(1)}, u32[]{:S(2)}) copy-start(bf16[384,384]{1,0:T(8,128)(2,1)S(1)} %collective-permute-done.11.refs_2_) | copy-start | bytes 884740
  12.4 65.9 %collective-permute-start.7 = (bf16[768,768]{1,0:T(8,128)(2,1)}, bf16[768,768]{1,0:T(8,128)(2,1)}, u32[]{:S(2)}, u32[]{:S(2)}) collective-permute-start(bf16[768,768]{1,0:T(8,128)(2,1)} %g0.1), channel_id=1, source_target_pairs={{0,1},{1,0},{2,3},{3,2},{4,5},{5,4},{6,7},{7,6},{8,9},{9,8},{10,11... | collective-permute-start | bytes 3538952 | tf_op jit(solution)/shard_map/ppermute | solution.py:35
  30.0 48.3 %collective-permute-start.9 = (bf16[768,768]{1,0:T(8,128)(2,1)}, bf16[768,768]{1,0:T(8,128)(2,1)}, u32[]{:S(2)}, u32[]{:S(2)}) collective-permute-start(bf16[768,768]{1,0:T(8,128)(2,1)} %collective-permute-done.8.g2), channel_id=1, source_target_pairs={{0,1},{1,0},{2,3},{3,2},{4,5},{5,4},{6,7},{7,6},{8,9},{9,8},{10,11... | collective-permute-start | bytes 3538952 | tf_op jit(solution)/shard_map/ppermute | solution.py:35
  30.0 37.0 %copy-start.5 = (bf16[384,384]{1,0:T(8,128)(2,1)}, bf16[384,384]{1,0:T(8,128)(2,1)S(1)}, u32[]{:S(2)}) copy-start(bf16[384,384]{1,0:T(8,128)(2,1)S(1)} %collective-permute-done.10.refs_1_) | copy-start | bytes 884740
  30.0 17.0 %collective-permute-start.13 = (bf16[384,384]{1,0:T(8,128)(2,1)}, bf16[384,384]{1,0:T(8,128)(2,1)S(1)}, u32[]{:S(2)}, u32[]{:S(2)}) collective-permute-start(bf16[384,384]{1,0:T(8,128)(2,1)} %refs_0_.1), channel_id=1, source_target_pairs={{0,16},{1,17},{2,18},{3,19},{4,20},{5,21},{6,22},{7,23},{8,24},{9,... | collective-permute-start | bytes 884744 | tf_op jit(solution)/shard_map/ppermute | solution.py:35
  47.0 20.1 %copy-start.7 = (bf16[384,384]{1,0:T(8,128)(2,1)}, bf16[384,384]{1,0:T(8,128)(2,1)S(1)}, u32[]{:S(2)}) copy-start(bf16[384,384]{1,0:T(8,128)(2,1)S(1)} %collective-permute-done.13.refs_4_) | copy-start | bytes 884740
  47.0 16.0 %collective-permute-start.15 = (bf16[384,384]{1,0:T(8,128)(2,1)S(1)}, bf16[384,384]{1,0:T(8,128)(2,1)S(1)}, u32[]{:S(2)}, u32[]{:S(2)}) collective-permute-start(bf16[384,384]{1,0:T(8,128)(2,1)S(1)} %collective-permute-done.11.refs_2_), channel_id=1, source_target_pairs={{0,16},{1,17},{2,18},{3,19},{4,20},{5,21},{6,22},{7,23},{8,24},{9,... | collective-permute-start | bytes 884744 | tf_op jit(solution)/shard_map/ppermute | solution.py:35
  47.0 17.4 %collective-permute-start.12 = (bf16[384,384]{1,0:T(8,128)(2,1)S(1)}, bf16[384,384]{1,0:T(8,128)(2,1)S(1)}, u32[]{:S(2)}, u32[]{:S(2)}) collective-permute-start(bf16[384,384]{1,0:T(8,128)(2,1)S(1)} %collective-permute-done.10.refs_1_), channel_id=1, source_target_pairs={{0,8},{1,9},{2,10},{3,11},{4,12},{5,13},{6,14},{7,15},{8,0},{9,1},... | collective-permute-start | bytes 884744 | tf_op jit(solution)/shard_map/ppermute | solution.py:35
  51.1 37.0 %collective-permute-start = (bf16[768,384]{1,0:T(8,128)(2,1)}, bf16[768,384]{1,0:T(8,128)(2,1)S(1)}, u32[]{:S(2)}, u32[]{:S(2)}) collective-permute-start(bf16[768,384]{1,0:T(8,128)(2,1)} %qa.9), channel_id=1, source_target_pairs={{1,4},{3,6},{4,1},{6,3},{9,12},{11,14},{12,9},{14,11},{17,20},{19,... | collective-permute-start | bytes 1769480 | tf_op jit(solution)/shard_map/ppermute | solution.py:35
  63.0 4.1 %copy-start.9 = (bf16[384,384]{1,0:T(8,128)(2,1)}, bf16[384,384]{1,0:T(8,128)(2,1)S(1)}, u32[]{:S(2)}) copy-start(bf16[384,384]{1,0:T(8,128)(2,1)S(1)} %collective-permute-done.15.refs_6_) | copy-start | bytes 884740
  63.0 9.9 %collective-permute-start.14 = (bf16[384,384]{1,0:T(8,128)(2,1)S(1)}, bf16[384,384]{1,0:T(8,128)(2,1)S(1)}, u32[]{:S(2)}, u32[]{:S(2)}) collective-permute-start(bf16[384,384]{1,0:T(8,128)(2,1)S(1)} %collective-permute-done.13.refs_4_), channel_id=1, source_target_pairs={{0,4},{1,5},{2,6},{3,7},{4,0},{5,1},{6,2},{7,3},{8,12},{9,13},{10,... | collective-permute-start | bytes 884744 | tf_op jit(solution)/shard_map/ppermute | solution.py:35
  64.4 0.7 copy-start.11
  65.1 12.0 %collective-permute-start.16 = (bf16[384,384]{1,0:T(8,128)(2,1)S(1)}, bf16[384,384]{1,0:T(8,128)(2,1)S(1)}, u32[]{:S(2)}, u32[]{:S(2)}) collective-permute-start(bf16[384,384]{1,0:T(8,128)(2,1)S(1)} %collective-permute-done.15.refs_6_), channel_id=1, source_target_pairs={{0,4},{1,5},{2,6},{3,7},{4,0},{5,1},{6,2},{7,3},{8,12},{9,13},{10,... | collective-permute-start | bytes 884744 | tf_op jit(solution)/shard_map/ppermute | solution.py:35
  66.9 12.3 %copy-start.1 = (bf16[768,768]{1,0:T(8,128)(2,1)S(1)}, bf16[768,768]{1,0:T(8,128)(2,1)}, u32[]{:S(2)}) copy-start(bf16[768,768]{1,0:T(8,128)(2,1)} %g0.1) | copy-start | bytes 3538948
  67.0 12.3 %copy-start.2 = (bf16[384,384]{1,0:T(8,128)(2,1)S(1)}, bf16[384,384]{1,0:T(8,128)(2,1)}, u32[]{:S(2)}) copy-start(bf16[384,384]{1,0:T(8,128)(2,1)} %refs_0_.1) | copy-start | bytes 884740
  67.0 12.3 %copy-start.12 = (bf16[384,384]{1,0:T(8,128)(2,1)S(1)}, bf16[384,384]{1,0:T(8,128)(2,1)}, u32[]{:S(2)}) copy-start(bf16[384,384]{1,0:T(8,128)(2,1)} %copy-done.11) | copy-start | bytes 884740
  67.1 22.2 %copy-start = (bf16[768,384]{1,0:T(8,128)(2,1)S(1)}, bf16[768,384]{1,0:T(8,128)(2,1)}, u32[]{:S(2)}) copy-start(bf16[768,384]{1,0:T(8,128)(2,1)} %qa.9) | copy-start | bytes 1769476
  72.9 16.4 %collective-permute-start.2 = (bf16[768,384]{1,0:T(8,128)(2,1)S(1)}, bf16[768,384]{1,0:T(8,128)(2,1)}, u32[]{:S(2)}, u32[]{:S(2)}) collective-permute-start(bf16[768,384]{1,0:T(8,128)(2,1)S(1)} %broadcast_select_fusion.1.refs_0_.ko), channel_id=1, source_target_pairs={{0,1},{1,0},{2,3},{3,2},{4,5},{5,4},{6,7},{7,6},{8,9},{9,8},{10,11... | collective-permute-start | bytes 1769480 | tf_op jit(solution)/shard_map/ppermute | solution.py:35
  77.1 19.8 %collective-permute-start.5 = (bf16[768,384]{1,0:T(8,128)(2,1)S(1)}, bf16[768,384]{1,0:T(8,128)(2,1)S(1)}, u32[]{:S(2)}, u32[]{:S(2)}) collective-permute-start(bf16[768,384]{1,0:T(8,128)(2,1)S(1)} %broadcast_select_fusion.1.refs_0_.ko), channel_id=1, source_target_pairs={{0,2},{1,8},{2,0},{3,10},{4,6},{5,12},{6,4},{7,14},{8,1},{9,16},{1... | collective-permute-start | bytes 1769480 | tf_op jit(solution)/shard_map/ppermute | solution.py:35
  78.3 11.0 %collective-permute-start.4 = (bf16[768,384]{1,0:T(8,128)(2,1)S(1)}, bf16[768,384]{1,0:T(8,128)(2,1)}, u32[]{:S(2)}, u32[]{:S(2)}) collective-permute-start(bf16[768,384]{1,0:T(8,128)(2,1)S(1)} %broadcast_select_fusion.refs_2_.vo), channel_id=1, source_target_pairs={{0,1},{1,0},{2,3},{3,2},{4,5},{5,4},{6,7},{7,6},{8,9},{9,8},{10,11... | collective-permute-start | bytes 1769480 | tf_op jit(solution)/shard_map/ppermute | solution.py:35
  78.3 18.6 %collective-permute-start.6 = (bf16[768,384]{1,0:T(8,128)(2,1)S(1)}, bf16[768,384]{1,0:T(8,128)(2,1)S(1)}, u32[]{:S(2)}, u32[]{:S(2)}) collective-permute-start(bf16[768,384]{1,0:T(8,128)(2,1)S(1)} %broadcast_select_fusion.refs_2_.vo), channel_id=1, source_target_pairs={{0,2},{1,8},{2,0},{3,10},{4,6},{5,12},{6,4},{7,14},{8,1},{9,16},{1... | collective-permute-start | bytes 1769480 | tf_op jit(solution)/shard_map/ppermute | solution.py:35
  79.2 1.0 copy-start.4
  80.2 1.0 copy-start.6
  81.2 1.0 copy-start.8
  82.1 1.0 copy-start.10
  88.1 13.4 %collective-permute-start.17 = (bf16[384,768]{1,0:T(8,128)(2,1)}, bf16[384,768]{1,0:T(8,128)(2,1)}, u32[]{:S(2)}, u32[]{:S(2)}) collective-permute-start(bf16[384,768]{1,0:T(8,128)(2,1)} %project.1.ga), channel_id=1, source_target_pairs={{0,2},{1,4},{2,0},{3,6},{4,1},{5,7},{6,3},{7,5},{8,10},{9,12},{10,... | collective-permute-start | bytes 1769480 | tf_op jit(solution)/shard_map/ppermute | solution.py:35
  106.2 20.1 %collective-permute-start.21 = (bf16[768,256]{1,0:T(8,128)(2,1)S(1)}, bf16[768,256]{1,0:T(8,128)(2,1)S(1)}, u32[]{:S(2)}, u32[]{:S(2)}) collective-permute-start(bf16[768,256]{1,0:T(8,128)(2,1)S(1)} %get-tuple-element.31), channel_id=1, source_target_pairs={{0,1},{1,0},{2,3},{3,2},{4,5},{5,4},{6,7},{7,6},{8,9},{9,8},{10,11... | collective-permute-start | bytes 1179656 | tf_op jit(solution)/shard_map/ppermute | solution.py:35
  106.4 20.6 %collective-permute-start.22 = (bf16[768,256]{1,0:T(8,128)(2,1)S(1)}, bf16[768,256]{1,0:T(8,128)(2,1)S(1)}, u32[]{:S(2)}, u32[]{:S(2)}) collective-permute-start(bf16[768,256]{1,0:T(8,128)(2,1)S(1)} %get-tuple-element.32), channel_id=1, source_target_pairs={{0,2},{1,8},{2,0},{3,10},{4,6},{5,12},{6,4},{7,14},{8,1},{9,16},{1... | collective-permute-start | bytes 1179656 | tf_op jit(solution)/shard_map/ppermute | solution.py:35
  107.9 12.2 %collective-permute-start.18 = (bf16[768,128]{1,0:T(8,128)(2,1)S(1)}, bf16[768,128]{1,0:T(8,128)(2,1)S(1)}, u32[]{:S(2)}, u32[]{:S(2)}) collective-permute-start(bf16[768,128]{1,0:T(8,128)(2,1)S(1)} %get-tuple-element.27), channel_id=1, source_target_pairs={{0,8},{1,4},{2,10},{3,6},{4,1},{5,13},{6,3},{7,15},{8,0},{9,12},{1... | collective-permute-start | bytes 589832 | tf_op jit(solution)/shard_map/ppermute | solution.py:35
  113.2 7.2 %collective-permute-start.19 = (bf16[768,128]{1,0:T(8,128)(2,1)S(1)}, bf16[768,128]{1,0:T(8,128)(2,1)S(1)}, u32[]{:S(2)}, u32[]{:S(2)}) collective-permute-start(bf16[768,128]{1,0:T(8,128)(2,1)S(1)} %get-tuple-element.28), channel_id=1, source_target_pairs={{0,8},{1,4},{2,10},{3,6},{4,1},{5,13},{6,3},{7,15},{8,0},{9,12},{1... | collective-permute-start | bytes 589832 | tf_op jit(solution)/shard_map/ppermute | solution.py:35
  119.6 5.7 %collective-permute-start.20 = (bf16[768,128]{1,0:T(8,128)(2,1)S(1)}, bf16[768,128]{1,0:T(8,128)(2,1)S(1)}, u32[]{:S(2)}, u32[]{:S(2)}) collective-permute-start(bf16[768,128]{1,0:T(8,128)(2,1)S(1)} %get-tuple-element.29), channel_id=1, source_target_pairs={{0,8},{1,4},{2,10},{3,6},{4,1},{5,13},{6,3},{7,15},{8,0},{9,12},{1... | collective-permute-start | bytes 589832 | tf_op jit(solution)/shard_map/ppermute | solution.py:35
  120.1 8.4 %collective-permute-start.23 = (bf16[768,256]{1,0:T(8,128)(2,1)S(1)}, bf16[768,256]{1,0:T(8,128)(2,1)S(1)}, u32[]{:S(2)}, u32[]{:S(2)}) collective-permute-start(bf16[768,256]{1,0:T(8,128)(2,1)S(1)} %get-tuple-element.34), channel_id=1, source_target_pairs={{0,1},{1,0},{2,3},{3,2},{4,5},{5,4},{6,7},{7,6},{8,9},{9,8},{10,11... | collective-permute-start | bytes 1179656 | tf_op jit(solution)/shard_map/ppermute | solution.py:35
  120.5 8.1 %collective-permute-start.24 = (bf16[768,256]{1,0:T(8,128)(2,1)S(1)}, bf16[768,256]{1,0:T(8,128)(2,1)S(1)}, u32[]{:S(2)}, u32[]{:S(2)}) collective-permute-start(bf16[768,256]{1,0:T(8,128)(2,1)S(1)} %get-tuple-element.35), channel_id=1, source_target_pairs={{0,2},{1,8},{2,0},{3,10},{4,6},{5,12},{6,4},{7,14},{8,1},{9,16},{1... | collective-permute-start | bytes 1179656 | tf_op jit(solution)/shard_map/ppermute | solution.py:35
  125.3 4.2 %collective-permute-start.25 = (bf16[768,256]{1,0:T(8,128)(2,1)S(1)}, bf16[768,256]{1,0:T(8,128)(2,1)S(1)}, u32[]{:S(2)}, u32[]{:S(2)}) collective-permute-start(bf16[768,256]{1,0:T(8,128)(2,1)S(1)} %get-tuple-element.37), channel_id=1, source_target_pairs={{0,1},{1,0},{2,3},{3,2},{4,5},{5,4},{6,7},{7,6},{8,9},{9,8},{10,11... | collective-permute-start | bytes 1179656 | tf_op jit(solution)/shard_map/ppermute | solution.py:35
  126.3 7.8 %collective-permute-start.26 = (bf16[768,256]{1,0:T(8,128)(2,1)S(1)}, bf16[768,256]{1,0:T(8,128)(2,1)S(1)}, u32[]{:S(2)}, u32[]{:S(2)}) collective-permute-start(bf16[768,256]{1,0:T(8,128)(2,1)S(1)} %get-tuple-element.38), channel_id=1, source_target_pairs={{0,2},{1,8},{2,0},{3,10},{4,6},{5,12},{6,4},{7,14},{8,1},{9,16},{1... | collective-permute-start | bytes 1179656 | tf_op jit(solution)/shard_map/ppermute | solution.py:35
  127.2 11.1 %collective-permute-start.27 = (bf16[768,256]{1,0:T(8,128)(2,1)S(1)}, bf16[768,256]{1,0:T(8,128)(2,1)S(1)}, u32[]{:S(2)}, u32[]{:S(2)}) collective-permute-start(bf16[768,256]{1,0:T(8,128)(2,1)S(1)} %add_convert_fusion.2), channel_id=1, source_target_pairs={{0,2},{1,4},{2,0},{3,6},{4,1},{5,7},{6,3},{7,5},{8,10},{9,12},{10,... | collective-permute-start | bytes 1179656 | tf_op jit(solution)/shard_map/ppermute | solution.py:35
  128.7 13.8 %collective-permute-start.28 = (bf16[768,256]{1,0:T(8,128)(2,1)S(1)}, bf16[768,256]{1,0:T(8,128)(2,1)S(1)}, u32[]{:S(2)}, u32[]{:S(2)}) collective-permute-start(bf16[768,256]{1,0:T(8,128)(2,1)S(1)} %add_convert_fusion.1), channel_id=1, source_target_pairs={{0,2},{1,4},{2,0},{3,6},{4,1},{5,7},{6,3},{7,5},{8,10},{9,12},{10,... | collective-permute-start | bytes 1179656 | tf_op jit(solution)/shard_map/ppermute | solution.py:35
  134.3 12.5 %collective-permute-start.29 = (bf16[768,256]{1,0:T(8,128)(2,1)S(1)}, bf16[768,256]{1,0:T(8,128)(2,1)S(1)}, u32[]{:S(2)}, u32[]{:S(2)}) collective-permute-start(bf16[768,256]{1,0:T(8,128)(2,1)S(1)} %add_convert_fusion), channel_id=1, source_target_pairs={{0,2},{1,4},{2,0},{3,6},{4,1},{5,7},{6,3},{7,5},{8,10},{9,12},{10,... | collective-permute-start | bytes 1179656 | tf_op jit(solution)/shard_map/ppermute | solution.py:35

commit v6 on v5

--- a/solution.py
+++ b/solution.py
@@ -112,78 +112,111 @@
     )(flags, *queries, *keys, *values)
 
 
-def backward_kernel(flag_ref, en, on, sn, ef, of, sf, ga, gb, qa, qb, ks, vs, ko, vo, kz, vz, *refs):
-    dq, own, side, away = refs
+def slab_terms(weight, part_grad, part_inner, query, k, v, out):
+    scale = 1.0 / math.sqrt(HD)
+    slope = dot(v, part_grad)
+    delta = (weight.astype(jnp.float32) * (slope - part_inner)).astype(jnp.bfloat16)
+    out[:, HD:] = dot(weight, part_grad, NT).astype(out.dtype)
+    out[:, :HD] = (dot(delta, query) * scale).astype(out.dtype)
+    return dot(k, delta, TN)
+
+
+def far_kernel(heads, flag_ref, on, sn, ef, of, sf, ga, gb, qa, qb, kz, vz, *refs):
+    grad_ref, inner_ref, dq = refs[:3]
+    stays = flag_ref[1] > 0
+    for head in range(heads):
+        part = slice(head * HD, (head + 1) * HD)
+        line = slice(head * 8, head * 8 + 1)
+        mass = slice(head * 8 + 1, head * 8 + 2)
+        query = jnp.where(stays, qa[:, part], qb[:, part])
+        grad = jnp.where(stays, ga[part, :], gb[part, :]).astype(jnp.float32)
+        near_top = sn[line, :]
+        far_top = jnp.where(flag_ref[0] > 0, sf[line, :], -jnp.inf)
+        top = jnp.maximum(near_top, far_top)
+        near_share, far_share = jnp.exp2(near_top - top), jnp.exp2(far_top - top)
+        inverse = 1.0 / (near_share * sn[mass, :] + far_share * sf[mass, :])
+        near_share, far_share = near_share * inverse, far_share * inverse
+        near_grad = (grad * near_share).astype(jnp.bfloat16)
+        far_grad = (grad * far_share).astype(jnp.bfloat16)
+        inner = jnp.sum(
+            on[part, :] * near_grad.astype(jnp.float32)
+            + of[part, :] * far_grad.astype(jnp.float32),
+            axis=0,
+            keepdims=True,
+        )
+        grad_ref[part, :] = near_grad
+        inner_ref[line, :] = inner * near_share
+        dq[part, :] = slab_terms(
+            ef[head],
+            far_grad,
+            inner * far_share,
+            query,
+            kz[:, part],
+            vz[:, part],
+            refs[3 + head],
+        )
+
+
+def backward_far(flags, near, away, grads, queries, far):
+    rows, width = queries[0].shape
+    heads = width // HD
+    vmem = pl.BlockSpec(memory_space=pltpu.VMEM)
+    operands = (*near[1:], *away, *grads, *queries, *far)
+    return pl.pallas_call(
+        functools.partial(far_kernel, heads),
+        in_specs=[pl.BlockSpec(memory_space=pltpu.SMEM)] + [vmem] * len(operands),
+        out_specs=[vmem] * (3 + heads),
+        out_shape=[
+            jax.ShapeDtypeStruct((width, rows), jnp.bfloat16),
+            jax.ShapeDtypeStruct((heads * 8, rows), jnp.float32),
+            jax.ShapeDtypeStruct((width, rows), jnp.float32),
+        ]
+        + [jax.ShapeDtypeStruct((rows, 2 * HD), jnp.bfloat16)] * heads,
+        compiler_params=pltpu.CompilerParams(vmem_limit_bytes=LIMIT),
+        name="backward_far",
+    )(flags, *operands)
+
+
+def near_kernel(flag_ref, en, grad, inner, dq_far, qa, qb, ks, vs, ko, vo, dq, own, side):
     rows = qa.shape[0]
-    scale = 1.0 / math.sqrt(HD)
-    stays = flag_ref[1] > 0
-    query = jnp.where(stays, qa[...], qb[...])
-    grad = jnp.where(stays, ga[...], gb[...]).astype(jnp.float32)
-    near_top = sn[0:1, :]
-    far_top = jnp.where(flag_ref[0] > 0, sf[0:1, :], -jnp.inf)
-    top = jnp.maximum(near_top, far_top)
-    near_share, far_share = jnp.exp2(near_top - top), jnp.exp2(far_top - top)
-    inverse = 1.0 / (near_share * sn[1:2, :] + far_share * sf[1:2, :])
-    near_share, far_share = near_share * inverse, far_share * inverse
-    near_grad = (grad * near_share).astype(jnp.bfloat16)
-    far_grad = (grad * far_share).astype(jnp.bfloat16)
-    inner = jnp.sum(
-        on[...] * near_grad.astype(jnp.float32) + of[...] * far_grad.astype(jnp.float32),
-        axis=0,
-        keepdims=True,
-    )
-    near_inner, far_inner = inner * near_share, inner * far_share
-    total = None
-    for weights, base, k, v, out, part_grad, part_inner in (
-        (ef, 0, kz, vz, away, far_grad, far_inner),
-        (en, rows, ks, vs, side, near_grad, near_inner),
-        (en, 0, ko, vo, own, near_grad, near_inner),
-    ):
-        weight = weights[0, base : base + rows, :]
-        slope = dot(v[...], part_grad)
-        delta = (weight.astype(jnp.float32) * (slope - part_inner)).astype(jnp.bfloat16)
-        out[:, HD:] = dot(weight, part_grad, NT).astype(out.dtype)
-        out[:, :HD] = (dot(delta, query) * scale).astype(out.dtype)
-        part = dot(k[...], delta, TN)
-        total = part if total is None else total + part
-    dq[...] = (total * scale).T.astype(dq.dtype)
-
-
-def backward(head, flags, near, away, grads, queries, side, own, far):
+    query = jnp.where(flag_ref[1] > 0, qa[...], qb[...])
+    total = dq_far[...]
+    for base, k, v, out in ((rows, ks, vs, side), (0, ko, vo, own)):
+        weight = en[0, base : base + rows, :]
+        total = total + slab_terms(
+            weight, grad[...], inner[0:1, :], query, k[...], v[...], out
+        )
+    dq[...] = (total * (1.0 / math.sqrt(HD))).T.astype(dq.dtype)
+
+
+def backward_near(head, flags, weights, grad, inner, dq_far, queries, side, own):
     rows, _ = queries[0].shape
     spec = pl.BlockSpec((rows, HD), lambda i: (0, head))
     flip = pl.BlockSpec((HD, rows), lambda i: (head, 0))
     stat = pl.BlockSpec((8, rows), lambda i: (head, 0))
 
-    def weight_spec(e):
-        return pl.BlockSpec((1,) + e.shape[1:], lambda i: (head, 0, 0))
-
     def whole(columns):
         return pl.BlockSpec((rows, columns), lambda i: (0, 0))
 
     return pl.pallas_call(
-        backward_kernel,
+        near_kernel,
         grid=(1,),
         in_specs=[
             pl.BlockSpec(memory_space=pltpu.SMEM),
-            weight_spec(near[0]),
+            pl.BlockSpec((1,) + weights.shape[1:], lambda i: (head, 0, 0)),
             flip,
             stat,
-            weight_spec(away[0]),
             flip,
-            stat,
         ]
-        + [flip] * 2
-        + [spec] * 8,
-        out_specs=[whole(HD)] + [whole(2 * HD)] * 3,
+        + [spec] * 6,
+        out_specs=[whole(HD), whole(2 * HD), whole(2 * HD)],
         out_shape=[
             jax.ShapeDtypeStruct((rows, HD), jnp.bfloat16),
             jax.ShapeDtypeStruct((rows, 2 * HD), jnp.float32),
             jax.ShapeDtypeStruct((rows, 2 * HD), jnp.bfloat16),
-            jax.ShapeDtypeStruct((rows, 2 * HD), jnp.bfloat16),
         ],
         compiler_params=pltpu.CompilerParams(vmem_limit_bytes=LIMIT),
-    )(flags, *near, *away, *grads, *queries, *side, *own, *far)
+    )(flags, weights, grad, inner, dq_far, *queries, *side, *own)
 
 
 def project_kernel(place_ref, g0, g1, g2, g3, *refs):
@@ -280,19 +313,23 @@
     away = soften(flags, query_pair, (far_k,), (far_v,))
 
     done = []
+    grad, inner, dq_far, *away_terms = backward_far(
+        flags, near, away, grad_pair, query_pair, (far_k, far_v)
+    )
+    far_terms = [send(f, far_route) for f in away_terms]
     for head in range(width // HD):
-        dq, own, side, far = backward(
+        dq, own, side = backward_near(
             head,
             flags,
-            near,
-            away,
-            grad_pair,
+            near[0],
+            grad,
+            inner,
+            dq_far,
             query_pair,
             (side_k, side_v),
             (keys, values),
-            (far_k, far_v),
-        )
-        far = send(far, far_route)
+        )
+        far = far_terms[head]
         side = send(side, side_route)
         own = (own + side.astype(jnp.float32) + far.astype(jnp.float32)).astype(jnp.bfloat16)
         done.append(((dq, send(dq, spare_route)), (own, send(own, busy_route))))

time: 149 us -> 140 us (0.940)
  waiting for transfers between devices: 76.3 us -> 64.9 us
    ppermute x30, waiting for transfers between devices: 76.3 us -> 64.9 us  [exchange(): return lax.ppermute(block, AXES, pairs)]
    unnamed x28 -> x32, local copies, waits for them, and re-layouts: 4.6 us -> 5.42 us
    pallas_call x3 -> x4, Pallas kernels: 14.3 us -> 14 us  [the longest x3 8.78 us: backward_near(): pl.pallas_call(near_kernel, grid=(1,), in_specs=[pl.BlockSpec(memory_spac...]
  transfers between devices with their start and end apart: 30 -> 30, of which waited for: 11 -> 12; matrix products, arithmetic and copies ran while one was open for 2% -> 2% of each run, Pallas kernels for 18% -> 19%
where the time goes in v6:
time: 140 us; the launch traced here: 138 us
  waiting for transfers between devices  64.9 us (46%)
  starting transfers between devices  31.1 us (22%)
  Pallas kernels  31.1 us (22%)
  local copies, waits for them, and re-layouts  5.58 us (4%)
  other arithmetic  4.28 us (3%)
    ppermute x30, waiting for transfers between devices, exchange(): return lax.ppermute(block, AXES, pairs)  64.9 us
    ppermute x30, starting transfers between devices, exchange(): return lax.ppermute(block, AXES, pairs)  31.1 us
    pallas_call x2, Pallas kernels, soften(): pl.pallas_call(functools.partial(soften_kernel, parts, tile), grid=(heads...  12.1 us
    pallas_call x3, Pallas kernels, backward_near(): pl.pallas_call(near_kernel, grid=(1,), in_specs=[pl.BlockSpec(memory_spac...  8.78 us
    unnamed x32, local copies, waits for them, and re-layouts  5.42 us
    pallas_call x1, Pallas kernels, backward_far(): pl.pallas_call(functools.partial(far_kernel, heads), in_specs=[pl.BlockSp...  5.22 us
    pallas_call x1, Pallas kernels, project(): pl.pallas_call(project_kernel, in_specs=[pl.BlockSpec(memory_space=pltpu....  4.99 us
  transfers between devices with their start and end apart: 30, of which 12 were waited for; matrix products, arithmetic and copies ran while one was open for 2% of the time, Pallas kernels for 19%

profile of v6, /device:TPU:0, one launch (start us, length us, event | category | flops | bytes accessed | tf_op | source)
XLA Modules:
  0.0 137.9 jit_solution(14602804148838514407)
XLA Ops:
  0.6 3.0 %collective-permute-start.8 = (bf16[768,768]{1,0:T(8,128)(2,1)}, bf16[768,768]{1,0:T(8,128)(2,1)}, u32[]{:S(2)}, u32[]{:S(2)}) collective-permute-start(bf16[768,768]{1,0:T(8,128)(2,1)} %g0.1), channel_id=1, source_target_pairs={{0,2},{1,3},{2,0},{3,1},{4,6},{5,7},{6,4},{7,5},{8,10},{9,11},{10,... | collective-permute-start | bytes 3538952 | tf_op jit(solution)/shard_map/ppermute | solution.py:35
  3.7 1.6 %collective-permute-start.11 = (bf16[384,384]{1,0:T(8,128)(2,1)}, bf16[384,384]{1,0:T(8,128)(2,1)S(1)}, u32[]{:S(2)}, u32[]{:S(2)}) collective-permute-start(bf16[384,384]{1,0:T(8,128)(2,1)} %refs_0_.1), channel_id=1, source_target_pairs={{0,8},{1,9},{2,10},{3,11},{4,12},{5,13},{6,14},{7,15},{8,0},{9,1},... | collective-permute-start | bytes 884744 | tf_op jit(solution)/shard_map/ppermute | solution.py:35
  5.2 1.5 %collective-permute-start.10 = (bf16[384,384]{1,0:T(8,128)(2,1)}, bf16[384,384]{1,0:T(8,128)(2,1)S(1)}, u32[]{:S(2)}, u32[]{:S(2)}) collective-permute-start(bf16[384,384]{1,0:T(8,128)(2,1)} %refs_0_.1), channel_id=1, source_target_pairs={{0,4},{1,5},{2,6},{3,7},{4,0},{5,1},{6,2},{7,3},{8,12},{9,13},{10,... | collective-permute-start | bytes 884744 | tf_op jit(solution)/shard_map/ppermute | solution.py:35
  6.8 2.6 %collective-permute-start.13 = (bf16[384,384]{1,0:T(8,128)(2,1)}, bf16[384,384]{1,0:T(8,128)(2,1)S(1)}, u32[]{:S(2)}, u32[]{:S(2)}) collective-permute-start(bf16[384,384]{1,0:T(8,128)(2,1)} %refs_0_.1), channel_id=1, source_target_pairs={{0,16},{1,17},{2,18},{3,19},{4,20},{5,21},{6,22},{7,23},{8,24},{9,... | collective-permute-start | bytes 884744 | tf_op jit(solution)/shard_map/ppermute | solution.py:35
  9.4 7.9 %collective-permute-done.11.refs_2_ = bf16[384,384]{1,0:T(8,128)(2,1)S(1)} collective-permute-done((bf16[384,384]{1,0:T(8,128)(2,1)}, bf16[384,384]{1,0:T(8,128)(2,1)S(1)}, u32[]{:S(2)}, u32[]{:S(2)}) %collective-permute-start.11) | collective-permute-done | bytes 294944 | tf_op jit(solution)/shard_map/ppermute | solution.py:35
  17.3 0.7 collective-permute-start.15
  18.0 0.7 copy-done.3
  18.7 11.3 %collective-permute-done.8.g2 = bf16[768,768]{1,0:T(8,128)(2,1)} collective-permute-done((bf16[768,768]{1,0:T(8,128)(2,1)}, bf16[768,768]{1,0:T(8,128)(2,1)}, u32[]{:S(2)}, u32[]{:S(2)}) %collective-permute-start.8) | collective-permute-done | bytes 1179680 | tf_op jit(solution)/shard_map/ppermute | solution.py:35
  30.0 0.7 collective-permute-start.1
  30.7 0.7 collective-permute-start.3
  31.4 3.4 %collective-permute-done.15.refs_6_ = bf16[384,384]{1,0:T(8,128)(2,1)S(1)} collective-permute-done((bf16[384,384]{1,0:T(8,128)(2,1)S(1)}, bf16[384,384]{1,0:T(8,128)(2,1)S(1)}, u32[]{:S(2)}, u32[]{:S(2)}) %collective-permute-start.15) | collective-permute-done | bytes 294944 | tf_op jit(solution)/shard_map/ppermute | solution.py:35
  34.8 9.4 %collective-permute-done.12.refs_3_ = bf16[384,384]{1,0:T(8,128)(2,1)S(1)} collective-permute-done((bf16[384,384]{1,0:T(8,128)(2,1)S(1)}, bf16[384,384]{1,0:T(8,128)(2,1)S(1)}, u32[]{:S(2)}, u32[]{:S(2)}) %collective-permute-start.12) | collective-permute-done | bytes 294944 | tf_op jit(solution)/shard_map/ppermute | solution.py:35
  44.2 0.7 collective-permute-start
  45.0 3.1 %collective-permute-start.14 = (bf16[384,384]{1,0:T(8,128)(2,1)S(1)}, bf16[384,384]{1,0:T(8,128)(2,1)S(1)}, u32[]{:S(2)}, u32[]{:S(2)}) collective-permute-start(bf16[384,384]{1,0:T(8,128)(2,1)S(1)} %collective-permute-done.13.refs_4_), channel_id=1, source_target_pairs={{0,4},{1,5},{2,6},{3,7},{4,0},{5,1},{6,2},{7,3},{8,12},{9,13},{10,... | collective-permute-start | bytes 884744 | tf_op jit(solution)/shard_map/ppermute | solution.py:35
  48.2 0.8 copy-done.14
  49.0 1.3 collective-permute-start.16
  50.3 1.2 broadcast_select_fusion.1.refs_0_.ko
  51.7 13.2 %collective-permute-done.14.refs_5_ = bf16[384,384]{1,0:T(8,128)(2,1)S(1)} collective-permute-done((bf16[384,384]{1,0:T(8,128)(2,1)S(1)}, bf16[384,384]{1,0:T(8,128)(2,1)S(1)}, u32[]{:S(2)}, u32[]{:S(2)}) %collective-permute-start.14) | collective-permute-done | bytes 294944 | tf_op jit(solution)/shard_map/ppermute | solution.py:35
  64.9 1.2 collective-permute-start.5
  66.1 2.0 %collective-permute-done.16.refs_7_ = bf16[384,384]{1,0:T(8,128)(2,1)S(1)} collective-permute-done((bf16[384,384]{1,0:T(8,128)(2,1)S(1)}, bf16[384,384]{1,0:T(8,128)(2,1)S(1)}, u32[]{:S(2)}, u32[]{:S(2)}) %collective-permute-start.16) | collective-permute-done | bytes 294944 | tf_op jit(solution)/shard_map/ppermute | solution.py:35
  68.1 1.2 collective-permute-start.6
  69.3 1.0 copy-done.6
  70.3 1.0 copy-done.8
  71.2 1.0 copy-done.10
  72.2 1.0 copy-done.12
  73.2 5.0 %project.1.ga = bf16[384,768]{1,0:T(8,128)(2,1)} custom-call(s32[3]{0:T(128)S(1)} %pad_add_fusion.place_ref, bf16[768,768]{1,0:T(8,128)(2,1)S(1)} %copy-done.1, bf16[768,768]{1,0:T(8,128)(2,1)} %collective-permute-done.7.g1, bf16[768,768]{1,0:T(8,128)(2,1)} %collective-permute-done.8.g2, bf16[768,768]{1,0:T(8,128)(2,1)} %collective-permute-done.9.g3, ...), custom_call_target="tpu_custom_call" | custom-call | tf_op jit(solution)/shard_map/project/pallas_call | solution.py:241
  78.2 1.5 %collective-permute-start.17 = (bf16[384,768]{1,0:T(8,128)(2,1)}, bf16[384,768]{1,0:T(8,128)(2,1)}, u32[]{:S(2)}, u32[]{:S(2)}) collective-permute-start(bf16[384,768]{1,0:T(8,128)(2,1)} %project.1.ga), channel_id=1, source_target_pairs={{0,2},{1,4},{2,0},{3,6},{4,1},{5,7},{6,3},{7,5},{8,10},{9,12},{10,... | collective-permute-start | bytes 1769480 | tf_op jit(solution)/shard_map/ppermute | solution.py:35
  79.7 1.5 %collective-permute-done.6.refs_1_.vz = bf16[768,384]{1,0:T(8,128)(2,1)} collective-permute-done((bf16[768,384]{1,0:T(8,128)(2,1)S(1)}, bf16[768,384]{1,0:T(8,128)(2,1)}, u32[]{:S(2)}, u32[]{:S(2)}) %collective-permute-start.6) | collective-permute-done | bytes 589856 | tf_op jit(solution)/shard_map/ppermute | solution.py:35
  81.3 4.6 %shard_map.77 = (bf16[3,768,768]{2,1,0:T(8,128)(2,1)S(1)}, f32[384,768]{1,0:T(8,128)S(1)}, f32[24,768]{1,0:T(8,128)S(1)}) custom-call(s32[2]{0:T(128)S(1)} %add_convert_fusion.3.flag_ref, bf16[768,384]{1,0:T(8,128)(2,1)S(1)} %copy-done, bf16[768,384]{1,0:T(8,128)(2,1)S(1)} %collective-permute-done.qb, bf16[768,384]{1,0:T(8,128)(2,1)} %collective-permute-done.5.refs_0_.kz, ...), custom_call_target="tpu_custom_call" | custom-call | tf_op jit(solution)/shard_map/pallas_call | solution.py:95
  85.9 7.5 %shard_map.76 = (bf16[3,1536,768]{2,1,0:T(8,128)(2,1)S(1)}, f32[384,768]{1,0:T(8,128)S(1)}, f32[24,768]{1,0:T(8,128)S(1)}) custom-call(s32[2]{0:T(128)S(1)} %add_convert_fusion.3.flag_ref, bf16[768,384]{1,0:T(8,128)(2,1)S(1)} %copy-done, bf16[768,384]{1,0:T(8,128)(2,1)S(1)} %collective-permute-done.qb, ...), custom_call_target="tpu_custom_call" | custom-call | tf_op jit(solution)/shard_map/pallas_call | solution.py:95
  93.4 5.2 %backward_far.1 = (bf16[384,768]{1,0:T(8,128)(2,1)S(1)}, f32[24,768]{1,0:T(8,128)S(1)}, f32[384,768]{1,0:T(8,128)S(1)}, bf16[768,256]{1,0:T(8,128)(2,1)S(1)}, bf...) custom-call(s32[2]{0:T(128)S(1)} %add_convert_fusion.3.flag_ref, f32[384,768]{1,0:T(8,128)S(1)} %get-tuple-element.25.on, ...), custom_call_target="tpu_custom_call" | custom-call | tf_op jit(solution)/shard_map/backward_far/pallas_call | solution.py:165
  98.6 1.3 collective-permute-start.26
  99.9 2.9 %shard_map.80 = (bf16[768,128]{1,0:T(8,128)(2,1)S(1)}, f32[768,256]{1,0:T(8,128)S(1)}, bf16[768,256]{1,0:T(8,128)(2,1)S(1)}) custom-call(s32[2]{0:T(128)S(1)} %add_convert_fusion.3.flag_ref, bf16[3,1536,768]{2,1,0:T(8,128)(2,1)S(1)} %get-tuple-element.24.en, bf16[384,768]{1,0:T(8,128)(2,1)S(1)} %get-tuple-element.30.grad, ...), custom_call_target="tpu_custom_call" | custom-call | tf_op jit(solution)/shard_map/pallas_call | solution.py:201
  102.9 1.0 collective-permute-start.20
  103.9 2.9 %shard_map.79 = (bf16[768,128]{1,0:T(8,128)(2,1)S(1)}, f32[768,256]{1,0:T(8,128)S(1)}, bf16[768,256]{1,0:T(8,128)(2,1)S(1)}) custom-call(s32[2]{0:T(128)S(1)} %add_convert_fusion.3.flag_ref, bf16[3,1536,768]{2,1,0:T(8,128)(2,1)S(1)} %get-tuple-element.24.en, bf16[384,768]{1,0:T(8,128)(2,1)S(1)} %get-tuple-element.30.grad, ...), custom_call_target="tpu_custom_call" | custom-call | tf_op jit(solution)/shard_map/pallas_call | solution.py:201
  106.8 1.2 collective-permute-start.19
  108.0 2.9 %shard_map.78 = (bf16[768,128]{1,0:T(8,128)(2,1)S(1)}, f32[768,256]{1,0:T(8,128)S(1)}, bf16[768,256]{1,0:T(8,128)(2,1)S(1)}) custom-call(s32[2]{0:T(128)S(1)} %add_convert_fusion.3.flag_ref, bf16[3,1536,768]{2,1,0:T(8,128)(2,1)S(1)} %get-tuple-element.24.en, bf16[384,768]{1,0:T(8,128)(2,1)S(1)} %get-tuple-element.30.grad, ...), custom_call_target="tpu_custom_call" | custom-call | tf_op jit(solution)/shard_map/pallas_call | solution.py:201
  110.9 1.0 collective-permute-start.18
  111.9 1.5 %collective-permute-start.22 = (bf16[768,256]{1,0:T(8,128)(2,1)S(1)}, bf16[768,256]{1,0:T(8,128)(2,1)S(1)}, u32[]{:S(2)}, u32[]{:S(2)}) collective-permute-start(bf16[768,256]{1,0:T(8,128)(2,1)S(1)} %get-tuple-element.38), channel_id=1, source_target_pairs={{0,2},{1,8},{2,0},{3,10},{4,6},{5,12},{6,4},{7,14},{8,1},{9,16},{1... | collective-permute-start | bytes 1179656 | tf_op jit(solution)/shard_map/ppermute | solution.py:35
  114.0 2.6 %collective-permute-done.18 = bf16[768,128]{1,0:T(8,128)(2,1)S(1)} collective-permute-done((bf16[768,128]{1,0:T(8,128)(2,1)S(1)}, bf16[768,128]{1,0:T(8,128)(2,1)S(1)}, u32[]{:S(2)}, u32[]{:S(2)}) %collective-permute-start.18) | collective-permute-done | bytes 196640 | tf_op jit(solution)/shard_map/ppermute | solution.py:35
  116.7 1.0 maximum_select_fusion
  118.3 2.1 %collective-permute-start.29 = (bf16[768,256]{1,0:T(8,128)(2,1)S(1)}, bf16[768,256]{1,0:T(8,128)(2,1)S(1)}, u32[]{:S(2)}, u32[]{:S(2)}) collective-permute-start(bf16[768,256]{1,0:T(8,128)(2,1)S(1)} %add_convert_fusion), channel_id=1, source_target_pairs={{0,2},{1,4},{2,0},{3,6},{4,1},{5,7},{6,3},{7,5},{8,10},{9,12},{10,... | collective-permute-start | bytes 1179656 | tf_op jit(solution)/shard_map/ppermute | solution.py:35
  120.4 3.5 %collective-permute-done.24 = bf16[768,256]{1,0:T(8,128)(2,1)S(1)} collective-permute-done((bf16[768,256]{1,0:T(8,128)(2,1)S(1)}, bf16[768,256]{1,0:T(8,128)(2,1)S(1)}, u32[]{:S(2)}, u32[]{:S(2)}) %collective-permute-start.24) | collective-permute-done | bytes 393248 | tf_op jit(solution)/shard_map/ppermute | solution.py:35
  124.0 1.6 %collective-permute-start.28 = (bf16[768,256]{1,0:T(8,128)(2,1)S(1)}, bf16[768,256]{1,0:T(8,128)(2,1)S(1)}, u32[]{:S(2)}, u32[]{:S(2)}) collective-permute-start(bf16[768,256]{1,0:T(8,128)(2,1)S(1)} %add_convert_fusion.1), channel_id=1, source_target_pairs={{0,2},{1,4},{2,0},{3,6},{4,1},{5,7},{6,3},{7,5},{8,10},{9,12},{10,... | collective-permute-start | bytes 1179656 | tf_op jit(solution)/shard_map/ppermute | solution.py:35
  126.5 1.6 %collective-permute-done.29 = bf16[768,256]{1,0:T(8,128)(2,1)S(1)} collective-permute-done((bf16[768,256]{1,0:T(8,128)(2,1)S(1)}, bf16[768,256]{1,0:T(8,128)(2,1)S(1)}, u32[]{:S(2)}, u32[]{:S(2)}) %collective-permute-start.29) | collective-permute-done | bytes 393248 | tf_op jit(solution)/shard_map/ppermute | solution.py:35
  128.1 4.2 %collective-permute-done.28 = bf16[768,256]{1,0:T(8,128)(2,1)S(1)} collective-permute-done((bf16[768,256]{1,0:T(8,128)(2,1)S(1)}, bf16[768,256]{1,0:T(8,128)(2,1)S(1)}, u32[]{:S(2)}, u32[]{:S(2)}) %collective-permute-start.28) | collective-permute-done | bytes 393248 | tf_op jit(solution)/shard_map/ppermute | solution.py:35
  132.3 4.2 %collective-permute-done.27 = bf16[768,256]{1,0:T(8,128)(2,1)S(1)} collective-permute-done((bf16[768,256]{1,0:T(8,128)(2,1)S(1)}, bf16[768,256]{1,0:T(8,128)(2,1)S(1)}, u32[]{:S(2)}, u32[]{:S(2)}) %collective-permute-start.27) | collective-permute-done | bytes 393248 | tf_op jit(solution)/shard_map/ppermute | solution.py:35
  136.6 1.4 maximum_select_fusion.1
  (66 shorter events, 2.8 us)
Async XLA Ops:
  0.6 50.9 %copy-start.13 = (bf16[768,384]{1,0:T(8,128)(2,1)S(1)}, bf16[768,384]{1,0:T(8,128)(2,1)}, u32[]{:S(2)}) copy-start(bf16[768,384]{1,0:T(8,128)(2,1)} %param.7) | copy-start | bytes 1769476
  0.6 29.3 %collective-permute-start.8 = (bf16[768,768]{1,0:T(8,128)(2,1)}, bf16[768,768]{1,0:T(8,128)(2,1)}, u32[]{:S(2)}, u32[]{:S(2)}) collective-permute-start(bf16[768,768]{1,0:T(8,128)(2,1)} %g0.1), channel_id=1, source_target_pairs={{0,2},{1,3},{2,0},{3,1},{4,6},{5,7},{6,4},{7,5},{8,10},{9,11},{10,... | collective-permute-start | bytes 3538952 | tf_op jit(solution)/shard_map/ppermute | solution.py:35
  3.7 13.6 %collective-permute-start.11 = (bf16[384,384]{1,0:T(8,128)(2,1)}, bf16[384,384]{1,0:T(8,128)(2,1)S(1)}, u32[]{:S(2)}, u32[]{:S(2)}) collective-permute-start(bf16[384,384]{1,0:T(8,128)(2,1)} %refs_0_.1), channel_id=1, source_target_pairs={{0,8},{1,9},{2,10},{3,11},{4,12},{5,13},{6,14},{7,15},{8,0},{9,1},... | collective-permute-start | bytes 884744 | tf_op jit(solution)/shard_map/ppermute | solution.py:35
  5.2 24.7 %collective-permute-start.10 = (bf16[384,384]{1,0:T(8,128)(2,1)}, bf16[384,384]{1,0:T(8,128)(2,1)S(1)}, u32[]{:S(2)}, u32[]{:S(2)}) collective-permute-start(bf16[384,384]{1,0:T(8,128)(2,1)} %refs_0_.1), channel_id=1, source_target_pairs={{0,4},{1,5},{2,6},{3,7},{4,0},{5,1},{6,2},{7,3},{8,12},{9,13},{10,... | collective-permute-start | bytes 884744 | tf_op jit(solution)/shard_map/ppermute | solution.py:35
  6.8 23.9 %collective-permute-start.13 = (bf16[384,384]{1,0:T(8,128)(2,1)}, bf16[384,384]{1,0:T(8,128)(2,1)S(1)}, u32[]{:S(2)}, u32[]{:S(2)}) collective-permute-start(bf16[384,384]{1,0:T(8,128)(2,1)} %refs_0_.1), channel_id=1, source_target_pairs={{0,16},{1,17},{2,18},{3,19},{4,20},{5,21},{6,22},{7,23},{8,24},{9,... | collective-permute-start | bytes 884744 | tf_op jit(solution)/shard_map/ppermute | solution.py:35
  17.3 17.5 %collective-permute-start.15 = (bf16[384,384]{1,0:T(8,128)(2,1)S(1)}, bf16[384,384]{1,0:T(8,128)(2,1)S(1)}, u32[]{:S(2)}, u32[]{:S(2)}) collective-permute-start(bf16[384,384]{1,0:T(8,128)(2,1)S(1)} %collective-permute-done.11.refs_2_), channel_id=1, source_target_pairs={{0,16},{1,17},{2,18},{3,19},{4,20},{5,21},{6,22},{7,23},{8,24},{9,... | collective-permute-start | bytes 884744 | tf_op jit(solution)/shard_map/ppermute | solution.py:35
  18.0 0.7 copy-start.3
  18.7 49.4 %collective-permute-start.7 = (bf16[768,768]{1,0:T(8,128)(2,1)}, bf16[768,768]{1,0:T(8,128)(2,1)}, u32[]{:S(2)}, u32[]{:S(2)}) collective-permute-start(bf16[768,768]{1,0:T(8,128)(2,1)} %g0.1), channel_id=1, source_target_pairs={{0,1},{1,0},{2,3},{3,2},{4,5},{5,4},{6,7},{7,6},{8,9},{9,8},{10,11... | collective-permute-start | bytes 3538952 | tf_op jit(solution)/shard_map/ppermute | solution.py:35
  30.0 39.3 %collective-permute-start.9 = (bf16[768,768]{1,0:T(8,128)(2,1)}, bf16[768,768]{1,0:T(8,128)(2,1)}, u32[]{:S(2)}, u32[]{:S(2)}) collective-permute-start(bf16[768,768]{1,0:T(8,128)(2,1)} %collective-permute-done.8.g2), channel_id=1, source_target_pairs={{0,1},{1,0},{2,3},{3,2},{4,5},{5,4},{6,7},{7,6},{8,9},{9,8},{10,11... | collective-permute-start | bytes 3538952 | tf_op jit(solution)/shard_map/ppermute | solution.py:35
  30.0 21.5 %copy-start.5 = (bf16[384,384]{1,0:T(8,128)(2,1)}, bf16[384,384]{1,0:T(8,128)(2,1)S(1)}, u32[]{:S(2)}) copy-start(bf16[384,384]{1,0:T(8,128)(2,1)S(1)} %collective-permute-done.10.refs_1_) | copy-start | bytes 884740
  30.0 15.0 %collective-permute-start.1 = (bf16[768,384]{1,0:T(8,128)(2,1)}, bf16[768,384]{1,0:T(8,128)(2,1)S(1)}, u32[]{:S(2)}, u32[]{:S(2)}) collective-permute-start(bf16[768,384]{1,0:T(8,128)(2,1)} %param.6), channel_id=1, source_target_pairs={{1,4},{3,6},{4,1},{6,3},{9,12},{11,14},{12,9},{14,11},{17,20},{19,... | collective-permute-start | bytes 1769480 | tf_op jit(solution)/shard_map/ppermute | solution.py:35
  30.7 21.0 %copy-start.7 = (bf16[384,384]{1,0:T(8,128)(2,1)}, bf16[384,384]{1,0:T(8,128)(2,1)S(1)}, u32[]{:S(2)}) copy-start(bf16[384,384]{1,0:T(8,128)(2,1)S(1)} %collective-permute-done.13.refs_4_) | copy-start | bytes 884740
  30.7 17.5 %collective-permute-start.3 = (bf16[768,384]{1,0:T(8,128)(2,1)}, bf16[768,384]{1,0:T(8,128)(2,1)S(1)}, u32[]{:S(2)}, u32[]{:S(2)}) collective-permute-start(bf16[768,384]{1,0:T(8,128)(2,1)} %param.7), channel_id=1, source_target_pairs={{1,4},{3,6},{4,1},{6,3},{9,12},{11,14},{12,9},{14,11},{17,20},{19,... | collective-permute-start | bytes 1769480 | tf_op jit(solution)/shard_map/ppermute | solution.py:35
  34.8 16.9 %copy-start.9 = (bf16[384,384]{1,0:T(8,128)(2,1)}, bf16[384,384]{1,0:T(8,128)(2,1)S(1)}, u32[]{:S(2)}) copy-start(bf16[384,384]{1,0:T(8,128)(2,1)S(1)} %collective-permute-done.15.refs_6_) | copy-start | bytes 884740
  34.8 9.4 %collective-permute-start.12 = (bf16[384,384]{1,0:T(8,128)(2,1)S(1)}, bf16[384,384]{1,0:T(8,128)(2,1)S(1)}, u32[]{:S(2)}, u32[]{:S(2)}) collective-permute-start(bf16[384,384]{1,0:T(8,128)(2,1)S(1)} %collective-permute-done.10.refs_1_), channel_id=1, source_target_pairs={{0,8},{1,9},{2,10},{3,11},{4,12},{5,13},{6,14},{7,15},{8,0},{9,1},... | collective-permute-start | bytes 884744 | tf_op jit(solution)/shard_map/ppermute | solution.py:35
  44.2 7.3 %copy-start.11 = (bf16[384,384]{1,0:T(8,128)(2,1)}, bf16[384,384]{1,0:T(8,128)(2,1)S(1)}, u32[]{:S(2)}) copy-start(bf16[384,384]{1,0:T(8,128)(2,1)S(1)} %collective-permute-done.12.refs_3_) | copy-start | bytes 884740
  44.2 33.9 %collective-permute-start = (bf16[768,384]{1,0:T(8,128)(2,1)}, bf16[768,384]{1,0:T(8,128)(2,1)S(1)}, u32[]{:S(2)}, u32[]{:S(2)}) collective-permute-start(bf16[768,384]{1,0:T(8,128)(2,1)} %qa.11), channel_id=1, source_target_pairs={{1,4},{3,6},{4,1},{6,3},{9,12},{11,14},{12,9},{14,11},{17,20},{19,... | collective-permute-start | bytes 1769480 | tf_op jit(solution)/shard_map/ppermute | solution.py:35
  45.0 19.9 %collective-permute-start.14 = (bf16[384,384]{1,0:T(8,128)(2,1)S(1)}, bf16[384,384]{1,0:T(8,128)(2,1)S(1)}, u32[]{:S(2)}, u32[]{:S(2)}) collective-permute-start(bf16[384,384]{1,0:T(8,128)(2,1)S(1)} %collective-permute-done.13.refs_4_), channel_id=1, source_target_pairs={{0,4},{1,5},{2,6},{3,7},{4,0},{5,1},{6,2},{7,3},{8,12},{9,13},{10,... | collective-permute-start | bytes 884744 | tf_op jit(solution)/shard_map/ppermute | solution.py:35
  48.2 0.8 copy-start.14
  49.0 19.1 %collective-permute-start.16 = (bf16[384,384]{1,0:T(8,128)(2,1)S(1)}, bf16[384,384]{1,0:T(8,128)(2,1)S(1)}, u32[]{:S(2)}, u32[]{:S(2)}) collective-permute-start(bf16[384,384]{1,0:T(8,128)(2,1)S(1)} %collective-permute-done.15.refs_6_), channel_id=1, source_target_pairs={{0,4},{1,5},{2,6},{3,7},{4,0},{5,1},{6,2},{7,3},{8,12},{9,13},{10,... | collective-permute-start | bytes 884744 | tf_op jit(solution)/shard_map/ppermute | solution.py:35
  50.3 1.2 copy-start.15
  51.5 17.8 %copy-start.1 = (bf16[768,768]{1,0:T(8,128)(2,1)S(1)}, bf16[768,768]{1,0:T(8,128)(2,1)}, u32[]{:S(2)}) copy-start(bf16[768,768]{1,0:T(8,128)(2,1)} %g0.1) | copy-start | bytes 3538948
  51.5 17.8 %copy-start.2 = (bf16[384,384]{1,0:T(8,128)(2,1)S(1)}, bf16[384,384]{1,0:T(8,128)(2,1)}, u32[]{:S(2)}) copy-start(bf16[384,384]{1,0:T(8,128)(2,1)} %refs_0_.1) | copy-start | bytes 884740
  51.6 17.8 %copy-start.4 = (bf16[384,384]{1,0:T(8,128)(2,1)S(1)}, bf16[384,384]{1,0:T(8,128)(2,1)}, u32[]{:S(2)}) copy-start(bf16[384,384]{1,0:T(8,128)(2,1)} %copy-done.3) | copy-start | bytes 884740
  51.7 29.6 %copy-start = (bf16[768,384]{1,0:T(8,128)(2,1)S(1)}, bf16[768,384]{1,0:T(8,128)(2,1)}, u32[]{:S(2)}) copy-start(bf16[768,384]{1,0:T(8,128)(2,1)} %qa.11) | copy-start | bytes 1769476
  64.9 14.8 %collective-permute-start.5 = (bf16[768,384]{1,0:T(8,128)(2,1)S(1)}, bf16[768,384]{1,0:T(8,128)(2,1)}, u32[]{:S(2)}, u32[]{:S(2)}) collective-permute-start(bf16[768,384]{1,0:T(8,128)(2,1)S(1)} %broadcast_select_fusion.1.refs_0_.ko), channel_id=1, source_target_pairs={{0,2},{1,8},{2,0},{3,10},{4,6},{5,12},{6,4},{7,14},{8,1},{9,16},{1... | collective-permute-start | bytes 1769480 | tf_op jit(solution)/shard_map/ppermute | solution.py:35
  68.1 17.8 %collective-permute-start.2 = (bf16[768,384]{1,0:T(8,128)(2,1)S(1)}, bf16[768,384]{1,0:T(8,128)(2,1)S(1)}, u32[]{:S(2)}, u32[]{:S(2)}) collective-permute-start(bf16[768,384]{1,0:T(8,128)(2,1)S(1)} %broadcast_select_fusion.1.refs_0_.ko), channel_id=1, source_target_pairs={{0,1},{1,0},{2,3},{3,2},{4,5},{5,4},{6,7},{7,6},{8,9},{9,8},{10,11... | collective-permute-start | bytes 1769480 | tf_op jit(solution)/shard_map/ppermute | solution.py:35
  68.1 13.1 %collective-permute-start.6 = (bf16[768,384]{1,0:T(8,128)(2,1)S(1)}, bf16[768,384]{1,0:T(8,128)(2,1)}, u32[]{:S(2)}, u32[]{:S(2)}) collective-permute-start(bf16[768,384]{1,0:T(8,128)(2,1)S(1)} %broadcast_select_fusion.refs_2_.vo), channel_id=1, source_target_pairs={{0,2},{1,8},{2,0},{3,10},{4,6},{5,12},{6,4},{7,14},{8,1},{9,16},{1... | collective-permute-start | bytes 1769480 | tf_op jit(solution)/shard_map/ppermute | solution.py:35
  69.3 16.6 %collective-permute-start.4 = (bf16[768,384]{1,0:T(8,128)(2,1)S(1)}, bf16[768,384]{1,0:T(8,128)(2,1)S(1)}, u32[]{:S(2)}, u32[]{:S(2)}) collective-permute-start(bf16[768,384]{1,0:T(8,128)(2,1)S(1)} %broadcast_select_fusion.refs_2_.vo), channel_id=1, source_target_pairs={{0,1},{1,0},{2,3},{3,2},{4,5},{5,4},{6,7},{7,6},{8,9},{9,8},{10,11... | collective-permute-start | bytes 1769480 | tf_op jit(solution)/shard_map/ppermute | solution.py:35
  69.3 1.0 copy-start.6
  70.3 1.0 copy-start.8
  71.2 1.0 copy-start.10
  72.2 1.0 copy-start.12
  78.2 15.2 %collective-permute-start.17 = (bf16[384,768]{1,0:T(8,128)(2,1)}, bf16[384,768]{1,0:T(8,128)(2,1)}, u32[]{:S(2)}, u32[]{:S(2)}) collective-permute-start(bf16[384,768]{1,0:T(8,128)(2,1)} %project.1.ga), channel_id=1, source_target_pairs={{0,2},{1,4},{2,0},{3,6},{4,1},{5,7},{6,3},{7,5},{8,10},{9,12},{10,... | collective-permute-start | bytes 1769480 | tf_op jit(solution)/shard_map/ppermute | solution.py:35
  98.6 19.0 %collective-permute-start.26 = (bf16[768,256]{1,0:T(8,128)(2,1)S(1)}, bf16[768,256]{1,0:T(8,128)(2,1)S(1)}, u32[]{:S(2)}, u32[]{:S(2)}) collective-permute-start(bf16[768,256]{1,0:T(8,128)(2,1)S(1)} %get-tuple-element.44), channel_id=1, source_target_pairs={{0,2},{1,8},{2,0},{3,10},{4,6},{5,12},{6,4},{7,14},{8,1},{9,16},{1... | collective-permute-start | bytes 1179656 | tf_op jit(solution)/shard_map/ppermute | solution.py:35
  102.8 15.3 %collective-permute-start.25 = (bf16[768,256]{1,0:T(8,128)(2,1)S(1)}, bf16[768,256]{1,0:T(8,128)(2,1)S(1)}, u32[]{:S(2)}, u32[]{:S(2)}) collective-permute-start(bf16[768,256]{1,0:T(8,128)(2,1)S(1)} %get-tuple-element.43), channel_id=1, source_target_pairs={{0,1},{1,0},{2,3},{3,2},{4,5},{5,4},{6,7},{7,6},{8,9},{9,8},{10,11... | collective-permute-start | bytes 1179656 | tf_op jit(solution)/shard_map/ppermute | solution.py:35
  102.9 9.0 %collective-permute-start.20 = (bf16[768,128]{1,0:T(8,128)(2,1)S(1)}, bf16[768,128]{1,0:T(8,128)(2,1)S(1)}, u32[]{:S(2)}, u32[]{:S(2)}) collective-permute-start(bf16[768,128]{1,0:T(8,128)(2,1)S(1)} %get-tuple-element.35), channel_id=1, source_target_pairs={{0,8},{1,4},{2,10},{3,6},{4,1},{5,13},{6,3},{7,15},{8,0},{9,12},{1... | collective-permute-start | bytes 589832 | tf_op jit(solution)/shard_map/ppermute | solution.py:35
  106.8 6.6 %collective-permute-start.19 = (bf16[768,128]{1,0:T(8,128)(2,1)S(1)}, bf16[768,128]{1,0:T(8,128)(2,1)S(1)}, u32[]{:S(2)}, u32[]{:S(2)}) collective-permute-start(bf16[768,128]{1,0:T(8,128)(2,1)S(1)} %get-tuple-element.34), channel_id=1, source_target_pairs={{0,8},{1,4},{2,10},{3,6},{4,1},{5,13},{6,3},{7,15},{8,0},{9,12},{1... | collective-permute-start | bytes 589832 | tf_op jit(solution)/shard_map/ppermute | solution.py:35
  110.9 5.7 %collective-permute-start.18 = (bf16[768,128]{1,0:T(8,128)(2,1)S(1)}, bf16[768,128]{1,0:T(8,128)(2,1)S(1)}, u32[]{:S(2)}, u32[]{:S(2)}) collective-permute-start(bf16[768,128]{1,0:T(8,128)(2,1)S(1)} %get-tuple-element.33), channel_id=1, source_target_pairs={{0,8},{1,4},{2,10},{3,6},{4,1},{5,13},{6,3},{7,15},{8,0},{9,12},{1... | collective-permute-start | bytes 589832 | tf_op jit(solution)/shard_map/ppermute | solution.py:35
  111.9 13.7 %collective-permute-start.22 = (bf16[768,256]{1,0:T(8,128)(2,1)S(1)}, bf16[768,256]{1,0:T(8,128)(2,1)S(1)}, u32[]{:S(2)}, u32[]{:S(2)}) collective-permute-start(bf16[768,256]{1,0:T(8,128)(2,1)S(1)} %get-tuple-element.38), channel_id=1, source_target_pairs={{0,2},{1,8},{2,0},{3,10},{4,6},{5,12},{6,4},{7,14},{8,1},{9,16},{1... | collective-permute-start | bytes 1179656 | tf_op jit(solution)/shard_map/ppermute | solution.py:35
  113.4 10.5 %collective-permute-start.24 = (bf16[768,256]{1,0:T(8,128)(2,1)S(1)}, bf16[768,256]{1,0:T(8,128)(2,1)S(1)}, u32[]{:S(2)}, u32[]{:S(2)}) collective-permute-start(bf16[768,256]{1,0:T(8,128)(2,1)S(1)} %get-tuple-element.41), channel_id=1, source_target_pairs={{0,2},{1,8},{2,0},{3,10},{4,6},{5,12},{6,4},{7,14},{8,1},{9,16},{1... | collective-permute-start | bytes 1179656 | tf_op jit(solution)/shard_map/ppermute | solution.py:35
  116.7 7.2 %collective-permute-start.23 = (bf16[768,256]{1,0:T(8,128)(2,1)S(1)}, bf16[768,256]{1,0:T(8,128)(2,1)S(1)}, u32[]{:S(2)}, u32[]{:S(2)}) collective-permute-start(bf16[768,256]{1,0:T(8,128)(2,1)S(1)} %get-tuple-element.40), channel_id=1, source_target_pairs={{0,1},{1,0},{2,3},{3,2},{4,5},{5,4},{6,7},{7,6},{8,9},{9,8},{10,11... | collective-permute-start | bytes 1179656 | tf_op jit(solution)/shard_map/ppermute | solution.py:35
  117.6 8.0 %collective-permute-start.21 = (bf16[768,256]{1,0:T(8,128)(2,1)S(1)}, bf16[768,256]{1,0:T(8,128)(2,1)S(1)}, u32[]{:S(2)}, u32[]{:S(2)}) collective-permute-start(bf16[768,256]{1,0:T(8,128)(2,1)S(1)} %get-tuple-element.37), channel_id=1, source_target_pairs={{0,1},{1,0},{2,3},{3,2},{4,5},{5,4},{6,7},{7,6},{8,9},{9,8},{10,11... | collective-permute-start | bytes 1179656 | tf_op jit(solution)/shard_map/ppermute | solution.py:35
  118.3 9.8 %collective-permute-start.29 = (bf16[768,256]{1,0:T(8,128)(2,1)S(1)}, bf16[768,256]{1,0:T(8,128)(2,1)S(1)}, u32[]{:S(2)}, u32[]{:S(2)}) collective-permute-start(bf16[768,256]{1,0:T(8,128)(2,1)S(1)} %add_convert_fusion), channel_id=1, source_target_pairs={{0,2},{1,4},{2,0},{3,6},{4,1},{5,7},{6,3},{7,5},{8,10},{9,12},{10,... | collective-permute-start | bytes 1179656 | tf_op jit(solution)/shard_map/ppermute | solution.py:35
  124.0 8.3 %collective-permute-start.28 = (bf16[768,256]{1,0:T(8,128)(2,1)S(1)}, bf16[768,256]{1,0:T(8,128)(2,1)S(1)}, u32[]{:S(2)}, u32[]{:S(2)}) collective-permute-start(bf16[768,256]{1,0:T(8,128)(2,1)S(1)} %add_convert_fusion.1), channel_id=1, source_target_pairs={{0,2},{1,4},{2,0},{3,6},{4,1},{5,7},{6,3},{7,5},{8,10},{9,12},{10,... | collective-permute-start | bytes 1179656 | tf_op jit(solution)/shard_map/ppermute | solution.py:35
  125.8 10.7 %collective-permute-start.27 = (bf16[768,256]{1,0:T(8,128)(2,1)S(1)}, bf16[768,256]{1,0:T(8,128)(2,1)S(1)}, u32[]{:S(2)}, u32[]{:S(2)}) collective-permute-start(bf16[768,256]{1,0:T(8,128)(2,1)S(1)} %add_convert_fusion.2), channel_id=1, source_target_pairs={{0,2},{1,4},{2,0},{3,6},{4,1},{5,7},{6,3},{7,5},{8,10},{9,12},{10,... | collective-permute-start | bytes 1179656 | tf_op jit(solution)/shard_map/ppermute | solution.py:35

commit v7 on v6

--- a/solution.py
+++ b/solution.py
@@ -121,15 +121,17 @@
     return dot(k, delta, TN)
 
 
-def far_kernel(heads, flag_ref, on, sn, ef, of, sf, ga, gb, qa, qb, kz, vz, *refs):
+def far_kernel(first, count, flag_ref, on, sn, ef, of, sf, ga, gb, qa, qb, kz, vz, *refs):
     grad_ref, inner_ref, dq = refs[:3]
     stays = flag_ref[1] > 0
-    for head in range(heads):
+    for i in range(count):
+        head = first + i
         part = slice(head * HD, (head + 1) * HD)
         line = slice(head * 8, head * 8 + 1)
         mass = slice(head * 8 + 1, head * 8 + 2)
+        mine = slice(i * HD, (i + 1) * HD)
         query = jnp.where(stays, qa[:, part], qb[:, part])
-        grad = jnp.where(stays, ga[part, :], gb[part, :]).astype(jnp.float32)
+        grad = jnp.where(stays, ga[mine, :], gb[mine, :]).astype(jnp.float32)
         near_top = sn[line, :]
         far_top = jnp.where(flag_ref[0] > 0, sf[line, :], -jnp.inf)
         top = jnp.maximum(near_top, far_top)
@@ -144,36 +146,35 @@
             axis=0,
             keepdims=True,
         )
-        grad_ref[part, :] = near_grad
-        inner_ref[line, :] = inner * near_share
-        dq[part, :] = slab_terms(
+        grad_ref[mine, :] = near_grad
+        inner_ref[i * 8 : i * 8 + 1, :] = inner * near_share
+        dq[mine, :] = slab_terms(
             ef[head],
             far_grad,
             inner * far_share,
             query,
             kz[:, part],
             vz[:, part],
-            refs[3 + head],
-        )
-
-
-def backward_far(flags, near, away, grads, queries, far):
-    rows, width = queries[0].shape
-    heads = width // HD
+            refs[3 + i],
+        )
+
+
+def backward_far(first, flags, near, away, grads, queries, far):
+    rows = queries[0].shape[0]
+    count = grads[0].shape[0] // HD
     vmem = pl.BlockSpec(memory_space=pltpu.VMEM)
     operands = (*near[1:], *away, *grads, *queries, *far)
     return pl.pallas_call(
-        functools.partial(far_kernel, heads),
+        functools.partial(far_kernel, first, count),
         in_specs=[pl.BlockSpec(memory_space=pltpu.SMEM)] + [vmem] * len(operands),
-        out_specs=[vmem] * (3 + heads),
+        out_specs=[vmem] * (3 + count),
         out_shape=[
-            jax.ShapeDtypeStruct((width, rows), jnp.bfloat16),
-            jax.ShapeDtypeStruct((heads * 8, rows), jnp.float32),
-            jax.ShapeDtypeStruct((width, rows), jnp.float32),
+            jax.ShapeDtypeStruct((count * HD, rows), jnp.bfloat16),
+            jax.ShapeDtypeStruct((count * 8, rows), jnp.float32),
+            jax.ShapeDtypeStruct((count * HD, rows), jnp.float32),
         ]
-        + [jax.ShapeDtypeStruct((rows, 2 * HD), jnp.bfloat16)] * heads,
+        + [jax.ShapeDtypeStruct((rows, 2 * HD), jnp.bfloat16)] * count,
         compiler_params=pltpu.CompilerParams(vmem_limit_bytes=LIMIT),
-        name="backward_far",
     )(flags, *operands)
 
 
@@ -189,11 +190,11 @@
     dq[...] = (total * (1.0 / math.sqrt(HD))).T.astype(dq.dtype)
 
 
-def backward_near(head, flags, weights, grad, inner, dq_far, queries, side, own):
+def backward_near(head, place, flags, weights, grad, inner, dq_far, queries, side, own):
     rows, _ = queries[0].shape
     spec = pl.BlockSpec((rows, HD), lambda i: (0, head))
-    flip = pl.BlockSpec((HD, rows), lambda i: (head, 0))
-    stat = pl.BlockSpec((8, rows), lambda i: (head, 0))
+    flip = pl.BlockSpec((HD, rows), lambda i: (place, 0))
+    stat = pl.BlockSpec((8, rows), lambda i: (place, 0))
 
     def whole(columns):
         return pl.BlockSpec((rows, columns), lambda i: (0, 0))
@@ -221,9 +222,9 @@
 
 def project_kernel(place_ref, g0, g1, g2, g3, *refs):
     shards = refs[:8]
-    out_ref, wbuf = refs[8:]
+    head_ref, rest_ref, wbuf = refs[8:]
     z, y, h = place_ref[0], place_ref[1], place_ref[2]
-    width = out_ref.shape[0]
+    width = shards[0].shape[0]
     for m in range(4):
         for n in range(2):
             column = pl.multiple_of((y ^ n) * width, width)
@@ -232,7 +233,9 @@
     for m, g in enumerate((g0, g1, g2, g3)):
         part = dot(wbuf[h ^ m], g[...], NT)
         total = part if total is None else total + part
-    out_ref[...] = total.astype(out_ref.dtype)
+    low = total.astype(jnp.bfloat16)
+    head_ref[...] = low[:HD]
+    rest_ref[...] = low[HD:]
 
 
 def project(place, grads, shards, rows, width):
@@ -241,8 +244,8 @@
     return pl.pallas_call(
         project_kernel,
         in_specs=[pl.BlockSpec(memory_space=pltpu.SMEM)] + [vmem] * 12,
-        out_specs=vmem,
-        out_shape=jax.ShapeDtypeStruct((width, rows), jnp.bfloat16),
+        out_specs=[vmem, vmem],
+        out_shape=[jax.ShapeDtypeStruct((n, rows), jnp.bfloat16) for n in (HD, width - HD)],
         scratch_shapes=[pltpu.VMEM((4, width, grads[0].shape[1]), jnp.bfloat16)],
         compiler_params=pltpu.CompilerParams(vmem_limit_bytes=LIMIT),
         name="project",
@@ -300,7 +303,7 @@
     side_k, side_v = send(keys, side_route), send(values, side_route)
     near = soften(flags, query_pair, (keys, side_k), (values, side_v))
     if square:
-        attn_grad = project(
+        attn_grads = project(
             jnp.stack([t // 2, y, h]).astype(jnp.int32), grads, shards, rows, width
         )
     else:
@@ -309,17 +312,21 @@
             lax.all_gather(grad_out, "head", axis=1, tiled=True),
             NT,
         ).astype(jnp.bfloat16)
-    grad_pair = (attn_grad, send(attn_grad, busy_route))
+        attn_grads = attn_grad[:HD], attn_grad[HD:]
+    grad_pairs = [(g, send(g, busy_route)) for g in attn_grads]
     away = soften(flags, query_pair, (far_k,), (far_v,))
 
     done = []
-    grad, inner, dq_far, *away_terms = backward_far(
-        flags, near, away, grad_pair, query_pair, (far_k, far_v)
-    )
-    far_terms = [send(f, far_route) for f in away_terms]
-    for head in range(width // HD):
+    shared = []
+    for first, pair in zip((0, 1), grad_pairs):
+        results = backward_far(first, flags, near, away, pair, query_pair, (far_k, far_v))
+        sums, terms = results[:3], results[3:]
+        for i, term in enumerate(terms):
+            shared.append((i, sums, send(term, far_route)))
+    for head, (place, (grad, inner, dq_far), far) in enumerate(shared):
         dq, own, side = backward_near(
             head,
+            place,
             flags,
             near[0],
             grad,
@@ -329,7 +336,6 @@
             (side_k, side_v),
             (keys, values),
         )
-        far = far_terms[head]
         side = send(side, side_route)
         own = (own + side.astype(jnp.float32) + far.astype(jnp.float32)).astype(jnp.bfloat16)
         done.append(((dq, send(dq, spare_route)), (own, send(own, busy_route))))

time: 140 us -> 153 us (1.093)
  starting transfers between devices: 31.1 us -> 40.2 us
  local copies, waits for them, and re-layouts: 5.58 us -> 11.3 us
    ppermute x30 -> x31, starting transfers between devices: 31.1 us -> 40.2 us  [exchange(): return lax.ppermute(block, AXES, pairs)]
    unnamed x32 -> x44, local copies, waits for them, and re-layouts: 5.42 us -> 11.2 us
    ppermute x30 -> x31, waiting for transfers between devices: 64.9 us -> 63.5 us  [exchange(): return lax.ppermute(block, AXES, pairs)]
    pallas_call x1 -> x2, Pallas kernels: 5.22 us -> 6.53 us  [backward_far(): pl.pallas_call(functools.partial(far_kernel, first, count), in_specs=[pl....]
  transfers between devices with their start and end apart: 30 -> 31, of which waited for: 12 -> 10; matrix products, arithmetic and copies ran while one was open for 2% -> 2% of each run, Pallas kernels for 19% -> 21%
where the time goes in v7:
time: 153 us; the launch traced here: 152 us
  waiting for transfers between devices  63.5 us (42%)
  starting transfers between devices  40.2 us (26%)
  Pallas kernels  32.2 us (21%)
  local copies, waits for them, and re-layouts  11.3 us (7%)
  other arithmetic  4.25 us (3%)
    ppermute x31, waiting for transfers between devices, exchange(): return lax.ppermute(block, AXES, pairs)  63.5 us
    ppermute x31, starting transfers between devices, exchange(): return lax.ppermute(block, AXES, pairs)  40.2 us
    pallas_call x2, Pallas kernels, soften(): pl.pallas_call(functools.partial(soften_kernel, parts, tile), grid=(heads...  12.1 us
    unnamed x44, local copies, waits for them, and re-layouts  11.2 us
    pallas_call x3, Pallas kernels, backward_near(): pl.pallas_call(near_kernel, grid=(1,), in_specs=[pl.BlockSpec(memory_spac...  8.77 us
    pallas_call x2, Pallas kernels, backward_far(): pl.pallas_call(functools.partial(far_kernel, first, count), in_specs=[pl....  6.53 us
    pallas_call x1, Pallas kernels, project(): pl.pallas_call(project_kernel, in_specs=[pl.BlockSpec(memory_space=pltpu....  4.78 us
  transfers between devices with their start and end apart: 31, of which 10 were waited for; matrix products, arithmetic and copies ran while one was open for 2% of the time, Pallas kernels for 21%

profile of v7, /device:TPU:0, one launch (start us, length us, event | category | flops | bytes accessed | tf_op | source)
XLA Modules:
  0.0 152.4 jit_solution(3912332992902905564)
XLA Ops:
  0.6 3.0 %collective-permute-start.8 = (bf16[768,768]{1,0:T(8,128)(2,1)}, bf16[768,768]{1,0:T(8,128)(2,1)}, u32[]{:S(2)}, u32[]{:S(2)}) collective-permute-start(bf16[768,768]{1,0:T(8,128)(2,1)} %g0.1), channel_id=1, source_target_pairs={{0,2},{1,3},{2,0},{3,1},{4,6},{5,7},{6,4},{7,5},{8,10},{9,11},{10,... | collective-permute-start | bytes 3538952 | tf_op jit(solution)/shard_map/ppermute | solution.py:35
  3.7 1.6 %collective-permute-start.11 = (bf16[384,384]{1,0:T(8,128)(2,1)}, bf16[384,384]{1,0:T(8,128)(2,1)S(1)}, u32[]{:S(2)}, u32[]{:S(2)}) collective-permute-start(bf16[384,384]{1,0:T(8,128)(2,1)} %refs_0_.1), channel_id=1, source_target_pairs={{0,8},{1,9},{2,10},{3,11},{4,12},{5,13},{6,14},{7,15},{8,0},{9,1},... | collective-permute-start | bytes 884744 | tf_op jit(solution)/shard_map/ppermute | solution.py:35
  5.2 1.5 collective-permute-start.10
  6.8 23.2 %collective-permute-done.8.g2 = bf16[768,768]{1,0:T(8,128)(2,1)} collective-permute-done((bf16[768,768]{1,0:T(8,128)(2,1)}, bf16[768,768]{1,0:T(8,128)(2,1)}, u32[]{:S(2)}, u32[]{:S(2)}) %collective-permute-start.8) | collective-permute-done | bytes 1179680 | tf_op jit(solution)/shard_map/ppermute | solution.py:35
  31.4 2.9 %collective-permute-start.13 = (bf16[384,384]{1,0:T(8,128)(2,1)}, bf16[384,384]{1,0:T(8,128)(2,1)S(1)}, u32[]{:S(2)}, u32[]{:S(2)}) collective-permute-start(bf16[384,384]{1,0:T(8,128)(2,1)} %refs_0_.1), channel_id=1, source_target_pairs={{0,16},{1,17},{2,18},{3,19},{4,20},{5,21},{6,22},{7,23},{8,24},{9,... | collective-permute-start | bytes 884744 | tf_op jit(solution)/shard_map/ppermute | solution.py:35
  34.3 13.1 %collective-permute-done.13.refs_4_ = bf16[384,384]{1,0:T(8,128)(2,1)S(1)} collective-permute-done((bf16[384,384]{1,0:T(8,128)(2,1)}, bf16[384,384]{1,0:T(8,128)(2,1)S(1)}, u32[]{:S(2)}, u32[]{:S(2)}) %collective-permute-start.13) | collective-permute-done | bytes 294944 | tf_op jit(solution)/shard_map/ppermute | solution.py:35
  47.4 5.1 %collective-permute-start.12 = (bf16[384,384]{1,0:T(8,128)(2,1)S(1)}, bf16[384,384]{1,0:T(8,128)(2,1)S(1)}, u32[]{:S(2)}, u32[]{:S(2)}) collective-permute-start(bf16[384,384]{1,0:T(8,128)(2,1)S(1)} %collective-permute-done.10.refs_1_), channel_id=1, source_target_pairs={{0,8},{1,9},{2,10},{3,11},{4,12},{5,13},{6,14},{7,15},{8,0},{9,1},... | collective-permute-start | bytes 884744 | tf_op jit(solution)/shard_map/ppermute | solution.py:35
  52.6 6.2 %collective-permute-start.14 = (bf16[384,384]{1,0:T(8,128)(2,1)S(1)}, bf16[384,384]{1,0:T(8,128)(2,1)S(1)}, u32[]{:S(2)}, u32[]{:S(2)}) collective-permute-start(bf16[384,384]{1,0:T(8,128)(2,1)S(1)} %collective-permute-done.13.refs_4_), channel_id=1, source_target_pairs={{0,4},{1,5},{2,6},{3,7},{4,0},{5,1},{6,2},{7,3},{8,12},{9,13},{10,... | collective-permute-start | bytes 884744 | tf_op jit(solution)/shard_map/ppermute | solution.py:35
  58.7 5.7 %collective-permute-done.15.refs_6_ = bf16[384,384]{1,0:T(8,128)(2,1)S(1)} collective-permute-done((bf16[384,384]{1,0:T(8,128)(2,1)S(1)}, bf16[384,384]{1,0:T(8,128)(2,1)S(1)}, u32[]{:S(2)}, u32[]{:S(2)}) %collective-permute-start.15) | collective-permute-done | bytes 294944 | tf_op jit(solution)/shard_map/ppermute | solution.py:35
  65.0 1.2 broadcast_select_fusion.1.refs_0_.ko
  67.8 1.8 %collective-permute-start.2 = (bf16[768,384]{1,0:T(8,128)(2,1)S(1)}, bf16[768,384]{1,0:T(8,128)(2,1)S(1)}, u32[]{:S(2)}, u32[]{:S(2)}) collective-permute-start(bf16[768,384]{1,0:T(8,128)(2,1)S(1)} %broadcast_select_fusion.1.refs_0_.ko), channel_id=1, source_target_pairs={{0,1},{1,0},{2,3},{3,2},{4,5},{5,4},{6,7},{7,6},{8,9},{9,8},{10,11... | collective-permute-start | bytes 1769480 | tf_op jit(solution)/shard_map/ppermute | solution.py:35
  69.6 3.8 %collective-permute-done.16.refs_7_ = bf16[384,384]{1,0:T(8,128)(2,1)S(1)} collective-permute-done((bf16[384,384]{1,0:T(8,128)(2,1)S(1)}, bf16[384,384]{1,0:T(8,128)(2,1)S(1)}, u32[]{:S(2)}, u32[]{:S(2)}) %collective-permute-start.16) | collective-permute-done | bytes 294944 | tf_op jit(solution)/shard_map/ppermute | solution.py:35
  74.1 2.1 %collective-permute-start.5 = (bf16[768,384]{1,0:T(8,128)(2,1)S(1)}, bf16[768,384]{1,0:T(8,128)(2,1)}, u32[]{:S(2)}, u32[]{:S(2)}) collective-permute-start(bf16[768,384]{1,0:T(8,128)(2,1)S(1)} %broadcast_select_fusion.1.refs_0_.ko), channel_id=1, source_target_pairs={{0,2},{1,8},{2,0},{3,10},{4,6},{5,12},{6,4},{7,14},{8,1},{9,16},{1... | collective-permute-start | bytes 1769480 | tf_op jit(solution)/shard_map/ppermute | solution.py:35
  76.4 1.3 copy-done.1
  77.7 1.0 copy-done.4
  78.6 1.0 copy-done.6
  79.6 1.0 copy-done.8
  80.6 1.0 copy-done.10
  81.5 1.0 copy-done.12
  82.5 1.0 copy-done.14
  83.5 1.0 copy-done.16
  84.4 1.0 copy-done.18
  85.4 4.8 %project.1 = (bf16[128,768]{1,0:T(8,128)(2,1)}, bf16[256,768]{1,0:T(8,128)(2,1)S(1)}) custom-call(s32[3]{0:T(128)S(1)} %pad_add_fusion.place_ref, bf16[768,768]{1,0:T(8,128)(2,1)S(1)} %copy-done.1, bf16[768,768]{1,0:T(8,128)(2,1)} %collective-permute-done.7.g1, bf16[768,768]{1,0:T(8,128)(2,1)} %collective-permute-done.8.g2, ...), custom_call_target="tpu_custom_call" | custom-call | tf_op jit(solution)/shard_map/project/pallas_call | solution.py:244
  90.2 0.7 copy-done.2
  90.9 1.9 %collective-permute-start.17 = (bf16[128,768]{1,0:T(8,128)(2,1)}, bf16[128,768]{1,0:T(8,128)(2,1)}, u32[]{:S(2)}, u32[]{:S(2)}) collective-permute-start(bf16[128,768]{1,0:T(8,128)(2,1)} %get-tuple-element.35.ga), channel_id=1, source_target_pairs={{0,2},{1,4},{2,0},{3,6},{4,1},{5,7},{6,3},{7,5},{8,10},{9,12},{10,... | collective-permute-start | bytes 589832 | tf_op jit(solution)/shard_map/ppermute | solution.py:35
  92.9 7.2 %shard_map.76 = (bf16[3,1536,768]{2,1,0:T(8,128)(2,1)S(1)}, f32[384,768]{1,0:T(8,128)S(1)}, f32[24,768]{1,0:T(8,128)S(1)}) custom-call(s32[2]{0:T(128)S(1)} %add_convert_fusion.3.flag_ref, bf16[768,384]{1,0:T(8,128)(2,1)S(1)} %copy-done, bf16[768,384]{1,0:T(8,128)(2,1)S(1)} %collective-permute-done.qb, ...), custom_call_target="tpu_custom_call" | custom-call | tf_op jit(solution)/shard_map/pallas_call | solution.py:95
  100.2 4.9 %shard_map.77 = (bf16[3,768,768]{2,1,0:T(8,128)(2,1)S(1)}, f32[384,768]{1,0:T(8,128)S(1)}, f32[24,768]{1,0:T(8,128)S(1)}) custom-call(s32[2]{0:T(128)S(1)} %add_convert_fusion.3.flag_ref, bf16[768,384]{1,0:T(8,128)(2,1)S(1)} %copy-done, bf16[768,384]{1,0:T(8,128)(2,1)S(1)} %collective-permute-done.qb, bf16[768,384]{1,0:T(8,128)(2,1)} %collective-permute-done.5.refs_0_.kz, ...), custom_call_target="tpu_custom_call" | custom-call | tf_op jit(solution)/shard_map/pallas_call | solution.py:95
  105.2 2.8 %shard_map.78 = (bf16[128,768]{1,0:T(8,128)(2,1)S(1)}, f32[8,768]{1,0:T(8,128)S(1)}, f32[128,768]{1,0:T(8,128)S(1)}, bf16[768,256]{1,0:T(8,128)(2,1)S(1)}) custom-call(s32[2]{0:T(128)S(1)} %add_convert_fusion.3.flag_ref, f32[384,768]{1,0:T(8,128)S(1)} %get-tuple-element.30.on, f32[24,768]{1,0:T(8,128)S(1)} %get-tuple-element.31.sn, ...), custom_call_target="tpu_custom_call" | custom-call | tf_op jit(solution)/shard_map/pallas_call | solution.py:167
  108.0 2.9 %shard_map.79 = (bf16[768,128]{1,0:T(8,128)(2,1)S(1)}, f32[768,256]{1,0:T(8,128)S(1)}, bf16[768,256]{1,0:T(8,128)(2,1)S(1)}) custom-call(s32[2]{0:T(128)S(1)} %add_convert_fusion.3.flag_ref, bf16[3,1536,768]{2,1,0:T(8,128)(2,1)S(1)} %get-tuple-element.29.en, bf16[128,768]{1,0:T(8,128)(2,1)S(1)} %get-tuple-element.36.grad, ...), custom_call_target="tpu_custom_call" | custom-call | tf_op jit(solution)/shard_map/pallas_call | solution.py:202
  111.0 2.0 %collective-permute-start.23 = (bf16[768,256]{1,0:T(8,128)(2,1)S(1)}, bf16[768,256]{1,0:T(8,128)(2,1)S(1)}, u32[]{:S(2)}, u32[]{:S(2)}) collective-permute-start(bf16[768,256]{1,0:T(8,128)(2,1)S(1)} %get-tuple-element.48), channel_id=1, source_target_pairs={{0,2},{1,8},{2,0},{3,10},{4,6},{5,12},{6,4},{7,14},{8,1},{9,16},{1... | collective-permute-start | bytes 1179656 | tf_op jit(solution)/shard_map/ppermute | solution.py:35
  113.2 3.7 %shard_map.80 = (bf16[256,768]{1,0:T(8,128)(2,1)S(1)}, f32[16,768]{1,0:T(8,128)S(1)}, f32[256,768]{1,0:T(8,128)S(1)}, bf16[768,256]{1,0:T(8,128)(2,1)S(1)}, bf16[768,256]{1,0:T(8,128)(2,1)S(1)}) custom-call(s32[2]{0:T(128)S(1)} %add_convert_fusion.3.flag_ref, f32[384,768]{1,0:T(8,128)S(1)} %get-tuple-element.30.on, f32[24,768]{1,0:T(8,128)S(1)} %get-tuple-element.31.sn, ...), custom_call_target="tpu_custom_call" | custom-call | tf_op jit(solution)/shard_map/pallas_call | solution.py:167
  116.9 2.9 %shard_map.81 = (bf16[768,128]{1,0:T(8,128)(2,1)S(1)}, f32[768,256]{1,0:T(8,128)S(1)}, bf16[768,256]{1,0:T(8,128)(2,1)S(1)}) custom-call(s32[2]{0:T(128)S(1)} %add_convert_fusion.3.flag_ref, bf16[3,1536,768]{2,1,0:T(8,128)(2,1)S(1)} %get-tuple-element.29.en, bf16[256,768]{1,0:T(8,128)(2,1)S(1)} %get-tuple-element.41.grad, ...), custom_call_target="tpu_custom_call" | custom-call | tf_op jit(solution)/shard_map/pallas_call | solution.py:202
  119.8 0.7 collective-permute-start.24
  120.6 1.4 collective-permute-start.25
  121.9 2.9 %shard_map.82 = (bf16[768,128]{1,0:T(8,128)(2,1)S(1)}, f32[768,256]{1,0:T(8,128)S(1)}, bf16[768,256]{1,0:T(8,128)(2,1)S(1)}) custom-call(s32[2]{0:T(128)S(1)} %add_convert_fusion.3.flag_ref, bf16[3,1536,768]{2,1,0:T(8,128)(2,1)S(1)} %get-tuple-element.29.en, bf16[256,768]{1,0:T(8,128)(2,1)S(1)} %get-tuple-element.41.grad, ...), custom_call_target="tpu_custom_call" | custom-call | tf_op jit(solution)/shard_map/pallas_call | solution.py:202
  125.3 1.7 %collective-permute-start.21 = (bf16[768,128]{1,0:T(8,128)(2,1)S(1)}, bf16[768,128]{1,0:T(8,128)(2,1)S(1)}, u32[]{:S(2)}, u32[]{:S(2)}) collective-permute-start(bf16[768,128]{1,0:T(8,128)(2,1)S(1)} %get-tuple-element.45), channel_id=1, source_target_pairs={{0,8},{1,4},{2,10},{3,6},{4,1},{5,13},{6,3},{7,15},{8,0},{9,12},{1... | collective-permute-start | bytes 589832 | tf_op jit(solution)/shard_map/ppermute | solution.py:35
  127.2 3.4 %collective-permute-done.20 = bf16[768,128]{1,0:T(8,128)(2,1)S(1)} collective-permute-done((bf16[768,128]{1,0:T(8,128)(2,1)S(1)}, bf16[768,128]{1,0:T(8,128)(2,1)S(1)}, u32[]{:S(2)}, u32[]{:S(2)}) %collective-permute-start.20) | collective-permute-done | bytes 196640 | tf_op jit(solution)/shard_map/ppermute | solution.py:35
  130.6 1.2 collective-permute-start.27
  131.8 0.9 collective-permute-done.21
  132.7 1.2 collective-permute-start.28
  134.0 1.0 maximum_select_fusion
  135.1 0.8 collective-permute-start.29
  136.0 2.4 %collective-permute-done.27 = bf16[768,256]{1,0:T(8,128)(2,1)S(1)} collective-permute-done((bf16[768,256]{1,0:T(8,128)(2,1)S(1)}, bf16[768,256]{1,0:T(8,128)(2,1)S(1)}, u32[]{:S(2)}, u32[]{:S(2)}) %collective-permute-start.27) | collective-permute-done | bytes 393248 | tf_op jit(solution)/shard_map/ppermute | solution.py:35
  138.5 1.3 collective-permute-start.30
  139.9 2.7 %collective-permute-done.28 = bf16[768,256]{1,0:T(8,128)(2,1)S(1)} collective-permute-done((bf16[768,256]{1,0:T(8,128)(2,1)S(1)}, bf16[768,256]{1,0:T(8,128)(2,1)S(1)}, u32[]{:S(2)}, u32[]{:S(2)}) %collective-permute-start.28) | collective-permute-done | bytes 393248 | tf_op jit(solution)/shard_map/ppermute | solution.py:35
  142.6 4.2 %collective-permute-done.29 = bf16[768,256]{1,0:T(8,128)(2,1)S(1)} collective-permute-done((bf16[768,256]{1,0:T(8,128)(2,1)S(1)}, bf16[768,256]{1,0:T(8,128)(2,1)S(1)}, u32[]{:S(2)}, u32[]{:S(2)}) %collective-permute-start.29) | collective-permute-done | bytes 393248 | tf_op jit(solution)/shard_map/ppermute | solution.py:35
  146.8 4.2 %collective-permute-done.30 = bf16[768,256]{1,0:T(8,128)(2,1)S(1)} collective-permute-done((bf16[768,256]{1,0:T(8,128)(2,1)S(1)}, bf16[768,256]{1,0:T(8,128)(2,1)S(1)}, u32[]{:S(2)}, u32[]{:S(2)}) %collective-permute-start.30) | collective-permute-done | bytes 393248 | tf_op jit(solution)/shard_map/ppermute | solution.py:35
  151.0 1.4 maximum_select_fusion.1
  (81 shorter events, 6.0 us)
Async XLA Ops:
  0.6 65.6 %copy-start = (bf16[768,384]{1,0:T(8,128)(2,1)S(1)}, bf16[768,384]{1,0:T(8,128)(2,1)}, u32[]{:S(2)}) copy-start(bf16[768,384]{1,0:T(8,128)(2,1)} %qa.13) | copy-start | bytes 1769476
  0.6 29.3 %collective-permute-start.8 = (bf16[768,768]{1,0:T(8,128)(2,1)}, bf16[768,768]{1,0:T(8,128)(2,1)}, u32[]{:S(2)}, u32[]{:S(2)}) collective-permute-start(bf16[768,768]{1,0:T(8,128)(2,1)} %g0.1), channel_id=1, source_target_pairs={{0,2},{1,3},{2,0},{3,1},{4,6},{5,7},{6,4},{7,5},{8,10},{9,11},{10,... | collective-permute-start | bytes 3538952 | tf_op jit(solution)/shard_map/ppermute | solution.py:35
  3.7 27.0 %collective-permute-start.11 = (bf16[384,384]{1,0:T(8,128)(2,1)}, bf16[384,384]{1,0:T(8,128)(2,1)S(1)}, u32[]{:S(2)}, u32[]{:S(2)}) collective-permute-start(bf16[384,384]{1,0:T(8,128)(2,1)} %refs_0_.1), channel_id=1, source_target_pairs={{0,8},{1,9},{2,10},{3,11},{4,12},{5,13},{6,14},{7,15},{8,0},{9,1},... | collective-permute-start | bytes 884744 | tf_op jit(solution)/shard_map/ppermute | solution.py:35
  5.2 26.1 %collective-permute-start.10 = (bf16[384,384]{1,0:T(8,128)(2,1)}, bf16[384,384]{1,0:T(8,128)(2,1)S(1)}, u32[]{:S(2)}, u32[]{:S(2)}) collective-permute-start(bf16[384,384]{1,0:T(8,128)(2,1)} %refs_0_.1), channel_id=1, source_target_pairs={{0,4},{1,5},{2,6},{3,7},{4,0},{5,1},{6,2},{7,3},{8,12},{9,13},{10,... | collective-permute-start | bytes 884744 | tf_op jit(solution)/shard_map/ppermute | solution.py:35
  6.8 67.3 %collective-permute-start.7 = (bf16[768,768]{1,0:T(8,128)(2,1)}, bf16[768,768]{1,0:T(8,128)(2,1)}, u32[]{:S(2)}, u32[]{:S(2)}) collective-permute-start(bf16[768,768]{1,0:T(8,128)(2,1)} %g0.1), channel_id=1, source_target_pairs={{0,1},{1,0},{2,3},{3,2},{4,5},{5,4},{6,7},{7,6},{8,9},{9,8},{10,11... | collective-permute-start | bytes 3538952 | tf_op jit(solution)/shard_map/ppermute | solution.py:35
  30.0 46.3 %collective-permute-start.9 = (bf16[768,768]{1,0:T(8,128)(2,1)}, bf16[768,768]{1,0:T(8,128)(2,1)}, u32[]{:S(2)}, u32[]{:S(2)}) collective-permute-start(bf16[768,768]{1,0:T(8,128)(2,1)} %collective-permute-done.8.g2), channel_id=1, source_target_pairs={{0,1},{1,0},{2,3},{3,2},{4,5},{5,4},{6,7},{7,6},{8,9},{9,8},{10,11... | collective-permute-start | bytes 3538952 | tf_op jit(solution)/shard_map/ppermute | solution.py:35
  30.0 17.5 %collective-permute-start.1 = (bf16[768,384]{1,0:T(8,128)(2,1)}, bf16[768,384]{1,0:T(8,128)(2,1)S(1)}, u32[]{:S(2)}, u32[]{:S(2)}) collective-permute-start(bf16[768,384]{1,0:T(8,128)(2,1)} %param.6), channel_id=1, source_target_pairs={{1,4},{3,6},{4,1},{6,3},{9,12},{11,14},{12,9},{14,11},{17,20},{19,... | collective-permute-start | bytes 1769480 | tf_op jit(solution)/shard_map/ppermute | solution.py:35
  30.7 35.6 %copy-start.5 = (bf16[384,384]{1,0:T(8,128)(2,1)}, bf16[384,384]{1,0:T(8,128)(2,1)S(1)}, u32[]{:S(2)}) copy-start(bf16[384,384]{1,0:T(8,128)(2,1)S(1)} %collective-permute-done.11.refs_2_) | copy-start | bytes 884740
  30.7 21.9 %collective-permute-start.3 = (bf16[768,384]{1,0:T(8,128)(2,1)}, bf16[768,384]{1,0:T(8,128)(2,1)S(1)}, u32[]{:S(2)}, u32[]{:S(2)}) collective-permute-start(bf16[768,384]{1,0:T(8,128)(2,1)} %param.7), channel_id=1, source_target_pairs={{1,4},{3,6},{4,1},{6,3},{9,12},{11,14},{12,9},{14,11},{17,20},{19,... | collective-permute-start | bytes 1769480 | tf_op jit(solution)/shard_map/ppermute | solution.py:35
  31.4 34.8 %copy-start.7 = (bf16[384,384]{1,0:T(8,128)(2,1)}, bf16[384,384]{1,0:T(8,128)(2,1)S(1)}, u32[]{:S(2)}) copy-start(bf16[384,384]{1,0:T(8,128)(2,1)S(1)} %collective-permute-done.10.refs_1_) | copy-start | bytes 884740
  31.4 16.0 %collective-permute-start.13 = (bf16[384,384]{1,0:T(8,128)(2,1)}, bf16[384,384]{1,0:T(8,128)(2,1)S(1)}, u32[]{:S(2)}, u32[]{:S(2)}) collective-permute-start(bf16[384,384]{1,0:T(8,128)(2,1)} %refs_0_.1), channel_id=1, source_target_pairs={{0,16},{1,17},{2,18},{3,19},{4,20},{5,21},{6,22},{7,23},{8,24},{9,... | collective-permute-start | bytes 884744 | tf_op jit(solution)/shard_map/ppermute | solution.py:35
  47.4 19.7 %copy-start.9 = (bf16[384,384]{1,0:T(8,128)(2,1)}, bf16[384,384]{1,0:T(8,128)(2,1)S(1)}, u32[]{:S(2)}) copy-start(bf16[384,384]{1,0:T(8,128)(2,1)S(1)} %collective-permute-done.13.refs_4_) | copy-start | bytes 884740
  47.4 17.0 %collective-permute-start.15 = (bf16[384,384]{1,0:T(8,128)(2,1)S(1)}, bf16[384,384]{1,0:T(8,128)(2,1)S(1)}, u32[]{:S(2)}, u32[]{:S(2)}) collective-permute-start(bf16[384,384]{1,0:T(8,128)(2,1)S(1)} %collective-permute-done.11.refs_2_), channel_id=1, source_target_pairs={{0,16},{1,17},{2,18},{3,19},{4,20},{5,21},{6,22},{7,23},{8,24},{9,... | collective-permute-start | bytes 884744 | tf_op jit(solution)/shard_map/ppermute | solution.py:35
  47.4 18.8 %collective-permute-start.12 = (bf16[384,384]{1,0:T(8,128)(2,1)S(1)}, bf16[384,384]{1,0:T(8,128)(2,1)S(1)}, u32[]{:S(2)}, u32[]{:S(2)}) collective-permute-start(bf16[384,384]{1,0:T(8,128)(2,1)S(1)} %collective-permute-done.10.refs_1_), channel_id=1, source_target_pairs={{0,8},{1,9},{2,10},{3,11},{4,12},{5,13},{6,14},{7,15},{8,0},{9,1},... | collective-permute-start | bytes 884744 | tf_op jit(solution)/shard_map/ppermute | solution.py:35
  52.5 14.4 %copy-start.19 = (bf16[768,384]{1,0:T(8,128)(2,1)S(1)}, bf16[768,384]{1,0:T(8,128)(2,1)}, u32[]{:S(2)}) copy-start(bf16[768,384]{1,0:T(8,128)(2,1)} %param.7) | copy-start | bytes 1769476
  52.6 11.9 %copy-start.20 = (bf16[768,384]{1,0:T(8,128)(2,1)}, bf16[768,384]{1,0:T(8,128)(2,1)S(1)}, u32[]{:S(2)}) copy-start(bf16[768,384]{1,0:T(8,128)(2,1)S(1)} %collective-permute-done.3) | copy-start | bytes 1769476
  52.6 14.6 %collective-permute-start.14 = (bf16[384,384]{1,0:T(8,128)(2,1)S(1)}, bf16[384,384]{1,0:T(8,128)(2,1)S(1)}, u32[]{:S(2)}, u32[]{:S(2)}) collective-permute-start(bf16[384,384]{1,0:T(8,128)(2,1)S(1)} %collective-permute-done.13.refs_4_), channel_id=1, source_target_pairs={{0,4},{1,5},{2,6},{3,7},{4,0},{5,1},{6,2},{7,3},{8,12},{9,13},{10,... | collective-permute-start | bytes 884744 | tf_op jit(solution)/shard_map/ppermute | solution.py:35
  64.4 2.7 %copy-start.11 = (bf16[384,384]{1,0:T(8,128)(2,1)}, bf16[384,384]{1,0:T(8,128)(2,1)S(1)}, u32[]{:S(2)}) copy-start(bf16[384,384]{1,0:T(8,128)(2,1)S(1)} %collective-permute-done.15.refs_6_) | copy-start | bytes 884740
  64.4 9.0 %collective-permute-start.16 = (bf16[384,384]{1,0:T(8,128)(2,1)S(1)}, bf16[384,384]{1,0:T(8,128)(2,1)S(1)}, u32[]{:S(2)}, u32[]{:S(2)}) collective-permute-start(bf16[384,384]{1,0:T(8,128)(2,1)S(1)} %collective-permute-done.15.refs_6_), channel_id=1, source_target_pairs={{0,4},{1,5},{2,6},{3,7},{4,0},{5,1},{6,2},{7,3},{8,12},{9,13},{10,... | collective-permute-start | bytes 884744 | tf_op jit(solution)/shard_map/ppermute | solution.py:35
  65.0 2.0 %copy-start.21 = (bf16[768,384]{1,0:T(8,128)(2,1)S(1)}, bf16[768,384]{1,0:T(8,128)(2,1)}, u32[]{:S(2)}) copy-start(bf16[768,384]{1,0:T(8,128)(2,1)} %copy-done.20) | copy-start | bytes 1769476
  66.3 24.6 %collective-permute-start = (bf16[768,384]{1,0:T(8,128)(2,1)S(1)}, bf16[768,384]{1,0:T(8,128)(2,1)S(1)}, u32[]{:S(2)}, u32[]{:S(2)}) collective-permute-start(bf16[768,384]{1,0:T(8,128)(2,1)S(1)} %copy-done), channel_id=1, source_target_pairs={{1,4},{3,6},{4,1},{6,3},{9,12},{11,14},{12,9},{14,11},{17,20},{19,... | collective-permute-start | bytes 1769480 | tf_op jit(solution)/shard_map/ppermute | solution.py:35
  67.8 25.1 %collective-permute-start.2 = (bf16[768,384]{1,0:T(8,128)(2,1)S(1)}, bf16[768,384]{1,0:T(8,128)(2,1)S(1)}, u32[]{:S(2)}, u32[]{:S(2)}) collective-permute-start(bf16[768,384]{1,0:T(8,128)(2,1)S(1)} %broadcast_select_fusion.1.refs_0_.ko), channel_id=1, source_target_pairs={{0,1},{1,0},{2,3},{3,2},{4,5},{5,4},{6,7},{7,6},{8,9},{9,8},{10,11... | collective-permute-start | bytes 1769480 | tf_op jit(solution)/shard_map/ppermute | solution.py:35
  74.1 18.8 %collective-permute-start.4 = (bf16[768,384]{1,0:T(8,128)(2,1)S(1)}, bf16[768,384]{1,0:T(8,128)(2,1)S(1)}, u32[]{:S(2)}, u32[]{:S(2)}) collective-permute-start(bf16[768,384]{1,0:T(8,128)(2,1)S(1)} %broadcast_select_fusion.refs_2_.vo), channel_id=1, source_target_pairs={{0,1},{1,0},{2,3},{3,2},{4,5},{5,4},{6,7},{7,6},{8,9},{9,8},{10,11... | collective-permute-start | bytes 1769480 | tf_op jit(solution)/shard_map/ppermute | solution.py:35
  74.1 26.1 %collective-permute-start.5 = (bf16[768,384]{1,0:T(8,128)(2,1)S(1)}, bf16[768,384]{1,0:T(8,128)(2,1)}, u32[]{:S(2)}, u32[]{:S(2)}) collective-permute-start(bf16[768,384]{1,0:T(8,128)(2,1)S(1)} %broadcast_select_fusion.1.refs_0_.ko), channel_id=1, source_target_pairs={{0,2},{1,8},{2,0},{3,10},{4,6},{5,12},{6,4},{7,14},{8,1},{9,16},{1... | collective-permute-start | bytes 1769480 | tf_op jit(solution)/shard_map/ppermute | solution.py:35
  76.2 24.0 %collective-permute-start.6 = (bf16[768,384]{1,0:T(8,128)(2,1)S(1)}, bf16[768,384]{1,0:T(8,128)(2,1)}, u32[]{:S(2)}, u32[]{:S(2)}) collective-permute-start(bf16[768,384]{1,0:T(8,128)(2,1)S(1)} %broadcast_select_fusion.refs_2_.vo), channel_id=1, source_target_pairs={{0,2},{1,8},{2,0},{3,10},{4,6},{5,12},{6,4},{7,14},{8,1},{9,16},{1... | collective-permute-start | bytes 1769480 | tf_op jit(solution)/shard_map/ppermute | solution.py:35
  76.4 1.3 copy-start.1
  77.7 1.0 copy-start.4
  78.6 1.0 copy-start.6
  79.6 1.0 copy-start.8
  80.6 1.0 copy-start.10
  81.5 1.0 copy-start.12
  82.5 1.0 copy-start.14
  83.5 1.0 copy-start.16
  90.9 14.3 %collective-permute-start.17 = (bf16[128,768]{1,0:T(8,128)(2,1)}, bf16[128,768]{1,0:T(8,128)(2,1)}, u32[]{:S(2)}, u32[]{:S(2)}) collective-permute-start(bf16[128,768]{1,0:T(8,128)(2,1)} %get-tuple-element.35.ga), channel_id=1, source_target_pairs={{0,2},{1,4},{2,0},{3,6},{4,1},{5,7},{6,3},{7,5},{8,10},{9,12},{10,... | collective-permute-start | bytes 589832 | tf_op jit(solution)/shard_map/ppermute | solution.py:35
  100.2 4.9 %copy-start.3 = (bf16[256,768]{1,0:T(8,128)(2,1)S(1)}, bf16[256,768]{1,0:T(8,128)(2,1)}, u32[]{:S(2)}) copy-start(bf16[256,768]{1,0:T(8,128)(2,1)} %copy-done.2) | copy-start | bytes 1179652
  105.1 8.1 %collective-permute-start.18 = (bf16[256,768]{1,0:T(8,128)(2,1)S(1)}, bf16[256,768]{1,0:T(8,128)(2,1)S(1)}, u32[]{:S(2)}, u32[]{:S(2)}) collective-permute-start(bf16[256,768]{1,0:T(8,128)(2,1)S(1)} %copy-done.3), channel_id=1, source_target_pairs={{0,2},{1,4},{2,0},{3,6},{4,1},{5,7},{6,3},{7,5},{8,10},{9,12},{10,... | collective-permute-start | bytes 1179656 | tf_op jit(solution)/shard_map/ppermute | solution.py:35
  111.0 13.9 %collective-permute-start.22 = (bf16[768,256]{1,0:T(8,128)(2,1)S(1)}, bf16[768,256]{1,0:T(8,128)(2,1)S(1)}, u32[]{:S(2)}, u32[]{:S(2)}) collective-permute-start(bf16[768,256]{1,0:T(8,128)(2,1)S(1)} %get-tuple-element.47), channel_id=1, source_target_pairs={{0,1},{1,0},{2,3},{3,2},{4,5},{5,4},{6,7},{7,6},{8,9},{9,8},{10,11... | collective-permute-start | bytes 1179656 | tf_op jit(solution)/shard_map/ppermute | solution.py:35
  111.0 14.2 %collective-permute-start.23 = (bf16[768,256]{1,0:T(8,128)(2,1)S(1)}, bf16[768,256]{1,0:T(8,128)(2,1)S(1)}, u32[]{:S(2)}, u32[]{:S(2)}) collective-permute-start(bf16[768,256]{1,0:T(8,128)(2,1)S(1)} %get-tuple-element.48), channel_id=1, source_target_pairs={{0,2},{1,8},{2,0},{3,10},{4,6},{5,12},{6,4},{7,14},{8,1},{9,16},{1... | collective-permute-start | bytes 1179656 | tf_op jit(solution)/shard_map/ppermute | solution.py:35
  113.0 14.1 %collective-permute-start.19 = (bf16[768,128]{1,0:T(8,128)(2,1)S(1)}, bf16[768,128]{1,0:T(8,128)(2,1)S(1)}, u32[]{:S(2)}, u32[]{:S(2)}) collective-permute-start(bf16[768,128]{1,0:T(8,128)(2,1)S(1)} %get-tuple-element.39), channel_id=1, source_target_pairs={{0,8},{1,4},{2,10},{3,6},{4,1},{5,13},{6,3},{7,15},{8,0},{9,12},{1... | collective-permute-start | bytes 589832 | tf_op jit(solution)/shard_map/ppermute | solution.py:35
  119.8 15.1 %collective-permute-start.24 = (bf16[768,256]{1,0:T(8,128)(2,1)S(1)}, bf16[768,256]{1,0:T(8,128)(2,1)S(1)}, u32[]{:S(2)}, u32[]{:S(2)}) collective-permute-start(bf16[768,256]{1,0:T(8,128)(2,1)S(1)} %get-tuple-element.50), channel_id=1, source_target_pairs={{0,1},{1,0},{2,3},{3,2},{4,5},{5,4},{6,7},{7,6},{8,9},{9,8},{10,11... | collective-permute-start | bytes 1179656 | tf_op jit(solution)/shard_map/ppermute | solution.py:35
  120.6 14.4 %collective-permute-start.25 = (bf16[768,256]{1,0:T(8,128)(2,1)S(1)}, bf16[768,256]{1,0:T(8,128)(2,1)S(1)}, u32[]{:S(2)}, u32[]{:S(2)}) collective-permute-start(bf16[768,256]{1,0:T(8,128)(2,1)S(1)} %get-tuple-element.51), channel_id=1, source_target_pairs={{0,2},{1,8},{2,0},{3,10},{4,6},{5,12},{6,4},{7,14},{8,1},{9,16},{1... | collective-permute-start | bytes 1179656 | tf_op jit(solution)/shard_map/ppermute | solution.py:35
  124.9 5.7 %collective-permute-start.20 = (bf16[768,128]{1,0:T(8,128)(2,1)S(1)}, bf16[768,128]{1,0:T(8,128)(2,1)S(1)}, u32[]{:S(2)}, u32[]{:S(2)}) collective-permute-start(bf16[768,128]{1,0:T(8,128)(2,1)S(1)} %get-tuple-element.44), channel_id=1, source_target_pairs={{0,8},{1,4},{2,10},{3,6},{4,1},{5,13},{6,3},{7,15},{8,0},{9,12},{1... | collective-permute-start | bytes 589832 | tf_op jit(solution)/shard_map/ppermute | solution.py:35
  125.3 7.4 %collective-permute-start.21 = (bf16[768,128]{1,0:T(8,128)(2,1)S(1)}, bf16[768,128]{1,0:T(8,128)(2,1)S(1)}, u32[]{:S(2)}, u32[]{:S(2)}) collective-permute-start(bf16[768,128]{1,0:T(8,128)(2,1)S(1)} %get-tuple-element.45), channel_id=1, source_target_pairs={{0,8},{1,4},{2,10},{3,6},{4,1},{5,13},{6,3},{7,15},{8,0},{9,12},{1... | collective-permute-start | bytes 589832 | tf_op jit(solution)/shard_map/ppermute | solution.py:35
  127.2 8.8 %collective-permute-start.26 = (bf16[768,256]{1,0:T(8,128)(2,1)S(1)}, bf16[768,256]{1,0:T(8,128)(2,1)S(1)}, u32[]{:S(2)}, u32[]{:S(2)}) collective-permute-start(bf16[768,256]{1,0:T(8,128)(2,1)S(1)} %get-tuple-element.53), channel_id=1, source_target_pairs={{0,1},{1,0},{2,3},{3,2},{4,5},{5,4},{6,7},{7,6},{8,9},{9,8},{10,11... | collective-permute-start | bytes 1179656 | tf_op jit(solution)/shard_map/ppermute | solution.py:35
  130.6 7.8 %collective-permute-start.27 = (bf16[768,256]{1,0:T(8,128)(2,1)S(1)}, bf16[768,256]{1,0:T(8,128)(2,1)S(1)}, u32[]{:S(2)}, u32[]{:S(2)}) collective-permute-start(bf16[768,256]{1,0:T(8,128)(2,1)S(1)} %get-tuple-element.54), channel_id=1, source_target_pairs={{0,2},{1,8},{2,0},{3,10},{4,6},{5,12},{6,4},{7,14},{8,1},{9,16},{1... | collective-permute-start | bytes 1179656 | tf_op jit(solution)/shard_map/ppermute | solution.py:35
  132.7 9.9 %collective-permute-start.28 = (bf16[768,256]{1,0:T(8,128)(2,1)S(1)}, bf16[768,256]{1,0:T(8,128)(2,1)S(1)}, u32[]{:S(2)}, u32[]{:S(2)}) collective-permute-start(bf16[768,256]{1,0:T(8,128)(2,1)S(1)} %add_convert_fusion.2), channel_id=1, source_target_pairs={{0,2},{1,4},{2,0},{3,6},{4,1},{5,7},{6,3},{7,5},{8,10},{9,12},{10,... | collective-permute-start | bytes 1179656 | tf_op jit(solution)/shard_map/ppermute | solution.py:35
  135.1 11.7 %collective-permute-start.29 = (bf16[768,256]{1,0:T(8,128)(2,1)S(1)}, bf16[768,256]{1,0:T(8,128)(2,1)S(1)}, u32[]{:S(2)}, u32[]{:S(2)}) collective-permute-start(bf16[768,256]{1,0:T(8,128)(2,1)S(1)} %add_convert_fusion.1), channel_id=1, source_target_pairs={{0,2},{1,4},{2,0},{3,6},{4,1},{5,7},{6,3},{7,5},{8,10},{9,12},{10,... | collective-permute-start | bytes 1179656 | tf_op jit(solution)/shard_map/ppermute | solution.py:35
  138.5 12.5 %collective-permute-start.30 = (bf16[768,256]{1,0:T(8,128)(2,1)S(1)}, bf16[768,256]{1,0:T(8,128)(2,1)S(1)}, u32[]{:S(2)}, u32[]{:S(2)}) collective-permute-start(bf16[768,256]{1,0:T(8,128)(2,1)S(1)} %add_convert_fusion), channel_id=1, source_target_pairs={{0,2},{1,4},{2,0},{3,6},{4,1},{5,7},{6,3},{7,5},{8,10},{9,12},{10,... | collective-permute-start | bytes 1179656 | tf_op jit(solution)/shard_map/ppermute | solution.py:35
  (5 other events, 4.0 us)

commit v8 on v7

--- a/solution.py
+++ b/solution.py
@@ -12,6 +12,7 @@
 HD = 128
 VT = 8
 AXES = ("tm", "head")
+EARLY = (1, 2, 4, 6)
 LIMIT = 24 << 20
 BIG = 768
 SMALL = 64
@@ -39,11 +40,24 @@
     return join(block.reshape(block.shape[0] // 8, 8, block.shape[1]), axis=0)
 
 
-def soften_kernel(parts, tile, flag_ref, qa, qb, *refs):
+def soften_kernel(parts, tile, staged, flag_ref, qa, qb, *refs):
+    rows = qa.shape[0]
     keys, values = refs[:parts], refs[parts : 2 * parts]
-    e_ref, o_ref, stat_ref, vt = refs[2 * parts : 2 * parts + 4]
-    held = refs[2 * parts + 4 :]
-    rows = qa.shape[0]
+    sources, refs = refs[2 * parts : 2 * parts + staged], refs[2 * parts + staged :]
+    e_ref, o_ref, stat_ref = refs[:3]
+    targets, refs = refs[3 : 3 + staged], refs[3 + staged :]
+    vt, held = refs[0], refs[1 : 1 + rows // tile]
+    copies = [
+        pltpu.make_async_copy(source, target, refs[-1].at[i])
+        for i, (source, target) in enumerate(zip(sources, targets))
+    ]
+    if staged:
+
+        @pl.when(pl.program_id(0) == 0)
+        def _():
+            for c in copies:
+                c.start()
+
     factor = math.log2(math.e) / math.sqrt(HD)
     query = jnp.where(flag_ref[1] > 0, qa[...], qb[...])
 
@@ -86,30 +100,41 @@
         if n > 0:
             gather(n - 1)
     gather(count - 1)
-
-
-def soften(flags, queries, keys, values):
+    if staged:
+
+        @pl.when(pl.program_id(0) == pl.num_programs(0) - 1)
+        def _():
+            for c in copies:
+                c.wait()
+
+
+def soften(flags, queries, keys, values, staged=()):
     rows, width = queries[0].shape
     parts, heads, tile = len(keys), width // HD, 256
     spec = pl.BlockSpec((rows, HD), lambda h: (0, h))
     return pl.pallas_call(
-        functools.partial(soften_kernel, parts, tile),
+        functools.partial(soften_kernel, parts, tile, len(staged)),
         grid=(heads,),
-        in_specs=[pl.BlockSpec(memory_space=pltpu.SMEM)] + [spec] * (2 + 2 * parts),
+        in_specs=[pl.BlockSpec(memory_space=pltpu.SMEM)]
+        + [spec] * (2 + 2 * parts)
+        + [pl.BlockSpec(memory_space=pl.ANY)] * len(staged),
         out_specs=[
             pl.BlockSpec((1, parts * rows, rows), lambda h: (h, 0, 0)),
             pl.BlockSpec((HD, rows), lambda h: (h, 0)),
             pl.BlockSpec((8, rows), lambda h: (h, 0)),
-        ],
+        ]
+        + [pl.BlockSpec(memory_space=pl.ANY)] * len(staged),
         out_shape=[
             jax.ShapeDtypeStruct((heads, parts * rows, rows), jnp.bfloat16),
             jax.ShapeDtypeStruct((heads * HD, rows), jnp.float32),
             jax.ShapeDtypeStruct((heads * 8, rows), jnp.float32),
-        ],
+        ]
+        + [jax.ShapeDtypeStruct(x.shape, x.dtype) for x in staged],
         scratch_shapes=[pltpu.VMEM((HD, parts * rows), jnp.bfloat16)]
-        + [pltpu.VMEM((parts * rows, tile), jnp.float32)] * (rows // tile),
+        + [pltpu.VMEM((parts * rows, tile), jnp.float32)] * (rows // tile)
+        + [pltpu.SemaphoreType.DMA((len(staged),))] * bool(staged),
         compiler_params=pltpu.CompilerParams(vmem_limit_bytes=LIMIT),
-    )(flags, *queries, *keys, *values)
+    )(flags, *queries, *keys, *values, *staged)
 
 
 def slab_terms(weight, part_grad, part_inner, query, k, v, out):
@@ -301,7 +326,13 @@
         shards = [w_out, w0y, w1, w1y, w2, w2y, w3, w3y]
     far_k, far_v = send(keys, far_route), send(values, far_route)
     side_k, side_v = send(keys, side_route), send(values, side_route)
-    near = soften(flags, query_pair, (keys, side_k), (values, side_v))
+    early = [*grads[1:3], *[shards[i] for i in EARLY]] if square else []
+    near = soften(flags, query_pair, (keys, side_k), (values, side_v), early)
+    near, early = near[:3], near[3:]
+    if square:
+        grads[1:3] = early[:2]
+        for i, shard in zip(EARLY, early[2:]):
+            shards[i] = shard
     if square:
         attn_grads = project(
             jnp.stack([t // 2, y, h]).astype(jnp.int32), grads, shards, rows, width

time: 153 us -> 137 us (0.90)
  local copies, waits for them, and re-layouts: 11.3 us -> 0.9 us
  starting transfers between devices: 40.2 us -> 29.9 us
  waiting for transfers between devices: 63.5 us -> 69.4 us
    unnamed x44 -> x12, local copies, waits for them, and re-layouts: 11.2 us -> 0.73 us
    ppermute x31, starting transfers between devices: 40.2 us -> 29.9 us  [exchange(): return lax.ppermute(block, AXES, pairs)]
    ppermute x31, waiting for transfers between devices: 63.5 us -> 69.4 us  [exchange(): return lax.ppermute(block, AXES, pairs)]
  transfers between devices with their start and end apart: 31 -> 31, of which waited for: 10 -> 14; matrix products, arithmetic and copies ran while one was open for 2% -> 2% of each run, Pallas kernels for 21% -> 23%
where the time goes in v8:
time: 137 us; the launch traced here: 136 us
  waiting for transfers between devices  69.4 us (51%)
  Pallas kernels  30.9 us (23%)
  starting transfers between devices  29.9 us (22%)
  other arithmetic  4.16 us (3%)
    ppermute x31, waiting for transfers between devices, exchange(): return lax.ppermute(block, AXES, pairs)  69.4 us
    ppermute x31, starting transfers between devices, exchange(): return lax.ppermute(block, AXES, pairs)  29.9 us
    pallas_call x2, Pallas kernels, soften(): pl.pallas_call(functools.partial(soften_kernel, parts, tile, len(staged))...  12.2 us
    pallas_call x3, Pallas kernels, backward_near(): pl.pallas_call(near_kernel, grid=(1,), in_specs=[pl.BlockSpec(memory_spac...  8.79 us
    pallas_call x2, Pallas kernels, backward_far(): pl.pallas_call(functools.partial(far_kernel, first, count), in_specs=[pl....  6.31 us
    pallas_call x1, Pallas kernels, project(): pl.pallas_call(project_kernel, in_specs=[pl.BlockSpec(memory_space=pltpu....  3.61 us
  transfers between devices with their start and end apart: 31, of which 14 were waited for; matrix products, arithmetic and copies ran while one was open for 2% of the time, Pallas kernels for 23%

profile of v8, /device:TPU:0, one launch (start us, length us, event | category | flops | bytes accessed | tf_op | source)
XLA Modules:
  0.0 136.2 jit_solution(8108843241526576762)
XLA Ops:
  0.6 3.0 %collective-permute-start.6 = (bf16[768,768]{1,0:T(8,128)(2,1)}, bf16[768,768]{1,0:T(8,128)(2,1)}, u32[]{:S(2)}, u32[]{:S(2)}) collective-permute-start(bf16[768,768]{1,0:T(8,128)(2,1)} %g0.1), channel_id=1, source_target_pairs={{0,2},{1,3},{2,0},{3,1},{4,6},{5,7},{6,4},{7,5},{8,10},{9,11},{10,... | collective-permute-start | bytes 3538952 | tf_op jit(solution)/shard_map/ppermute | solution.py:36
  3.7 0.7 collective-permute-start.1
  4.4 1.6 %collective-permute-start.8 = (bf16[384,384]{1,0:T(8,128)(2,1)}, bf16[384,384]{1,0:T(8,128)(2,1)}, u32[]{:S(2)}, u32[]{:S(2)}) collective-permute-start(bf16[384,384]{1,0:T(8,128)(2,1)} %refs_0_.1), channel_id=1, source_target_pairs={{0,8},{1,9},{2,10},{3,11},{4,12},{5,13},{6,14},{7,15},{8,0},{9,1},... | collective-permute-start | bytes 884744 | tf_op jit(solution)/shard_map/ppermute | solution.py:36
  6.0 2.7 %collective-permute-start.7 = (bf16[384,384]{1,0:T(8,128)(2,1)}, bf16[384,384]{1,0:T(8,128)(2,1)}, u32[]{:S(2)}, u32[]{:S(2)}) collective-permute-start(bf16[384,384]{1,0:T(8,128)(2,1)} %refs_0_.1), channel_id=1, source_target_pairs={{0,4},{1,5},{2,6},{3,7},{4,0},{5,1},{6,2},{7,3},{8,12},{9,13},{10,... | collective-permute-start | bytes 884744 | tf_op jit(solution)/shard_map/ppermute | solution.py:36
  8.8 1.5 %collective-permute-start.3 = (bf16[768,384]{1,0:T(8,128)(2,1)}, bf16[768,384]{1,0:T(8,128)(2,1)}, u32[]{:S(2)}, u32[]{:S(2)}) collective-permute-start(bf16[768,384]{1,0:T(8,128)(2,1)} %param.7), channel_id=1, source_target_pairs={{1,4},{3,6},{4,1},{6,3},{9,12},{11,14},{12,9},{14,11},{17,20},{19,... | collective-permute-start | bytes 1769480 | tf_op jit(solution)/shard_map/ppermute | solution.py:36
  10.2 2.5 %collective-permute-done.8.refs_7_ = bf16[384,384]{1,0:T(8,128)(2,1)} collective-permute-done((bf16[384,384]{1,0:T(8,128)(2,1)}, bf16[384,384]{1,0:T(8,128)(2,1)}, u32[]{:S(2)}, u32[]{:S(2)}) %collective-permute-start.8) | collective-permute-done | bytes 294944 | tf_op jit(solution)/shard_map/ppermute | solution.py:36
  12.8 0.7 collective-permute-start
  13.4 8.1 %collective-permute-done.7.refs_6_ = bf16[384,384]{1,0:T(8,128)(2,1)} collective-permute-done((bf16[384,384]{1,0:T(8,128)(2,1)}, bf16[384,384]{1,0:T(8,128)(2,1)}, u32[]{:S(2)}, u32[]{:S(2)}) %collective-permute-start.7) | collective-permute-done | bytes 294944 | tf_op jit(solution)/shard_map/ppermute | solution.py:36
  21.6 2.6 %collective-permute-start.9 = (bf16[384,384]{1,0:T(8,128)(2,1)}, bf16[384,384]{1,0:T(8,128)(2,1)}, u32[]{:S(2)}, u32[]{:S(2)}) collective-permute-start(bf16[384,384]{1,0:T(8,128)(2,1)} %refs_0_.1), channel_id=1, source_target_pairs={{0,16},{1,17},{2,18},{3,19},{4,20},{5,21},{6,22},{7,23},{8,24},{9,... | collective-permute-start | bytes 884744 | tf_op jit(solution)/shard_map/ppermute | solution.py:36
  24.2 5.8 %collective-permute-done.6.refs_5_ = bf16[768,768]{1,0:T(8,128)(2,1)} collective-permute-done((bf16[768,768]{1,0:T(8,128)(2,1)}, bf16[768,768]{1,0:T(8,128)(2,1)}, u32[]{:S(2)}, u32[]{:S(2)}) %collective-permute-start.6) | collective-permute-done | bytes 1179680 | tf_op jit(solution)/shard_map/ppermute | solution.py:36
  30.0 1.1 broadcast_select_fusion.1.refs_0_.ko
  31.1 7.4 %collective-permute-done.9.refs_8_ = bf16[384,384]{1,0:T(8,128)(2,1)} collective-permute-done((bf16[384,384]{1,0:T(8,128)(2,1)}, bf16[384,384]{1,0:T(8,128)(2,1)}, u32[]{:S(2)}, u32[]{:S(2)}) %collective-permute-start.9) | collective-permute-done | bytes 294944 | tf_op jit(solution)/shard_map/ppermute | solution.py:36
  38.7 1.6 %collective-permute-start.4 = (bf16[768,384]{1,0:T(8,128)(2,1)S(1)}, bf16[768,384]{1,0:T(8,128)(2,1)S(1)}, u32[]{:S(2)}, u32[]{:S(2)}) collective-permute-start(bf16[768,384]{1,0:T(8,128)(2,1)S(1)} %broadcast_select_fusion.refs_2_.vo), channel_id=1, source_target_pairs={{0,1},{1,0},{2,3},{3,2},{4,5},{5,4},{6,7},{7,6},{8,9},{9,8},{10,11... | collective-permute-start | bytes 1769480 | tf_op jit(solution)/shard_map/ppermute | solution.py:36
  40.3 14.4 %collective-permute-done.10.refs_9_ = bf16[384,384]{1,0:T(8,128)(2,1)} collective-permute-done((bf16[384,384]{1,0:T(8,128)(2,1)}, bf16[384,384]{1,0:T(8,128)(2,1)}, u32[]{:S(2)}, u32[]{:S(2)}) %collective-permute-start.10) | collective-permute-done | bytes 294944 | tf_op jit(solution)/shard_map/ppermute | solution.py:36
  54.6 7.9 %collective-permute-done.14.refs_3_ = bf16[384,384]{1,0:T(8,128)(2,1)S(1)} collective-permute-done((bf16[384,384]{1,0:T(8,128)(2,1)}, bf16[384,384]{1,0:T(8,128)(2,1)S(1)}, u32[]{:S(2)}, u32[]{:S(2)}) %collective-permute-start.14) | collective-permute-done | bytes 294944 | tf_op jit(solution)/shard_map/ppermute | solution.py:36
  62.6 0.7 copy-done.3
  63.3 0.5 collective-permute-start.11
  63.8 1.5 %collective-permute-start.12 = (bf16[768,384]{1,0:T(8,128)(2,1)S(1)}, bf16[768,384]{1,0:T(8,128)(2,1)}, u32[]{:S(2)}, u32[]{:S(2)}) collective-permute-start(bf16[768,384]{1,0:T(8,128)(2,1)S(1)} %broadcast_select_fusion.refs_2_.vo), channel_id=1, source_target_pairs={{0,2},{1,8},{2,0},{3,10},{4,6},{5,12},{6,4},{7,14},{8,1},{9,16},{1... | collective-permute-start | bytes 1769480 | tf_op jit(solution)/shard_map/ppermute | solution.py:36
  65.4 2.0 %collective-permute-start.16 = (bf16[384,384]{1,0:T(8,128)(2,1)}, bf16[384,384]{1,0:T(8,128)(2,1)}, u32[]{:S(2)}, u32[]{:S(2)}) collective-permute-start(bf16[384,384]{1,0:T(8,128)(2,1)} %collective-permute-done.10.refs_9_), channel_id=1, source_target_pairs={{0,4},{1,5},{2,6},{3,7},{4,0},{5,1},{6,2},{7,3},{8,12},{9,13},{10,... | collective-permute-start | bytes 884744 | tf_op jit(solution)/shard_map/ppermute | solution.py:36
  67.5 7.4 %shard_map.76 = (bf16[3,1536,768]{2,1,0:T(8,128)(2,1)S(1)}, f32[384,768]{1,0:T(8,128)S(1)}, f32[24,768]{1,0:T(8,128)S(1)}, bf16[768,768]{1,0:T(8,128)(2,1)S(1)},...) custom-call(s32[2]{0:T(128)S(1)} %add_convert_fusion.3.flag_ref, ...), custom_call_target="tpu_custom_call" | custom-call | tf_op jit(solution)/shard_map/pallas_call | solution.py:115
  74.9 0.6 collective-permute-done.15.refs_5_
  75.5 3.8 %collective-permute-done.16.refs_7_ = bf16[384,384]{1,0:T(8,128)(2,1)} collective-permute-done((bf16[384,384]{1,0:T(8,128)(2,1)}, bf16[384,384]{1,0:T(8,128)(2,1)}, u32[]{:S(2)}, u32[]{:S(2)}) %collective-permute-start.16) | collective-permute-done | bytes 294944 | tf_op jit(solution)/shard_map/ppermute | solution.py:36
  79.3 3.6 %project.1 = (bf16[128,768]{1,0:T(8,128)(2,1)S(1)}, bf16[256,768]{1,0:T(8,128)(2,1)S(1)}) custom-call(s32[3]{0:T(128)S(1)} %pad_add_fusion.place_ref, bf16[768,768]{1,0:T(8,128)(2,1)S(1)} %copy-done.1, bf16[768,768]{1,0:T(8,128)(2,1)S(1)} %get-tuple-element.41.g1, bf16[768,768]{1,0:T(8,128)(2,1)S(1)} %get-tuple-element.42.g2, ...), custom_call_target="tpu_custom_call" | custom-call | tf_op jit(solution)/shard_map/project/pallas_call | solution.py:269
  82.9 0.6 collective-permute-start.17
  83.5 4.9 %shard_map.77 = (bf16[3,768,768]{2,1,0:T(8,128)(2,1)S(1)}, f32[384,768]{1,0:T(8,128)S(1)}, f32[24,768]{1,0:T(8,128)S(1)}) custom-call(s32[2]{0:T(128)S(1)} %add_convert_fusion.3.flag_ref, bf16[768,384]{1,0:T(8,128)(2,1)S(1)} %copy-done, bf16[768,384]{1,0:T(8,128)(2,1)S(1)} %collective-permute-done.qb, bf16[768,384]{1,0:T(8,128)(2,1)} %collective-permute-done.11.refs_0_.kz, ...), custom_call_target="tpu_custom_call" | custom-call | tf_op jit(solution)/shard_map/pallas_call | solution.py:115
  88.4 1.5 %collective-permute-start.18 = (bf16[256,768]{1,0:T(8,128)(2,1)S(1)}, bf16[256,768]{1,0:T(8,128)(2,1)S(1)}, u32[]{:S(2)}, u32[]{:S(2)}) collective-permute-start(bf16[256,768]{1,0:T(8,128)(2,1)S(1)} %get-tuple-element.52.ga), channel_id=1, source_target_pairs={{0,2},{1,4},{2,0},{3,6},{4,1},{5,7},{6,3},{7,5},{8,10},{9,12},{10,... | collective-permute-start | bytes 1179656 | tf_op jit(solution)/shard_map/ppermute | solution.py:36
  90.0 2.6 %shard_map.78 = (bf16[128,768]{1,0:T(8,128)(2,1)S(1)}, f32[8,768]{1,0:T(8,128)S(1)}, f32[128,768]{1,0:T(8,128)S(1)}, bf16[768,256]{1,0:T(8,128)(2,1)S(1)}) custom-call(s32[2]{0:T(128)S(1)} %add_convert_fusion.3.flag_ref, f32[384,768]{1,0:T(8,128)S(1)} %get-tuple-element.36.on, f32[24,768]{1,0:T(8,128)S(1)} %get-tuple-element.37.sn, ...), custom_call_target="tpu_custom_call" | custom-call | tf_op jit(solution)/shard_map/pallas_call | solution.py:192
  92.5 2.9 %shard_map.79 = (bf16[768,128]{1,0:T(8,128)(2,1)S(1)}, f32[768,256]{1,0:T(8,128)S(1)}, bf16[768,256]{1,0:T(8,128)(2,1)S(1)}) custom-call(s32[2]{0:T(128)S(1)} %add_convert_fusion.3.flag_ref, bf16[3,1536,768]{2,1,0:T(8,128)(2,1)S(1)} %get-tuple-element.35.en, bf16[128,768]{1,0:T(8,128)(2,1)S(1)} %get-tuple-element.48.grad, ...), custom_call_target="tpu_custom_call" | custom-call | tf_op jit(solution)/shard_map/pallas_call | solution.py:227
  95.6 0.6 collective-permute-start.23
  96.2 1.5 %collective-permute-start.19 = (bf16[768,128]{1,0:T(8,128)(2,1)S(1)}, bf16[768,128]{1,0:T(8,128)(2,1)S(1)}, u32[]{:S(2)}, u32[]{:S(2)}) collective-permute-start(bf16[768,128]{1,0:T(8,128)(2,1)S(1)} %get-tuple-element.51), channel_id=1, source_target_pairs={{0,8},{1,4},{2,10},{3,6},{4,1},{5,13},{6,3},{7,15},{8,0},{9,12},{1... | collective-permute-start | bytes 589832 | tf_op jit(solution)/shard_map/ppermute | solution.py:36
  97.7 3.7 %shard_map.80 = (bf16[256,768]{1,0:T(8,128)(2,1)S(1)}, f32[16,768]{1,0:T(8,128)S(1)}, f32[256,768]{1,0:T(8,128)S(1)}, bf16[768,256]{1,0:T(8,128)(2,1)S(1)}, bf16[768,256]{1,0:T(8,128)(2,1)S(1)}) custom-call(s32[2]{0:T(128)S(1)} %add_convert_fusion.3.flag_ref, f32[384,768]{1,0:T(8,128)S(1)} %get-tuple-element.36.on, f32[24,768]{1,0:T(8,128)S(1)} %get-tuple-element.37.sn, ...), custom_call_target="tpu_custom_call" | custom-call | tf_op jit(solution)/shard_map/pallas_call | solution.py:192
  101.4 2.9 %shard_map.81 = (bf16[768,128]{1,0:T(8,128)(2,1)S(1)}, f32[768,256]{1,0:T(8,128)S(1)}, bf16[768,256]{1,0:T(8,128)(2,1)S(1)}) custom-call(s32[2]{0:T(128)S(1)} %add_convert_fusion.3.flag_ref, bf16[3,1536,768]{2,1,0:T(8,128)(2,1)S(1)} %get-tuple-element.35.en, bf16[256,768]{1,0:T(8,128)(2,1)S(1)} %get-tuple-element.53.grad, ...), custom_call_target="tpu_custom_call" | custom-call | tf_op jit(solution)/shard_map/pallas_call | solution.py:227
  104.4 0.6 collective-permute-start.25
  105.1 2.9 %shard_map.82 = (bf16[768,128]{1,0:T(8,128)(2,1)S(1)}, f32[768,256]{1,0:T(8,128)S(1)}, bf16[768,256]{1,0:T(8,128)(2,1)S(1)}) custom-call(s32[2]{0:T(128)S(1)} %add_convert_fusion.3.flag_ref, bf16[3,1536,768]{2,1,0:T(8,128)(2,1)S(1)} %get-tuple-element.35.en, bf16[256,768]{1,0:T(8,128)(2,1)S(1)} %get-tuple-element.53.grad, ...), custom_call_target="tpu_custom_call" | custom-call | tf_op jit(solution)/shard_map/pallas_call | solution.py:227
  108.0 1.6 %collective-permute-start.20 = (bf16[768,128]{1,0:T(8,128)(2,1)S(1)}, bf16[768,128]{1,0:T(8,128)(2,1)S(1)}, u32[]{:S(2)}, u32[]{:S(2)}) collective-permute-start(bf16[768,128]{1,0:T(8,128)(2,1)S(1)} %get-tuple-element.56), channel_id=1, source_target_pairs={{0,8},{1,4},{2,10},{3,6},{4,1},{5,13},{6,3},{7,15},{8,0},{9,12},{1... | collective-permute-start | bytes 589832 | tf_op jit(solution)/shard_map/ppermute | solution.py:36
  110.3 0.6 collective-permute-start.26
  110.9 3.6 %collective-permute-done.20 = bf16[768,128]{1,0:T(8,128)(2,1)S(1)} collective-permute-done((bf16[768,128]{1,0:T(8,128)(2,1)S(1)}, bf16[768,128]{1,0:T(8,128)(2,1)S(1)}, u32[]{:S(2)}, u32[]{:S(2)}) %collective-permute-start.20) | collective-permute-done | bytes 196640 | tf_op jit(solution)/shard_map/ppermute | solution.py:36
  114.4 0.8 collective-permute-start.27
  115.2 1.3 collective-permute-done.21
  116.5 0.8 collective-permute-start.28
  117.3 1.0 maximum_select_fusion
  118.5 1.3 collective-permute-start.29
  119.8 2.4 %collective-permute-done.27 = bf16[768,256]{1,0:T(8,128)(2,1)S(1)} collective-permute-done((bf16[768,256]{1,0:T(8,128)(2,1)S(1)}, bf16[768,256]{1,0:T(8,128)(2,1)S(1)}, u32[]{:S(2)}, u32[]{:S(2)}) %collective-permute-start.27) | collective-permute-done | bytes 393248 | tf_op jit(solution)/shard_map/ppermute | solution.py:36
  122.4 0.8 collective-permute-start.30
  123.3 3.1 %collective-permute-done.28 = bf16[768,256]{1,0:T(8,128)(2,1)S(1)} collective-permute-done((bf16[768,256]{1,0:T(8,128)(2,1)S(1)}, bf16[768,256]{1,0:T(8,128)(2,1)S(1)}, u32[]{:S(2)}, u32[]{:S(2)}) %collective-permute-start.28) | collective-permute-done | bytes 393248 | tf_op jit(solution)/shard_map/ppermute | solution.py:36
  126.4 4.2 %collective-permute-done.29 = bf16[768,256]{1,0:T(8,128)(2,1)S(1)} collective-permute-done((bf16[768,256]{1,0:T(8,128)(2,1)S(1)}, bf16[768,256]{1,0:T(8,128)(2,1)S(1)}, u32[]{:S(2)}, u32[]{:S(2)}) %collective-permute-start.29) | collective-permute-done | bytes 393248 | tf_op jit(solution)/shard_map/ppermute | solution.py:36
  130.7 4.2 %collective-permute-done.30 = bf16[768,256]{1,0:T(8,128)(2,1)S(1)} collective-permute-done((bf16[768,256]{1,0:T(8,128)(2,1)S(1)}, bf16[768,256]{1,0:T(8,128)(2,1)S(1)}, u32[]{:S(2)}, u32[]{:S(2)}) %collective-permute-start.30) | collective-permute-done | bytes 393248 | tf_op jit(solution)/shard_map/ppermute | solution.py:36
  134.9 1.4 %maximum_select_fusion.1 = (bf16[768,384]{1,0:T(8,128)(2,1)}, bf16[768,384]{1,0:T(8,128)(2,1)}) fusion(bf16[768,128]{1,0:T(8,128)(2,1)S(1)} %get-tuple-element.78, bf16[768,128]{1,0:T(8,128)(2,1)S(1)} %get-tuple-element.76, bf16[768,128]{1,0:T(8,128)(2,1)S(1)} %get-tuple-element.74, bf16[768,128]{1,0:T(8,128)(2,1)S(1)} %get-tuple-element.72, ...), kind=kLoop, calls=%fused_computation.4 | loop fusion | flops 7667712 | bytes 3538945 | tf_op jit(solution)/shard_map/jit(_where)/select_n | solution.py:378
  (49 shorter events, 1.6 us)
Async XLA Ops:
  0.6 37.9 %copy-start.5 = (bf16[768,384]{1,0:T(8,128)(2,1)S(1)}, bf16[768,384]{1,0:T(8,128)(2,1)}, u32[]{:S(2)}) copy-start(bf16[768,384]{1,0:T(8,128)(2,1)} %param.7) | copy-start | bytes 1769476
  0.6 29.3 %collective-permute-start.6 = (bf16[768,768]{1,0:T(8,128)(2,1)}, bf16[768,768]{1,0:T(8,128)(2,1)}, u32[]{:S(2)}, u32[]{:S(2)}) collective-permute-start(bf16[768,768]{1,0:T(8,128)(2,1)} %g0.1), channel_id=1, source_target_pairs={{0,2},{1,3},{2,0},{3,1},{4,6},{5,7},{6,4},{7,5},{8,10},{9,11},{10,... | collective-permute-start | bytes 3538952 | tf_op jit(solution)/shard_map/ppermute | solution.py:36
  3.7 17.9 %collective-permute-start.1 = (bf16[768,384]{1,0:T(8,128)(2,1)}, bf16[768,384]{1,0:T(8,128)(2,1)S(1)}, u32[]{:S(2)}, u32[]{:S(2)}) collective-permute-start(bf16[768,384]{1,0:T(8,128)(2,1)} %param.6), channel_id=1, source_target_pairs={{1,4},{3,6},{4,1},{6,3},{9,12},{11,14},{12,9},{14,11},{17,20},{19,... | collective-permute-start | bytes 1769480 | tf_op jit(solution)/shard_map/ppermute | solution.py:36
  4.4 8.4 %collective-permute-start.8 = (bf16[384,384]{1,0:T(8,128)(2,1)}, bf16[384,384]{1,0:T(8,128)(2,1)}, u32[]{:S(2)}, u32[]{:S(2)}) collective-permute-start(bf16[384,384]{1,0:T(8,128)(2,1)} %refs_0_.1), channel_id=1, source_target_pairs={{0,8},{1,9},{2,10},{3,11},{4,12},{5,13},{6,14},{7,15},{8,0},{9,1},... | collective-permute-start | bytes 884744 | tf_op jit(solution)/shard_map/ppermute | solution.py:36
  6.0 15.6 %collective-permute-start.7 = (bf16[384,384]{1,0:T(8,128)(2,1)}, bf16[384,384]{1,0:T(8,128)(2,1)}, u32[]{:S(2)}, u32[]{:S(2)}) collective-permute-start(bf16[384,384]{1,0:T(8,128)(2,1)} %refs_0_.1), channel_id=1, source_target_pairs={{0,4},{1,5},{2,6},{3,7},{4,0},{5,1},{6,2},{7,3},{8,12},{9,13},{10,... | collective-permute-start | bytes 884744 | tf_op jit(solution)/shard_map/ppermute | solution.py:36
  8.8 29.8 %collective-permute-start.3 = (bf16[768,384]{1,0:T(8,128)(2,1)}, bf16[768,384]{1,0:T(8,128)(2,1)}, u32[]{:S(2)}, u32[]{:S(2)}) collective-permute-start(bf16[768,384]{1,0:T(8,128)(2,1)} %param.7), channel_id=1, source_target_pairs={{1,4},{3,6},{4,1},{6,3},{9,12},{11,14},{12,9},{14,11},{17,20},{19,... | collective-permute-start | bytes 1769480 | tf_op jit(solution)/shard_map/ppermute | solution.py:36
  12.8 25.9 %collective-permute-start = (bf16[768,384]{1,0:T(8,128)(2,1)}, bf16[768,384]{1,0:T(8,128)(2,1)S(1)}, u32[]{:S(2)}, u32[]{:S(2)}) collective-permute-start(bf16[768,384]{1,0:T(8,128)(2,1)} %qa.13), channel_id=1, source_target_pairs={{1,4},{3,6},{4,1},{6,3},{9,12},{11,14},{12,9},{14,11},{17,20},{19,... | collective-permute-start | bytes 1769480 | tf_op jit(solution)/shard_map/ppermute | solution.py:36
  21.6 43.8 %collective-permute-start.5 = (bf16[768,768]{1,0:T(8,128)(2,1)}, bf16[768,768]{1,0:T(8,128)(2,1)}, u32[]{:S(2)}, u32[]{:S(2)}) collective-permute-start(bf16[768,768]{1,0:T(8,128)(2,1)} %g0.1), channel_id=1, source_target_pairs={{0,1},{1,0},{2,3},{3,2},{4,5},{5,4},{6,7},{7,6},{8,9},{9,8},{10,11... | collective-permute-start | bytes 3538952 | tf_op jit(solution)/shard_map/ppermute | solution.py:36
  21.6 17.0 %collective-permute-start.9 = (bf16[384,384]{1,0:T(8,128)(2,1)}, bf16[384,384]{1,0:T(8,128)(2,1)}, u32[]{:S(2)}, u32[]{:S(2)}) collective-permute-start(bf16[384,384]{1,0:T(8,128)(2,1)} %refs_0_.1), channel_id=1, source_target_pairs={{0,16},{1,17},{2,18},{3,19},{4,20},{5,21},{6,22},{7,23},{8,24},{9,... | collective-permute-start | bytes 884744 | tf_op jit(solution)/shard_map/ppermute | solution.py:36
  30.0 49.4 %collective-permute-start.13 = (bf16[768,768]{1,0:T(8,128)(2,1)}, bf16[768,768]{1,0:T(8,128)(2,1)}, u32[]{:S(2)}, u32[]{:S(2)}) collective-permute-start(bf16[768,768]{1,0:T(8,128)(2,1)} %collective-permute-done.6.refs_5_), channel_id=1, source_target_pairs={{0,1},{1,0},{2,3},{3,2},{4,5},{5,4},{6,7},{7,6},{8,9},{9,8},{10,11... | collective-permute-start | bytes 3538952 | tf_op jit(solution)/shard_map/ppermute | solution.py:36
  31.1 36.4 %copy-start = (bf16[768,384]{1,0:T(8,128)(2,1)S(1)}, bf16[768,384]{1,0:T(8,128)(2,1)}, u32[]{:S(2)}) copy-start(bf16[768,384]{1,0:T(8,128)(2,1)} %qa.13) | copy-start | bytes 1769476
  38.5 16.1 %collective-permute-start.10 = (bf16[384,384]{1,0:T(8,128)(2,1)}, bf16[384,384]{1,0:T(8,128)(2,1)}, u32[]{:S(2)}, u32[]{:S(2)}) collective-permute-start(bf16[384,384]{1,0:T(8,128)(2,1)} %collective-permute-done.8.refs_7_), channel_id=1, source_target_pairs={{0,16},{1,17},{2,18},{3,19},{4,20},{5,21},{6,22},{7,23},{8,24},{9,... | collective-permute-start | bytes 884744 | tf_op jit(solution)/shard_map/ppermute | solution.py:36
  38.5 25.3 %collective-permute-start.2 = (bf16[768,384]{1,0:T(8,128)(2,1)S(1)}, bf16[768,384]{1,0:T(8,128)(2,1)S(1)}, u32[]{:S(2)}, u32[]{:S(2)}) collective-permute-start(bf16[768,384]{1,0:T(8,128)(2,1)S(1)} %broadcast_select_fusion.1.refs_0_.ko), channel_id=1, source_target_pairs={{0,1},{1,0},{2,3},{3,2},{4,5},{5,4},{6,7},{7,6},{8,9},{9,8},{10,11... | collective-permute-start | bytes 1769480 | tf_op jit(solution)/shard_map/ppermute | solution.py:36
  38.7 26.6 %collective-permute-start.4 = (bf16[768,384]{1,0:T(8,128)(2,1)S(1)}, bf16[768,384]{1,0:T(8,128)(2,1)S(1)}, u32[]{:S(2)}, u32[]{:S(2)}) collective-permute-start(bf16[768,384]{1,0:T(8,128)(2,1)S(1)} %broadcast_select_fusion.refs_2_.vo), channel_id=1, source_target_pairs={{0,1},{1,0},{2,3},{3,2},{4,5},{5,4},{6,7},{7,6},{8,9},{9,8},{10,11... | collective-permute-start | bytes 1769480 | tf_op jit(solution)/shard_map/ppermute | solution.py:36
  54.6 7.9 %collective-permute-start.14 = (bf16[384,384]{1,0:T(8,128)(2,1)}, bf16[384,384]{1,0:T(8,128)(2,1)S(1)}, u32[]{:S(2)}, u32[]{:S(2)}) collective-permute-start(bf16[384,384]{1,0:T(8,128)(2,1)} %collective-permute-done.7.refs_6_), channel_id=1, source_target_pairs={{0,8},{1,9},{2,10},{3,11},{4,12},{5,13},{6,14},{7,15},{8,0},{9,1},... | collective-permute-start | bytes 884744 | tf_op jit(solution)/shard_map/ppermute | solution.py:36
  62.6 0.7 copy-start.3
  63.3 20.3 %collective-permute-start.11 = (bf16[768,384]{1,0:T(8,128)(2,1)S(1)}, bf16[768,384]{1,0:T(8,128)(2,1)}, u32[]{:S(2)}, u32[]{:S(2)}) collective-permute-start(bf16[768,384]{1,0:T(8,128)(2,1)S(1)} %broadcast_select_fusion.1.refs_0_.ko), channel_id=1, source_target_pairs={{0,2},{1,8},{2,0},{3,10},{4,6},{5,12},{6,4},{7,14},{8,1},{9,16},{1... | collective-permute-start | bytes 1769480 | tf_op jit(solution)/shard_map/ppermute | solution.py:36
  63.8 19.7 %collective-permute-start.12 = (bf16[768,384]{1,0:T(8,128)(2,1)S(1)}, bf16[768,384]{1,0:T(8,128)(2,1)}, u32[]{:S(2)}, u32[]{:S(2)}) collective-permute-start(bf16[768,384]{1,0:T(8,128)(2,1)S(1)} %broadcast_select_fusion.refs_2_.vo), channel_id=1, source_target_pairs={{0,2},{1,8},{2,0},{3,10},{4,6},{5,12},{6,4},{7,14},{8,1},{9,16},{1... | collective-permute-start | bytes 1769480 | tf_op jit(solution)/shard_map/ppermute | solution.py:36
  65.3 10.2 %collective-permute-start.15 = (bf16[384,384]{1,0:T(8,128)(2,1)}, bf16[384,384]{1,0:T(8,128)(2,1)}, u32[]{:S(2)}, u32[]{:S(2)}) collective-permute-start(bf16[384,384]{1,0:T(8,128)(2,1)} %collective-permute-done.9.refs_8_), channel_id=1, source_target_pairs={{0,4},{1,5},{2,6},{3,7},{4,0},{5,1},{6,2},{7,3},{8,12},{9,13},{10,... | collective-permute-start | bytes 884744 | tf_op jit(solution)/shard_map/ppermute | solution.py:36
  65.4 13.9 %collective-permute-start.16 = (bf16[384,384]{1,0:T(8,128)(2,1)}, bf16[384,384]{1,0:T(8,128)(2,1)}, u32[]{:S(2)}, u32[]{:S(2)}) collective-permute-start(bf16[384,384]{1,0:T(8,128)(2,1)} %collective-permute-done.10.refs_9_), channel_id=1, source_target_pairs={{0,4},{1,5},{2,6},{3,7},{4,0},{5,1},{6,2},{7,3},{8,12},{9,13},{10,... | collective-permute-start | bytes 884744 | tf_op jit(solution)/shard_map/ppermute | solution.py:36
  67.5 11.8 %copy-start.1 = (bf16[768,768]{1,0:T(8,128)(2,1)S(1)}, bf16[768,768]{1,0:T(8,128)(2,1)}, u32[]{:S(2)}) copy-start(bf16[768,768]{1,0:T(8,128)(2,1)} %g0.1) | copy-start | bytes 3538948
  67.5 11.8 %copy-start.2 = (bf16[384,384]{1,0:T(8,128)(2,1)S(1)}, bf16[384,384]{1,0:T(8,128)(2,1)}, u32[]{:S(2)}) copy-start(bf16[384,384]{1,0:T(8,128)(2,1)} %refs_0_.1) | copy-start | bytes 884740
  67.5 11.8 %copy-start.4 = (bf16[384,384]{1,0:T(8,128)(2,1)S(1)}, bf16[384,384]{1,0:T(8,128)(2,1)}, u32[]{:S(2)}) copy-start(bf16[384,384]{1,0:T(8,128)(2,1)} %copy-done.3) | copy-start | bytes 884740
  82.9 7.0 %collective-permute-start.17 = (bf16[128,768]{1,0:T(8,128)(2,1)S(1)}, bf16[128,768]{1,0:T(8,128)(2,1)S(1)}, u32[]{:S(2)}, u32[]{:S(2)}) collective-permute-start(bf16[128,768]{1,0:T(8,128)(2,1)S(1)} %get-tuple-element.47.ga), channel_id=1, source_target_pairs={{0,2},{1,4},{2,0},{3,6},{4,1},{5,7},{6,3},{7,5},{8,10},{9,12},{10,... | collective-permute-start | bytes 589832 | tf_op jit(solution)/shard_map/ppermute | solution.py:36
  88.4 9.3 %collective-permute-start.18 = (bf16[256,768]{1,0:T(8,128)(2,1)S(1)}, bf16[256,768]{1,0:T(8,128)(2,1)S(1)}, u32[]{:S(2)}, u32[]{:S(2)}) collective-permute-start(bf16[256,768]{1,0:T(8,128)(2,1)S(1)} %get-tuple-element.52.ga), channel_id=1, source_target_pairs={{0,2},{1,4},{2,0},{3,6},{4,1},{5,7},{6,3},{7,5},{8,10},{9,12},{10,... | collective-permute-start | bytes 1179656 | tf_op jit(solution)/shard_map/ppermute | solution.py:36
  95.5 12.5 %collective-permute-start.22 = (bf16[768,256]{1,0:T(8,128)(2,1)S(1)}, bf16[768,256]{1,0:T(8,128)(2,1)S(1)}, u32[]{:S(2)}, u32[]{:S(2)}) collective-permute-start(bf16[768,256]{1,0:T(8,128)(2,1)S(1)} %get-tuple-element.59), channel_id=1, source_target_pairs={{0,1},{1,0},{2,3},{3,2},{4,5},{5,4},{6,7},{7,6},{8,9},{9,8},{10,11... | collective-permute-start | bytes 1179656 | tf_op jit(solution)/shard_map/ppermute | solution.py:36
  95.6 14.0 %collective-permute-start.23 = (bf16[768,256]{1,0:T(8,128)(2,1)S(1)}, bf16[768,256]{1,0:T(8,128)(2,1)S(1)}, u32[]{:S(2)}, u32[]{:S(2)}) collective-permute-start(bf16[768,256]{1,0:T(8,128)(2,1)S(1)} %get-tuple-element.60), channel_id=1, source_target_pairs={{0,2},{1,8},{2,0},{3,10},{4,6},{5,12},{6,4},{7,14},{8,1},{9,16},{1... | collective-permute-start | bytes 1179656 | tf_op jit(solution)/shard_map/ppermute | solution.py:36
  96.2 14.1 %collective-permute-start.19 = (bf16[768,128]{1,0:T(8,128)(2,1)S(1)}, bf16[768,128]{1,0:T(8,128)(2,1)S(1)}, u32[]{:S(2)}, u32[]{:S(2)}) collective-permute-start(bf16[768,128]{1,0:T(8,128)(2,1)S(1)} %get-tuple-element.51), channel_id=1, source_target_pairs={{0,8},{1,4},{2,10},{3,6},{4,1},{5,13},{6,3},{7,15},{8,0},{9,12},{1... | collective-permute-start | bytes 589832 | tf_op jit(solution)/shard_map/ppermute | solution.py:36
  104.4 14.0 %collective-permute-start.24 = (bf16[768,256]{1,0:T(8,128)(2,1)S(1)}, bf16[768,256]{1,0:T(8,128)(2,1)S(1)}, u32[]{:S(2)}, u32[]{:S(2)}) collective-permute-start(bf16[768,256]{1,0:T(8,128)(2,1)S(1)} %get-tuple-element.62), channel_id=1, source_target_pairs={{0,1},{1,0},{2,3},{3,2},{4,5},{5,4},{6,7},{7,6},{8,9},{9,8},{10,11... | collective-permute-start | bytes 1179656 | tf_op jit(solution)/shard_map/ppermute | solution.py:36
  104.4 13.9 %collective-permute-start.25 = (bf16[768,256]{1,0:T(8,128)(2,1)S(1)}, bf16[768,256]{1,0:T(8,128)(2,1)S(1)}, u32[]{:S(2)}, u32[]{:S(2)}) collective-permute-start(bf16[768,256]{1,0:T(8,128)(2,1)S(1)} %get-tuple-element.63), channel_id=1, source_target_pairs={{0,2},{1,8},{2,0},{3,10},{4,6},{5,12},{6,4},{7,14},{8,1},{9,16},{1... | collective-permute-start | bytes 1179656 | tf_op jit(solution)/shard_map/ppermute | solution.py:36
  108.0 6.4 %collective-permute-start.20 = (bf16[768,128]{1,0:T(8,128)(2,1)S(1)}, bf16[768,128]{1,0:T(8,128)(2,1)S(1)}, u32[]{:S(2)}, u32[]{:S(2)}) collective-permute-start(bf16[768,128]{1,0:T(8,128)(2,1)S(1)} %get-tuple-element.56), channel_id=1, source_target_pairs={{0,8},{1,4},{2,10},{3,6},{4,1},{5,13},{6,3},{7,15},{8,0},{9,12},{1... | collective-permute-start | bytes 589832 | tf_op jit(solution)/shard_map/ppermute | solution.py:36
  109.6 7.0 %collective-permute-start.21 = (bf16[768,128]{1,0:T(8,128)(2,1)S(1)}, bf16[768,128]{1,0:T(8,128)(2,1)S(1)}, u32[]{:S(2)}, u32[]{:S(2)}) collective-permute-start(bf16[768,128]{1,0:T(8,128)(2,1)S(1)} %get-tuple-element.57), channel_id=1, source_target_pairs={{0,8},{1,4},{2,10},{3,6},{4,1},{5,13},{6,3},{7,15},{8,0},{9,12},{1... | collective-permute-start | bytes 589832 | tf_op jit(solution)/shard_map/ppermute | solution.py:36
  110.3 9.5 %collective-permute-start.26 = (bf16[768,256]{1,0:T(8,128)(2,1)S(1)}, bf16[768,256]{1,0:T(8,128)(2,1)S(1)}, u32[]{:S(2)}, u32[]{:S(2)}) collective-permute-start(bf16[768,256]{1,0:T(8,128)(2,1)S(1)} %get-tuple-element.65), channel_id=1, source_target_pairs={{0,1},{1,0},{2,3},{3,2},{4,5},{5,4},{6,7},{7,6},{8,9},{9,8},{10,11... | collective-permute-start | bytes 1179656 | tf_op jit(solution)/shard_map/ppermute | solution.py:36
  114.4 7.8 %collective-permute-start.27 = (bf16[768,256]{1,0:T(8,128)(2,1)S(1)}, bf16[768,256]{1,0:T(8,128)(2,1)S(1)}, u32[]{:S(2)}, u32[]{:S(2)}) collective-permute-start(bf16[768,256]{1,0:T(8,128)(2,1)S(1)} %get-tuple-element.66), channel_id=1, source_target_pairs={{0,2},{1,8},{2,0},{3,10},{4,6},{5,12},{6,4},{7,14},{8,1},{9,16},{1... | collective-permute-start | bytes 1179656 | tf_op jit(solution)/shard_map/ppermute | solution.py:36
  116.5 9.9 %collective-permute-start.28 = (bf16[768,256]{1,0:T(8,128)(2,1)S(1)}, bf16[768,256]{1,0:T(8,128)(2,1)S(1)}, u32[]{:S(2)}, u32[]{:S(2)}) collective-permute-start(bf16[768,256]{1,0:T(8,128)(2,1)S(1)} %add_convert_fusion.2), channel_id=1, source_target_pairs={{0,2},{1,4},{2,0},{3,6},{4,1},{5,7},{6,3},{7,5},{8,10},{9,12},{10,... | collective-permute-start | bytes 1179656 | tf_op jit(solution)/shard_map/ppermute | solution.py:36
  118.5 12.2 %collective-permute-start.29 = (bf16[768,256]{1,0:T(8,128)(2,1)S(1)}, bf16[768,256]{1,0:T(8,128)(2,1)S(1)}, u32[]{:S(2)}, u32[]{:S(2)}) collective-permute-start(bf16[768,256]{1,0:T(8,128)(2,1)S(1)} %add_convert_fusion.1), channel_id=1, source_target_pairs={{0,2},{1,4},{2,0},{3,6},{4,1},{5,7},{6,3},{7,5},{8,10},{9,12},{10,... | collective-permute-start | bytes 1179656 | tf_op jit(solution)/shard_map/ppermute | solution.py:36
  122.4 12.5 %collective-permute-start.30 = (bf16[768,256]{1,0:T(8,128)(2,1)S(1)}, bf16[768,256]{1,0:T(8,128)(2,1)S(1)}, u32[]{:S(2)}, u32[]{:S(2)}) collective-permute-start(bf16[768,256]{1,0:T(8,128)(2,1)S(1)} %add_convert_fusion), channel_id=1, source_target_pairs={{0,2},{1,4},{2,0},{3,6},{4,1},{5,7},{6,3},{7,5},{8,10},{9,12},{10,... | collective-permute-start | bytes 1179656 | tf_op jit(solution)/shard_map/ppermute | solution.py:36

commit v9 on v8

--- a/solution.py
+++ b/solution.py
@@ -378,11 +378,8 @@
         return jnp.where(stays, kept, received)
 
     first = collect(0, slice(0, HD))
-    return (
-        first,
-        collect(1, slice(0, HD)),
-        collect(1, slice(HD, 2 * HD)),
-    )
+    rest = collect(1, slice(0, HD)), collect(1, slice(HD, 2 * HD))
+    return (first, *rest)
 
 
 def solution(mesh):

time: 137 us -> 137 us (level)
  no operation moved by 1% of the time
where the time goes in v9:
time: 137 us; the launch traced here: 136 us
  waiting for transfers between devices  69.4 us (51%)
  Pallas kernels  30.9 us (23%)
  starting transfers between devices  29.9 us (22%)
  other arithmetic  4.16 us (3%)
    ppermute x31, waiting for transfers between devices, exchange(): return lax.ppermute(block, AXES, pairs)  69.4 us
    ppermute x31, starting transfers between devices, exchange(): return lax.ppermute(block, AXES, pairs)  29.9 us
    pallas_call x2, Pallas kernels, soften(): pl.pallas_call(functools.partial(soften_kernel, parts, tile, len(staged))...  12.2 us
    pallas_call x3, Pallas kernels, backward_near(): pl.pallas_call(near_kernel, grid=(1,), in_specs=[pl.BlockSpec(memory_spac...  8.79 us
    pallas_call x2, Pallas kernels, backward_far(): pl.pallas_call(functools.partial(far_kernel, first, count), in_specs=[pl....  6.31 us
    pallas_call x1, Pallas kernels, project(): pl.pallas_call(project_kernel, in_specs=[pl.BlockSpec(memory_space=pltpu....  3.61 us
  transfers between devices with their start and end apart: 31, of which 14 were waited for; matrix products, arithmetic and copies ran while one was open for 2% of the time, Pallas kernels for 23%

profile of v9, /device:TPU:0, one launch (start us, length us, event | category | flops | bytes accessed | tf_op | source)
XLA Modules:
  0.0 136.2 jit_solution(8108843241526576762)
XLA Ops:
  0.6 3.0 %collective-permute-start.6 = (bf16[768,768]{1,0:T(8,128)(2,1)}, bf16[768,768]{1,0:T(8,128)(2,1)}, u32[]{:S(2)}, u32[]{:S(2)}) collective-permute-start(bf16[768,768]{1,0:T(8,128)(2,1)} %g0.1), channel_id=1, source_target_pairs={{0,2},{1,3},{2,0},{3,1},{4,6},{5,7},{6,4},{7,5},{8,10},{9,11},{10,... | collective-permute-start | bytes 3538952 | tf_op jit(solution)/shard_map/ppermute | solution.py:36
  3.7 0.7 collective-permute-start.1
  4.4 1.6 %collective-permute-start.8 = (bf16[384,384]{1,0:T(8,128)(2,1)}, bf16[384,384]{1,0:T(8,128)(2,1)}, u32[]{:S(2)}, u32[]{:S(2)}) collective-permute-start(bf16[384,384]{1,0:T(8,128)(2,1)} %refs_0_.1), channel_id=1, source_target_pairs={{0,8},{1,9},{2,10},{3,11},{4,12},{5,13},{6,14},{7,15},{8,0},{9,1},... | collective-permute-start | bytes 884744 | tf_op jit(solution)/shard_map/ppermute | solution.py:36
  6.0 2.7 %collective-permute-start.7 = (bf16[384,384]{1,0:T(8,128)(2,1)}, bf16[384,384]{1,0:T(8,128)(2,1)}, u32[]{:S(2)}, u32[]{:S(2)}) collective-permute-start(bf16[384,384]{1,0:T(8,128)(2,1)} %refs_0_.1), channel_id=1, source_target_pairs={{0,4},{1,5},{2,6},{3,7},{4,0},{5,1},{6,2},{7,3},{8,12},{9,13},{10,... | collective-permute-start | bytes 884744 | tf_op jit(solution)/shard_map/ppermute | solution.py:36
  8.8 1.5 %collective-permute-start.3 = (bf16[768,384]{1,0:T(8,128)(2,1)}, bf16[768,384]{1,0:T(8,128)(2,1)}, u32[]{:S(2)}, u32[]{:S(2)}) collective-permute-start(bf16[768,384]{1,0:T(8,128)(2,1)} %param.7), channel_id=1, source_target_pairs={{1,4},{3,6},{4,1},{6,3},{9,12},{11,14},{12,9},{14,11},{17,20},{19,... | collective-permute-start | bytes 1769480 | tf_op jit(solution)/shard_map/ppermute | solution.py:36
  10.2 2.5 %collective-permute-done.8.refs_7_ = bf16[384,384]{1,0:T(8,128)(2,1)} collective-permute-done((bf16[384,384]{1,0:T(8,128)(2,1)}, bf16[384,384]{1,0:T(8,128)(2,1)}, u32[]{:S(2)}, u32[]{:S(2)}) %collective-permute-start.8) | collective-permute-done | bytes 294944 | tf_op jit(solution)/shard_map/ppermute | solution.py:36
  12.8 0.7 collective-permute-start
  13.4 8.1 %collective-permute-done.7.refs_6_ = bf16[384,384]{1,0:T(8,128)(2,1)} collective-permute-done((bf16[384,384]{1,0:T(8,128)(2,1)}, bf16[384,384]{1,0:T(8,128)(2,1)}, u32[]{:S(2)}, u32[]{:S(2)}) %collective-permute-start.7) | collective-permute-done | bytes 294944 | tf_op jit(solution)/shard_map/ppermute | solution.py:36
  21.6 2.6 %collective-permute-start.9 = (bf16[384,384]{1,0:T(8,128)(2,1)}, bf16[384,384]{1,0:T(8,128)(2,1)}, u32[]{:S(2)}, u32[]{:S(2)}) collective-permute-start(bf16[384,384]{1,0:T(8,128)(2,1)} %refs_0_.1), channel_id=1, source_target_pairs={{0,16},{1,17},{2,18},{3,19},{4,20},{5,21},{6,22},{7,23},{8,24},{9,... | collective-permute-start | bytes 884744 | tf_op jit(solution)/shard_map/ppermute | solution.py:36
  24.2 5.8 %collective-permute-done.6.refs_5_ = bf16[768,768]{1,0:T(8,128)(2,1)} collective-permute-done((bf16[768,768]{1,0:T(8,128)(2,1)}, bf16[768,768]{1,0:T(8,128)(2,1)}, u32[]{:S(2)}, u32[]{:S(2)}) %collective-permute-start.6) | collective-permute-done | bytes 1179680 | tf_op jit(solution)/shard_map/ppermute | solution.py:36
  30.0 1.1 broadcast_select_fusion.1.refs_0_.ko
  31.1 7.4 %collective-permute-done.9.refs_8_ = bf16[384,384]{1,0:T(8,128)(2,1)} collective-permute-done((bf16[384,384]{1,0:T(8,128)(2,1)}, bf16[384,384]{1,0:T(8,128)(2,1)}, u32[]{:S(2)}, u32[]{:S(2)}) %collective-permute-start.9) | collective-permute-done | bytes 294944 | tf_op jit(solution)/shard_map/ppermute | solution.py:36
  38.7 1.6 %collective-permute-start.4 = (bf16[768,384]{1,0:T(8,128)(2,1)S(1)}, bf16[768,384]{1,0:T(8,128)(2,1)S(1)}, u32[]{:S(2)}, u32[]{:S(2)}) collective-permute-start(bf16[768,384]{1,0:T(8,128)(2,1)S(1)} %broadcast_select_fusion.refs_2_.vo), channel_id=1, source_target_pairs={{0,1},{1,0},{2,3},{3,2},{4,5},{5,4},{6,7},{7,6},{8,9},{9,8},{10,11... | collective-permute-start | bytes 1769480 | tf_op jit(solution)/shard_map/ppermute | solution.py:36
  40.3 14.4 %collective-permute-done.10.refs_9_ = bf16[384,384]{1,0:T(8,128)(2,1)} collective-permute-done((bf16[384,384]{1,0:T(8,128)(2,1)}, bf16[384,384]{1,0:T(8,128)(2,1)}, u32[]{:S(2)}, u32[]{:S(2)}) %collective-permute-start.10) | collective-permute-done | bytes 294944 | tf_op jit(solution)/shard_map/ppermute | solution.py:36
  54.6 7.9 %collective-permute-done.14.refs_3_ = bf16[384,384]{1,0:T(8,128)(2,1)S(1)} collective-permute-done((bf16[384,384]{1,0:T(8,128)(2,1)}, bf16[384,384]{1,0:T(8,128)(2,1)S(1)}, u32[]{:S(2)}, u32[]{:S(2)}) %collective-permute-start.14) | collective-permute-done | bytes 294944 | tf_op jit(solution)/shard_map/ppermute | solution.py:36
  62.6 0.7 copy-done.3
  63.3 0.5 collective-permute-start.11
  63.8 1.5 %collective-permute-start.12 = (bf16[768,384]{1,0:T(8,128)(2,1)S(1)}, bf16[768,384]{1,0:T(8,128)(2,1)}, u32[]{:S(2)}, u32[]{:S(2)}) collective-permute-start(bf16[768,384]{1,0:T(8,128)(2,1)S(1)} %broadcast_select_fusion.refs_2_.vo), channel_id=1, source_target_pairs={{0,2},{1,8},{2,0},{3,10},{4,6},{5,12},{6,4},{7,14},{8,1},{9,16},{1... | collective-permute-start | bytes 1769480 | tf_op jit(solution)/shard_map/ppermute | solution.py:36
  65.4 2.0 %collective-permute-start.16 = (bf16[384,384]{1,0:T(8,128)(2,1)}, bf16[384,384]{1,0:T(8,128)(2,1)}, u32[]{:S(2)}, u32[]{:S(2)}) collective-permute-start(bf16[384,384]{1,0:T(8,128)(2,1)} %collective-permute-done.10.refs_9_), channel_id=1, source_target_pairs={{0,4},{1,5},{2,6},{3,7},{4,0},{5,1},{6,2},{7,3},{8,12},{9,13},{10,... | collective-permute-start | bytes 884744 | tf_op jit(solution)/shard_map/ppermute | solution.py:36
  67.5 7.4 %shard_map.76 = (bf16[3,1536,768]{2,1,0:T(8,128)(2,1)S(1)}, f32[384,768]{1,0:T(8,128)S(1)}, f32[24,768]{1,0:T(8,128)S(1)}, bf16[768,768]{1,0:T(8,128)(2,1)S(1)},...) custom-call(s32[2]{0:T(128)S(1)} %add_convert_fusion.3.flag_ref, ...), custom_call_target="tpu_custom_call" | custom-call | tf_op jit(solution)/shard_map/pallas_call | solution.py:115
  74.9 0.6 collective-permute-done.15.refs_5_
  75.5 3.8 %collective-permute-done.16.refs_7_ = bf16[384,384]{1,0:T(8,128)(2,1)} collective-permute-done((bf16[384,384]{1,0:T(8,128)(2,1)}, bf16[384,384]{1,0:T(8,128)(2,1)}, u32[]{:S(2)}, u32[]{:S(2)}) %collective-permute-start.16) | collective-permute-done | bytes 294944 | tf_op jit(solution)/shard_map/ppermute | solution.py:36
  79.3 3.6 %project.1 = (bf16[128,768]{1,0:T(8,128)(2,1)S(1)}, bf16[256,768]{1,0:T(8,128)(2,1)S(1)}) custom-call(s32[3]{0:T(128)S(1)} %pad_add_fusion.place_ref, bf16[768,768]{1,0:T(8,128)(2,1)S(1)} %copy-done.1, bf16[768,768]{1,0:T(8,128)(2,1)S(1)} %get-tuple-element.41.g1, bf16[768,768]{1,0:T(8,128)(2,1)S(1)} %get-tuple-element.42.g2, ...), custom_call_target="tpu_custom_call" | custom-call | tf_op jit(solution)/shard_map/project/pallas_call | solution.py:269
  82.9 0.6 collective-permute-start.17
  83.5 4.9 %shard_map.77 = (bf16[3,768,768]{2,1,0:T(8,128)(2,1)S(1)}, f32[384,768]{1,0:T(8,128)S(1)}, f32[24,768]{1,0:T(8,128)S(1)}) custom-call(s32[2]{0:T(128)S(1)} %add_convert_fusion.3.flag_ref, bf16[768,384]{1,0:T(8,128)(2,1)S(1)} %copy-done, bf16[768,384]{1,0:T(8,128)(2,1)S(1)} %collective-permute-done.qb, bf16[768,384]{1,0:T(8,128)(2,1)} %collective-permute-done.11.refs_0_.kz, ...), custom_call_target="tpu_custom_call" | custom-call | tf_op jit(solution)/shard_map/pallas_call | solution.py:115
  88.4 1.5 %collective-permute-start.18 = (bf16[256,768]{1,0:T(8,128)(2,1)S(1)}, bf16[256,768]{1,0:T(8,128)(2,1)S(1)}, u32[]{:S(2)}, u32[]{:S(2)}) collective-permute-start(bf16[256,768]{1,0:T(8,128)(2,1)S(1)} %get-tuple-element.52.ga), channel_id=1, source_target_pairs={{0,2},{1,4},{2,0},{3,6},{4,1},{5,7},{6,3},{7,5},{8,10},{9,12},{10,... | collective-permute-start | bytes 1179656 | tf_op jit(solution)/shard_map/ppermute | solution.py:36
  90.0 2.6 %shard_map.78 = (bf16[128,768]{1,0:T(8,128)(2,1)S(1)}, f32[8,768]{1,0:T(8,128)S(1)}, f32[128,768]{1,0:T(8,128)S(1)}, bf16[768,256]{1,0:T(8,128)(2,1)S(1)}) custom-call(s32[2]{0:T(128)S(1)} %add_convert_fusion.3.flag_ref, f32[384,768]{1,0:T(8,128)S(1)} %get-tuple-element.36.on, f32[24,768]{1,0:T(8,128)S(1)} %get-tuple-element.37.sn, ...), custom_call_target="tpu_custom_call" | custom-call | tf_op jit(solution)/shard_map/pallas_call | solution.py:192
  92.5 2.9 %shard_map.79 = (bf16[768,128]{1,0:T(8,128)(2,1)S(1)}, f32[768,256]{1,0:T(8,128)S(1)}, bf16[768,256]{1,0:T(8,128)(2,1)S(1)}) custom-call(s32[2]{0:T(128)S(1)} %add_convert_fusion.3.flag_ref, bf16[3,1536,768]{2,1,0:T(8,128)(2,1)S(1)} %get-tuple-element.35.en, bf16[128,768]{1,0:T(8,128)(2,1)S(1)} %get-tuple-element.48.grad, ...), custom_call_target="tpu_custom_call" | custom-call | tf_op jit(solution)/shard_map/pallas_call | solution.py:227
  95.6 0.6 collective-permute-start.23
  96.2 1.5 %collective-permute-start.19 = (bf16[768,128]{1,0:T(8,128)(2,1)S(1)}, bf16[768,128]{1,0:T(8,128)(2,1)S(1)}, u32[]{:S(2)}, u32[]{:S(2)}) collective-permute-start(bf16[768,128]{1,0:T(8,128)(2,1)S(1)} %get-tuple-element.51), channel_id=1, source_target_pairs={{0,8},{1,4},{2,10},{3,6},{4,1},{5,13},{6,3},{7,15},{8,0},{9,12},{1... | collective-permute-start | bytes 589832 | tf_op jit(solution)/shard_map/ppermute | solution.py:36
  97.7 3.7 %shard_map.80 = (bf16[256,768]{1,0:T(8,128)(2,1)S(1)}, f32[16,768]{1,0:T(8,128)S(1)}, f32[256,768]{1,0:T(8,128)S(1)}, bf16[768,256]{1,0:T(8,128)(2,1)S(1)}, bf16[768,256]{1,0:T(8,128)(2,1)S(1)}) custom-call(s32[2]{0:T(128)S(1)} %add_convert_fusion.3.flag_ref, f32[384,768]{1,0:T(8,128)S(1)} %get-tuple-element.36.on, f32[24,768]{1,0:T(8,128)S(1)} %get-tuple-element.37.sn, ...), custom_call_target="tpu_custom_call" | custom-call | tf_op jit(solution)/shard_map/pallas_call | solution.py:192
  101.4 2.9 %shard_map.81 = (bf16[768,128]{1,0:T(8,128)(2,1)S(1)}, f32[768,256]{1,0:T(8,128)S(1)}, bf16[768,256]{1,0:T(8,128)(2,1)S(1)}) custom-call(s32[2]{0:T(128)S(1)} %add_convert_fusion.3.flag_ref, bf16[3,1536,768]{2,1,0:T(8,128)(2,1)S(1)} %get-tuple-element.35.en, bf16[256,768]{1,0:T(8,128)(2,1)S(1)} %get-tuple-element.53.grad, ...), custom_call_target="tpu_custom_call" | custom-call | tf_op jit(solution)/shard_map/pallas_call | solution.py:227
  104.4 0.6 collective-permute-start.25
  105.1 2.9 %shard_map.82 = (bf16[768,128]{1,0:T(8,128)(2,1)S(1)}, f32[768,256]{1,0:T(8,128)S(1)}, bf16[768,256]{1,0:T(8,128)(2,1)S(1)}) custom-call(s32[2]{0:T(128)S(1)} %add_convert_fusion.3.flag_ref, bf16[3,1536,768]{2,1,0:T(8,128)(2,1)S(1)} %get-tuple-element.35.en, bf16[256,768]{1,0:T(8,128)(2,1)S(1)} %get-tuple-element.53.grad, ...), custom_call_target="tpu_custom_call" | custom-call | tf_op jit(solution)/shard_map/pallas_call | solution.py:227
  108.0 1.6 %collective-permute-start.20 = (bf16[768,128]{1,0:T(8,128)(2,1)S(1)}, bf16[768,128]{1,0:T(8,128)(2,1)S(1)}, u32[]{:S(2)}, u32[]{:S(2)}) collective-permute-start(bf16[768,128]{1,0:T(8,128)(2,1)S(1)} %get-tuple-element.56), channel_id=1, source_target_pairs={{0,8},{1,4},{2,10},{3,6},{4,1},{5,13},{6,3},{7,15},{8,0},{9,12},{1... | collective-permute-start | bytes 589832 | tf_op jit(solution)/shard_map/ppermute | solution.py:36
  110.3 0.6 collective-permute-start.26
  110.9 3.6 %collective-permute-done.20 = bf16[768,128]{1,0:T(8,128)(2,1)S(1)} collective-permute-done((bf16[768,128]{1,0:T(8,128)(2,1)S(1)}, bf16[768,128]{1,0:T(8,128)(2,1)S(1)}, u32[]{:S(2)}, u32[]{:S(2)}) %collective-permute-start.20) | collective-permute-done | bytes 196640 | tf_op jit(solution)/shard_map/ppermute | solution.py:36
  114.4 0.8 collective-permute-start.27
  115.2 1.3 collective-permute-done.21
  116.5 0.8 collective-permute-start.28
  117.3 1.0 maximum_select_fusion
  118.5 1.3 collective-permute-start.29
  119.8 2.4 %collective-permute-done.27 = bf16[768,256]{1,0:T(8,128)(2,1)S(1)} collective-permute-done((bf16[768,256]{1,0:T(8,128)(2,1)S(1)}, bf16[768,256]{1,0:T(8,128)(2,1)S(1)}, u32[]{:S(2)}, u32[]{:S(2)}) %collective-permute-start.27) | collective-permute-done | bytes 393248 | tf_op jit(solution)/shard_map/ppermute | solution.py:36
  122.4 0.8 collective-permute-start.30
  123.3 3.1 %collective-permute-done.28 = bf16[768,256]{1,0:T(8,128)(2,1)S(1)} collective-permute-done((bf16[768,256]{1,0:T(8,128)(2,1)S(1)}, bf16[768,256]{1,0:T(8,128)(2,1)S(1)}, u32[]{:S(2)}, u32[]{:S(2)}) %collective-permute-start.28) | collective-permute-done | bytes 393248 | tf_op jit(solution)/shard_map/ppermute | solution.py:36
  126.4 4.2 %collective-permute-done.29 = bf16[768,256]{1,0:T(8,128)(2,1)S(1)} collective-permute-done((bf16[768,256]{1,0:T(8,128)(2,1)S(1)}, bf16[768,256]{1,0:T(8,128)(2,1)S(1)}, u32[]{:S(2)}, u32[]{:S(2)}) %collective-permute-start.29) | collective-permute-done | bytes 393248 | tf_op jit(solution)/shard_map/ppermute | solution.py:36
  130.7 4.2 %collective-permute-done.30 = bf16[768,256]{1,0:T(8,128)(2,1)S(1)} collective-permute-done((bf16[768,256]{1,0:T(8,128)(2,1)S(1)}, bf16[768,256]{1,0:T(8,128)(2,1)S(1)}, u32[]{:S(2)}, u32[]{:S(2)}) %collective-permute-start.30) | collective-permute-done | bytes 393248 | tf_op jit(solution)/shard_map/ppermute | solution.py:36
  134.9 1.4 %maximum_select_fusion.1 = (bf16[768,384]{1,0:T(8,128)(2,1)}, bf16[768,384]{1,0:T(8,128)(2,1)}) fusion(bf16[768,128]{1,0:T(8,128)(2,1)S(1)} %get-tuple-element.78, bf16[768,128]{1,0:T(8,128)(2,1)S(1)} %get-tuple-element.76, bf16[768,128]{1,0:T(8,128)(2,1)S(1)} %get-tuple-element.74, bf16[768,128]{1,0:T(8,128)(2,1)S(1)} %get-tuple-element.72, ...), kind=kLoop, calls=%fused_computation.4 | loop fusion | flops 7667712 | bytes 3538945 | tf_op jit(solution)/shard_map/jit(_where)/select_n | solution.py:378
  (49 shorter events, 1.6 us)
Async XLA Ops:
  0.6 37.9 %copy-start.5 = (bf16[768,384]{1,0:T(8,128)(2,1)S(1)}, bf16[768,384]{1,0:T(8,128)(2,1)}, u32[]{:S(2)}) copy-start(bf16[768,384]{1,0:T(8,128)(2,1)} %param.7) | copy-start | bytes 1769476
  0.6 29.3 %collective-permute-start.6 = (bf16[768,768]{1,0:T(8,128)(2,1)}, bf16[768,768]{1,0:T(8,128)(2,1)}, u32[]{:S(2)}, u32[]{:S(2)}) collective-permute-start(bf16[768,768]{1,0:T(8,128)(2,1)} %g0.1), channel_id=1, source_target_pairs={{0,2},{1,3},{2,0},{3,1},{4,6},{5,7},{6,4},{7,5},{8,10},{9,11},{10,... | collective-permute-start | bytes 3538952 | tf_op jit(solution)/shard_map/ppermute | solution.py:36
  3.7 17.9 %collective-permute-start.1 = (bf16[768,384]{1,0:T(8,128)(2,1)}, bf16[768,384]{1,0:T(8,128)(2,1)S(1)}, u32[]{:S(2)}, u32[]{:S(2)}) collective-permute-start(bf16[768,384]{1,0:T(8,128)(2,1)} %param.6), channel_id=1, source_target_pairs={{1,4},{3,6},{4,1},{6,3},{9,12},{11,14},{12,9},{14,11},{17,20},{19,... | collective-permute-start | bytes 1769480 | tf_op jit(solution)/shard_map/ppermute | solution.py:36
  4.4 8.4 %collective-permute-start.8 = (bf16[384,384]{1,0:T(8,128)(2,1)}, bf16[384,384]{1,0:T(8,128)(2,1)}, u32[]{:S(2)}, u32[]{:S(2)}) collective-permute-start(bf16[384,384]{1,0:T(8,128)(2,1)} %refs_0_.1), channel_id=1, source_target_pairs={{0,8},{1,9},{2,10},{3,11},{4,12},{5,13},{6,14},{7,15},{8,0},{9,1},... | collective-permute-start | bytes 884744 | tf_op jit(solution)/shard_map/ppermute | solution.py:36
  6.0 15.6 %collective-permute-start.7 = (bf16[384,384]{1,0:T(8,128)(2,1)}, bf16[384,384]{1,0:T(8,128)(2,1)}, u32[]{:S(2)}, u32[]{:S(2)}) collective-permute-start(bf16[384,384]{1,0:T(8,128)(2,1)} %refs_0_.1), channel_id=1, source_target_pairs={{0,4},{1,5},{2,6},{3,7},{4,0},{5,1},{6,2},{7,3},{8,12},{9,13},{10,... | collective-permute-start | bytes 884744 | tf_op jit(solution)/shard_map/ppermute | solution.py:36
  8.8 29.8 %collective-permute-start.3 = (bf16[768,384]{1,0:T(8,128)(2,1)}, bf16[768,384]{1,0:T(8,128)(2,1)}, u32[]{:S(2)}, u32[]{:S(2)}) collective-permute-start(bf16[768,384]{1,0:T(8,128)(2,1)} %param.7), channel_id=1, source_target_pairs={{1,4},{3,6},{4,1},{6,3},{9,12},{11,14},{12,9},{14,11},{17,20},{19,... | collective-permute-start | bytes 1769480 | tf_op jit(solution)/shard_map/ppermute | solution.py:36
  12.8 25.9 %collective-permute-start = (bf16[768,384]{1,0:T(8,128)(2,1)}, bf16[768,384]{1,0:T(8,128)(2,1)S(1)}, u32[]{:S(2)}, u32[]{:S(2)}) collective-permute-start(bf16[768,384]{1,0:T(8,128)(2,1)} %qa.13), channel_id=1, source_target_pairs={{1,4},{3,6},{4,1},{6,3},{9,12},{11,14},{12,9},{14,11},{17,20},{19,... | collective-permute-start | bytes 1769480 | tf_op jit(solution)/shard_map/ppermute | solution.py:36
  21.6 43.8 %collective-permute-start.5 = (bf16[768,768]{1,0:T(8,128)(2,1)}, bf16[768,768]{1,0:T(8,128)(2,1)}, u32[]{:S(2)}, u32[]{:S(2)}) collective-permute-start(bf16[768,768]{1,0:T(8,128)(2,1)} %g0.1), channel_id=1, source_target_pairs={{0,1},{1,0},{2,3},{3,2},{4,5},{5,4},{6,7},{7,6},{8,9},{9,8},{10,11... | collective-permute-start | bytes 3538952 | tf_op jit(solution)/shard_map/ppermute | solution.py:36
  21.6 17.0 %collective-permute-start.9 = (bf16[384,384]{1,0:T(8,128)(2,1)}, bf16[384,384]{1,0:T(8,128)(2,1)}, u32[]{:S(2)}, u32[]{:S(2)}) collective-permute-start(bf16[384,384]{1,0:T(8,128)(2,1)} %refs_0_.1), channel_id=1, source_target_pairs={{0,16},{1,17},{2,18},{3,19},{4,20},{5,21},{6,22},{7,23},{8,24},{9,... | collective-permute-start | bytes 884744 | tf_op jit(solution)/shard_map/ppermute | solution.py:36
  30.0 49.4 %collective-permute-start.13 = (bf16[768,768]{1,0:T(8,128)(2,1)}, bf16[768,768]{1,0:T(8,128)(2,1)}, u32[]{:S(2)}, u32[]{:S(2)}) collective-permute-start(bf16[768,768]{1,0:T(8,128)(2,1)} %collective-permute-done.6.refs_5_), channel_id=1, source_target_pairs={{0,1},{1,0},{2,3},{3,2},{4,5},{5,4},{6,7},{7,6},{8,9},{9,8},{10,11... | collective-permute-start | bytes 3538952 | tf_op jit(solution)/shard_map/ppermute | solution.py:36
  31.1 36.4 %copy-start = (bf16[768,384]{1,0:T(8,128)(2,1)S(1)}, bf16[768,384]{1,0:T(8,128)(2,1)}, u32[]{:S(2)}) copy-start(bf16[768,384]{1,0:T(8,128)(2,1)} %qa.13) | copy-start | bytes 1769476
  38.5 16.1 %collective-permute-start.10 = (bf16[384,384]{1,0:T(8,128)(2,1)}, bf16[384,384]{1,0:T(8,128)(2,1)}, u32[]{:S(2)}, u32[]{:S(2)}) collective-permute-start(bf16[384,384]{1,0:T(8,128)(2,1)} %collective-permute-done.8.refs_7_), channel_id=1, source_target_pairs={{0,16},{1,17},{2,18},{3,19},{4,20},{5,21},{6,22},{7,23},{8,24},{9,... | collective-permute-start | bytes 884744 | tf_op jit(solution)/shard_map/ppermute | solution.py:36
  38.5 25.3 %collective-permute-start.2 = (bf16[768,384]{1,0:T(8,128)(2,1)S(1)}, bf16[768,384]{1,0:T(8,128)(2,1)S(1)}, u32[]{:S(2)}, u32[]{:S(2)}) collective-permute-start(bf16[768,384]{1,0:T(8,128)(2,1)S(1)} %broadcast_select_fusion.1.refs_0_.ko), channel_id=1, source_target_pairs={{0,1},{1,0},{2,3},{3,2},{4,5},{5,4},{6,7},{7,6},{8,9},{9,8},{10,11... | collective-permute-start | bytes 1769480 | tf_op jit(solution)/shard_map/ppermute | solution.py:36
  38.7 26.6 %collective-permute-start.4 = (bf16[768,384]{1,0:T(8,128)(2,1)S(1)}, bf16[768,384]{1,0:T(8,128)(2,1)S(1)}, u32[]{:S(2)}, u32[]{:S(2)}) collective-permute-start(bf16[768,384]{1,0:T(8,128)(2,1)S(1)} %broadcast_select_fusion.refs_2_.vo), channel_id=1, source_target_pairs={{0,1},{1,0},{2,3},{3,2},{4,5},{5,4},{6,7},{7,6},{8,9},{9,8},{10,11... | collective-permute-start | bytes 1769480 | tf_op jit(solution)/shard_map/ppermute | solution.py:36
  54.6 7.9 %collective-permute-start.14 = (bf16[384,384]{1,0:T(8,128)(2,1)}, bf16[384,384]{1,0:T(8,128)(2,1)S(1)}, u32[]{:S(2)}, u32[]{:S(2)}) collective-permute-start(bf16[384,384]{1,0:T(8,128)(2,1)} %collective-permute-done.7.refs_6_), channel_id=1, source_target_pairs={{0,8},{1,9},{2,10},{3,11},{4,12},{5,13},{6,14},{7,15},{8,0},{9,1},... | collective-permute-start | bytes 884744 | tf_op jit(solution)/shard_map/ppermute | solution.py:36
  62.6 0.7 copy-start.3
  63.3 20.3 %collective-permute-start.11 = (bf16[768,384]{1,0:T(8,128)(2,1)S(1)}, bf16[768,384]{1,0:T(8,128)(2,1)}, u32[]{:S(2)}, u32[]{:S(2)}) collective-permute-start(bf16[768,384]{1,0:T(8,128)(2,1)S(1)} %broadcast_select_fusion.1.refs_0_.ko), channel_id=1, source_target_pairs={{0,2},{1,8},{2,0},{3,10},{4,6},{5,12},{6,4},{7,14},{8,1},{9,16},{1... | collective-permute-start | bytes 1769480 | tf_op jit(solution)/shard_map/ppermute | solution.py:36
  63.8 19.7 %collective-permute-start.12 = (bf16[768,384]{1,0:T(8,128)(2,1)S(1)}, bf16[768,384]{1,0:T(8,128)(2,1)}, u32[]{:S(2)}, u32[]{:S(2)}) collective-permute-start(bf16[768,384]{1,0:T(8,128)(2,1)S(1)} %broadcast_select_fusion.refs_2_.vo), channel_id=1, source_target_pairs={{0,2},{1,8},{2,0},{3,10},{4,6},{5,12},{6,4},{7,14},{8,1},{9,16},{1... | collective-permute-start | bytes 1769480 | tf_op jit(solution)/shard_map/ppermute | solution.py:36
  65.3 10.2 %collective-permute-start.15 = (bf16[384,384]{1,0:T(8,128)(2,1)}, bf16[384,384]{1,0:T(8,128)(2,1)}, u32[]{:S(2)}, u32[]{:S(2)}) collective-permute-start(bf16[384,384]{1,0:T(8,128)(2,1)} %collective-permute-done.9.refs_8_), channel_id=1, source_target_pairs={{0,4},{1,5},{2,6},{3,7},{4,0},{5,1},{6,2},{7,3},{8,12},{9,13},{10,... | collective-permute-start | bytes 884744 | tf_op jit(solution)/shard_map/ppermute | solution.py:36
  65.4 13.9 %collective-permute-start.16 = (bf16[384,384]{1,0:T(8,128)(2,1)}, bf16[384,384]{1,0:T(8,128)(2,1)}, u32[]{:S(2)}, u32[]{:S(2)}) collective-permute-start(bf16[384,384]{1,0:T(8,128)(2,1)} %collective-permute-done.10.refs_9_), channel_id=1, source_target_pairs={{0,4},{1,5},{2,6},{3,7},{4,0},{5,1},{6,2},{7,3},{8,12},{9,13},{10,... | collective-permute-start | bytes 884744 | tf_op jit(solution)/shard_map/ppermute | solution.py:36
  67.5 11.8 %copy-start.1 = (bf16[768,768]{1,0:T(8,128)(2,1)S(1)}, bf16[768,768]{1,0:T(8,128)(2,1)}, u32[]{:S(2)}) copy-start(bf16[768,768]{1,0:T(8,128)(2,1)} %g0.1) | copy-start | bytes 3538948
  67.5 11.8 %copy-start.2 = (bf16[384,384]{1,0:T(8,128)(2,1)S(1)}, bf16[384,384]{1,0:T(8,128)(2,1)}, u32[]{:S(2)}) copy-start(bf16[384,384]{1,0:T(8,128)(2,1)} %refs_0_.1) | copy-start | bytes 884740
  67.5 11.8 %copy-start.4 = (bf16[384,384]{1,0:T(8,128)(2,1)S(1)}, bf16[384,384]{1,0:T(8,128)(2,1)}, u32[]{:S(2)}) copy-start(bf16[384,384]{1,0:T(8,128)(2,1)} %copy-done.3) | copy-start | bytes 884740
  82.9 7.0 %collective-permute-start.17 = (bf16[128,768]{1,0:T(8,128)(2,1)S(1)}, bf16[128,768]{1,0:T(8,128)(2,1)S(1)}, u32[]{:S(2)}, u32[]{:S(2)}) collective-permute-start(bf16[128,768]{1,0:T(8,128)(2,1)S(1)} %get-tuple-element.47.ga), channel_id=1, source_target_pairs={{0,2},{1,4},{2,0},{3,6},{4,1},{5,7},{6,3},{7,5},{8,10},{9,12},{10,... | collective-permute-start | bytes 589832 | tf_op jit(solution)/shard_map/ppermute | solution.py:36
  88.4 9.3 %collective-permute-start.18 = (bf16[256,768]{1,0:T(8,128)(2,1)S(1)}, bf16[256,768]{1,0:T(8,128)(2,1)S(1)}, u32[]{:S(2)}, u32[]{:S(2)}) collective-permute-start(bf16[256,768]{1,0:T(8,128)(2,1)S(1)} %get-tuple-element.52.ga), channel_id=1, source_target_pairs={{0,2},{1,4},{2,0},{3,6},{4,1},{5,7},{6,3},{7,5},{8,10},{9,12},{10,... | collective-permute-start | bytes 1179656 | tf_op jit(solution)/shard_map/ppermute | solution.py:36
  95.5 12.5 %collective-permute-start.22 = (bf16[768,256]{1,0:T(8,128)(2,1)S(1)}, bf16[768,256]{1,0:T(8,128)(2,1)S(1)}, u32[]{:S(2)}, u32[]{:S(2)}) collective-permute-start(bf16[768,256]{1,0:T(8,128)(2,1)S(1)} %get-tuple-element.59), channel_id=1, source_target_pairs={{0,1},{1,0},{2,3},{3,2},{4,5},{5,4},{6,7},{7,6},{8,9},{9,8},{10,11... | collective-permute-start | bytes 1179656 | tf_op jit(solution)/shard_map/ppermute | solution.py:36
  95.6 14.0 %collective-permute-start.23 = (bf16[768,256]{1,0:T(8,128)(2,1)S(1)}, bf16[768,256]{1,0:T(8,128)(2,1)S(1)}, u32[]{:S(2)}, u32[]{:S(2)}) collective-permute-start(bf16[768,256]{1,0:T(8,128)(2,1)S(1)} %get-tuple-element.60), channel_id=1, source_target_pairs={{0,2},{1,8},{2,0},{3,10},{4,6},{5,12},{6,4},{7,14},{8,1},{9,16},{1... | collective-permute-start | bytes 1179656 | tf_op jit(solution)/shard_map/ppermute | solution.py:36
  96.2 14.1 %collective-permute-start.19 = (bf16[768,128]{1,0:T(8,128)(2,1)S(1)}, bf16[768,128]{1,0:T(8,128)(2,1)S(1)}, u32[]{:S(2)}, u32[]{:S(2)}) collective-permute-start(bf16[768,128]{1,0:T(8,128)(2,1)S(1)} %get-tuple-element.51), channel_id=1, source_target_pairs={{0,8},{1,4},{2,10},{3,6},{4,1},{5,13},{6,3},{7,15},{8,0},{9,12},{1... | collective-permute-start | bytes 589832 | tf_op jit(solution)/shard_map/ppermute | solution.py:36
  104.4 14.0 %collective-permute-start.24 = (bf16[768,256]{1,0:T(8,128)(2,1)S(1)}, bf16[768,256]{1,0:T(8,128)(2,1)S(1)}, u32[]{:S(2)}, u32[]{:S(2)}) collective-permute-start(bf16[768,256]{1,0:T(8,128)(2,1)S(1)} %get-tuple-element.62), channel_id=1, source_target_pairs={{0,1},{1,0},{2,3},{3,2},{4,5},{5,4},{6,7},{7,6},{8,9},{9,8},{10,11... | collective-permute-start | bytes 1179656 | tf_op jit(solution)/shard_map/ppermute | solution.py:36
  104.4 13.9 %collective-permute-start.25 = (bf16[768,256]{1,0:T(8,128)(2,1)S(1)}, bf16[768,256]{1,0:T(8,128)(2,1)S(1)}, u32[]{:S(2)}, u32[]{:S(2)}) collective-permute-start(bf16[768,256]{1,0:T(8,128)(2,1)S(1)} %get-tuple-element.63), channel_id=1, source_target_pairs={{0,2},{1,8},{2,0},{3,10},{4,6},{5,12},{6,4},{7,14},{8,1},{9,16},{1... | collective-permute-start | bytes 1179656 | tf_op jit(solution)/shard_map/ppermute | solution.py:36
  108.0 6.4 %collective-permute-start.20 = (bf16[768,128]{1,0:T(8,128)(2,1)S(1)}, bf16[768,128]{1,0:T(8,128)(2,1)S(1)}, u32[]{:S(2)}, u32[]{:S(2)}) collective-permute-start(bf16[768,128]{1,0:T(8,128)(2,1)S(1)} %get-tuple-element.56), channel_id=1, source_target_pairs={{0,8},{1,4},{2,10},{3,6},{4,1},{5,13},{6,3},{7,15},{8,0},{9,12},{1... | collective-permute-start | bytes 589832 | tf_op jit(solution)/shard_map/ppermute | solution.py:36
  109.6 7.0 %collective-permute-start.21 = (bf16[768,128]{1,0:T(8,128)(2,1)S(1)}, bf16[768,128]{1,0:T(8,128)(2,1)S(1)}, u32[]{:S(2)}, u32[]{:S(2)}) collective-permute-start(bf16[768,128]{1,0:T(8,128)(2,1)S(1)} %get-tuple-element.57), channel_id=1, source_target_pairs={{0,8},{1,4},{2,10},{3,6},{4,1},{5,13},{6,3},{7,15},{8,0},{9,12},{1... | collective-permute-start | bytes 589832 | tf_op jit(solution)/shard_map/ppermute | solution.py:36
  110.3 9.5 %collective-permute-start.26 = (bf16[768,256]{1,0:T(8,128)(2,1)S(1)}, bf16[768,256]{1,0:T(8,128)(2,1)S(1)}, u32[]{:S(2)}, u32[]{:S(2)}) collective-permute-start(bf16[768,256]{1,0:T(8,128)(2,1)S(1)} %get-tuple-element.65), channel_id=1, source_target_pairs={{0,1},{1,0},{2,3},{3,2},{4,5},{5,4},{6,7},{7,6},{8,9},{9,8},{10,11... | collective-permute-start | bytes 1179656 | tf_op jit(solution)/shard_map/ppermute | solution.py:36
  114.4 7.8 %collective-permute-start.27 = (bf16[768,256]{1,0:T(8,128)(2,1)S(1)}, bf16[768,256]{1,0:T(8,128)(2,1)S(1)}, u32[]{:S(2)}, u32[]{:S(2)}) collective-permute-start(bf16[768,256]{1,0:T(8,128)(2,1)S(1)} %get-tuple-element.66), channel_id=1, source_target_pairs={{0,2},{1,8},{2,0},{3,10},{4,6},{5,12},{6,4},{7,14},{8,1},{9,16},{1... | collective-permute-start | bytes 1179656 | tf_op jit(solution)/shard_map/ppermute | solution.py:36
  116.5 9.9 %collective-permute-start.28 = (bf16[768,256]{1,0:T(8,128)(2,1)S(1)}, bf16[768,256]{1,0:T(8,128)(2,1)S(1)}, u32[]{:S(2)}, u32[]{:S(2)}) collective-permute-start(bf16[768,256]{1,0:T(8,128)(2,1)S(1)} %add_convert_fusion.2), channel_id=1, source_target_pairs={{0,2},{1,4},{2,0},{3,6},{4,1},{5,7},{6,3},{7,5},{8,10},{9,12},{10,... | collective-permute-start | bytes 1179656 | tf_op jit(solution)/shard_map/ppermute | solution.py:36
  118.5 12.2 %collective-permute-start.29 = (bf16[768,256]{1,0:T(8,128)(2,1)S(1)}, bf16[768,256]{1,0:T(8,128)(2,1)S(1)}, u32[]{:S(2)}, u32[]{:S(2)}) collective-permute-start(bf16[768,256]{1,0:T(8,128)(2,1)S(1)} %add_convert_fusion.1), channel_id=1, source_target_pairs={{0,2},{1,4},{2,0},{3,6},{4,1},{5,7},{6,3},{7,5},{8,10},{9,12},{10,... | collective-permute-start | bytes 1179656 | tf_op jit(solution)/shard_map/ppermute | solution.py:36
  122.4 12.5 %collective-permute-start.30 = (bf16[768,256]{1,0:T(8,128)(2,1)S(1)}, bf16[768,256]{1,0:T(8,128)(2,1)S(1)}, u32[]{:S(2)}, u32[]{:S(2)}) collective-permute-start(bf16[768,256]{1,0:T(8,128)(2,1)S(1)} %add_convert_fusion), channel_id=1, source_target_pairs={{0,2},{1,4},{2,0},{3,6},{4,1},{5,7},{6,3},{7,5},{8,10},{9,12},{10,... | collective-permute-start | bytes 1179656 | tf_op jit(solution)/shard_map/ppermute | solution.py:36
